TPU v7x, 256 devices: a whole 4x4x8 slice. The times are simulated.
256 devices in a mesh: grp: 4 (over x), req: 64 (over y, z, core).
Axes of the slice: x: 4, y: 4, z: 8, core: 2. Of those that a mesh axis runs over, the one named last changes fastest.
Arguments:
- mix_inputs: bfloat16 [512, 16, 8, 384], P('req', None, 'grp'), may hold values from -6 to 6
- conv_weight: float32 [4, 8, 384], P(None, 'grp'), may hold values from -3 to 3
- forget_bias: float32 [8, 128], P('grp'), may hold values from -2 to 4
- norm_gain: float32 [8, 128], P('grp'), may hold values from 0.1 to 1.9
- out_weight: bfloat16 [1024, 2048], P('grp'), may hold values from -0.1875 to 0.1875
- resid: bfloat16 [512, 16, 2048], P('req'), may hold values from -6 to 6
- ffn_gain: float32 [2048], replicated, may hold values from 0.1 to 1.9
- gate_weight: bfloat16 [2048, 2816], P(None, 'grp'), may hold values from -0.125 to 0.125
- up_weight: bfloat16 [2048, 2816], P(None, 'grp'), may hold values from -0.125 to 0.125
- down_weight: bfloat16 [2816, 2048], P('grp'), may hold values from -0.109375 to 0.109375
- held_states: float32 [512, 8, 128, 128], P('req', 'grp'), may hold values from -6 to 6
- held_edges: bfloat16 [512, 3, 8, 384], P('req', None, 'grp'), may hold values from -6 to 6
- draft_lengths: int32 [512], replicated, may hold values from 1 to 16, as said below
- accepted: int32 [512], replicated, may hold values from 1 to 16, as said below
- owner_row: int32 [512], replicated, may hold values from 0 to 511, as said below
Outputs:
- layer_out: bfloat16 [512, 16, 2048], P('req', None, 'grp')
- kept_states: float32 [512, 8, 128, 128], P('req', 'grp')
- kept_edges: bfloat16 [512, 3, 8, 384], P('req', None, 'grp')
Inputs may be any that keep to these rules, and one draw needn't show every extreme that they name: draft_lengths[i] + draft_lengths[i + 256] = 17 for i < 256, so the live tokens number 68 per index of req on average; the first 8 requests have 16 tokens each. accepted[i] lies between 1 and draft_lengths[i]. owner_row is a permutation made of pairwise swaps: a request among the last 4 of index d of req may take the row of a request among the first 4 of index d + 1 (modulo the size of req), which then takes its row; every other request keeps its own row. So at most 4 requests of one index take rows of one neighbour, and index 0 reaches that most in every draw.
All inputs are finite; a program needn't handle non-finite values.
Results may differ from a plain program's by a relative error of at most 0.017.
Values may be sent and summed in bfloat16 or wider, within the bound.
No kernel may reach another device: no remote copies, remote signals or barrier semaphores. Data moves between devices by JAX's collectives and lax.ppermute only.
A program may use at most 64 MiB of HBM per device.

v0:
```python
import jax
import jax.numpy as jnp
from jax import lax
from jax.sharding import PartitionSpec as P

DK = 128
DRAFT = 16
CONV = 4


def extended(block, sides, width):
    for axis, dim in sides:
        count = lax.axis_size(axis)
        forward = [(i, i + 1) for i in range(count - 1)]
        forward.append((count - 1, 0))
        backward = [(target, source) for source, target in forward]
        low = lax.ppermute(
            lax.slice_in_dim(block, block.shape[dim] - width, None, axis=dim), axis, forward
        )
        high = lax.ppermute(lax.slice_in_dim(block, 0, width, axis=dim), axis, backward)
        block = jnp.concatenate([low, block, high], axis=dim)
    return block


def run_mixer(
    draft_inputs, conv_edges, carried_over, conv_weight, forget_bias, norm_gain, accept_count
):
    window_bf = jnp.concatenate([conv_edges, draft_inputs], axis=1)
    window = window_bf.astype(jnp.float32)
    conv_out = conv_weight[0] * window[:, 0:DRAFT]
    for shift_pos in range(1, CONV):
        conv_out = conv_out + conv_weight[shift_pos] * window[:, shift_pos : shift_pos + DRAFT]
    queries = jax.nn.silu(conv_out[..., :DK]) * DK ** (-0.5)
    forget = jax.nn.sigmoid(conv_out[..., DK : 2 * DK] + forget_bias)
    values_in = jax.nn.silu(conv_out[..., 2 * DK :])
    accept_col = accept_count[:, None, None, None]

    def advance(carry, step_in):
        current_step, kept_state = carry
        present_query, forget_now, value_now, position = step_in
        current_step = (
            forget_now[..., None] * current_step
            + (1.0 - forget_now)[..., None] * value_now[:, :, None, :]
        )
        present_head = jnp.einsum(
            "rhk,rhkv->rhv", present_query, current_step, precision=lax.Precision.HIGHEST
        )
        kept_state = jnp.where(position == accept_col - 1, current_step, kept_state)
        return ((current_step, kept_state), present_head)

    positions = jnp.arange(DRAFT, dtype=jnp.int32)
    scanned = (
        jnp.moveaxis(queries, 1, 0),
        jnp.moveaxis(forget, 1, 0),
        jnp.moveaxis(values_in, 1, 0),
        positions,
    )
    (state_end, kept_state), head_outs = lax.scan(advance, (carried_over, carried_over), scanned)
    head_outs = jnp.moveaxis(head_outs, 0, 1)
    inverse_scale = lax.rsqrt(jnp.mean(head_outs * head_outs, axis=-1, keepdims=True) + 1e-05)
    mixed_out = (head_outs * inverse_scale * norm_gain).astype(jnp.bfloat16)
    edges_out = jax.vmap(
        lambda window_row, start_at: lax.dynamic_slice_in_dim(window_row, start_at, CONV - 1, 0)
    )(window_bf, accept_count)
    return (mixed_out, kept_state, edges_out)


def local_rows(global_rows, device_index, per_dev, req_count):
    holder_dev = global_rows // per_dev
    relative = (holder_dev - device_index + 1) % req_count
    return relative * per_dev + global_rows % per_dev


def pack_carry(carried_over, conv_edges):
    per_dev, edge_len, heads_per_device, channels = conv_edges.shape
    moved = jnp.transpose(conv_edges, (0, 2, 1, 3)).astype(jnp.float32)
    moved = moved.reshape(per_dev, heads_per_device, edge_len * channels // DK, DK)
    return jnp.concatenate([carried_over, moved], axis=2)


def unpack_carry(packed):
    per_dev, heads_per_device = (packed.shape[0], packed.shape[1])
    carried_over = packed[:, :, :DK]
    edge_part = packed[:, :, DK:].reshape(per_dev, heads_per_device, CONV - 1, 3 * DK)
    return (carried_over, jnp.transpose(edge_part, (0, 2, 1, 3)).astype(jnp.bfloat16))


def states_near(packed, per_dev):
    return extended(packed, (("req", 0),), per_dev)


def feed_forward(normed, gate_weight, up_weight, down_weight):
    gate_pre = jnp.dot(normed, gate_weight, preferred_element_type=jnp.float32)
    up_pre = jnp.dot(normed, up_weight, preferred_element_type=jnp.float32)
    hidden = (jax.nn.silu(gate_pre) * up_pre).astype(jnp.bfloat16)
    partial_value = jnp.dot(hidden, down_weight, preferred_element_type=jnp.float32)
    return lax.psum_scatter(
        partial_value.astype(jnp.bfloat16), "grp", scatter_dimension=1, tiled=True
    )


def shards(
    mix_inputs,
    conv_weight,
    forget_bias,
    norm_gain,
    out_weight,
    resid,
    ffn_gain,
    gate_weight,
    up_weight,
    down_weight,
    held_states,
    held_edges,
    draft_lengths,
    accepted,
    owner_row,
):
    per_dev = mix_inputs.shape[0]
    req_count = lax.axis_size("req")
    device_index = lax.axis_index("req")
    all_requests = draft_lengths.shape[0]
    request_ids = jnp.arange(all_requests, dtype=jnp.int32)
    own_rows = device_index * per_dev + jnp.arange(per_dev, dtype=jnp.int32)
    inverse = jnp.zeros((all_requests,), jnp.int32).at[owner_row].set(request_ids)
    nearby = states_near(pack_carry(held_states, held_edges), per_dev)
    picked = nearby[local_rows(owner_row[own_rows], device_index, per_dev, req_count)]
    carried_over, conv_edges = unpack_carry(picked)
    mixed_out, kept_here, edges_here = run_mixer(
        mix_inputs,
        conv_edges,
        carried_over,
        conv_weight,
        forget_bias,
        norm_gain,
        accepted[own_rows],
    )
    returned = states_near(pack_carry(kept_here, edges_here), per_dev)
    kept_states, kept_edges = unpack_carry(
        returned[local_rows(inverse[own_rows], device_index, per_dev, req_count)]
    )
    slot_count = per_dev * DRAFT
    model_width = resid.shape[2]
    slice_width = model_width // lax.axis_size("grp")
    col_start = lax.axis_index("grp") * slice_width
    resid_rows = resid.reshape(slot_count, model_width)
    partial_value = jnp.dot(
        mixed_out.reshape(slot_count, -1), out_weight, preferred_element_type=jnp.float32
    )
    projected = lax.psum(partial_value, "grp")
    stream = (resid_rows.astype(jnp.float32) + projected).astype(jnp.bfloat16)
    stream_f = stream.astype(jnp.float32)
    mean_sq = jnp.mean(stream_f * stream_f, axis=-1, keepdims=True)
    normed = (stream_f * lax.rsqrt(mean_sq + 1e-05) * ffn_gain).astype(jnp.bfloat16)
    stream_part = lax.dynamic_slice_in_dim(stream_f, col_start, slice_width, 1)
    live_all = jnp.arange(DRAFT, dtype=jnp.int32)[None, :] < draft_lengths[:, None]
    live_mask = live_all.reshape(req_count, slot_count)[device_index]
    down_rows = feed_forward(normed, gate_weight, up_weight, down_weight)
    summed = (stream_part + down_rows.astype(jnp.float32)).astype(jnp.bfloat16)
    layer_out = jnp.where(live_mask[:, None], summed, jnp.zeros_like(summed)).reshape(
        per_dev, DRAFT, slice_width
    )
    return (layer_out, kept_states, kept_edges)


def solution(mesh):
    return jax.shard_map(
        shards,
        mesh=mesh,
        in_specs=(
            P("req", None, "grp", None),
            P(None, "grp", None),
            P("grp", None),
            P("grp", None),
            P("grp", None),
            P("req", None, None),
            P(),
            P(None, "grp"),
            P(None, "grp"),
            P("grp", None),
            P("req", "grp", None, None),
            P("req", None, "grp", None),
            P(),
            P(),
            P(),
        ),
        out_specs=(P("req", None, "grp"), P("req", "grp", None, None), P("req", None, "grp", None)),
        check_vma=False,
    )
```

profile of v0, /device:TPU:6, one launch (start us, length us, event | category | flops | bytes accessed | tf_op | source)
XLA Modules:
  0.0 263.2 jit_solution(12973487423842821497)
XLA Ops:
  8.2 2.1 copy.103
  12.9 7.7 %collective-permute-start.1 = (f32[8,2,137,128]{3,0,2,1:T(8,128)}, f32[8,2,137,128]{3,0,2,1:T(8,128)}, u32[]{:S(2)}, u32[]{:S(2)}) collective-permute-start(f32[8,2,137,128]{3,0,2,1:T(8,128)} %copy.105), channel_id=1, source_target_pairs={{1,0},{2,1},{3,2},{4,3},{5,4},{6,5},{7,6},{8,7},{9,8},{10,9},{11,1... | collective-permute-start | bytes 3366920 | tf_op jit(solution)/shard_map/ppermute | solution.py:20
  22.1 12.0 %collective-permute-done.1 = f32[8,2,137,128]{3,0,2,1:T(8,128)} collective-permute-done((f32[8,2,137,128]{3,0,2,1:T(8,128)}, f32[8,2,137,128]{3,0,2,1:T(8,128)}, u32[]{:S(2)}, u32[]{:S(2)}) %collective-permute-start.1) | collective-permute-done | bytes 1122336 | tf_op jit(solution)/shard_map/ppermute | solution.py:20
  35.9 3.4 %collective-permute-done = f32[8,2,137,128]{3,0,2,1:T(8,128)} collective-permute-done((f32[8,2,137,128]{3,0,2,1:T(8,128)}, f32[8,2,137,128]{3,0,2,1:T(8,128)}, u32[]{:S(2)}, u32[]{:S(2)}) %collective-permute-start) | collective-permute-done | bytes 1122336 | tf_op jit(solution)/shard_map/ppermute | solution.py:17
  41.1 3.4 %pad_maximum_fusion = f32[24,2,137,128]{3,1,2,0:T(2,128)} fusion(f32[8,2,137,128]{3,1,2,0:T(2,128)S(1)} %copy.108, f32[8,2,9,128]{3,1,2,0:T(2,128)S(1)} %bitcast.131, f32[8,2,128,128]{3,1,2,0:T(2,128)S(1)} %copy-done.7, f32[8,2,137,128]{3,1,2,0:T(2,128)S(1)} %copy.107), kind=kLoop, calls=%fused_computation.18 | loop fusion | flops 2525184 | bytes 6733824 | tf_op jit(solution)/shard_map/concatenate | solution.py:21
  44.5 4.6 %gather_fusion.1 = f32[8,2,137,128]{3,1,2,0:T(2,128)} fusion(f32[24,2,137,128]{3,1,2,0:T(2,128)} %pad_maximum_fusion, s32[1024]{0:T(1024)S(1)} %pad_clamp_fusion.1), kind=kCustom, calls=%fused_computation.1 | custom fusion | bytes 2244640 | tf_op jit(solution)/shard_map/gather | solution.py:127
  55.0 116.7 %while.16 = (s32[]{:T(128)}, f32[8,2,128,128]{3,2,1,0:T(8,128)}, f32[8,2,128,128]{3,2,1,0:T(8,128)}, f32[16,8,2,128]{3,2,1,0:T(2,128)S(1)}, f32[16,8,2,128]{3,0,...) while((s32[]{:T(128)}, f32[8,2,128,128]{3,2,1,0:T(8,128)}, ...), condition=%wide.region_1.2_spmd, body=%wide.region_0.0_spmd.sunk | while | flops 4196370 | bytes 5349561 | solution.py:58
  57.2 2.9 %broadcast_select_fusion.2 = (f32[8,2,128,128]{3,2,1,0:T(8,128)}, f32[8,2,128,128]{3,2,1,0:T(8,128)}) fusion(f32[8,2,128,128]{3,2,1,0:T(8,128)} %get-tuple-element.281, pred[8]{0:T(512)(128)(4,1)S(1)} %compare_bitcast_fusion.2, f32[8,2,128]{2,1,0:T(2,128)S(1)} %bitcast.127, f32[8,2,128]{2,1,0:T(2,128)S(1)} %broadcast_subtract_fusion.2, ...), kind=kLoop, calls=%fused_computation.8.clone.1 | loop fusion | flops 1048576 | bytes 4218888 | tf_op jit(solution)/shard_map/while/body/eval_jaxpr/jit(_where)/select_n | solution.py:48
  60.1 2.2 fusion.58
  64.5 2.9 %broadcast_select_fusion.2 = (f32[8,2,128,128]{3,2,1,0:T(8,128)}, f32[8,2,128,128]{3,2,1,0:T(8,128)}) fusion(f32[8,2,128,128]{3,2,1,0:T(8,128)} %get-tuple-element.281, pred[8]{0:T(512)(128)(4,1)S(1)} %compare_bitcast_fusion.2, f32[8,2,128]{2,1,0:T(2,128)S(1)} %bitcast.127, f32[8,2,128]{2,1,0:T(2,128)S(1)} %broadcast_subtract_fusion.2, ...), kind=kLoop, calls=%fused_computation.8.clone.1 | loop fusion | flops 1048576 | bytes 4218888 | tf_op jit(solution)/shard_map/while/body/eval_jaxpr/jit(_where)/select_n | solution.py:48
  67.4 2.2 fusion.58
  71.8 2.9 %broadcast_select_fusion.2 = (f32[8,2,128,128]{3,2,1,0:T(8,128)}, f32[8,2,128,128]{3,2,1,0:T(8,128)}) fusion(f32[8,2,128,128]{3,2,1,0:T(8,128)} %get-tuple-element.281, pred[8]{0:T(512)(128)(4,1)S(1)} %compare_bitcast_fusion.2, f32[8,2,128]{2,1,0:T(2,128)S(1)} %bitcast.127, f32[8,2,128]{2,1,0:T(2,128)S(1)} %broadcast_subtract_fusion.2, ...), kind=kLoop, calls=%fused_computation.8.clone.1 | loop fusion | flops 1048576 | bytes 4218888 | tf_op jit(solution)/shard_map/while/body/eval_jaxpr/jit(_where)/select_n | solution.py:48
  74.7 2.2 fusion.58
  79.1 2.9 %broadcast_select_fusion.2 = (f32[8,2,128,128]{3,2,1,0:T(8,128)}, f32[8,2,128,128]{3,2,1,0:T(8,128)}) fusion(f32[8,2,128,128]{3,2,1,0:T(8,128)} %get-tuple-element.281, pred[8]{0:T(512)(128)(4,1)S(1)} %compare_bitcast_fusion.2, f32[8,2,128]{2,1,0:T(2,128)S(1)} %bitcast.127, f32[8,2,128]{2,1,0:T(2,128)S(1)} %broadcast_subtract_fusion.2, ...), kind=kLoop, calls=%fused_computation.8.clone.1 | loop fusion | flops 1048576 | bytes 4218888 | tf_op jit(solution)/shard_map/while/body/eval_jaxpr/jit(_where)/select_n | solution.py:48
  82.0 2.2 fusion.58
  86.4 2.9 %broadcast_select_fusion.2 = (f32[8,2,128,128]{3,2,1,0:T(8,128)}, f32[8,2,128,128]{3,2,1,0:T(8,128)}) fusion(f32[8,2,128,128]{3,2,1,0:T(8,128)} %get-tuple-element.281, pred[8]{0:T(512)(128)(4,1)S(1)} %compare_bitcast_fusion.2, f32[8,2,128]{2,1,0:T(2,128)S(1)} %bitcast.127, f32[8,2,128]{2,1,0:T(2,128)S(1)} %broadcast_subtract_fusion.2, ...), kind=kLoop, calls=%fused_computation.8.clone.1 | loop fusion | flops 1048576 | bytes 4218888 | tf_op jit(solution)/shard_map/while/body/eval_jaxpr/jit(_where)/select_n | solution.py:48
  89.3 2.2 fusion.58
  93.7 2.9 %broadcast_select_fusion.2 = (f32[8,2,128,128]{3,2,1,0:T(8,128)}, f32[8,2,128,128]{3,2,1,0:T(8,128)}) fusion(f32[8,2,128,128]{3,2,1,0:T(8,128)} %get-tuple-element.281, pred[8]{0:T(512)(128)(4,1)S(1)} %compare_bitcast_fusion.2, f32[8,2,128]{2,1,0:T(2,128)S(1)} %bitcast.127, f32[8,2,128]{2,1,0:T(2,128)S(1)} %broadcast_subtract_fusion.2, ...), kind=kLoop, calls=%fused_computation.8.clone.1 | loop fusion | flops 1048576 | bytes 4218888 | tf_op jit(solution)/shard_map/while/body/eval_jaxpr/jit(_where)/select_n | solution.py:48
  96.6 2.2 fusion.58
  100.9 2.9 %broadcast_select_fusion.2 = (f32[8,2,128,128]{3,2,1,0:T(8,128)}, f32[8,2,128,128]{3,2,1,0:T(8,128)}) fusion(f32[8,2,128,128]{3,2,1,0:T(8,128)} %get-tuple-element.281, pred[8]{0:T(512)(128)(4,1)S(1)} %compare_bitcast_fusion.2, f32[8,2,128]{2,1,0:T(2,128)S(1)} %bitcast.127, f32[8,2,128]{2,1,0:T(2,128)S(1)} %broadcast_subtract_fusion.2, ...), kind=kLoop, calls=%fused_computation.8.clone.1 | loop fusion | flops 1048576 | bytes 4218888 | tf_op jit(solution)/shard_map/while/body/eval_jaxpr/jit(_where)/select_n | solution.py:48
  103.9 2.2 fusion.58
  108.2 2.9 %broadcast_select_fusion.2 = (f32[8,2,128,128]{3,2,1,0:T(8,128)}, f32[8,2,128,128]{3,2,1,0:T(8,128)}) fusion(f32[8,2,128,128]{3,2,1,0:T(8,128)} %get-tuple-element.281, pred[8]{0:T(512)(128)(4,1)S(1)} %compare_bitcast_fusion.2, f32[8,2,128]{2,1,0:T(2,128)S(1)} %bitcast.127, f32[8,2,128]{2,1,0:T(2,128)S(1)} %broadcast_subtract_fusion.2, ...), kind=kLoop, calls=%fused_computation.8.clone.1 | loop fusion | flops 1048576 | bytes 4218888 | tf_op jit(solution)/shard_map/while/body/eval_jaxpr/jit(_where)/select_n | solution.py:48
  111.1 2.2 fusion.58
  115.5 2.9 %broadcast_select_fusion.2 = (f32[8,2,128,128]{3,2,1,0:T(8,128)}, f32[8,2,128,128]{3,2,1,0:T(8,128)}) fusion(f32[8,2,128,128]{3,2,1,0:T(8,128)} %get-tuple-element.281, pred[8]{0:T(512)(128)(4,1)S(1)} %compare_bitcast_fusion.2, f32[8,2,128]{2,1,0:T(2,128)S(1)} %bitcast.127, f32[8,2,128]{2,1,0:T(2,128)S(1)} %broadcast_subtract_fusion.2, ...), kind=kLoop, calls=%fused_computation.8.clone.1 | loop fusion | flops 1048576 | bytes 4218888 | tf_op jit(solution)/shard_map/while/body/eval_jaxpr/jit(_where)/select_n | solution.py:48
  118.4 2.2 fusion.58
  122.8 2.9 %broadcast_select_fusion.2 = (f32[8,2,128,128]{3,2,1,0:T(8,128)}, f32[8,2,128,128]{3,2,1,0:T(8,128)}) fusion(f32[8,2,128,128]{3,2,1,0:T(8,128)} %get-tuple-element.281, pred[8]{0:T(512)(128)(4,1)S(1)} %compare_bitcast_fusion.2, f32[8,2,128]{2,1,0:T(2,128)S(1)} %bitcast.127, f32[8,2,128]{2,1,0:T(2,128)S(1)} %broadcast_subtract_fusion.2, ...), kind=kLoop, calls=%fused_computation.8.clone.1 | loop fusion | flops 1048576 | bytes 4218888 | tf_op jit(solution)/shard_map/while/body/eval_jaxpr/jit(_where)/select_n | solution.py:48
  125.7 2.2 fusion.58
  130.1 2.9 %broadcast_select_fusion.2 = (f32[8,2,128,128]{3,2,1,0:T(8,128)}, f32[8,2,128,128]{3,2,1,0:T(8,128)}) fusion(f32[8,2,128,128]{3,2,1,0:T(8,128)} %get-tuple-element.281, pred[8]{0:T(512)(128)(4,1)S(1)} %compare_bitcast_fusion.2, f32[8,2,128]{2,1,0:T(2,128)S(1)} %bitcast.127, f32[8,2,128]{2,1,0:T(2,128)S(1)} %broadcast_subtract_fusion.2, ...), kind=kLoop, calls=%fused_computation.8.clone.1 | loop fusion | flops 1048576 | bytes 4218888 | tf_op jit(solution)/shard_map/while/body/eval_jaxpr/jit(_where)/select_n | solution.py:48
  133.0 2.2 fusion.58
  137.4 2.9 %broadcast_select_fusion.2 = (f32[8,2,128,128]{3,2,1,0:T(8,128)}, f32[8,2,128,128]{3,2,1,0:T(8,128)}) fusion(f32[8,2,128,128]{3,2,1,0:T(8,128)} %get-tuple-element.281, pred[8]{0:T(512)(128)(4,1)S(1)} %compare_bitcast_fusion.2, f32[8,2,128]{2,1,0:T(2,128)S(1)} %bitcast.127, f32[8,2,128]{2,1,0:T(2,128)S(1)} %broadcast_subtract_fusion.2, ...), kind=kLoop, calls=%fused_computation.8.clone.1 | loop fusion | flops 1048576 | bytes 4218888 | tf_op jit(solution)/shard_map/while/body/eval_jaxpr/jit(_where)/select_n | solution.py:48
  140.3 2.2 fusion.58
  144.7 2.9 %broadcast_select_fusion.2 = (f32[8,2,128,128]{3,2,1,0:T(8,128)}, f32[8,2,128,128]{3,2,1,0:T(8,128)}) fusion(f32[8,2,128,128]{3,2,1,0:T(8,128)} %get-tuple-element.281, pred[8]{0:T(512)(128)(4,1)S(1)} %compare_bitcast_fusion.2, f32[8,2,128]{2,1,0:T(2,128)S(1)} %bitcast.127, f32[8,2,128]{2,1,0:T(2,128)S(1)} %broadcast_subtract_fusion.2, ...), kind=kLoop, calls=%fused_computation.8.clone.1 | loop fusion | flops 1048576 | bytes 4218888 | tf_op jit(solution)/shard_map/while/body/eval_jaxpr/jit(_where)/select_n | solution.py:48
  147.6 2.2 fusion.58
  152.0 2.9 %broadcast_select_fusion.2 = (f32[8,2,128,128]{3,2,1,0:T(8,128)}, f32[8,2,128,128]{3,2,1,0:T(8,128)}) fusion(f32[8,2,128,128]{3,2,1,0:T(8,128)} %get-tuple-element.281, pred[8]{0:T(512)(128)(4,1)S(1)} %compare_bitcast_fusion.2, f32[8,2,128]{2,1,0:T(2,128)S(1)} %bitcast.127, f32[8,2,128]{2,1,0:T(2,128)S(1)} %broadcast_subtract_fusion.2, ...), kind=kLoop, calls=%fused_computation.8.clone.1 | loop fusion | flops 1048576 | bytes 4218888 | tf_op jit(solution)/shard_map/while/body/eval_jaxpr/jit(_where)/select_n | solution.py:48
  154.9 2.2 fusion.58
  159.3 2.9 %broadcast_select_fusion.2 = (f32[8,2,128,128]{3,2,1,0:T(8,128)}, f32[8,2,128,128]{3,2,1,0:T(8,128)}) fusion(f32[8,2,128,128]{3,2,1,0:T(8,128)} %get-tuple-element.281, pred[8]{0:T(512)(128)(4,1)S(1)} %compare_bitcast_fusion.2, f32[8,2,128]{2,1,0:T(2,128)S(1)} %bitcast.127, f32[8,2,128]{2,1,0:T(2,128)S(1)} %broadcast_subtract_fusion.2, ...), kind=kLoop, calls=%fused_computation.8.clone.1 | loop fusion | flops 1048576 | bytes 4218888 | tf_op jit(solution)/shard_map/while/body/eval_jaxpr/jit(_where)/select_n | solution.py:48
  162.2 2.2 fusion.58
  166.6 2.9 %broadcast_select_fusion.2 = (f32[8,2,128,128]{3,2,1,0:T(8,128)}, f32[8,2,128,128]{3,2,1,0:T(8,128)}) fusion(f32[8,2,128,128]{3,2,1,0:T(8,128)} %get-tuple-element.281, pred[8]{0:T(512)(128)(4,1)S(1)} %compare_bitcast_fusion.2, f32[8,2,128]{2,1,0:T(2,128)S(1)} %bitcast.127, f32[8,2,128]{2,1,0:T(2,128)S(1)} %broadcast_subtract_fusion.2, ...), kind=kLoop, calls=%fused_computation.8.clone.1 | loop fusion | flops 1048576 | bytes 4218888 | tf_op jit(solution)/shard_map/while/body/eval_jaxpr/jit(_where)/select_n | solution.py:48
  169.5 2.2 fusion.58
  172.5 2.5 fusion.25
  175.3 2.6 scatter_custom_fusion
  179.7 2.1 copy.121
  186.1 34.2 %all-reduce.3.cloned.1.call-done = f32[128,2048]{1,0:T(8,128)} async-done(((f32[128,2048]{1,0:T(8,128)}), f32[128,2048]{1,0:T(8,128)}) %all-reduce.3.cloned.1.call-update) | async-done | bytes 1048592 | tf_op jit(solution)/shard_map/psum | solution.py:150
  222.8 2.8 %fusion.46 = f32[128,704]{0,1:T(8,128)S(1)} fusion(bf16[2048,704]{0,1:T(8,128)(2,1)} %param.24, f32[128,2048]{1,0:T(8,128)S(1)} %get-tuple-element.194, f32[2048]{0:T(1024)S(1)} %copy-done.9, f32[128]{0:T(128)S(1)} %add_rsqrt_fusion.1), kind=kOutput, calls=%fused_computation.115 | convolution fusion | flops 369885184 | bytes 4301312 | tf_op jit(solution)/shard_map/dot_general | solution.py:93
  225.6 5.2 %convolution_convert_fusion = bf16[128,2048]{1,0:T(8,128)(2,1)} fusion(bf16[704,2048]{1,0:T(8,128)(2,1)S(1)} %copy-done, bf16[2048,704]{0,1:T(8,128)(2,1)} %param.25, f32[128,704]{0,1:T(8,128)S(1)} %fusion.46, f32[128,2048]{1,0:T(8,128)} %copy-done.4, f32[2048]{0:T(1024)S(1)} %copy-done.9, f32[128]{0:T(128)S(1)} %add_rsqrt_fusion.1), kind=kOutput, calls=%fused_computation.20 | convolution fusion | flops 739786752 | bytes 7709184 | tf_op jit(solution)/shard_map/dot_general | solution.py:96
  230.9 5.3 %pad_maximum_fusion.1 = f32[24,2,137,128]{3,1,2,0:T(2,128)} fusion(f32[8,2,137,128]{3,1,2,0:T(2,128)} %collective-permute-done.3, f32[8,2,9,128]{3,1,2,0:T(2,128)S(1)} %bitcast.129, f32[8,2,128,128]{3,1,2,0:T(2,128)} %copy-done.5, f32[8,2,137,128]{3,1,2,0:T(2,128)} %collective-permute-done.2), kind=kLoop, calls=%fused_computation.19 | loop fusion | flops 2525184 | bytes 6733824 | tf_op jit(solution)/shard_map/concatenate | solution.py:21
  236.2 4.6 %gather_fusion.4 = f32[8,2,137,128]{3,1,2,0:T(2,128)} fusion(f32[24,2,137,128]{3,1,2,0:T(2,128)} %pad_maximum_fusion.1, s32[1024]{0:T(1024)S(1)} %pad_clamp_fusion), kind=kCustom, calls=%fused_computation.4 | custom fusion | bytes 2244640 | tf_op jit(solution)/shard_map/gather | solution.py:140
  243.9 10.8 %reduce-scatter.2.cloned.1.call-done = bf16[128,512]{1,0:T(8,128)(2,1)} async-done(((bf16[128,2048]{1,0:T(8,128)(2,1)}), bf16[128,512]{1,0:T(8,128)(2,1)}) %reduce-scatter.2.cloned.1.call-update) | async-done | bytes 131088 | tf_op jit(solution)/shard_map/reduce_scatter | solution.py:97
  (174 shorter events, 63.8 us)
Async XLA Ops:
  7.2 218.5 %copy-start = (bf16[704,2048]{1,0:T(8,128)(2,1)S(1)}, bf16[704,2048]{1,0:T(8,128)(2,1)}, u32[]{:S(2)}) copy-start(bf16[704,2048]{1,0:T(8,128)(2,1)} %param.26) | copy-start | bytes 8650756
  7.2 213.1 %all-reduce.3.cloned.1.call-start = ((), (), s32[]{:S(2)}) async-start(), calls=%async_computation.1 | async-start | bytes 2097152 | tf_op jit(solution)/shard_map/psum | solution.py:150
  8.2 12.4 %copy-start.8 = (bf16[8,16,2,384]{3,2,1,0:T(2,128)(2,1)S(1)}, bf16[8,16,2,384]{3,2,1,0:T(2,128)(2,1)}, u32[]{:S(2)}) copy-start(bf16[8,16,2,384]{3,2,1,0:T(2,128)(2,1)} %param.17) | copy-start | bytes 589828
  10.3 1.0 copy-start.6
  10.3 10.4 %copy-start.2 = (s32[512]{0:T(512)S(1)}, s32[512]{0:T(512)}, u32[]{:S(2)}) copy-start(s32[512]{0:T(512)} %param.31) | copy-start | bytes 6148
  10.3 11.0 %copy-start.3 = (s32[512]{0:T(512)S(1)}, s32[512]{0:T(512)}, u32[]{:S(2)}) copy-start(s32[512]{0:T(512)} %param.30) | copy-start | bytes 6148
  11.2 10.8 %copy-start.10 = (f32[4,2,384]{2,1,0:T(2,128)S(1)}, f32[4,2,384]{2,1,0:T(2,128)}, u32[]{:S(2)}) copy-start(f32[4,2,384]{2,1,0:T(2,128)} %param.18) | copy-start | bytes 36868
  12.9 21.2 %collective-permute-start.1 = (f32[8,2,137,128]{3,0,2,1:T(8,128)}, f32[8,2,137,128]{3,0,2,1:T(8,128)}, u32[]{:S(2)}, u32[]{:S(2)}) collective-permute-start(f32[8,2,137,128]{3,0,2,1:T(8,128)} %copy.105), channel_id=1, source_target_pairs={{1,0},{2,1},{3,2},{4,3},{5,4},{6,5},{7,6},{8,7},{9,8},{10,9},{11,1... | collective-permute-start | bytes 3366920 | tf_op jit(solution)/shard_map/ppermute | solution.py:20
  20.6 18.6 %collective-permute-start = (f32[8,2,137,128]{3,0,2,1:T(8,128)}, f32[8,2,137,128]{3,0,2,1:T(8,128)}, u32[]{:S(2)}, u32[]{:S(2)}) collective-permute-start(f32[8,2,137,128]{3,0,2,1:T(8,128)} %copy.105), channel_id=1, source_target_pairs={{0,1},{1,2},{2,3},{3,4},{4,5},{5,6},{6,7},{7,8},{8,9},{9,10},{10,1... | collective-permute-start | bytes 3366920 | tf_op jit(solution)/shard_map/ppermute | solution.py:17
  22.0 19.1 %copy-start.7 = (f32[8,2,128,128]{3,1,2,0:T(2,128)S(1)}, f32[8,2,128,128]{3,1,2,0:T(2,128)}, u32[]{:S(2)}) copy-start(f32[8,2,128,128]{3,1,2,0:T(2,128)} %copy-done.6) | copy-start | bytes 3145732
  49.1 1.3 slice-start
  50.5 1.0 copy-start.1
  51.4 2.7 %copy-start.12 = (f32[2,128]{1,0:T(2,128)S(1)}, f32[2,128]{1,0:T(2,128)}, u32[]{:S(2)}) copy-start(f32[2,128]{1,0:T(2,128)} %param.19) | copy-start | bytes 3076
  55.0 117.2 %copy-start.13 = (f32[2,128]{1,0:T(2,128)S(1)}, f32[2,128]{1,0:T(2,128)}, u32[]{:S(2)}) copy-start(f32[2,128]{1,0:T(2,128)} %param.20) | copy-start | bytes 3076
  171.7 3.4 %copy-start.11 = (s32[512]{0:T(512)S(1)}, s32[512]{0:T(512)}, u32[]{:S(2)}) copy-start(s32[512]{0:T(512)} %param.29) | copy-start | bytes 6148
  175.0 79.6 %reduce-scatter.2.cloned.1.call-start = ((), (), s32[]{:S(2)}) async-start(), calls=%async_computation.2 | async-start | bytes 655360 | tf_op jit(solution)/shard_map/reduce_scatter | solution.py:97
  181.8 1.0 copy-start.5
  181.8 41.0 %copy-start.9 = (f32[2048]{0:T(1024)S(1)}, f32[2048]{0:T(1024)}, u32[]{:S(2)}) copy-start(f32[2048]{0:T(1024)} %param.23) | copy-start | bytes 24580
  184.2 46.6 %collective-permute-start.3 = (f32[8,2,137,128]{3,1,2,0:T(2,128)}, f32[8,2,137,128]{3,1,2,0:T(2,128)}, u32[]{:S(2)}, u32[]{:S(2)}) collective-permute-start(f32[8,2,137,128]{3,1,2,0:T(2,128)} %pad_maximum_fusion.3), channel_id=1, source_target_pairs={{1,0},{2,1},{3,2},{4,3},{5,4},{6,5},{7,6},{8,7},{9,8},{10,9},{11,1... | collective-permute-start | bytes 3366920 | tf_op jit(solution)/shard_map/ppermute | solution.py:20
  186.1 44.8 %collective-permute-start.2 = (f32[8,2,137,128]{3,1,2,0:T(2,128)}, f32[8,2,137,128]{3,1,2,0:T(2,128)}, u32[]{:S(2)}, u32[]{:S(2)}) collective-permute-start(f32[8,2,137,128]{3,1,2,0:T(2,128)} %pad_maximum_fusion.3), channel_id=1, source_target_pairs={{0,1},{1,2},{2,3},{3,4},{4,5},{5,6},{6,7},{7,8},{8,9},{9,10},{10,1... | collective-permute-start | bytes 3366920 | tf_op jit(solution)/shard_map/ppermute | solution.py:17
  221.8 1.0 copy-start.4
  240.8 1.3 slice-start.1
Sparse Core Ops, SparseCore 0:
  175.1 45.0 all-reduce.2
  230.9 23.6 reduce-scatter.1
where the time goes:
time: 268 us; the launch traced here: 263 us
  other arithmetic  74.2 us (28%)
  waiting for transfers between devices  60.3 us (22%)
  local copies, waits for them, and re-layouts  58.9 us (22%)
  matrix products  45.4 us (17%)
  between operations  14.4 us (5%)
  starting transfers between devices  9.65 us (4%)
    select_n x16, other arithmetic, advance(): kept_state = jnp.where(position == accept_col - 1, current_step, kept_state)  46.5 us
    dot_general x16, matrix products, advance(): jnp.einsum('rhk,rhkv->rhv', present_query, current_step, precision=lax.Pr...  34.9 us
    psum x1, waiting for transfers between devices, shards(): projected = lax.psum(partial_value, 'grp')  34.2 us
    dynamic_slice x32, local copies, waits for them, and re-layouts, run_mixer(): lax.scan(advance, (carried_over, carried_over), scanned)  24.7 us
    ppermute x2, waiting for transfers between devices, extended(): lax.ppermute(lax.slice_in_dim(block, 0, width, axis=dim), axis, backward)  12 us
    reduce_scatter x1, waiting for transfers between devices, feed_forward(): lax.psum_scatter(partial_value.astype(jnp.bfloat16), 'grp', scatter_dimen...  10.8 us
    eq x16, other arithmetic, advance(): kept_state = jnp.where(position == accept_col - 1, current_step, kept_state)  9.97 us
    ppermute x2, starting transfers between devices, extended(): lax.ppermute(lax.slice_in_dim(block, 0, width, axis=dim), axis, backward)  9.57 us
  transfers between devices with their start and end apart: 6, of which 4 were waited for; matrix products, arithmetic and copies ran while one was open for 13% of the time, Pallas kernels for 0%

commit v1 on v0

v1 whole, which is shorter than its diff:
```python
import jax
import jax.numpy as jnp
from jax import lax
from jax.experimental import pallas as pl
from jax.experimental.pallas import tpu as pltpu
from jax.sharding import PartitionSpec as P

DK = 128
DRAFT = 16
CONV = 4
HALF = 4
ROWS = 2 * HALF
BF = jnp.bfloat16
F32 = jnp.float32
VM = pl.BlockSpec(memory_space=pltpu.VMEM)
SM = pl.BlockSpec(memory_space=pltpu.SMEM)


def source_of(owner_ref, row):
    me = lax.axis_index("req")
    partner = owner_ref[me * ROWS + row]
    local = partner // ROWS == me
    return partner, local, partner % HALF


def mixer_kernel(
    owner_ref,
    accept_ref,
    own_ref,
    low_ref,
    high_ref,
    edge_ref,
    state_ref,
    conv_ref,
    bias_ref,
    gain_ref,
    mixed_low_ref,
    mixed_high_ref,
    value_ref,
    weight_ref,
    decay_ref,
    edges_out_ref,
    window,
    query_scr,
    forget_scr,
):
    heads = 2
    for row in range(ROWS):
        _, local, place = source_of(owner_ref, row)
        other_ref = low_ref if row < HALF else high_ref
        own = own_ref[row].astype(F32)
        other = other_ref[place].astype(F32)
        picked = jnp.where(local, own, other)
        edge = edge_ref[row].astype(F32)
        for block in range(3):
            columns = slice(block * DK, (block + 1) * DK)
            window[row, block, 8:40, :] = picked[:, columns]
            window[row, block, 2:8, :] = edge[:, columns]

    sub_iota = lax.broadcasted_iota(jnp.int32, (1, DRAFT, DK), 1)

    def pair(step, _):
        base = step * 2
        for sub in range(2):
            row = base + sub
            for head in range(heads):
                sums = []
                for block in range(3):
                    acc = None
                    for shift in range(CONV):
                        taps = conv_ref[shift, head, block * DK : (block + 1) * DK]
                        start = 2 + 2 * shift + head
                        rows = window[row, block, pl.ds(start, DRAFT, stride=2), :]
                        term = taps[None, :] * rows
                        acc = term if acc is None else acc + term
                    sums.append(acc)
                slot = sub * heads + head
                queries, gates, values = sums
                query_scr[slot] = queries * jax.nn.sigmoid(queries) * DK ** (-0.5)
                forget_scr[slot] = jax.nn.sigmoid(gates + bias_ref[head, :][None, :])
                value_ref[row, head] = values * jax.nn.sigmoid(values)
        queries = query_scr[...]
        forget = forget_scr[...]
        values = value_ref[pl.ds(base, 2)].reshape(4, DRAFT, DK)
        lengths = []
        for sub in range(2):
            partner, _, _ = source_of(owner_ref, base + sub)
            lengths.append(accept_ref[partner])
        weights = jnp.zeros((4, DRAFT, DK), F32)
        kept = [jnp.zeros((heads, DRAFT, DK), F32) for _ in range(2)]
        kept_decay = [jnp.zeros((heads, 1, DK), F32) for _ in range(2)]
        decay = jnp.ones((4, 1, DK), F32)
        head_rows = []
        query_rows = []
        for t in range(DRAFT):
            forget_t = forget[:, t : t + 1, :]
            query_t = queries[:, t : t + 1, :]
            decay = decay * forget_t
            weights = jnp.where(sub_iota == t, 1.0 - forget_t, weights * forget_t)
            scores = jnp.sum(weights * query_t, axis=-1, keepdims=True)
            head_rows.append(jnp.sum(scores * values, axis=1, keepdims=True))
            query_rows.append(query_t * decay)
            for sub in range(2):
                now = lengths[sub] == t + 1
                part = slice(sub * heads, (sub + 1) * heads)
                kept[sub] = jnp.where(now, weights[part], kept[sub])
                kept_decay[sub] = jnp.where(now, decay[part], kept_decay[sub])
        local_out = jnp.concatenate(head_rows, axis=1)
        decayed = jnp.concatenate(query_rows, axis=1)
        for sub in range(2):
            row = base + sub
            weight_ref[row] = kept[sub]
            decay_ref[row] = kept_decay[sub]
            for head in range(heads):
                slot = sub * heads + head
                out = local_out[slot] + jnp.dot(
                    decayed[slot],
                    state_ref[row, head],
                    preferred_element_type=F32,
                    precision=lax.Precision.HIGHEST,
                )
                scale = lax.rsqrt(jnp.mean(out * out, axis=-1, keepdims=True) + 1e-05)
                mixed = (out * scale * gain_ref[head, :][None, :]).astype(BF)
                columns = slice(head * DK, (head + 1) * DK)

                @pl.when(row < HALF)
                def _():
                    mixed_low_ref[jnp.minimum(row, HALF - 1), :, columns] = mixed

                @pl.when(row >= HALF)
                def _():
                    mixed_high_ref[jnp.maximum(row - HALF, 0), :, columns] = mixed

        return 0

    lax.fori_loop(0, ROWS // 2, pair, 0)
    for row in range(ROWS):
        partner, _, _ = source_of(owner_ref, row)
        start = 2 + 2 * accept_ref[partner]
        for block in range(3):
            turned = pltpu.roll(window[row, block], 40 - start, 0)
            columns = slice(block * DK, (block + 1) * DK)
            edges_out_ref[row, :, columns] = turned[:6].astype(BF)


def mixer(owner, accept, own, low, high, edges, states, conv, bias, gain):
    shape = jax.ShapeDtypeStruct
    return pl.pallas_call(
        mixer_kernel,
        name="mixer",
        out_shape=(
            shape((HALF, DRAFT, 2 * DK), BF),
            shape((HALF, DRAFT, 2 * DK), BF),
            shape((ROWS, 2, DRAFT, DK), F32),
            shape((ROWS, 2, DRAFT, DK), F32),
            shape((ROWS, 2, 1, DK), F32),
            shape((ROWS, 6, 3 * DK), BF),
        ),
        in_specs=[SM, SM] + [VM] * 8,
        out_specs=tuple([VM] * 6),
        scratch_shapes=[
            pltpu.VMEM((ROWS, 3, 40, DK), F32),
            pltpu.VMEM((4, DRAFT, DK), F32),
            pltpu.VMEM((4, DRAFT, DK), F32),
        ],
        cost_estimate=pl.CostEstimate(
            flops=20_000_000, bytes_accessed=2_000_000, transcendentals=400_000
        ),
    )(owner, accept, own, low, high, edges, states, conv, bias, gain)


def keep_kernel(state_ref, value_ref, weight_ref, decay_ref, kept_ref):
    for row in range(ROWS):
        for head in range(2):
            update = lax.dot_general(
                weight_ref[row, head],
                value_ref[row, head],
                (((0,), (0,)), ((), ())),
                preferred_element_type=F32,
                precision=lax.Precision.HIGHEST,
            )
            column = jnp.transpose(jnp.broadcast_to(decay_ref[row, head], (DK, DK)))
            kept_ref[row, head] = column * state_ref[row, head] + update


def keep(states, values, weights, decay):
    return pl.pallas_call(
        keep_kernel,
        name="keep",
        out_shape=jax.ShapeDtypeStruct(states.shape, F32),
        in_specs=[VM] * 4,
        out_specs=VM,
        cost_estimate=pl.CostEstimate(
            flops=20_000_000, bytes_accessed=3_000_000, transcendentals=0
        ),
    )(states, values, weights, decay)


def columns_of(step, width):
    place = (lax.axis_index("grp") + step) % 4
    return pl.ds(pl.multiple_of(place * width, width), width)


def project_kernel(
    owner_ref, low_ref, high_ref, from_low_ref, from_high_ref, weight_ref, resid_ref,
    own_ref, next_ref, far_ref, prev_ref, rows_scr,
):
    width = own_ref.shape[1]
    for row in range(ROWS):
        _, local, place = source_of(owner_ref, row)
        mine = low_ref[row] if row < HALF else high_ref[row - HALF]
        other = from_low_ref[place] if row < HALF else from_high_ref[place]
        picked = jnp.where(local, mine.astype(F32), other.astype(F32)).astype(BF)
        rows_scr[row * DRAFT : (row + 1) * DRAFT, :] = picked
    rows = rows_scr[...]
    for step, out_ref in ((2, far_ref), (1, next_ref), (3, prev_ref)):
        part = jnp.dot(rows, weight_ref[:, columns_of(step, width)], preferred_element_type=F32)
        out_ref[...] = part.astype(BF)
    part = jnp.dot(rows, weight_ref[:, columns_of(0, width)], preferred_element_type=F32)
    own_ref[...] = part + resid_ref[:, columns_of(0, width)].astype(F32)


def project(owner, low, high, from_low, from_high, weight, resid):
    slots, model = resid.shape
    width = model // 4
    shape = jax.ShapeDtypeStruct
    return pl.pallas_call(
        project_kernel,
        name="project",
        out_shape=(
            shape((slots, width), F32),
            shape((slots, width), BF),
            shape((slots, width), BF),
            shape((slots, width), BF),
        ),
        in_specs=[SM] + [VM] * 6,
        out_specs=tuple([VM] * 4),
        scratch_shapes=[pltpu.VMEM((slots, 2 * DK), BF)],
        cost_estimate=pl.CostEstimate(
            flops=140_000_000, bytes_accessed=2_000_000, transcendentals=0
        ),
    )(owner, low, high, from_low, from_high, weight, resid)


def ffn_kernel(
    length_ref, own_ref, next_ref, far_ref, prev_ref, gain_ref, gate_ref, up_ref, down_ref,
    own_out_ref, next_out_ref, far_out_ref, prev_out_ref, normed_scr,
):
    width = own_ref.shape[1]
    parts = ((0, own_ref), (1, next_ref), (2, far_ref), (3, prev_ref))
    total = None
    for _, ref in parts:
        block = ref[...].astype(F32)
        square = jnp.sum(block * block, axis=-1, keepdims=True)
        total = square if total is None else total + square
    scale = lax.rsqrt(total / (4 * width) + 1e-05)
    for step, ref in parts:
        columns = columns_of(step, width)
        normed_scr[:, columns] = (ref[...].astype(F32) * scale * gain_ref[:, columns]).astype(BF)
    normed = normed_scr[...]
    dims = (((1,), (1,)), ((), ()))
    gate = lax.dot_general(normed, gate_ref[...], dims, preferred_element_type=F32)
    up = lax.dot_general(normed, up_ref[...], dims, preferred_element_type=F32)
    hidden = (gate * jax.nn.sigmoid(gate) * up).astype(BF)
    me = lax.axis_index("req")
    position = lax.broadcasted_iota(jnp.int32, (DRAFT, 1), 0)
    live = jnp.concatenate(
        [(position < length_ref[me * ROWS + row]).astype(F32) for row in range(ROWS)], axis=0
    )
    for step, out_ref in ((2, far_out_ref), (1, next_out_ref), (3, prev_out_ref)):
        part = jnp.dot(hidden, down_ref[:, columns_of(step, width)], preferred_element_type=F32)
        out_ref[...] = (part * live).astype(BF)
    part = jnp.dot(hidden, down_ref[:, columns_of(0, width)], preferred_element_type=F32)
    own_out_ref[...] = (part + own_ref[...].astype(F32)) * live


def ffn(lengths, own, following, far, preceding, gain, gate_t, up_t, down):
    slots, width = own.shape
    shape = jax.ShapeDtypeStruct
    return pl.pallas_call(
        ffn_kernel,
        name="ffn",
        out_shape=(
            shape((slots, width), F32),
            shape((slots, width), BF),
            shape((slots, width), BF),
            shape((slots, width), BF),
        ),
        in_specs=[SM] + [VM] * 8,
        out_specs=tuple([VM] * 4),
        scratch_shapes=[pltpu.VMEM((slots, 4 * width), BF)],
        cost_estimate=pl.CostEstimate(
            flops=1_100_000_000, bytes_accessed=9_000_000, transcendentals=100_000
        ),
    )(lengths, own, following, far, preceding, gain, gate_t, up_t, down)


def shifted(block, axis, step):
    count = lax.axis_size(axis)
    return lax.ppermute(block, axis, [(i, (i + step) % count) for i in range(count)])


def shards(
    mix_inputs,
    conv_weight,
    forget_bias,
    norm_gain,
    out_weight,
    resid,
    ffn_gain,
    gate_weight,
    up_weight,
    down_weight,
    held_states,
    held_edges,
    draft_lengths,
    accepted,
    owner_row,
):
    slots = ROWS * DRAFT
    lanes = 3 * DK
    low = shifted(mix_inputs[HALF:].reshape(HALF, 2 * DRAFT, lanes), "req", 1)
    high = shifted(mix_inputs[:HALF].reshape(HALF, 2 * DRAFT, lanes), "req", -1)
    own = mix_inputs.reshape(ROWS, 2 * DRAFT, lanes)
    edges = held_edges.reshape(ROWS, 6, lanes)
    mixed_low, mixed_high, values, weights, decay, edges_out = mixer(
        owner_row, accepted, own, low, high, edges, held_states,
        conv_weight, forget_bias, norm_gain,
    )
    from_low = shifted(mixed_high, "req", 1)
    from_high = shifted(mixed_low, "req", -1)
    kept_states = keep(held_states, values, weights, decay)
    kept_edges = edges_out.reshape(held_edges.shape)
    rows = resid.reshape(slots, resid.shape[2])
    own_part, to_next, to_far, to_prev = project(
        owner_row, mixed_low, mixed_high, from_low, from_high, out_weight, rows
    )
    far = shifted(to_far, "grp", 2)
    following = shifted(to_next, "grp", 1)
    preceding = shifted(to_prev, "grp", -1)
    stream = (
        own_part + far.astype(F32) + following.astype(F32) + preceding.astype(F32)
    ).astype(BF)
    far = shifted(stream, "grp", 2)
    preceding = shifted(stream, "grp", 1)
    following = shifted(stream, "grp", -1)
    own_part, to_next, to_far, to_prev = ffn(
        draft_lengths, stream, following, far, preceding, ffn_gain[None, :],
        gate_weight.T, up_weight.T, down_weight,
    )
    far = shifted(to_far, "grp", 2)
    following = shifted(to_next, "grp", 1)
    preceding = shifted(to_prev, "grp", -1)
    layer_out = (
        own_part + far.astype(F32) + following.astype(F32) + preceding.astype(F32)
    ).astype(BF)
    return (layer_out.reshape(ROWS, DRAFT, -1), kept_states, kept_edges)


def solution(mesh):
    return jax.shard_map(
        shards,
        mesh=mesh,
        in_specs=(
            P("req", None, "grp", None),
            P(None, "grp", None),
            P("grp", None),
            P("grp", None),
            P("grp", None),
            P("req", None, None),
            P(),
            P(None, "grp"),
            P(None, "grp"),
            P("grp", None),
            P("req", "grp", None, None),
            P("req", None, "grp", None),
            P(),
            P(),
            P(),
        ),
        out_specs=(P("req", None, "grp"), P("req", "grp", None, None), P("req", None, "grp", None)),
        check_vma=False,
    )
```

time: 268 us -> 76.2 us (0.28); the launches traced: 263 us -> 75.9 us
  other arithmetic: 74.2 us -> 2.69 us
  local copies, waits for them, and re-layouts: 58.9 us -> 7.43 us
  matrix products: 45.4 us -> 0 us
  waiting for transfers between devices: 60.3 us -> 24 us
  Pallas kernels: 0 us -> 20.6 us
  between operations: 14.4 us -> 0.71 us
  starting transfers between devices: 9.65 us -> 20.5 us
    select_n x21 -> x0, other arithmetic: 48.3 us -> none  [the longest x16 46.5 us: advance(): kept_state = jnp.where(position == accept_col - 1, current_step, kept_state)]
    dot_general x19 -> x0, matrix products: 45.4 us -> none  [the longest x16 34.9 us: advance(): jnp.einsum('rhk,rhkv->rhv', present_query, current_step, precision=lax.Pr...]
    psum x1 -> x0, waiting for transfers between devices: 34.2 us -> none  [shards(): projected = lax.psum(partial_value, 'grp')]
    dynamic_slice x32 -> x0, local copies, waits for them, and re-layouts: 24.7 us -> none  [run_mixer(): lax.scan(advance, (carried_over, carried_over), scanned)]
    pallas_call x0 -> x4, Pallas kernels: none -> 20.6 us  [the longest x1 7.63 us: mixer(): pl.pallas_call(mixer_kernel, name='mixer', out_shape=(shape((HALF, DRAFT,...]
    gather x6 -> x0, local copies, waits for them, and re-layouts: 11.8 us -> none  [the longest x1 4.62 us: shards(): returned[local_rows(inverse[own_rows], device_index, per_dev, req_count)]]
    concatenate x5 -> x0, other arithmetic: 11.6 us -> none  [the longest x2 8.68 us: extended(): block = jnp.concatenate([low, block, high], axis=dim)]
    ppermute x4 -> x13, starting transfers between devices: 9.57 us -> 20.5 us  [shifted(): lax.ppermute(block, axis, [(i, (i + step) % count) for i in range(count)])]
  transfers between devices with their start and end apart: 6 -> 13, of which waited for: 4 -> 9; matrix products, arithmetic and copies ran while one was open for 13% -> 5% of each run, Pallas kernels for 0% -> 4%
where the time goes in v1:
time: 76.2 us; the launch traced here: 75.9 us
  waiting for transfers between devices  24 us (31%)
  Pallas kernels  20.6 us (27%)
  starting transfers between devices  20.5 us (27%)
  local copies, waits for them, and re-layouts  7.43 us (10%)
  other arithmetic  2.69 us (4%)
    ppermute x13, waiting for transfers between devices, shifted(): lax.ppermute(block, axis, [(i, (i + step) % count) for i in range(count)])  24 us
    ppermute x13, starting transfers between devices, shifted(): lax.ppermute(block, axis, [(i, (i + step) % count) for i in range(count)])  20.5 us
    pallas_call x1, Pallas kernels, mixer(): pl.pallas_call(mixer_kernel, name='mixer', out_shape=(shape((HALF, DRAFT,...  7.63 us
    pallas_call x1, Pallas kernels, ffn(): pl.pallas_call(ffn_kernel, name='ffn', out_shape=(shape((slots, width), F...  7.12 us
    unnamed x20, local copies, waits for them, and re-layouts  3.97 us
    pallas_call x1, Pallas kernels, keep(): pl.pallas_call(keep_kernel, name='keep', out_shape=jax.ShapeDtypeStruct(s...  3.32 us
    pallas_call x1, Pallas kernels, project(): pl.pallas_call(project_kernel, name='project', out_shape=(shape((slots, w...  2.54 us
    reshape x1, local copies, waits for them, and re-layouts, shards(): own = mix_inputs.reshape(ROWS, 2 * DRAFT, lanes)  1.68 us
  transfers between devices with their start and end apart: 13, of which 9 were waited for; matrix products, arithmetic and copies ran while one was open for 5% of the time, Pallas kernels for 4%

profile of v1, /device:TPU:6, one launch (start us, length us, event | category | flops | bytes accessed | tf_op | source)
XLA Modules:
  0.0 75.9 jit_solution(10298773425404754821)
XLA Ops:
  0.6 1.1 %fusion = (bf16[4,16,2,384]{3,2,1,0:T(2,128)(2,1)S(1)}, bf16[4,16,2,384]{3,2,1,0:T(2,128)(2,1)S(1)}) fusion(bf16[8,16,2,384]{3,2,1,0:T(2,128)(2,1)} %param.15), kind=kLoop, calls=%fused_computation.2 | loop fusion | bytes 393216 | tf_op jit(solution)/shard_map/slice | solution.py:323
  1.8 0.1 collective-permute-start
  1.9 7.8 %collective-permute-start.1 = (bf16[4,32,384]{2,1,0:T(8,128)(2,1)S(1)}, bf16[4,32,384]{2,1,0:T(8,128)(2,1)S(1)}, u32[]{:S(2)}, u32[]{:S(2)}) collective-permute-start(bf16[4,32,384]{2,1,0:T(8,128)(2,1)S(1)} %reshape.29), channel_id=1, source_target_pairs={{0,63},{1,0},{2,1},{3,2},{4,3},{5,4},{6,5},{7,6},{8,7},{9,8},{10,9... | collective-permute-start | bytes 294920 | tf_op jit(solution)/shard_map/ppermute | solution.py:300
  9.7 1.7 %reshape.27.own_ref = bf16[8,32,384]{2,1,0:T(8,128)(2,1)} reshape(bf16[8,16,2,384]{3,2,1,0:T(2,128)(2,1)} %param.15) | data formatting | bytes 393216 | tf_op jit(solution)/shard_map/reshape | solution.py:324
  11.4 0.8 %copy.18 = bf16[8,3,2,384]{3,0,2,1:T(8,128)(2,1)S(1)} copy(bf16[8,3,2,384]{3,2,1,0:T(2,128)(2,1)} %param.26) | data formatting | bytes 73728 | tf_op args[11]
  12.2 0.6 copy.19.edge_ref
  12.8 0.0 collective-permute-done.low_ref
  12.8 0.0 copy-start.4
  12.8 0.0 collective-permute-done.1.high_ref
  12.8 0.6 copy-done.4
  13.4 0.6 copy-done.5
  14.1 7.6 %mixer.1 = (bf16[4,16,256]{2,1,0:T(8,128)(2,1)}, bf16[4,16,256]{2,1,0:T(8,128)(2,1)}, f32[8,2,16,128]{3,2,1,0:T(8,128)}, f32[8,2,16,128]{3,2,1,0:T(8,128)}, f32[...) custom-call(s32[512]{0:T(512)} %owner_ref.3, s32[512]{0:T(512)} %accept_ref.1, bf16[8,32,384]{2,1,0:T(8,128)(2,1)} %reshape.27.own_ref, ...), custom_call_target="tpu_custom_call" | custom-call | flops 20000000 | bytes 2000000 | tf_op jit(solution)/shard_map/mixer/pallas_call | solution.py:148
  21.7 3.7 %collective-permute-start.3 = (bf16[4,16,256]{2,1,0:T(8,128)(2,1)}, bf16[4,16,256]{2,1,0:T(8,128)(2,1)S(1)}, u32[]{:S(2)}, u32[]{:S(2)}) collective-permute-start(bf16[4,16,256]{2,1,0:T(8,128)(2,1)} %get-tuple-element.17.low_ref), channel_id=1, source_target_pairs={{0,63},{1,0},{2,1},{3,2},{4,3},{5,4},{6,5},{7,6},{8,7},{9,8},{10,9... | collective-permute-start | bytes 98312 | tf_op jit(solution)/shard_map/ppermute | solution.py:300
  25.4 0.0 collective-permute-start.2
  25.4 1.9 %collective-permute-done.3.from_high_ref = bf16[4,16,256]{2,1,0:T(8,128)(2,1)S(1)} collective-permute-done((bf16[4,16,256]{2,1,0:T(8,128)(2,1)}, bf16[4,16,256]{2,1,0:T(8,128)(2,1)S(1)}, u32[]{:S(2)}, u32[]{:S(2)}) %collective-permute-start.3) | collective-permute-done | bytes 32800 | tf_op jit(solution)/shard_map/ppermute | solution.py:300
  27.3 5.0 %collective-permute-done.2.from_low_ref = bf16[4,16,256]{2,1,0:T(8,128)(2,1)S(1)} collective-permute-done((bf16[4,16,256]{2,1,0:T(8,128)(2,1)}, bf16[4,16,256]{2,1,0:T(8,128)(2,1)S(1)}, u32[]{:S(2)}, u32[]{:S(2)}) %collective-permute-start.2) | collective-permute-done | bytes 32800 | tf_op jit(solution)/shard_map/ppermute | solution.py:300
  32.3 0.0 copy-done.7
  32.3 0.6 copy-done.8
  32.9 2.5 %project.1 = (f32[128,512]{1,0:T(8,128)}, bf16[128,512]{1,0:T(8,128)(2,1)}, bf16[128,512]{1,0:T(8,128)(2,1)}, bf16[128,512]{1,0:T(8,128)(2,1)}) custom-call(s32[512]{0:T(512)} %owner_ref.3, bf16[4,16,256]{2,1,0:T(8,128)(2,1)} %get-tuple-element.17.low_ref, bf16[4,16,256]{2,1,0:T(8,128)(2,1)} %get-tuple-element.18.high_ref, bf16[4,16,256]{2,1,0:T(8,128)(2,1)} %copy-done.8, ...), custom_call_target="tpu_custom_call" | custom-call | flops 140000000 | bytes 2000000 | tf_op jit(solution)/shard_map/project/pallas_call | solution.py:227
  35.4 1.4 %collective-permute-start.4 = (bf16[128,512]{1,0:T(8,128)(2,1)}, bf16[128,512]{1,0:T(8,128)(2,1)S(1)}, u32[]{:S(2)}, u32[]{:S(2)}) collective-permute-start(bf16[128,512]{1,0:T(8,128)(2,1)} %get-tuple-element.20), channel_id=1, source_target_pairs={{0,128},{64,192},{128,0},{192,64},{1,129},{65,193},{129,1},{193,65... | collective-permute-start | bytes 393224 | tf_op jit(solution)/shard_map/ppermute | solution.py:300
  36.8 2.1 %collective-permute-start.5 = (bf16[128,512]{1,0:T(8,128)(2,1)}, bf16[128,512]{1,0:T(8,128)(2,1)S(1)}, u32[]{:S(2)}, u32[]{:S(2)}) collective-permute-start(bf16[128,512]{1,0:T(8,128)(2,1)} %get-tuple-element.21), channel_id=1, source_target_pairs={{0,64},{64,128},{128,192},{192,0},{1,65},{65,129},{129,193},{193,1... | collective-permute-start | bytes 393224 | tf_op jit(solution)/shard_map/ppermute | solution.py:300
  38.9 0.0 collective-permute-start.6
  38.9 3.2 %collective-permute-done.4 = bf16[128,512]{1,0:T(8,128)(2,1)S(1)} collective-permute-done((bf16[128,512]{1,0:T(8,128)(2,1)}, bf16[128,512]{1,0:T(8,128)(2,1)S(1)}, u32[]{:S(2)}, u32[]{:S(2)}) %collective-permute-start.4) | collective-permute-done | bytes 131104 | tf_op jit(solution)/shard_map/ppermute | solution.py:300
  42.1 0.6 collective-permute-done.5
  42.7 5.0 %collective-permute-done.6 = bf16[128,512]{1,0:T(8,128)(2,1)S(1)} collective-permute-done((bf16[128,512]{1,0:T(8,128)(2,1)}, bf16[128,512]{1,0:T(8,128)(2,1)S(1)}, u32[]{:S(2)}, u32[]{:S(2)}) %collective-permute-start.6) | collective-permute-done | bytes 131104 | tf_op jit(solution)/shard_map/ppermute | solution.py:300
  47.7 1.0 %add_convert_fusion.1.own_ref = bf16[128,512]{1,0:T(8,128)(2,1)S(1)} fusion(bf16[128,512]{1,0:T(8,128)(2,1)S(1)} %collective-permute-done.6, bf16[128,512]{1,0:T(8,128)(2,1)S(1)} %collective-permute-done.5, f32[128,512]{1,0:T(8,128)} %get-tuple-element.19, bf16[128,512]{1,0:T(8,128)(2,1)S(1)} %collective-permute-done.4), kind=kLoop, calls=%fused_computation.1 | loop fusion | flops 458752 | bytes 786432 | tf_op jit(solution)/shard_map/convert_element_type | solution.py:343
  48.7 0.0 copy-start
  48.8 0.1 collective-permute-start.9
  48.8 0.1 collective-permute-start.8
  48.9 1.9 %collective-permute-start.7 = (bf16[128,512]{1,0:T(8,128)(2,1)S(1)}, bf16[128,512]{1,0:T(8,128)(2,1)S(1)}, u32[]{:S(2)}, u32[]{:S(2)}) collective-permute-start(bf16[128,512]{1,0:T(8,128)(2,1)S(1)} %add_convert_fusion.1.own_ref), channel_id=1, source_target_pairs={{0,192},{64,0},{128,64},{192,128},{1,193},{65,1},{129,65},{193,129... | collective-permute-start | bytes 393224 | tf_op jit(solution)/shard_map/ppermute | solution.py:300
  50.9 2.9 %collective-permute-done.9.prev_ref = bf16[128,512]{1,0:T(8,128)(2,1)S(1)} collective-permute-done((bf16[128,512]{1,0:T(8,128)(2,1)S(1)}, bf16[128,512]{1,0:T(8,128)(2,1)S(1)}, u32[]{:S(2)}, u32[]{:S(2)}) %collective-permute-start.9) | collective-permute-done | bytes 131104 | tf_op jit(solution)/shard_map/ppermute | solution.py:300
  53.8 1.6 %collective-permute-done.8.far_ref = bf16[128,512]{1,0:T(8,128)(2,1)S(1)} collective-permute-done((bf16[128,512]{1,0:T(8,128)(2,1)S(1)}, bf16[128,512]{1,0:T(8,128)(2,1)S(1)}, u32[]{:S(2)}, u32[]{:S(2)}) %collective-permute-start.8) | collective-permute-done | bytes 131104 | tf_op jit(solution)/shard_map/ppermute | solution.py:300
  55.4 1.4 %collective-permute-done.7.next_ref = bf16[128,512]{1,0:T(8,128)(2,1)S(1)} collective-permute-done((bf16[128,512]{1,0:T(8,128)(2,1)S(1)}, bf16[128,512]{1,0:T(8,128)(2,1)S(1)}, u32[]{:S(2)}, u32[]{:S(2)}) %collective-permute-start.7) | collective-permute-done | bytes 131104 | tf_op jit(solution)/shard_map/ppermute | solution.py:300
  56.8 0.0 copy-done
  56.8 0.0 copy-done.1
  56.8 0.0 copy-done.2
  56.8 0.6 copy-done.3
  57.5 7.1 %ffn.1 = (f32[128,512]{1,0:T(8,128)}, bf16[128,512]{1,0:T(8,128)(2,1)}, bf16[128,512]{1,0:T(8,128)(2,1)}, bf16[128,512]{1,0:T(8,128)(2,1)}) custom-call(s32[512]{0:T(512)} %length_ref.1, bf16[128,512]{1,0:T(8,128)(2,1)} %copy-done, bf16[128,512]{1,0:T(8,128)(2,1)} %copy-done.3, bf16[128,512]{1,0:T(8,128)(2,1)} %copy-done.2, bf16[128,512]{1,0:T(8,128)(2,1)} %copy-done.1, ...), custom_call_target="tpu_custom_call" | custom-call | flops 1100000000 | bytes 9000000 | tf_op jit(solution)/shard_map/ffn/pallas_call | solution.py:280
  64.6 0.7 collective-permute-start.10
  65.3 2.5 %collective-permute-start.11 = (bf16[128,512]{1,0:T(8,128)(2,1)}, bf16[128,512]{1,0:T(8,128)(2,1)S(1)}, u32[]{:S(2)}, u32[]{:S(2)}) collective-permute-start(bf16[128,512]{1,0:T(8,128)(2,1)} %get-tuple-element.25), channel_id=1, source_target_pairs={{0,64},{64,128},{128,192},{192,0},{1,65},{65,129},{129,193},{193,1... | collective-permute-start | bytes 393224 | tf_op jit(solution)/shard_map/ppermute | solution.py:300
  67.8 0.0 collective-permute-start.12
  67.8 0.0 copy-done.6
  67.8 0.6 copy.21
  68.5 3.3 %keep.1 = f32[8,2,128,128]{3,2,1,0:T(8,128)} custom-call(f32[8,2,128,128]{3,2,1,0:T(8,128)} %state_ref.3, f32[8,2,16,128]{3,2,1,0:T(8,128)} %get-tuple-element.27.value_ref, f32[8,2,16,128]{3,2,1,0:T(8,128)} %get-tuple-element.28.weight_ref, f32[8,2,1,128]{3,2,1,0:T(1,128)} %get-tuple-element.29.decay_ref), custom_call_target="tpu_custom_call" | custom-call | flops 20000000 | bytes 3000000 | tf_op jit(solution)/shard_map/keep/pallas_call | solution.py:187
  71.8 0.0 collective-permute-done.10
  71.8 0.0 collective-permute-done.11
  71.8 2.4 %collective-permute-done.12 = bf16[128,512]{1,0:T(8,128)(2,1)S(1)} collective-permute-done((bf16[128,512]{1,0:T(8,128)(2,1)}, bf16[128,512]{1,0:T(8,128)(2,1)S(1)}, u32[]{:S(2)}, u32[]{:S(2)}) %collective-permute-start.12) | collective-permute-done | bytes 131104 | tf_op jit(solution)/shard_map/ppermute | solution.py:300
  74.2 1.7 %add_convert_fusion = bf16[128,512]{1,0:T(8,128)(2,1)} fusion(bf16[128,512]{1,0:T(8,128)(2,1)S(1)} %collective-permute-done.12, bf16[128,512]{1,0:T(8,128)(2,1)S(1)} %collective-permute-done.11, f32[128,512]{1,0:T(8,128)} %get-tuple-element.23, bf16[128,512]{1,0:T(8,128)(2,1)S(1)} %collective-permute-done.10), kind=kLoop, calls=%fused_computation | loop fusion | flops 458752 | bytes 786432 | tf_op jit(solution)/shard_map/convert_element_type | solution.py:356
  (10 shorter events, 0.1 us)
Async XLA Ops:
  1.8 11.0 %collective-permute-start = (bf16[4,32,384]{2,1,0:T(8,128)(2,1)S(1)}, bf16[4,32,384]{2,1,0:T(8,128)(2,1)S(1)}, u32[]{:S(2)}, u32[]{:S(2)}) collective-permute-start(bf16[4,32,384]{2,1,0:T(8,128)(2,1)S(1)} %reshape.28), channel_id=1, source_target_pairs={{0,1},{1,2},{2,3},{3,4},{4,5},{5,6},{6,7},{7,8},{8,9},{9,10},{10,1... | collective-permute-start | bytes 294920 | tf_op jit(solution)/shard_map/ppermute | solution.py:300
  1.9 10.9 %collective-permute-start.1 = (bf16[4,32,384]{2,1,0:T(8,128)(2,1)S(1)}, bf16[4,32,384]{2,1,0:T(8,128)(2,1)S(1)}, u32[]{:S(2)}, u32[]{:S(2)}) collective-permute-start(bf16[4,32,384]{2,1,0:T(8,128)(2,1)S(1)} %reshape.29), channel_id=1, source_target_pairs={{0,63},{1,0},{2,1},{3,2},{4,3},{5,4},{6,5},{7,6},{8,7},{9,8},{10,9... | collective-permute-start | bytes 294920 | tf_op jit(solution)/shard_map/ppermute | solution.py:300
  12.8 0.6 copy-start.4
  13.4 0.6 copy-start.5
  21.7 5.6 %collective-permute-start.3 = (bf16[4,16,256]{2,1,0:T(8,128)(2,1)}, bf16[4,16,256]{2,1,0:T(8,128)(2,1)S(1)}, u32[]{:S(2)}, u32[]{:S(2)}) collective-permute-start(bf16[4,16,256]{2,1,0:T(8,128)(2,1)} %get-tuple-element.17.low_ref), channel_id=1, source_target_pairs={{0,63},{1,0},{2,1},{3,2},{4,3},{5,4},{6,5},{7,6},{8,7},{9,8},{10,9... | collective-permute-start | bytes 98312 | tf_op jit(solution)/shard_map/ppermute | solution.py:300
  25.4 6.9 %collective-permute-start.2 = (bf16[4,16,256]{2,1,0:T(8,128)(2,1)}, bf16[4,16,256]{2,1,0:T(8,128)(2,1)S(1)}, u32[]{:S(2)}, u32[]{:S(2)}) collective-permute-start(bf16[4,16,256]{2,1,0:T(8,128)(2,1)} %get-tuple-element.18.high_ref), channel_id=1, source_target_pairs={{0,1},{1,2},{2,3},{3,4},{4,5},{5,6},{6,7},{7,8},{8,9},{9,10},{10,1... | collective-permute-start | bytes 98312 | tf_op jit(solution)/shard_map/ppermute | solution.py:300
  27.3 5.0 %copy-start.7 = (bf16[4,16,256]{2,1,0:T(8,128)(2,1)}, bf16[4,16,256]{2,1,0:T(8,128)(2,1)S(1)}, u32[]{:S(2)}) copy-start(bf16[4,16,256]{2,1,0:T(8,128)(2,1)S(1)} %collective-permute-done.3.from_high_ref) | copy-start | bytes 98308
  32.3 0.6 copy-start.8
  35.4 6.7 %collective-permute-start.4 = (bf16[128,512]{1,0:T(8,128)(2,1)}, bf16[128,512]{1,0:T(8,128)(2,1)S(1)}, u32[]{:S(2)}, u32[]{:S(2)}) collective-permute-start(bf16[128,512]{1,0:T(8,128)(2,1)} %get-tuple-element.20), channel_id=1, source_target_pairs={{0,128},{64,192},{128,0},{192,64},{1,129},{65,193},{129,1},{193,65... | collective-permute-start | bytes 393224 | tf_op jit(solution)/shard_map/ppermute | solution.py:300
  36.8 5.9 %collective-permute-start.5 = (bf16[128,512]{1,0:T(8,128)(2,1)}, bf16[128,512]{1,0:T(8,128)(2,1)S(1)}, u32[]{:S(2)}, u32[]{:S(2)}) collective-permute-start(bf16[128,512]{1,0:T(8,128)(2,1)} %get-tuple-element.21), channel_id=1, source_target_pairs={{0,64},{64,128},{128,192},{192,0},{1,65},{65,129},{129,193},{193,1... | collective-permute-start | bytes 393224 | tf_op jit(solution)/shard_map/ppermute | solution.py:300
  38.9 8.8 %collective-permute-start.6 = (bf16[128,512]{1,0:T(8,128)(2,1)}, bf16[128,512]{1,0:T(8,128)(2,1)S(1)}, u32[]{:S(2)}, u32[]{:S(2)}) collective-permute-start(bf16[128,512]{1,0:T(8,128)(2,1)} %get-tuple-element.22), channel_id=1, source_target_pairs={{0,192},{64,0},{128,64},{192,128},{1,193},{65,1},{129,65},{193,129... | collective-permute-start | bytes 393224 | tf_op jit(solution)/shard_map/ppermute | solution.py:300
  48.7 8.1 %copy-start = (bf16[128,512]{1,0:T(8,128)(2,1)}, bf16[128,512]{1,0:T(8,128)(2,1)S(1)}, u32[]{:S(2)}) copy-start(bf16[128,512]{1,0:T(8,128)(2,1)S(1)} %add_convert_fusion.1.own_ref) | copy-start | bytes 393220
  48.8 5.0 %collective-permute-start.9 = (bf16[128,512]{1,0:T(8,128)(2,1)S(1)}, bf16[128,512]{1,0:T(8,128)(2,1)S(1)}, u32[]{:S(2)}, u32[]{:S(2)}) collective-permute-start(bf16[128,512]{1,0:T(8,128)(2,1)S(1)} %add_convert_fusion.1.own_ref), channel_id=1, source_target_pairs={{0,64},{64,128},{128,192},{192,0},{1,65},{65,129},{129,193},{193,1... | collective-permute-start | bytes 393224 | tf_op jit(solution)/shard_map/ppermute | solution.py:300
  48.8 6.6 %collective-permute-start.8 = (bf16[128,512]{1,0:T(8,128)(2,1)S(1)}, bf16[128,512]{1,0:T(8,128)(2,1)S(1)}, u32[]{:S(2)}, u32[]{:S(2)}) collective-permute-start(bf16[128,512]{1,0:T(8,128)(2,1)S(1)} %add_convert_fusion.1.own_ref), channel_id=1, source_target_pairs={{0,128},{64,192},{128,0},{192,64},{1,129},{65,193},{129,1},{193,65... | collective-permute-start | bytes 393224 | tf_op jit(solution)/shard_map/ppermute | solution.py:300
  48.9 7.9 %collective-permute-start.7 = (bf16[128,512]{1,0:T(8,128)(2,1)S(1)}, bf16[128,512]{1,0:T(8,128)(2,1)S(1)}, u32[]{:S(2)}, u32[]{:S(2)}) collective-permute-start(bf16[128,512]{1,0:T(8,128)(2,1)S(1)} %add_convert_fusion.1.own_ref), channel_id=1, source_target_pairs={{0,192},{64,0},{128,64},{192,128},{1,193},{65,1},{129,65},{193,129... | collective-permute-start | bytes 393224 | tf_op jit(solution)/shard_map/ppermute | solution.py:300
  53.8 3.0 %copy-start.1 = (bf16[128,512]{1,0:T(8,128)(2,1)}, bf16[128,512]{1,0:T(8,128)(2,1)S(1)}, u32[]{:S(2)}) copy-start(bf16[128,512]{1,0:T(8,128)(2,1)S(1)} %collective-permute-done.9.prev_ref) | copy-start | bytes 393220
  55.4 1.4 %copy-start.2 = (bf16[128,512]{1,0:T(8,128)(2,1)}, bf16[128,512]{1,0:T(8,128)(2,1)S(1)}, u32[]{:S(2)}) copy-start(bf16[128,512]{1,0:T(8,128)(2,1)S(1)} %collective-permute-done.8.far_ref) | copy-start | bytes 393220
  56.8 0.7 copy-start.3
  57.5 10.4 %copy-start.6 = (bf16[8,6,384]{2,1,0:T(8,128)(2,1)S(1)}, bf16[8,6,384]{2,1,0:T(8,128)(2,1)}, u32[]{:S(2)}) copy-start(bf16[8,6,384]{2,1,0:T(8,128)(2,1)} %get-tuple-element.30) | copy-start | bytes 110596
  64.6 7.2 %collective-permute-start.10 = (bf16[128,512]{1,0:T(8,128)(2,1)}, bf16[128,512]{1,0:T(8,128)(2,1)S(1)}, u32[]{:S(2)}, u32[]{:S(2)}) collective-permute-start(bf16[128,512]{1,0:T(8,128)(2,1)} %get-tuple-element.24), channel_id=1, source_target_pairs={{0,128},{64,192},{128,0},{192,64},{1,129},{65,193},{129,1},{193,65... | collective-permute-start | bytes 393224 | tf_op jit(solution)/shard_map/ppermute | solution.py:300
  65.3 6.5 %collective-permute-start.11 = (bf16[128,512]{1,0:T(8,128)(2,1)}, bf16[128,512]{1,0:T(8,128)(2,1)S(1)}, u32[]{:S(2)}, u32[]{:S(2)}) collective-permute-start(bf16[128,512]{1,0:T(8,128)(2,1)} %get-tuple-element.25), channel_id=1, source_target_pairs={{0,64},{64,128},{128,192},{192,0},{1,65},{65,129},{129,193},{193,1... | collective-permute-start | bytes 393224 | tf_op jit(solution)/shard_map/ppermute | solution.py:300
  67.8 6.4 %collective-permute-start.12 = (bf16[128,512]{1,0:T(8,128)(2,1)}, bf16[128,512]{1,0:T(8,128)(2,1)S(1)}, u32[]{:S(2)}, u32[]{:S(2)}) collective-permute-start(bf16[128,512]{1,0:T(8,128)(2,1)} %get-tuple-element.26), channel_id=1, source_target_pairs={{0,192},{64,0},{128,64},{192,128},{1,193},{65,1},{129,65},{193,129... | collective-permute-start | bytes 393224 | tf_op jit(solution)/shard_map/ppermute | solution.py:300

commit v2 on v1

--- a/solution.py
+++ b/solution.py
@@ -11,6 +11,7 @@
 HALF = 4
 ROWS = 2 * HALF
 BF = jnp.bfloat16
+PARAMS = pltpu.CompilerParams(vmem_limit_bytes=12 * 1024 * 1024)
 F32 = jnp.float32
 VM = pl.BlockSpec(memory_space=pltpu.VMEM)
 SM = pl.BlockSpec(memory_space=pltpu.SMEM)
@@ -163,6 +164,7 @@
             pltpu.VMEM((4, DRAFT, DK), F32),
             pltpu.VMEM((4, DRAFT, DK), F32),
         ],
+        compiler_params=PARAMS,
         cost_estimate=pl.CostEstimate(
             flops=20_000_000, bytes_accessed=2_000_000, transcendentals=400_000
         ),
@@ -190,6 +192,7 @@
         out_shape=jax.ShapeDtypeStruct(states.shape, F32),
         in_specs=[VM] * 4,
         out_specs=VM,
+        compiler_params=PARAMS,
         cost_estimate=pl.CostEstimate(
             flops=20_000_000, bytes_accessed=3_000_000, transcendentals=0
         ),
@@ -236,6 +239,7 @@
         in_specs=[SM] + [VM] * 6,
         out_specs=tuple([VM] * 4),
         scratch_shapes=[pltpu.VMEM((slots, 2 * DK), BF)],
+        compiler_params=PARAMS,
         cost_estimate=pl.CostEstimate(
             flops=140_000_000, bytes_accessed=2_000_000, transcendentals=0
         ),
@@ -289,6 +293,7 @@
         in_specs=[SM] + [VM] * 8,
         out_specs=tuple([VM] * 4),
         scratch_shapes=[pltpu.VMEM((slots, 4 * width), BF)],
+        compiler_params=PARAMS,
         cost_estimate=pl.CostEstimate(
             flops=1_100_000_000, bytes_accessed=9_000_000, transcendentals=100_000
         ),

time: 76.2 us -> 73.7 us (0.967)
  Pallas kernels: 20.6 us -> 12.2 us
  local copies, waits for them, and re-layouts: 7.43 us -> 13 us
  other arithmetic: 2.69 us -> 0.8 us
  starting transfers between devices: 20.5 us -> 22.1 us
    unnamed x20 -> x30, local copies, waits for them, and re-layouts: 3.97 us -> 10.8 us
    pallas_call x1, Pallas kernels: 7.12 us -> 3.2 us  [ffn(): pl.pallas_call(ffn_kernel, name='ffn', out_shape=(shape((slots, width), F...]
    ppermute x13, starting transfers between devices: 20.5 us -> 22.1 us  [shifted(): lax.ppermute(block, axis, [(i, (i + step) % count) for i in range(count)])]
    pallas_call x1, Pallas kernels: 2.54 us -> 0.89 us  [project(): pl.pallas_call(project_kernel, name='project', out_shape=(shape((slots, w...]
    pallas_call x1, Pallas kernels: 7.63 us -> 6.09 us  [mixer(): pl.pallas_call(mixer_kernel, name='mixer', out_shape=(shape((HALF, DRAFT,...]
    pallas_call x1, Pallas kernels: 3.32 us -> 2.03 us  [keep(): pl.pallas_call(keep_kernel, name='keep', out_shape=jax.ShapeDtypeStruct(s...]
    convert_element_type x1, other arithmetic: 1.02 us -> 0.07 us  [shards(): stream = (own_part + far.astype(F32) + following.astype(F32) + preceding....]
    convert_element_type x1, other arithmetic: 1.67 us -> 0.73 us  [shards(): layer_out = (own_part + far.astype(F32) + following.astype(F32) + precedi...]
  transfers between devices with their start and end apart: 13 -> 13, of which waited for: 9 -> 12; matrix products, arithmetic and copies ran while one was open for 5% -> 3% of each run, Pallas kernels for 4% -> 3%
where the time goes in v2:
time: 73.7 us; the launch traced here: 73.3 us
  waiting for transfers between devices  24.4 us (33%)
  starting transfers between devices  22.1 us (30%)
  local copies, waits for them, and re-layouts  13 us (18%)
  Pallas kernels  12.2 us (17%)
  other arithmetic  0.8 us (1%)
  between operations  0.76 us (1%)
    ppermute x13, waiting for transfers between devices, shifted(): lax.ppermute(block, axis, [(i, (i + step) % count) for i in range(count)])  24.4 us
    ppermute x13, starting transfers between devices, shifted(): lax.ppermute(block, axis, [(i, (i + step) % count) for i in range(count)])  22.1 us
    unnamed x30, local copies, waits for them, and re-layouts  10.8 us
    pallas_call x1, Pallas kernels, mixer(): pl.pallas_call(mixer_kernel, name='mixer', out_shape=(shape((HALF, DRAFT,...  6.09 us
    pallas_call x1, Pallas kernels, ffn(): pl.pallas_call(ffn_kernel, name='ffn', out_shape=(shape((slots, width), F...  3.2 us
    pallas_call x1, Pallas kernels, keep(): pl.pallas_call(keep_kernel, name='keep', out_shape=jax.ShapeDtypeStruct(s...  2.03 us
  transfers between devices with their start and end apart: 13, of which 12 were waited for; matrix products, arithmetic and copies ran while one was open for 3% of the time, Pallas kernels for 3%

profile of v2, /device:TPU:6, one launch (start us, length us, event | category | flops | bytes accessed | tf_op | source)
XLA Modules:
  0.0 73.3 jit_solution(6389688872097360310)
XLA Ops:
  0.6 0.0 copy-start.5
  0.7 1.2 %fusion = (bf16[4,16,2,384]{3,2,1,0:T(2,128)(2,1)S(1)}, bf16[4,16,2,384]{3,2,1,0:T(2,128)(2,1)S(1)}) fusion(bf16[8,16,2,384]{3,2,1,0:T(2,128)(2,1)} %param.15), kind=kLoop, calls=%fused_computation.2 | loop fusion | bytes 393216 | tf_op jit(solution)/shard_map/slice | solution.py:328
  1.9 0.1 collective-permute-start
  2.0 7.8 %collective-permute-start.1 = (bf16[4,32,384]{2,1,0:T(8,128)(2,1)S(1)}, bf16[4,32,384]{2,1,0:T(8,128)(2,1)S(1)}, u32[]{:S(2)}, u32[]{:S(2)}) collective-permute-start(bf16[4,32,384]{2,1,0:T(8,128)(2,1)S(1)} %reshape.29), channel_id=1, source_target_pairs={{0,63},{1,0},{2,1},{3,2},{4,3},{5,4},{6,5},{7,6},{8,7},{9,8},{10,9... | collective-permute-start | bytes 294920 | tf_op jit(solution)/shard_map/ppermute | solution.py:305
  9.8 1.0 %reshape.27.own_ref = bf16[8,32,384]{2,1,0:T(8,128)(2,1)S(1)} reshape(bf16[8,16,2,384]{3,2,1,0:T(2,128)(2,1)} %param.15) | data formatting | bytes 393216 | tf_op jit(solution)/shard_map/reshape | solution.py:329
  10.8 0.8 %copy.18 = bf16[8,3,2,384]{3,0,2,1:T(8,128)(2,1)S(1)} copy(bf16[8,3,2,384]{3,2,1,0:T(2,128)(2,1)} %param.26) | data formatting | bytes 73728 | tf_op args[11]
  11.6 0.4 collective-permute-done.low_ref
  12.0 0.0 collective-permute-done.1.high_ref
  12.1 1.2 %copy-done = f32[8,2,128,128]{3,2,1,0:T(8,128)S(1)} copy-done((f32[8,2,128,128]{3,2,1,0:T(8,128)S(1)}, f32[8,2,128,128]{3,2,1,0:T(8,128)}, u32[]{:S(2)}) %copy-start) | copy-done | bytes 1048600
  13.3 0.7 copy-done.7
  14.0 0.7 copy-done.8
  14.7 0.7 copy-done.10
  15.3 0.7 copy-done.12
  16.0 0.7 copy-done.13
  16.7 6.1 %mixer.1 = (bf16[4,16,256]{2,1,0:T(8,128)(2,1)S(1)}, bf16[4,16,256]{2,1,0:T(8,128)(2,1)S(1)}, f32[8,2,16,128]{3,2,1,0:T(8,128)S(1)}, f32[8,2,16,128]{3,2,1,0:T(8...) custom-call(s32[512]{0:T(512)S(1)} %copy-done.8, s32[512]{0:T(512)S(1)} %copy-done.10, ...), custom_call_target="tpu_custom_call" | custom-call | flops 20000000 | bytes 2000000 | tf_op jit(solution)/shard_map/mixer/pallas_call | solution.py:149
  22.8 5.2 %collective-permute-start.3 = (bf16[4,16,256]{2,1,0:T(8,128)(2,1)S(1)}, bf16[4,16,256]{2,1,0:T(8,128)(2,1)S(1)}, u32[]{:S(2)}, u32[]{:S(2)}) collective-permute-start(bf16[4,16,256]{2,1,0:T(8,128)(2,1)S(1)} %get-tuple-element.17.low_ref), channel_id=1, source_target_pairs={{0,63},{1,0},{2,1},{3,2},{4,3},{5,4},{6,5},{7,6},{8,7},{9,8},{10,9... | collective-permute-start | bytes 98312 | tf_op jit(solution)/shard_map/ppermute | solution.py:305
  28.0 0.0 collective-permute-start.2
  28.0 1.6 %collective-permute-done.3.from_high_ref = bf16[4,16,256]{2,1,0:T(8,128)(2,1)S(1)} collective-permute-done((bf16[4,16,256]{2,1,0:T(8,128)(2,1)S(1)}, bf16[4,16,256]{2,1,0:T(8,128)(2,1)S(1)}, u32[]{:S(2)}, u32[]{:S(2)}) %collective-permute-start.3) | collective-permute-done | bytes 32800 | tf_op jit(solution)/shard_map/ppermute | solution.py:305
  29.6 5.1 %collective-permute-done.2.from_low_ref = bf16[4,16,256]{2,1,0:T(8,128)(2,1)S(1)} collective-permute-done((bf16[4,16,256]{2,1,0:T(8,128)(2,1)S(1)}, bf16[4,16,256]{2,1,0:T(8,128)(2,1)S(1)}, u32[]{:S(2)}, u32[]{:S(2)}) %collective-permute-start.2) | collective-permute-done | bytes 32800 | tf_op jit(solution)/shard_map/ppermute | solution.py:305
  34.7 0.0 copy-done.5
  34.7 1.0 %copy-done.6 = bf16[8,16,2048]{2,1,0:T(8,128)(2,1)S(1)} copy-done((bf16[8,16,2048]{2,1,0:T(8,128)(2,1)S(1)}, bf16[8,16,2048]{2,1,0:T(8,128)(2,1)}, u32[]{:S(2)}) %copy-start.6) | copy-done | bytes 524312
  35.7 0.9 %project.1 = (f32[128,512]{1,0:T(8,128)S(1)}, bf16[128,512]{1,0:T(8,128)(2,1)S(1)}, bf16[128,512]{1,0:T(8,128)(2,1)S(1)}, bf16[128,512]{1,0:T(8,128)(2,1)S(1)}) custom-call(s32[512]{0:T(512)S(1)} %copy-done.8, bf16[4,16,256]{2,1,0:T(8,128)(2,1)S(1)} %get-tuple-element.17.low_ref, bf16[4,16,256]{2,1,0:T(8,128)(2,1)S(1)} %get-tuple-element.18.high_ref, ...), custom_call_target="tpu_custom_call" | custom-call | flops 140000000 | bytes 2000000 | tf_op jit(solution)/shard_map/project/pallas_call | solution.py:230
  36.6 1.5 %collective-permute-start.4 = (bf16[128,512]{1,0:T(8,128)(2,1)S(1)}, bf16[128,512]{1,0:T(8,128)(2,1)S(1)}, u32[]{:S(2)}, u32[]{:S(2)}) collective-permute-start(bf16[128,512]{1,0:T(8,128)(2,1)S(1)} %get-tuple-element.20), channel_id=1, source_target_pairs={{0,128},{64,192},{128,0},{192,64},{1,129},{65,193},{129,1},{193,65... | collective-permute-start | bytes 393224 | tf_op jit(solution)/shard_map/ppermute | solution.py:305
  38.1 2.1 %collective-permute-start.5 = (bf16[128,512]{1,0:T(8,128)(2,1)S(1)}, bf16[128,512]{1,0:T(8,128)(2,1)S(1)}, u32[]{:S(2)}, u32[]{:S(2)}) collective-permute-start(bf16[128,512]{1,0:T(8,128)(2,1)S(1)} %get-tuple-element.21), channel_id=1, source_target_pairs={{0,64},{64,128},{128,192},{192,0},{1,65},{65,129},{129,193},{193,1... | collective-permute-start | bytes 393224 | tf_op jit(solution)/shard_map/ppermute | solution.py:305
  40.2 0.0 collective-permute-start.6
  40.2 3.0 %collective-permute-done.4 = bf16[128,512]{1,0:T(8,128)(2,1)S(1)} collective-permute-done((bf16[128,512]{1,0:T(8,128)(2,1)S(1)}, bf16[128,512]{1,0:T(8,128)(2,1)S(1)}, u32[]{:S(2)}, u32[]{:S(2)}) %collective-permute-start.4) | collective-permute-done | bytes 131104 | tf_op jit(solution)/shard_map/ppermute | solution.py:305
  43.2 1.0 %collective-permute-done.5 = bf16[128,512]{1,0:T(8,128)(2,1)S(1)} collective-permute-done((bf16[128,512]{1,0:T(8,128)(2,1)S(1)}, bf16[128,512]{1,0:T(8,128)(2,1)S(1)}, u32[]{:S(2)}, u32[]{:S(2)}) %collective-permute-start.5) | collective-permute-done | bytes 131104 | tf_op jit(solution)/shard_map/ppermute | solution.py:305
  44.2 3.9 %collective-permute-done.6 = bf16[128,512]{1,0:T(8,128)(2,1)S(1)} collective-permute-done((bf16[128,512]{1,0:T(8,128)(2,1)S(1)}, bf16[128,512]{1,0:T(8,128)(2,1)S(1)}, u32[]{:S(2)}, u32[]{:S(2)}) %collective-permute-start.6) | collective-permute-done | bytes 131104 | tf_op jit(solution)/shard_map/ppermute | solution.py:305
  48.1 0.1 add_convert_fusion.1.own_ref
  48.2 0.1 collective-permute-start.9
  48.3 0.7 collective-permute-start.8
  49.0 1.3 %collective-permute-start.7 = (bf16[128,512]{1,0:T(8,128)(2,1)S(1)}, bf16[128,512]{1,0:T(8,128)(2,1)S(1)}, u32[]{:S(2)}, u32[]{:S(2)}) collective-permute-start(bf16[128,512]{1,0:T(8,128)(2,1)S(1)} %add_convert_fusion.1.own_ref), channel_id=1, source_target_pairs={{0,192},{64,0},{128,64},{192,128},{1,193},{65,1},{129,65},{193,129... | collective-permute-start | bytes 393224 | tf_op jit(solution)/shard_map/ppermute | solution.py:305
  50.3 2.9 %collective-permute-done.9.prev_ref = bf16[128,512]{1,0:T(8,128)(2,1)S(1)} collective-permute-done((bf16[128,512]{1,0:T(8,128)(2,1)S(1)}, bf16[128,512]{1,0:T(8,128)(2,1)S(1)}, u32[]{:S(2)}, u32[]{:S(2)}) %collective-permute-start.9) | collective-permute-done | bytes 131104 | tf_op jit(solution)/shard_map/ppermute | solution.py:305
  53.2 1.6 %collective-permute-done.8.far_ref = bf16[128,512]{1,0:T(8,128)(2,1)S(1)} collective-permute-done((bf16[128,512]{1,0:T(8,128)(2,1)S(1)}, bf16[128,512]{1,0:T(8,128)(2,1)S(1)}, u32[]{:S(2)}, u32[]{:S(2)}) %collective-permute-start.8) | collective-permute-done | bytes 131104 | tf_op jit(solution)/shard_map/ppermute | solution.py:305
  54.8 1.4 %collective-permute-done.7.next_ref = bf16[128,512]{1,0:T(8,128)(2,1)S(1)} collective-permute-done((bf16[128,512]{1,0:T(8,128)(2,1)S(1)}, bf16[128,512]{1,0:T(8,128)(2,1)S(1)}, u32[]{:S(2)}, u32[]{:S(2)}) %collective-permute-start.7) | collective-permute-done | bytes 131104 | tf_op jit(solution)/shard_map/ppermute | solution.py:305
  56.2 0.0 copy-start.3
  56.2 1.8 %copy-done.3 = bf16[2048,704]{0,1:T(8,128)(2,1)S(1)} copy-done((bf16[2048,704]{0,1:T(8,128)(2,1)S(1)}, bf16[2048,704]{0,1:T(8,128)(2,1)}, u32[]{:S(2)}) %copy-start.3) | copy-done | bytes 2883608
  58.0 1.8 %copy-done.4 = bf16[704,2048]{1,0:T(8,128)(2,1)S(1)} copy-done((bf16[704,2048]{1,0:T(8,128)(2,1)S(1)}, bf16[704,2048]{1,0:T(8,128)(2,1)}, u32[]{:S(2)}) %copy-start.4) | copy-done | bytes 2883608
  59.9 3.2 %ffn.1 = (f32[128,512]{1,0:T(8,128)S(1)}, bf16[128,512]{1,0:T(8,128)(2,1)S(1)}, bf16[128,512]{1,0:T(8,128)(2,1)S(1)}, bf16[128,512]{1,0:T(8,128)(2,1)S(1)}) custom-call(s32[512]{0:T(512)S(1)} %copy-done.11, bf16[128,512]{1,0:T(8,128)(2,1)S(1)} %add_convert_fusion.1.own_ref, bf16[128,512]{1,0:T(8,128)(2,1)S(1)} %collective-permute-done.7.next_ref, ...), custom_call_target="tpu_custom_call" | custom-call | flops 1100000000 | bytes 9000000 | tf_op jit(solution)/shard_map/ffn/pallas_call | solution.py:284
  63.1 0.8 %collective-permute-start.10 = (bf16[128,512]{1,0:T(8,128)(2,1)S(1)}, bf16[128,512]{1,0:T(8,128)(2,1)S(1)}, u32[]{:S(2)}, u32[]{:S(2)}) collective-permute-start(bf16[128,512]{1,0:T(8,128)(2,1)S(1)} %get-tuple-element.24), channel_id=1, source_target_pairs={{0,128},{64,192},{128,0},{192,64},{1,129},{65,193},{129,1},{193,65... | collective-permute-start | bytes 393224 | tf_op jit(solution)/shard_map/ppermute | solution.py:305
  63.9 2.5 %collective-permute-start.11 = (bf16[128,512]{1,0:T(8,128)(2,1)S(1)}, bf16[128,512]{1,0:T(8,128)(2,1)S(1)}, u32[]{:S(2)}, u32[]{:S(2)}) collective-permute-start(bf16[128,512]{1,0:T(8,128)(2,1)S(1)} %get-tuple-element.25), channel_id=1, source_target_pairs={{0,64},{64,128},{128,192},{192,0},{1,65},{65,129},{129,193},{193,1... | collective-permute-start | bytes 393224 | tf_op jit(solution)/shard_map/ppermute | solution.py:305
  66.4 0.0 collective-permute-start.12
  66.4 0.6 copy.21
  67.0 2.0 %keep.1 = f32[8,2,128,128]{3,2,1,0:T(8,128)} custom-call(f32[8,2,128,128]{3,2,1,0:T(8,128)S(1)} %copy-done.1, f32[8,2,16,128]{3,2,1,0:T(8,128)S(1)} %get-tuple-element.27.value_ref, f32[8,2,16,128]{3,2,1,0:T(8,128)S(1)} %get-tuple-element.28.weight_ref, f32[8,2,1,128]{3,2,1,0:T(1,128)S(1)} %get-tuple-element.29.decay_ref), custom_call_target="tpu_custom_call" | custom-call | flops 20000000 | bytes 3000000 | tf_op jit(solution)/shard_map/keep/pallas_call | solution.py:189
  69.1 0.6 collective-permute-done.10
  69.6 0.4 collective-permute-done.11
  70.1 2.5 %collective-permute-done.12 = bf16[128,512]{1,0:T(8,128)(2,1)S(1)} collective-permute-done((bf16[128,512]{1,0:T(8,128)(2,1)S(1)}, bf16[128,512]{1,0:T(8,128)(2,1)S(1)}, u32[]{:S(2)}, u32[]{:S(2)}) %collective-permute-start.12) | collective-permute-done | bytes 131104 | tf_op jit(solution)/shard_map/ppermute | solution.py:305
  72.5 0.7 add_convert_fusion
  (20 shorter events, 0.1 us)
Async XLA Ops:
  0.6 34.1 %copy-start.5 = (bf16[256,2048]{1,0:T(8,128)(2,1)S(1)}, bf16[256,2048]{1,0:T(8,128)(2,1)}, u32[]{:S(2)}) copy-start(bf16[256,2048]{1,0:T(8,128)(2,1)} %weight_ref.1) | copy-start | bytes 3145732
  0.6 55.6 %copy-start.11 = (s32[512]{0:T(512)S(1)}, s32[512]{0:T(512)}, u32[]{:S(2)}) copy-start(s32[512]{0:T(512)} %length_ref.1) | copy-start | bytes 6148
  0.7 55.6 %copy-start.9 = (f32[2048]{0:T(1024)S(1)}, f32[2048]{0:T(1024)}, u32[]{:S(2)}) copy-start(f32[2048]{0:T(1024)} %param.21) | copy-start | bytes 24580
  1.9 10.1 %collective-permute-start = (bf16[4,32,384]{2,1,0:T(8,128)(2,1)S(1)}, bf16[4,32,384]{2,1,0:T(8,128)(2,1)S(1)}, u32[]{:S(2)}, u32[]{:S(2)}) collective-permute-start(bf16[4,32,384]{2,1,0:T(8,128)(2,1)S(1)} %reshape.28), channel_id=1, source_target_pairs={{0,1},{1,2},{2,3},{3,4},{4,5},{5,6},{6,7},{7,8},{8,9},{9,10},{10,1... | collective-permute-start | bytes 294920 | tf_op jit(solution)/shard_map/ppermute | solution.py:305
  2.0 10.0 %collective-permute-start.1 = (bf16[4,32,384]{2,1,0:T(8,128)(2,1)S(1)}, bf16[4,32,384]{2,1,0:T(8,128)(2,1)S(1)}, u32[]{:S(2)}, u32[]{:S(2)}) collective-permute-start(bf16[4,32,384]{2,1,0:T(8,128)(2,1)S(1)} %reshape.29), channel_id=1, source_target_pairs={{0,63},{1,0},{2,1},{3,2},{4,3},{5,4},{6,5},{7,6},{8,7},{9,8},{10,9... | collective-permute-start | bytes 294920 | tf_op jit(solution)/shard_map/ppermute | solution.py:305
  12.0 1.2 %copy-start = (f32[8,2,128,128]{3,2,1,0:T(8,128)S(1)}, f32[8,2,128,128]{3,2,1,0:T(8,128)}, u32[]{:S(2)}) copy-start(f32[8,2,128,128]{3,2,1,0:T(8,128)} %state_ref.3) | copy-start | bytes 3145732
  13.3 0.7 copy-start.7
  14.0 0.7 copy-start.8
  14.7 0.7 copy-start.10
  15.3 0.7 copy-start.12
  16.0 0.7 copy-start.13
  16.7 39.5 %copy-start.2 = (bf16[2048,704]{0,1:T(8,128)(2,1)S(1)}, bf16[2048,704]{0,1:T(8,128)(2,1)}, u32[]{:S(2)}) copy-start(bf16[2048,704]{0,1:T(8,128)(2,1)} %param.22) | copy-start | bytes 8650756
  22.8 6.8 %collective-permute-start.3 = (bf16[4,16,256]{2,1,0:T(8,128)(2,1)S(1)}, bf16[4,16,256]{2,1,0:T(8,128)(2,1)S(1)}, u32[]{:S(2)}, u32[]{:S(2)}) collective-permute-start(bf16[4,16,256]{2,1,0:T(8,128)(2,1)S(1)} %get-tuple-element.17.low_ref), channel_id=1, source_target_pairs={{0,63},{1,0},{2,1},{3,2},{4,3},{5,4},{6,5},{7,6},{8,7},{9,8},{10,9... | collective-permute-start | bytes 98312 | tf_op jit(solution)/shard_map/ppermute | solution.py:305
  28.0 6.7 %collective-permute-start.2 = (bf16[4,16,256]{2,1,0:T(8,128)(2,1)S(1)}, bf16[4,16,256]{2,1,0:T(8,128)(2,1)S(1)}, u32[]{:S(2)}, u32[]{:S(2)}) collective-permute-start(bf16[4,16,256]{2,1,0:T(8,128)(2,1)S(1)} %get-tuple-element.18.high_ref), channel_id=1, source_target_pairs={{0,1},{1,2},{2,3},{3,4},{4,5},{5,6},{6,7},{7,8},{8,9},{9,10},{10,1... | collective-permute-start | bytes 98312 | tf_op jit(solution)/shard_map/ppermute | solution.py:305
  34.7 1.0 %copy-start.6 = (bf16[8,16,2048]{2,1,0:T(8,128)(2,1)S(1)}, bf16[8,16,2048]{2,1,0:T(8,128)(2,1)}, u32[]{:S(2)}) copy-start(bf16[8,16,2048]{2,1,0:T(8,128)(2,1)} %param.20) | copy-start | bytes 1572868
  36.6 6.6 %collective-permute-start.4 = (bf16[128,512]{1,0:T(8,128)(2,1)S(1)}, bf16[128,512]{1,0:T(8,128)(2,1)S(1)}, u32[]{:S(2)}, u32[]{:S(2)}) collective-permute-start(bf16[128,512]{1,0:T(8,128)(2,1)S(1)} %get-tuple-element.20), channel_id=1, source_target_pairs={{0,128},{64,192},{128,0},{192,64},{1,129},{65,193},{129,1},{193,65... | collective-permute-start | bytes 393224 | tf_op jit(solution)/shard_map/ppermute | solution.py:305
  38.1 6.1 %collective-permute-start.5 = (bf16[128,512]{1,0:T(8,128)(2,1)S(1)}, bf16[128,512]{1,0:T(8,128)(2,1)S(1)}, u32[]{:S(2)}, u32[]{:S(2)}) collective-permute-start(bf16[128,512]{1,0:T(8,128)(2,1)S(1)} %get-tuple-element.21), channel_id=1, source_target_pairs={{0,64},{64,128},{128,192},{192,0},{1,65},{65,129},{129,193},{193,1... | collective-permute-start | bytes 393224 | tf_op jit(solution)/shard_map/ppermute | solution.py:305
  40.2 7.9 %collective-permute-start.6 = (bf16[128,512]{1,0:T(8,128)(2,1)S(1)}, bf16[128,512]{1,0:T(8,128)(2,1)S(1)}, u32[]{:S(2)}, u32[]{:S(2)}) collective-permute-start(bf16[128,512]{1,0:T(8,128)(2,1)S(1)} %get-tuple-element.22), channel_id=1, source_target_pairs={{0,192},{64,0},{128,64},{192,128},{1,193},{65,1},{129,65},{193,129... | collective-permute-start | bytes 393224 | tf_op jit(solution)/shard_map/ppermute | solution.py:305
  48.2 5.0 %collective-permute-start.9 = (bf16[128,512]{1,0:T(8,128)(2,1)S(1)}, bf16[128,512]{1,0:T(8,128)(2,1)S(1)}, u32[]{:S(2)}, u32[]{:S(2)}) collective-permute-start(bf16[128,512]{1,0:T(8,128)(2,1)S(1)} %add_convert_fusion.1.own_ref), channel_id=1, source_target_pairs={{0,64},{64,128},{128,192},{192,0},{1,65},{65,129},{129,193},{193,1... | collective-permute-start | bytes 393224 | tf_op jit(solution)/shard_map/ppermute | solution.py:305
  48.3 6.6 %collective-permute-start.8 = (bf16[128,512]{1,0:T(8,128)(2,1)S(1)}, bf16[128,512]{1,0:T(8,128)(2,1)S(1)}, u32[]{:S(2)}, u32[]{:S(2)}) collective-permute-start(bf16[128,512]{1,0:T(8,128)(2,1)S(1)} %add_convert_fusion.1.own_ref), channel_id=1, source_target_pairs={{0,128},{64,192},{128,0},{192,64},{1,129},{65,193},{129,1},{193,65... | collective-permute-start | bytes 393224 | tf_op jit(solution)/shard_map/ppermute | solution.py:305
  49.0 7.3 %collective-permute-start.7 = (bf16[128,512]{1,0:T(8,128)(2,1)S(1)}, bf16[128,512]{1,0:T(8,128)(2,1)S(1)}, u32[]{:S(2)}, u32[]{:S(2)}) collective-permute-start(bf16[128,512]{1,0:T(8,128)(2,1)S(1)} %add_convert_fusion.1.own_ref), channel_id=1, source_target_pairs={{0,192},{64,0},{128,64},{192,128},{1,193},{65,1},{129,65},{193,129... | collective-permute-start | bytes 393224 | tf_op jit(solution)/shard_map/ppermute | solution.py:305
  56.2 1.8 %copy-start.3 = (bf16[2048,704]{0,1:T(8,128)(2,1)S(1)}, bf16[2048,704]{0,1:T(8,128)(2,1)}, u32[]{:S(2)}) copy-start(bf16[2048,704]{0,1:T(8,128)(2,1)} %param.23) | copy-start | bytes 8650756
  58.0 1.8 %copy-start.4 = (bf16[704,2048]{1,0:T(8,128)(2,1)S(1)}, bf16[704,2048]{1,0:T(8,128)(2,1)}, u32[]{:S(2)}) copy-start(bf16[704,2048]{1,0:T(8,128)(2,1)} %down_ref.1) | copy-start | bytes 8650756
  59.9 7.2 %copy-start.1 = (f32[8,2,128,128]{3,2,1,0:T(8,128)S(1)}, f32[8,2,128,128]{3,2,1,0:T(8,128)}, u32[]{:S(2)}) copy-start(f32[8,2,128,128]{3,2,1,0:T(8,128)} %state_ref.3) | copy-start | bytes 3145732
  63.1 6.6 %collective-permute-start.10 = (bf16[128,512]{1,0:T(8,128)(2,1)S(1)}, bf16[128,512]{1,0:T(8,128)(2,1)S(1)}, u32[]{:S(2)}, u32[]{:S(2)}) collective-permute-start(bf16[128,512]{1,0:T(8,128)(2,1)S(1)} %get-tuple-element.24), channel_id=1, source_target_pairs={{0,128},{64,192},{128,0},{192,64},{1,129},{65,193},{129,1},{193,65... | collective-permute-start | bytes 393224 | tf_op jit(solution)/shard_map/ppermute | solution.py:305
  63.9 6.2 %collective-permute-start.11 = (bf16[128,512]{1,0:T(8,128)(2,1)S(1)}, bf16[128,512]{1,0:T(8,128)(2,1)S(1)}, u32[]{:S(2)}, u32[]{:S(2)}) collective-permute-start(bf16[128,512]{1,0:T(8,128)(2,1)S(1)} %get-tuple-element.25), channel_id=1, source_target_pairs={{0,64},{64,128},{128,192},{192,0},{1,65},{65,129},{129,193},{193,1... | collective-permute-start | bytes 393224 | tf_op jit(solution)/shard_map/ppermute | solution.py:305
  66.4 6.2 %collective-permute-start.12 = (bf16[128,512]{1,0:T(8,128)(2,1)S(1)}, bf16[128,512]{1,0:T(8,128)(2,1)S(1)}, u32[]{:S(2)}, u32[]{:S(2)}) collective-permute-start(bf16[128,512]{1,0:T(8,128)(2,1)S(1)} %get-tuple-element.26), channel_id=1, source_target_pairs={{0,192},{64,0},{128,64},{192,128},{1,193},{65,1},{129,65},{193,129... | collective-permute-start | bytes 393224 | tf_op jit(solution)/shard_map/ppermute | solution.py:305

commit v3 on v2

v3 whole, which is shorter than its diff:
```python
import jax
import jax.numpy as jnp
from jax import lax
from jax.experimental import pallas as pl
from jax.experimental.pallas import tpu as pltpu
from jax.sharding import PartitionSpec as P

DK = 128
DRAFT = 16
CONV = 4
HALF = 4
ROWS = 2 * HALF
BF = jnp.bfloat16
PARAMS = pltpu.CompilerParams(vmem_limit_bytes=12 * 1024 * 1024)
F32 = jnp.float32
PACKED = 2 * DK + 3 * DRAFT
VM = pl.BlockSpec(memory_space=pltpu.VMEM)
SM = pl.BlockSpec(memory_space=pltpu.SMEM)
HB = pl.BlockSpec(memory_space=pltpu.HBM)


def source_of(owner_ref, row):
    me = lax.axis_index("req")
    partner = owner_ref[me * ROWS + row]
    local = partner // ROWS == me
    return partner, local, partner % HALF


def block_of(block):
    return slice(block * DK, (block + 1) * DK)


def call(kernel, out_shape, in_specs, scratch, flops, moved, *args):
    return pl.pallas_call(
        kernel,
        name=kernel.__name__,
        out_shape=out_shape,
        in_specs=in_specs,
        out_specs=jax.tree.map(lambda _: VM, out_shape),
        scratch_shapes=scratch,
        compiler_params=PARAMS,
        cost_estimate=pl.CostEstimate(flops=flops, bytes_accessed=moved, transcendentals=0),
    )(*args)


def pack(state_ref, edge_ref, low_ref, high_ref, states, edges, rows_scr, sems, edge_sem):
    copies = [
        pltpu.make_async_copy(state_ref.at[row], states.at[row], sems.at[row])
        for row in range(ROWS)
    ]
    edge_copy = pltpu.make_async_copy(edge_ref, edges, edge_sem)
    edge_copy.start()
    for copy in copies:
        copy.start()
    rows_scr[...] = jnp.zeros_like(rows_scr)
    edge_copy.wait()
    for row in range(ROWS):
        out_ref = low_ref if row < HALF else high_ref
        place = row % HALF
        for step in range(CONV - 1):
            both = edges[row, step].astype(F32)
            for block in range(3):
                rows_scr[row, block, 2 * step : 2 * step + 2, :] = both[:, block_of(block)]
        for block in range(3):
            start = 2 * DK + block * DRAFT
            out_ref[place, start : start + DRAFT, :] = rows_scr[row, block].astype(BF)
    for row in range(ROWS):
        out_ref = low_ref if row < HALF else high_ref
        copies[row].wait()
        for head in range(2):
            out_ref[row % HALF, block_of(head), :] = states[row, head].astype(BF)


def pack_call(states, edges):
    half = jax.ShapeDtypeStruct((HALF, PACKED, DK), BF)
    return call(
        pack, (half, half), [HB, HB],
        [
            pltpu.VMEM(states.shape, F32),
            pltpu.VMEM(edges.shape, BF),
            pltpu.VMEM((ROWS, 3, DRAFT, DK), F32),
            pltpu.SemaphoreType.DMA((ROWS,)),
            pltpu.SemaphoreType.DMA,
        ],
        1_000_000, 2_000_000, states, edges,
    )


def fill_window(window, row, drafts):
    for step in range(DRAFT):
        both = drafts[step].astype(F32)
        for block in range(3):
            window[row, block, 8 + 2 * step : 10 + 2 * step, :] = both[:, block_of(block)]


def convolve(window, conv_ref, row, head, block):
    total = None
    for shift in range(CONV):
        taps = conv_ref[shift, head, block_of(block)]
        rows = window[row, block, pl.ds(2 + 2 * shift + head, DRAFT, stride=2), :]
        term = taps[None, :] * rows
        total = term if total is None else total + term
    return total


def as_query(x):
    return x * jax.nn.sigmoid(x) * DK ** (-0.5)


def as_value(x):
    return x * jax.nn.sigmoid(x)


def prepare(
    draft_ref, conv_hbm, bias_hbm, gain_hbm, gate_hbm, up_hbm, down_hbm,
    query_ref, forget_ref, value_ref, conv_ref, bias_ref, gain_ref, gate_ref, up_ref, down_ref,
    drafts, window, sems,
):
    pairs = (
        (draft_ref, drafts), (conv_hbm, conv_ref), (bias_hbm, bias_ref), (gain_hbm, gain_ref),
        (gate_hbm, gate_ref), (up_hbm, up_ref), (down_hbm, down_ref),
    )
    copies = [
        pltpu.make_async_copy(src, dst, sems.at[i]) for i, (src, dst) in enumerate(pairs)
    ]
    for copy in copies:
        copy.start()
    window[...] = jnp.zeros_like(window)
    for copy in copies[:4]:
        copy.wait()
    for row in range(ROWS):
        fill_window(window, row, drafts[row])
    half = DRAFT // 2
    for row in range(ROWS):
        for head in range(2):
            queries, gates, values = [
                convolve(window, conv_ref, row, head, block) for block in range(3)
            ]
            query_ref[row, head, :half] = queries[:half]
            query_ref[row, head, half:] = as_query(queries[half:])
            gates = gates + bias_ref[head, :][None, :]
            forget_ref[row, head, :half] = gates[:half]
            forget_ref[row, head, half:] = jax.nn.sigmoid(gates[half:])
            value_ref[row, head, :half] = values[:half]
            value_ref[row, head, half:] = as_value(values[half:])
    for copy in copies[4:]:
        copy.wait()


def prepare_call(drafts, conv, bias, gain, gate_t, up_t, down):
    rows = jax.ShapeDtypeStruct((ROWS, 2, DRAFT, DK), F32)
    copied = [jax.ShapeDtypeStruct(x.shape, x.dtype) for x in (conv, bias, gain, gate_t, up_t, down)]
    return call(
        prepare, (rows, rows, rows, *copied), [HB] * 7,
        [
            pltpu.VMEM(drafts.shape, BF),
            pltpu.VMEM((ROWS, 3, 40, DK), F32),
            pltpu.SemaphoreType.DMA((7,)),
        ],
        5_000_000, 18_000_000, drafts, conv, bias, gain, gate_t, up_t, down,
    )


def mixer(
    owner_ref, low_ref, high_ref, from_low_ref, from_high_ref, query_ref, forget_ref, value_ref,
    conv_ref, bias_ref, gain_ref, mixed_ref, edges, states, query_scr, forget_scr, value_scr,
):
    half = DRAFT // 2
    edges[...] = jnp.zeros_like(edges)
    for row in range(ROWS):
        _, local, place = source_of(owner_ref, row)
        mine_ref, other_ref = (low_ref, from_low_ref) if row < HALF else (high_ref, from_high_ref)
        for block in range(3):
            start = 2 * DK + block * DRAFT
            mine = mine_ref[row % HALF, start : start + DRAFT, :].astype(F32)
            other = other_ref[place, start : start + DRAFT, :].astype(F32)
            edges[row, block, :DRAFT, :] = jnp.where(local, mine, other)

        @pl.when(local)
        def _():
            states[row] = mine_ref[row % HALF, : 2 * DK, :]

        @pl.when(jnp.logical_not(local))
        def _():
            states[row] = other_ref[place, : 2 * DK, :]

    sub_iota = lax.broadcasted_iota(jnp.int32, (1, DRAFT, DK), 1)

    def pair(step, _):
        base = step * 2
        for sub in range(2):
            row = base + sub
            for head in range(2):
                slot = sub * 2 + head
                for block, (in_ref, out, act) in enumerate(
                    (
                        (query_ref, query_scr, as_query),
                        (forget_ref, forget_scr, jax.nn.sigmoid),
                        (value_ref, value_scr, as_value),
                    )
                ):
                    first = in_ref[row, head, :half]
                    for shift in range(CONV - 1):
                        taps = conv_ref[shift, head, block_of(block)]
                        rows = edges[row, block, pl.ds(2 * shift + head, half, stride=2), :]
                        first = first + taps[None, :] * rows
                    out[slot, :half] = act(first)
                    out[slot, half:] = in_ref[row, head, half:]
        queries = query_scr[...]
        forget = forget_scr[...]
        values = value_scr[...]
        weights = jnp.zeros((4, DRAFT, DK), F32)
        decay = jnp.ones((4, 1, DK), F32)
        head_rows = []
        query_rows = []
        for t in range(DRAFT):
            forget_t = forget[:, t : t + 1, :]
            query_t = queries[:, t : t + 1, :]
            decay = decay * forget_t
            weights = jnp.where(sub_iota == t, 1.0 - forget_t, weights * forget_t)
            scores = jnp.sum(weights * query_t, axis=-1, keepdims=True)
            head_rows.append(jnp.sum(scores * values, axis=1, keepdims=True))
            query_rows.append(query_t * decay)
        local_out = jnp.concatenate(head_rows, axis=1)
        decayed = jnp.concatenate(query_rows, axis=1)
        for sub in range(2):
            row = base + sub
            for head in range(2):
                slot = sub * 2 + head
                fine = decayed[slot]
                coarse = fine.astype(BF)
                stacked = jnp.concatenate([coarse, (fine - coarse.astype(F32)).astype(BF)], axis=0)
                both = jnp.dot(
                    stacked, states[row, block_of(head), :], preferred_element_type=F32
                )
                out = local_out[slot] + (both[:DRAFT] + both[DRAFT:])
                scale = lax.rsqrt(jnp.mean(out * out, axis=-1, keepdims=True) + 1e-05)
                mixed_ref[row, :, block_of(head)] = (
                    out * scale * gain_ref[head, :][None, :]
                ).astype(BF)
        return 0

    lax.fori_loop(0, ROWS // 2, pair, 0)


def mixer_call(owner, low, high, from_low, from_high, queries, forget, values, conv, bias, gain):
    return call(
        mixer, jax.ShapeDtypeStruct((ROWS, DRAFT, 2 * DK), BF), [SM] + [VM] * 10,
        [
            pltpu.VMEM((ROWS, 3, 24, DK), F32),
            pltpu.VMEM((ROWS, 2 * DK, DK), BF),
            pltpu.VMEM((4, DRAFT, DK), F32),
            pltpu.VMEM((4, DRAFT, DK), F32),
            pltpu.VMEM((4, DRAFT, DK), F32),
        ],
        20_000_000, 2_000_000,
        owner, low, high, from_low, from_high, queries, forget, values, conv, bias, gain,
    )


def later(x, shift):
    return jnp.concatenate([x[shift:], jnp.ones((shift, DK), F32)], axis=0)


def keep(
    owner_ref, accept_ref, draft_ref, low_ref, high_ref, edge_ref, state_ref, conv_ref, bias_ref,
    kept_ref, edges_out_ref, drafts, edges, states, picked, window, sems,
):
    state_copies = [
        pltpu.make_async_copy(state_ref.at[row], states.at[row], sems.at[row])
        for row in range(ROWS)
    ]
    draft_copy = pltpu.make_async_copy(draft_ref, drafts, sems.at[ROWS])
    edge_copy = pltpu.make_async_copy(edge_ref, edges, sems.at[ROWS + 1])
    draft_copy.start()
    edge_copy.start()
    for copy in state_copies:
        copy.start()
    draft_copy.wait()
    edge_copy.wait()
    position = lax.broadcasted_iota(jnp.int32, (DRAFT, DK), 0)
    for row in range(ROWS):
        partner, local, place = source_of(owner_ref, row)
        other_ref = low_ref if row < HALF else high_ref

        @pl.when(local)
        def _():
            picked[row] = drafts[row]

        @pl.when(jnp.logical_not(local))
        def _():
            picked[row] = other_ref[place]

    for row in range(ROWS):
        fill_window(window, row, picked[row])
        for step in range(CONV - 1):
            both = edges[row, step].astype(F32)
            for block in range(3):
                window[row, block, 2 + 2 * step : 4 + 2 * step, :] = both[:, block_of(block)]
    for row in range(ROWS):
        partner, _, _ = source_of(owner_ref, row)
        length = accept_ref[partner]
        state_copies[row].wait()
        for head in range(2):
            gates = convolve(window, conv_ref, row, head, 1) + bias_ref[head, :][None, :]
            values = as_value(convolve(window, conv_ref, row, head, 2))
            forget = jax.nn.sigmoid(gates)
            inside = position < length
            weights = jnp.where(inside, 1.0 - forget, 0.0)
            factors = jnp.where(inside, forget, 1.0)
            after = later(factors, 1)
            for shift in (1, 2, 4, 8):
                after = after * later(after, shift)
            update = lax.dot_general(
                weights * after,
                values,
                (((0,), (0,)), ((), ())),
                preferred_element_type=F32,
                precision=lax.Precision.HIGHEST,
            )
            decay = (factors * after)[:1, :]
            column = jnp.transpose(jnp.broadcast_to(decay, (DK, DK)))
            kept_ref[row, head] = column * states[row, head] + update
        for block in range(3):
            turned = pltpu.roll(window[row, block], 38 - 2 * length, 0)
            for step in range(CONV - 1):
                edges_out_ref[row, step, :, block_of(block)] = turned[
                    2 * step : 2 * step + 2
                ].astype(BF)


def keep_call(owner, accept, drafts, low, high, edges, states, conv, bias):
    shape = jax.ShapeDtypeStruct
    return call(
        keep, (shape(states.shape, F32), shape(edges.shape, BF)),
        [SM, SM, HB, VM, VM, HB, HB, VM, VM],
        [
            pltpu.VMEM(drafts.shape, BF),
            pltpu.VMEM(edges.shape, BF),
            pltpu.VMEM(states.shape, F32),
            pltpu.VMEM(drafts.shape, BF),
            pltpu.VMEM((ROWS, 3, 40, DK), F32),
            pltpu.SemaphoreType.DMA((ROWS + 2,)),
        ],
        20_000_000, 3_000_000, owner, accept, drafts, low, high, edges, states, conv, bias,
    )


def columns_of(step, width):
    place = (lax.axis_index("grp") + step) % 4
    return pl.ds(pl.multiple_of(place * width, width), width)


def project_kernel(
    rows_ref, weight_ref, resid_ref, own_ref, next_ref, far_ref, prev_ref,
):
    width = own_ref.shape[1]
    rows = rows_ref[...]
    for step, out_ref in ((2, far_ref), (1, next_ref), (3, prev_ref)):
        part = jnp.dot(rows, weight_ref[:, columns_of(step, width)], preferred_element_type=F32)
        out_ref[...] = part.astype(BF)
    part = jnp.dot(rows, weight_ref[:, columns_of(0, width)], preferred_element_type=F32)
    own_ref[...] = part + resid_ref[:, columns_of(0, width)].astype(F32)


def project(rows, weight, resid):
    slots, model = resid.shape
    width = model // 4
    shape = jax.ShapeDtypeStruct
    return pl.pallas_call(
        project_kernel,
        name="project",
        out_shape=(
            shape((slots, width), F32),
            shape((slots, width), BF),
            shape((slots, width), BF),
            shape((slots, width), BF),
        ),
        in_specs=[VM] * 3,
        out_specs=tuple([VM] * 4),
        compiler_params=PARAMS,
        cost_estimate=pl.CostEstimate(
            flops=140_000_000, bytes_accessed=2_000_000, transcendentals=0
        ),
    )(rows, weight, resid)


def ffn_kernel(
    length_ref, own_ref, next_ref, far_ref, prev_ref, gain_ref, gate_ref, up_ref, down_ref,
    own_out_ref, next_out_ref, far_out_ref, prev_out_ref, normed_scr,
):
    width = own_ref.shape[1]
    parts = ((0, own_ref), (1, next_ref), (2, far_ref), (3, prev_ref))
    total = None
    for _, ref in parts:
        block = ref[...].astype(F32)
        square = jnp.sum(block * block, axis=-1, keepdims=True)
        total = square if total is None else total + square
    scale = lax.rsqrt(total / (4 * width) + 1e-05)
    for step, ref in parts:
        columns = columns_of(step, width)
        normed_scr[:, columns] = (ref[...].astype(F32) * scale * gain_ref[:, columns]).astype(BF)
    normed = normed_scr[...]
    dims = (((1,), (1,)), ((), ()))
    gate = lax.dot_general(normed, gate_ref[...], dims, preferred_element_type=F32)
    up = lax.dot_general(normed, up_ref[...], dims, preferred_element_type=F32)
    hidden = (gate * jax.nn.sigmoid(gate) * up).astype(BF)
    me = lax.axis_index("req")
    position = lax.broadcasted_iota(jnp.int32, (DRAFT, 1), 0)
    live = jnp.concatenate(
        [(position < length_ref[me * ROWS + row]).astype(F32) for row in range(ROWS)], axis=0
    )
    for step, out_ref in ((2, far_out_ref), (1, next_out_ref), (3, prev_out_ref)):
        part = jnp.dot(hidden, down_ref[:, columns_of(step, width)], preferred_element_type=F32)
        out_ref[...] = (part * live).astype(BF)
    part = jnp.dot(hidden, down_ref[:, columns_of(0, width)], preferred_element_type=F32)
    own_out_ref[...] = (part + own_ref[...].astype(F32)) * live


def ffn(lengths, own, following, far, preceding, gain, gate_t, up_t, down):
    slots, width = own.shape
    shape = jax.ShapeDtypeStruct
    return pl.pallas_call(
        ffn_kernel,
        name="ffn",
        out_shape=(
            shape((slots, width), F32),
            shape((slots, width), BF),
            shape((slots, width), BF),
            shape((slots, width), BF),
        ),
        in_specs=[SM] + [VM] * 8,
        out_specs=tuple([VM] * 4),
        scratch_shapes=[pltpu.VMEM((slots, 4 * width), BF)],
        compiler_params=PARAMS,
        cost_estimate=pl.CostEstimate(
            flops=1_100_000_000, bytes_accessed=9_000_000, transcendentals=100_000
        ),
    )(lengths, own, following, far, preceding, gain, gate_t, up_t, down)


def shifted(block, axis, step):
    count = lax.axis_size(axis)
    return lax.ppermute(block, axis, [(i, (i + step) % count) for i in range(count)])


def shards(
    mix_inputs,
    conv_weight,
    forget_bias,
    norm_gain,
    out_weight,
    resid,
    ffn_gain,
    gate_weight,
    up_weight,
    down_weight,
    held_states,
    held_edges,
    draft_lengths,
    accepted,
    owner_row,
):
    slots = ROWS * DRAFT
    low, high = pack_call(held_states, held_edges)
    from_low = shifted(high, "req", 1)
    from_high = shifted(low, "req", -1)
    queries, forget, values, conv, bias, gain, gate_t, up_t, down = prepare_call(
        mix_inputs, conv_weight, forget_bias, norm_gain,
        gate_weight.T, up_weight.T, down_weight,
    )
    mixed = mixer_call(
        owner_row, low, high, from_low, from_high, queries, forget, values, conv, bias, gain
    )
    drafts_low = shifted(mix_inputs[HALF:], "req", 1)
    drafts_high = shifted(mix_inputs[:HALF], "req", -1)
    kept_states, kept_edges = keep_call(
        owner_row, accepted, mix_inputs, drafts_low, drafts_high, held_edges, held_states,
        conv, bias,
    )
    own_part, to_next, to_far, to_prev = project(
        mixed.reshape(slots, -1), out_weight, resid.reshape(slots, -1)
    )
    far = shifted(to_far, "grp", 2)
    following = shifted(to_next, "grp", 1)
    preceding = shifted(to_prev, "grp", -1)
    stream = (
        own_part + far.astype(F32) + following.astype(F32) + preceding.astype(F32)
    ).astype(BF)
    far = shifted(stream, "grp", 2)
    preceding = shifted(stream, "grp", 1)
    following = shifted(stream, "grp", -1)
    own_part, to_next, to_far, to_prev = ffn(
        draft_lengths, stream, following, far, preceding, ffn_gain[None, :], gate_t, up_t, down
    )
    far = shifted(to_far, "grp", 2)
    following = shifted(to_next, "grp", 1)
    preceding = shifted(to_prev, "grp", -1)
    layer_out = (
        own_part + far.astype(F32) + following.astype(F32) + preceding.astype(F32)
    ).astype(BF)
    return (layer_out.reshape(ROWS, DRAFT, -1), kept_states, kept_edges)


def solution(mesh):
    return jax.shard_map(
        shards,
        mesh=mesh,
        in_specs=(
            P("req", None, "grp", None),
            P(None, "grp", None),
            P("grp", None),
            P("grp", None),
            P("grp", None),
            P("req", None, None),
            P(),
            P(None, "grp"),
            P(None, "grp"),
            P("grp", None),
            P("req", "grp", None, None),
            P("req", None, "grp", None),
            P(),
            P(),
            P(),
        ),
        out_specs=(P("req", None, "grp"), P("req", "grp", None, None), P("req", None, "grp", None)),
        check_vma=False,
    )
```

time: 73.7 us -> 70.1 us (0.951)
  the two profiles are of different devices: /device:TPU:6 before, /device:TPU:4 now
where the time goes in v3:
time: 70.1 us; the launch traced here: 69.7 us
  starting transfers between devices  26.2 us (37%)
  waiting for transfers between devices  16.4 us (23%)
  Pallas kernels  14.9 us (21%)
  local copies, waits for them, and re-layouts  10.6 us (15%)
  between operations  0.85 us (1%)
  other arithmetic  0.79 us (1%)
    ppermute x13, starting transfers between devices, shifted(): lax.ppermute(block, axis, [(i, (i + step) % count) for i in range(count)])  26.2 us
    ppermute x13, waiting for transfers between devices, shifted(): lax.ppermute(block, axis, [(i, (i + step) % count) for i in range(count)])  16.4 us
    pallas_call x4, Pallas kernels, call(): pl.pallas_call(kernel, name=kernel.__name__, out_shape=out_shape, in_spec...  11.3 us
    unnamed x36, local copies, waits for them, and re-layouts  10.5 us
    pallas_call x1, Pallas kernels, ffn(): pl.pallas_call(ffn_kernel, name='ffn', out_shape=(shape((slots, width), F...  3.21 us
  transfers between devices with their start and end apart: 13, of which 7 were waited for; matrix products, arithmetic and copies ran while one was open for 0% of the time, Pallas kernels for 11%

profile of v3, /device:TPU:4, one launch (start us, length us, event | category | flops | bytes accessed | tf_op | source)
XLA Modules:
  0.0 69.7 jit_solution(9110348022699860583)
XLA Ops:
  0.6 0.0 copy-start
  0.6 1.2 %copy-done = f32[8,2,128,128]{3,2,1,0:T(8,128)S(1)} copy-done((f32[8,2,128,128]{3,2,1,0:T(8,128)S(1)}, f32[8,2,128,128]{3,2,1,0:T(8,128)}, u32[]{:S(2)}) %copy-start) | copy-done | bytes 1048600
  1.9 0.8 %copy-done.9 = bf16[8,3,2,384]{3,2,1,0:T(2,128)(2,1)S(1)} copy-done((bf16[8,3,2,384]{3,2,1,0:T(2,128)(2,1)S(1)}, bf16[8,3,2,384]{3,2,1,0:T(2,128)(2,1)}, u32[]{:S(2)}) %copy-start.9) | copy-done | bytes 36888
  2.6 1.6 %pack.1 = (bf16[4,304,128]{2,1,0:T(8,128)(2,1)S(1)}, bf16[4,304,128]{2,1,0:T(8,128)(2,1)S(1)}) custom-call(f32[8,2,128,128]{3,2,1,0:T(8,128)S(1)} %copy-done, bf16[8,3,2,384]{3,2,1,0:T(2,128)(2,1)S(1)} %copy-done.9), custom_call_target="tpu_custom_call" | custom-call | flops 1000000 | bytes 2000000 | tf_op jit(solution)/shard_map/pack/pallas_call | solution.py:34
  4.2 0.1 collective-permute-start
  4.3 7.8 %collective-permute-start.1 = (bf16[4,304,128]{2,1,0:T(8,128)(2,1)S(1)}, bf16[4,304,128]{2,1,0:T(8,128)(2,1)S(1)}, u32[]{:S(2)}, u32[]{:S(2)}) collective-permute-start(bf16[4,304,128]{2,1,0:T(8,128)(2,1)S(1)} %get-tuple-element.24.low_ref), channel_id=1, source_target_pairs={{0,63},{1,0},{2,1},{3,2},{4,3},{5,4},{6,5},{7,6},{8,7},{9,8},{10,9... | collective-permute-start | bytes 933896 | tf_op jit(solution)/shard_map/ppermute | solution.py:444
  12.1 1.8 %copy-done.2 = bf16[2048,704]{0,1:T(8,128)(2,1)S(1)} copy-done((bf16[2048,704]{0,1:T(8,128)(2,1)S(1)}, bf16[2048,704]{0,1:T(8,128)(2,1)}, u32[]{:S(2)}) %copy-start.2) | copy-done | bytes 2883608
  13.9 1.8 %copy-done.3 = bf16[2048,704]{0,1:T(8,128)(2,1)S(1)} copy-done((bf16[2048,704]{0,1:T(8,128)(2,1)S(1)}, bf16[2048,704]{0,1:T(8,128)(2,1)}, u32[]{:S(2)}) %copy-start.3) | copy-done | bytes 2883608
  15.7 1.8 %copy-done.4 = bf16[704,2048]{1,0:T(8,128)(2,1)S(1)} copy-done((bf16[704,2048]{1,0:T(8,128)(2,1)S(1)}, bf16[704,2048]{1,0:T(8,128)(2,1)}, u32[]{:S(2)}) %copy-start.4) | copy-done | bytes 2883608
  17.6 0.9 %copy-done.5 = bf16[8,16,2,384]{3,2,1,0:T(2,128)(2,1)S(1)} copy-done((bf16[8,16,2,384]{3,2,1,0:T(2,128)(2,1)S(1)}, bf16[8,16,2,384]{3,2,1,0:T(2,128)(2,1)}, u32[]{:S(2)}) %copy-start.5) | copy-done | bytes 196632
  18.5 0.7 %copy-done.11 = f32[4,2,384]{2,1,0:T(2,128)S(1)} copy-done((f32[4,2,384]{2,1,0:T(2,128)S(1)}, f32[4,2,384]{2,1,0:T(2,128)}, u32[]{:S(2)}) %copy-start.11) | copy-done | bytes 12312
  19.2 0.7 copy-done.16
  19.9 0.7 copy-done.17
  20.6 1.2 %prepare.1 = (f32[8,2,16,128]{3,2,1,0:T(8,128)S(1)}, f32[8,2,16,128]{3,2,1,0:T(8,128)S(1)}, f32[8,2,16,128]{3,2,1,0:T(8,128)S(1)}, f32[4,2,384]{2,1,0:T(2,128)S(...) custom-call(bf16[8,16,2,384]{3,2,1,0:T(2,128)(2,1)S(1)} %copy-done.5, ...), custom_call_target="tpu_custom_call" | custom-call | flops 5000000 | bytes 18000000 | tf_op jit(solution)/shard_map/prepare/pallas_call | solution.py:34
  21.8 0.0 copy-start.13
  21.8 0.0 copy-start.14
  21.8 0.0 collective-permute-done.from_low_ref
  21.8 0.0 collective-permute-done.1.from_high_ref
  21.8 2.1 %mixer.1 = bf16[8,16,256]{2,1,0:T(8,128)(2,1)S(1)} custom-call(s32[512]{0:T(512)S(1)} %copy-done.12, bf16[4,304,128]{2,1,0:T(8,128)(2,1)S(1)} %get-tuple-element.24.low_ref, bf16[4,304,128]{2,1,0:T(8,128)(2,1)S(1)} %get-tuple-element.25.high_ref, bf16[4,304,128]{2,1,0:T(8,128)(2,1)S(1)} %collective-permute-done.from_low_ref, ...), custom_call_target="tpu_custom_call" | custom-call | flops 20000000 | bytes 2000000 | tf_op jit(solution)/shard_map/mixer/pallas_call | solution.py:34
  24.0 0.3 project.1
  24.3 0.6 collective-permute-start.2
  24.9 2.1 %collective-permute-start.3 = (bf16[128,512]{1,0:T(8,128)(2,1)S(1)}, bf16[128,512]{1,0:T(8,128)(2,1)S(1)}, u32[]{:S(2)}, u32[]{:S(2)}) collective-permute-start(bf16[128,512]{1,0:T(8,128)(2,1)S(1)} %get-tuple-element.34), channel_id=1, source_target_pairs={{0,64},{64,128},{128,192},{192,0},{1,65},{65,129},{129,193},{193,1... | collective-permute-start | bytes 393224 | tf_op jit(solution)/shard_map/ppermute | solution.py:444
  27.0 0.1 collective-permute-start.4
  27.1 4.3 %collective-permute-done.2 = bf16[128,512]{1,0:T(8,128)(2,1)S(1)} collective-permute-done((bf16[128,512]{1,0:T(8,128)(2,1)S(1)}, bf16[128,512]{1,0:T(8,128)(2,1)S(1)}, u32[]{:S(2)}, u32[]{:S(2)}) %collective-permute-start.2) | collective-permute-done | bytes 131104 | tf_op jit(solution)/shard_map/ppermute | solution.py:444
  31.3 1.1 %collective-permute-done.3 = bf16[128,512]{1,0:T(8,128)(2,1)S(1)} collective-permute-done((bf16[128,512]{1,0:T(8,128)(2,1)S(1)}, bf16[128,512]{1,0:T(8,128)(2,1)S(1)}, u32[]{:S(2)}, u32[]{:S(2)}) %collective-permute-start.3) | collective-permute-done | bytes 131104 | tf_op jit(solution)/shard_map/ppermute | solution.py:444
  32.4 1.5 %collective-permute-done.4 = bf16[128,512]{1,0:T(8,128)(2,1)S(1)} collective-permute-done((bf16[128,512]{1,0:T(8,128)(2,1)S(1)}, bf16[128,512]{1,0:T(8,128)(2,1)S(1)}, u32[]{:S(2)}, u32[]{:S(2)}) %collective-permute-start.4) | collective-permute-done | bytes 131104 | tf_op jit(solution)/shard_map/ppermute | solution.py:444
  33.9 0.1 add_convert_fusion.1.own_ref
  34.0 0.8 %collective-permute-start.5 = (bf16[128,512]{1,0:T(8,128)(2,1)S(1)}, bf16[128,512]{1,0:T(8,128)(2,1)S(1)}, u32[]{:S(2)}, u32[]{:S(2)}) collective-permute-start(bf16[128,512]{1,0:T(8,128)(2,1)S(1)} %add_convert_fusion.1.own_ref), channel_id=1, source_target_pairs={{0,192},{64,0},{128,64},{192,128},{1,193},{65,1},{129,65},{193,129... | collective-permute-start | bytes 393224 | tf_op jit(solution)/shard_map/ppermute | solution.py:444
  34.8 4.2 %collective-permute-start.6 = (bf16[128,512]{1,0:T(8,128)(2,1)S(1)}, bf16[128,512]{1,0:T(8,128)(2,1)S(1)}, u32[]{:S(2)}, u32[]{:S(2)}) collective-permute-start(bf16[128,512]{1,0:T(8,128)(2,1)S(1)} %add_convert_fusion.1.own_ref), channel_id=1, source_target_pairs={{0,128},{64,192},{128,0},{192,64},{1,129},{65,193},{129,1},{193,65... | collective-permute-start | bytes 393224 | tf_op jit(solution)/shard_map/ppermute | solution.py:444
  39.0 0.0 collective-permute-start.7
  39.0 0.9 %collective-permute-done.5.next_ref = bf16[128,512]{1,0:T(8,128)(2,1)S(1)} collective-permute-done((bf16[128,512]{1,0:T(8,128)(2,1)S(1)}, bf16[128,512]{1,0:T(8,128)(2,1)S(1)}, u32[]{:S(2)}, u32[]{:S(2)}) %collective-permute-start.5) | collective-permute-done | bytes 131104 | tf_op jit(solution)/shard_map/ppermute | solution.py:444
  39.8 2.1 %collective-permute-done.6.far_ref = bf16[128,512]{1,0:T(8,128)(2,1)S(1)} collective-permute-done((bf16[128,512]{1,0:T(8,128)(2,1)S(1)}, bf16[128,512]{1,0:T(8,128)(2,1)S(1)}, u32[]{:S(2)}, u32[]{:S(2)}) %collective-permute-start.6) | collective-permute-done | bytes 131104 | tf_op jit(solution)/shard_map/ppermute | solution.py:444
  41.9 4.3 %collective-permute-done.7.prev_ref = bf16[128,512]{1,0:T(8,128)(2,1)S(1)} collective-permute-done((bf16[128,512]{1,0:T(8,128)(2,1)S(1)}, bf16[128,512]{1,0:T(8,128)(2,1)S(1)}, u32[]{:S(2)}, u32[]{:S(2)}) %collective-permute-start.7) | collective-permute-done | bytes 131104 | tf_op jit(solution)/shard_map/ppermute | solution.py:444
  46.2 0.0 copy-start.10
  46.2 0.0 copy-start.15
  46.2 3.2 %ffn.1 = (f32[128,512]{1,0:T(8,128)S(1)}, bf16[128,512]{1,0:T(8,128)(2,1)S(1)}, bf16[128,512]{1,0:T(8,128)(2,1)S(1)}, bf16[128,512]{1,0:T(8,128)(2,1)S(1)}) custom-call(s32[512]{0:T(512)S(1)} %copy-done.14, bf16[128,512]{1,0:T(8,128)(2,1)S(1)} %add_convert_fusion.1.own_ref, bf16[128,512]{1,0:T(8,128)(2,1)S(1)} %collective-permute-done.5.next_ref, ...), custom_call_target="tpu_custom_call" | custom-call | flops 1100000000 | bytes 9000000 | tf_op jit(solution)/shard_map/ffn/pallas_call | solution.py:423
  49.4 0.1 collective-permute-start.10
  49.5 2.8 %collective-permute-start.8 = (bf16[128,512]{1,0:T(8,128)(2,1)S(1)}, bf16[128,512]{1,0:T(8,128)(2,1)S(1)}, u32[]{:S(2)}, u32[]{:S(2)}) collective-permute-start(bf16[128,512]{1,0:T(8,128)(2,1)S(1)} %get-tuple-element.40), channel_id=1, source_target_pairs={{0,128},{64,192},{128,0},{192,64},{1,129},{65,193},{129,1},{193,65... | collective-permute-start | bytes 393224 | tf_op jit(solution)/shard_map/ppermute | solution.py:444
  52.3 2.5 %collective-permute-start.9 = (bf16[128,512]{1,0:T(8,128)(2,1)S(1)}, bf16[128,512]{1,0:T(8,128)(2,1)S(1)}, u32[]{:S(2)}, u32[]{:S(2)}) collective-permute-start(bf16[128,512]{1,0:T(8,128)(2,1)S(1)} %get-tuple-element.41), channel_id=1, source_target_pairs={{0,64},{64,128},{128,192},{192,0},{1,65},{65,129},{129,193},{193,1... | collective-permute-start | bytes 393224 | tf_op jit(solution)/shard_map/ppermute | solution.py:444
  54.9 0.1 fusion
  55.0 0.1 collective-permute-start.11
  55.1 5.1 %collective-permute-start.12 = (bf16[4,16,2,384]{3,2,1,0:T(2,128)(2,1)S(1)}, bf16[4,16,2,384]{3,2,1,0:T(2,128)(2,1)S(1)}, u32[]{:S(2)}, u32[]{:S(2)}) collective-permute-start(bf16[4,16,2,384]{3,2,1,0:T(2,128)(2,1)S(1)} %get-tuple-element.45), channel_id=1, source_target_pairs={{0,63},{1,0},{2,1},{3,2},{4,3},{5,4},{6,5},{7,6},{8,7},{9,8},{10,9... | collective-permute-start | bytes 294920 | tf_op jit(solution)/shard_map/ppermute | solution.py:444
  60.2 2.3 %collective-permute-done.11.low_ref = bf16[4,16,2,384]{3,2,1,0:T(2,128)(2,1)S(1)} collective-permute-done((bf16[4,16,2,384]{3,2,1,0:T(2,128)(2,1)S(1)}, bf16[4,16,2,384]{3,2,1,0:T(2,128)(2,1)S(1)}, u32[]{:S(2)}, u32[]{:S(2)}) %collective-permute-start.11) | collective-permute-done | bytes 98336 | tf_op jit(solution)/shard_map/ppermute | solution.py:444
  62.5 0.0 collective-permute-done.12.high_ref
  62.5 6.4 %keep.1 = (f32[8,2,128,128]{3,2,1,0:T(8,128)}, bf16[8,3,2,384]{3,2,1,0:T(2,128)(2,1)}) custom-call(s32[512]{0:T(512)S(1)} %copy-done.12, s32[512]{0:T(512)S(1)} %copy-done.15, bf16[8,16,2,384]{3,2,1,0:T(2,128)(2,1)S(1)} %copy-done.6, bf16[4,16,2,384]{3,2,1,0:T(2,128)(2,1)S(1)} %collective-permute-done.11.low_ref, ...), custom_call_target="tpu_custom_call" | custom-call | flops 20000000 | bytes 3000000 | tf_op jit(solution)/shard_map/keep/pallas_call | solution.py:34
  68.9 0.0 collective-permute-done.10
  68.9 0.0 collective-permute-done.9
  69.0 0.7 %add_convert_fusion = bf16[128,512]{1,0:T(8,128)(2,1)} fusion(bf16[128,512]{1,0:T(8,128)(2,1)S(1)} %collective-permute-done.10, bf16[128,512]{1,0:T(8,128)(2,1)S(1)} %collective-permute-done.9, f32[128,512]{1,0:T(8,128)S(1)} %get-tuple-element.39, bf16[128,512]{1,0:T(8,128)(2,1)S(1)} %collective-permute-done.8), kind=kLoop, calls=%fused_computation | loop fusion | flops 458752 | bytes 786432 | tf_op jit(solution)/shard_map/convert_element_type | solution.py:501
  (23 shorter events, 0.0 us)
Async XLA Ops:
  0.6 1.2 %copy-start = (f32[8,2,128,128]{3,2,1,0:T(8,128)S(1)}, f32[8,2,128,128]{3,2,1,0:T(8,128)}, u32[]{:S(2)}) copy-start(f32[8,2,128,128]{3,2,1,0:T(8,128)} %state_ref.3) | copy-start | bytes 3145732
  1.9 0.8 %copy-start.9 = (bf16[8,3,2,384]{3,2,1,0:T(2,128)(2,1)S(1)}, bf16[8,3,2,384]{3,2,1,0:T(2,128)(2,1)}, u32[]{:S(2)}) copy-start(bf16[8,3,2,384]{3,2,1,0:T(2,128)(2,1)} %edge_ref.3) | copy-start | bytes 110596
  4.2 17.6 %collective-permute-start = (bf16[4,304,128]{2,1,0:T(8,128)(2,1)S(1)}, bf16[4,304,128]{2,1,0:T(8,128)(2,1)S(1)}, u32[]{:S(2)}, u32[]{:S(2)}) collective-permute-start(bf16[4,304,128]{2,1,0:T(8,128)(2,1)S(1)} %get-tuple-element.25.high_ref), channel_id=1, source_target_pairs={{0,1},{1,2},{2,3},{3,4},{4,5},{5,6},{6,7},{7,8},{8,9},{9,10},{10,1... | collective-permute-start | bytes 933896 | tf_op jit(solution)/shard_map/ppermute | solution.py:444
  4.3 17.5 %collective-permute-start.1 = (bf16[4,304,128]{2,1,0:T(8,128)(2,1)S(1)}, bf16[4,304,128]{2,1,0:T(8,128)(2,1)S(1)}, u32[]{:S(2)}, u32[]{:S(2)}) collective-permute-start(bf16[4,304,128]{2,1,0:T(8,128)(2,1)S(1)} %get-tuple-element.24.low_ref), channel_id=1, source_target_pairs={{0,63},{1,0},{2,1},{3,2},{4,3},{5,4},{6,5},{7,6},{8,7},{9,8},{10,9... | collective-permute-start | bytes 933896 | tf_op jit(solution)/shard_map/ppermute | solution.py:444
  12.1 1.8 %copy-start.2 = (bf16[2048,704]{0,1:T(8,128)(2,1)S(1)}, bf16[2048,704]{0,1:T(8,128)(2,1)}, u32[]{:S(2)}) copy-start(bf16[2048,704]{0,1:T(8,128)(2,1)} %param.22) | copy-start | bytes 8650756
  13.9 1.8 %copy-start.3 = (bf16[2048,704]{0,1:T(8,128)(2,1)S(1)}, bf16[2048,704]{0,1:T(8,128)(2,1)}, u32[]{:S(2)}) copy-start(bf16[2048,704]{0,1:T(8,128)(2,1)} %param.23) | copy-start | bytes 8650756
  15.7 1.8 %copy-start.4 = (bf16[704,2048]{1,0:T(8,128)(2,1)S(1)}, bf16[704,2048]{1,0:T(8,128)(2,1)}, u32[]{:S(2)}) copy-start(bf16[704,2048]{1,0:T(8,128)(2,1)} %down_hbm.1) | copy-start | bytes 8650756
  17.6 0.9 %copy-start.5 = (bf16[8,16,2,384]{3,2,1,0:T(2,128)(2,1)S(1)}, bf16[8,16,2,384]{3,2,1,0:T(2,128)(2,1)}, u32[]{:S(2)}) copy-start(bf16[8,16,2,384]{3,2,1,0:T(2,128)(2,1)} %draft_ref.3) | copy-start | bytes 589828
  18.5 0.7 %copy-start.11 = (f32[4,2,384]{2,1,0:T(2,128)S(1)}, f32[4,2,384]{2,1,0:T(2,128)}, u32[]{:S(2)}) copy-start(f32[4,2,384]{2,1,0:T(2,128)} %conv_hbm.1) | copy-start | bytes 36868
  19.2 0.7 copy-start.16
  19.9 0.7 copy-start.17
  20.6 1.3 %copy-start.12 = (s32[512]{0:T(512)S(1)}, s32[512]{0:T(512)}, u32[]{:S(2)}) copy-start(s32[512]{0:T(512)} %owner_ref.3) | copy-start | bytes 6148
  20.6 3.4 %copy-start.7 = (bf16[256,2048]{1,0:T(8,128)(2,1)S(1)}, bf16[256,2048]{1,0:T(8,128)(2,1)}, u32[]{:S(2)}) copy-start(bf16[256,2048]{1,0:T(8,128)(2,1)} %weight_ref.1) | copy-start | bytes 3145732
  20.6 3.4 %copy-start.8 = (bf16[8,16,2048]{2,1,0:T(8,128)(2,1)S(1)}, bf16[8,16,2048]{2,1,0:T(8,128)(2,1)}, u32[]{:S(2)}) copy-start(bf16[8,16,2048]{2,1,0:T(8,128)(2,1)} %param.20) | copy-start | bytes 1572868
  21.8 24.4 %copy-start.13 = (f32[2048]{0:T(1024)S(1)}, f32[2048]{0:T(1024)}, u32[]{:S(2)}) copy-start(f32[2048]{0:T(1024)} %param.21) | copy-start | bytes 24580
  21.8 24.4 %copy-start.14 = (s32[512]{0:T(512)S(1)}, s32[512]{0:T(512)}, u32[]{:S(2)}) copy-start(s32[512]{0:T(512)} %length_ref.1) | copy-start | bytes 6148
  24.3 7.0 %collective-permute-start.2 = (bf16[128,512]{1,0:T(8,128)(2,1)S(1)}, bf16[128,512]{1,0:T(8,128)(2,1)S(1)}, u32[]{:S(2)}, u32[]{:S(2)}) collective-permute-start(bf16[128,512]{1,0:T(8,128)(2,1)S(1)} %get-tuple-element.33), channel_id=1, source_target_pairs={{0,128},{64,192},{128,0},{192,64},{1,129},{65,193},{129,1},{193,65... | collective-permute-start | bytes 393224 | tf_op jit(solution)/shard_map/ppermute | solution.py:444
  24.9 7.5 %collective-permute-start.3 = (bf16[128,512]{1,0:T(8,128)(2,1)S(1)}, bf16[128,512]{1,0:T(8,128)(2,1)S(1)}, u32[]{:S(2)}, u32[]{:S(2)}) collective-permute-start(bf16[128,512]{1,0:T(8,128)(2,1)S(1)} %get-tuple-element.34), channel_id=1, source_target_pairs={{0,64},{64,128},{128,192},{192,0},{1,65},{65,129},{129,193},{193,1... | collective-permute-start | bytes 393224 | tf_op jit(solution)/shard_map/ppermute | solution.py:444
  27.0 6.9 %collective-permute-start.4 = (bf16[128,512]{1,0:T(8,128)(2,1)S(1)}, bf16[128,512]{1,0:T(8,128)(2,1)S(1)}, u32[]{:S(2)}, u32[]{:S(2)}) collective-permute-start(bf16[128,512]{1,0:T(8,128)(2,1)S(1)} %get-tuple-element.35), channel_id=1, source_target_pairs={{0,192},{64,0},{128,64},{192,128},{1,193},{65,1},{129,65},{193,129... | collective-permute-start | bytes 393224 | tf_op jit(solution)/shard_map/ppermute | solution.py:444
  34.0 5.9 %collective-permute-start.5 = (bf16[128,512]{1,0:T(8,128)(2,1)S(1)}, bf16[128,512]{1,0:T(8,128)(2,1)S(1)}, u32[]{:S(2)}, u32[]{:S(2)}) collective-permute-start(bf16[128,512]{1,0:T(8,128)(2,1)S(1)} %add_convert_fusion.1.own_ref), channel_id=1, source_target_pairs={{0,192},{64,0},{128,64},{192,128},{1,193},{65,1},{129,65},{193,129... | collective-permute-start | bytes 393224 | tf_op jit(solution)/shard_map/ppermute | solution.py:444
  34.8 7.1 %collective-permute-start.6 = (bf16[128,512]{1,0:T(8,128)(2,1)S(1)}, bf16[128,512]{1,0:T(8,128)(2,1)S(1)}, u32[]{:S(2)}, u32[]{:S(2)}) collective-permute-start(bf16[128,512]{1,0:T(8,128)(2,1)S(1)} %add_convert_fusion.1.own_ref), channel_id=1, source_target_pairs={{0,128},{64,192},{128,0},{192,64},{1,129},{65,193},{129,1},{193,65... | collective-permute-start | bytes 393224 | tf_op jit(solution)/shard_map/ppermute | solution.py:444
  39.0 7.2 %collective-permute-start.7 = (bf16[128,512]{1,0:T(8,128)(2,1)S(1)}, bf16[128,512]{1,0:T(8,128)(2,1)S(1)}, u32[]{:S(2)}, u32[]{:S(2)}) collective-permute-start(bf16[128,512]{1,0:T(8,128)(2,1)S(1)} %add_convert_fusion.1.own_ref), channel_id=1, source_target_pairs={{0,64},{64,128},{128,192},{192,0},{1,65},{65,129},{129,193},{193,1... | collective-permute-start | bytes 393224 | tf_op jit(solution)/shard_map/ppermute | solution.py:444
  46.2 8.7 %copy-start.6 = (bf16[8,16,2,384]{3,2,1,0:T(2,128)(2,1)S(1)}, bf16[8,16,2,384]{3,2,1,0:T(2,128)(2,1)}, u32[]{:S(2)}) copy-start(bf16[8,16,2,384]{3,2,1,0:T(2,128)(2,1)} %draft_ref.3) | copy-start | bytes 589828
  46.2 16.3 %copy-start.1 = (f32[8,2,128,128]{3,2,1,0:T(8,128)S(1)}, f32[8,2,128,128]{3,2,1,0:T(8,128)}, u32[]{:S(2)}) copy-start(f32[8,2,128,128]{3,2,1,0:T(8,128)} %state_ref.3) | copy-start | bytes 3145732
  46.2 16.3 %copy-start.10 = (bf16[8,3,2,384]{3,2,1,0:T(2,128)(2,1)S(1)}, bf16[8,3,2,384]{3,2,1,0:T(2,128)(2,1)}, u32[]{:S(2)}) copy-start(bf16[8,3,2,384]{3,2,1,0:T(2,128)(2,1)} %edge_ref.3) | copy-start | bytes 110596
  46.2 16.3 %copy-start.15 = (s32[512]{0:T(512)S(1)}, s32[512]{0:T(512)}, u32[]{:S(2)}) copy-start(s32[512]{0:T(512)} %accept_ref.1) | copy-start | bytes 6148
  49.4 19.5 %collective-permute-start.10 = (bf16[128,512]{1,0:T(8,128)(2,1)S(1)}, bf16[128,512]{1,0:T(8,128)(2,1)S(1)}, u32[]{:S(2)}, u32[]{:S(2)}) collective-permute-start(bf16[128,512]{1,0:T(8,128)(2,1)S(1)} %get-tuple-element.42), channel_id=1, source_target_pairs={{0,192},{64,0},{128,64},{192,128},{1,193},{65,1},{129,65},{193,129... | collective-permute-start | bytes 393224 | tf_op jit(solution)/shard_map/ppermute | solution.py:444
  49.5 19.4 %collective-permute-start.8 = (bf16[128,512]{1,0:T(8,128)(2,1)S(1)}, bf16[128,512]{1,0:T(8,128)(2,1)S(1)}, u32[]{:S(2)}, u32[]{:S(2)}) collective-permute-start(bf16[128,512]{1,0:T(8,128)(2,1)S(1)} %get-tuple-element.40), channel_id=1, source_target_pairs={{0,128},{64,192},{128,0},{192,64},{1,129},{65,193},{129,1},{193,65... | collective-permute-start | bytes 393224 | tf_op jit(solution)/shard_map/ppermute | solution.py:444
  52.3 16.6 %collective-permute-start.9 = (bf16[128,512]{1,0:T(8,128)(2,1)S(1)}, bf16[128,512]{1,0:T(8,128)(2,1)S(1)}, u32[]{:S(2)}, u32[]{:S(2)}) collective-permute-start(bf16[128,512]{1,0:T(8,128)(2,1)S(1)} %get-tuple-element.41), channel_id=1, source_target_pairs={{0,64},{64,128},{128,192},{192,0},{1,65},{65,129},{129,193},{193,1... | collective-permute-start | bytes 393224 | tf_op jit(solution)/shard_map/ppermute | solution.py:444
  55.0 7.4 %collective-permute-start.11 = (bf16[4,16,2,384]{3,2,1,0:T(2,128)(2,1)S(1)}, bf16[4,16,2,384]{3,2,1,0:T(2,128)(2,1)S(1)}, u32[]{:S(2)}, u32[]{:S(2)}) collective-permute-start(bf16[4,16,2,384]{3,2,1,0:T(2,128)(2,1)S(1)} %get-tuple-element.46), channel_id=1, source_target_pairs={{0,1},{1,2},{2,3},{3,4},{4,5},{5,6},{6,7},{7,8},{8,9},{9,10},{10,1... | collective-permute-start | bytes 294920 | tf_op jit(solution)/shard_map/ppermute | solution.py:444
  55.1 7.4 %collective-permute-start.12 = (bf16[4,16,2,384]{3,2,1,0:T(2,128)(2,1)S(1)}, bf16[4,16,2,384]{3,2,1,0:T(2,128)(2,1)S(1)}, u32[]{:S(2)}, u32[]{:S(2)}) collective-permute-start(bf16[4,16,2,384]{3,2,1,0:T(2,128)(2,1)S(1)} %get-tuple-element.45), channel_id=1, source_target_pairs={{0,63},{1,0},{2,1},{3,2},{4,3},{5,4},{6,5},{7,6},{8,7},{9,8},{10,9... | collective-permute-start | bytes 294920 | tf_op jit(solution)/shard_map/ppermute | solution.py:444

commit v4 on v3

--- a/solution.py
+++ b/solution.py
@@ -347,7 +347,7 @@
 
 
 def columns_of(step, width):
-    place = (lax.axis_index("grp") + step) % 4
+    place = lax.bitwise_xor(lax.axis_index("grp"), step)
     return pl.ds(pl.multiple_of(place * width, width), width)
 
 
@@ -439,6 +439,14 @@
     )(lengths, own, following, far, preceding, gain, gate_t, up_t, down)
 
 
+def in_hbm(array):
+    return pltpu.with_memory_space_constraint(array, pltpu.HBM)
+
+
+def swapped(block, step):
+    return lax.ppermute(block, "grp", [(i, i ^ step) for i in range(4)])
+
+
 def shifted(block, axis, step):
     count = lax.axis_size(axis)
     return lax.ppermute(block, axis, [(i, (i + step) % count) for i in range(count)])
@@ -462,43 +470,46 @@
     owner_row,
 ):
     slots = ROWS * DRAFT
-    low, high = pack_call(held_states, held_edges)
+    drafts = in_hbm(mix_inputs)
+    states = in_hbm(held_states)
+    held = in_hbm(held_edges)
+    low, high = pack_call(states, held)
     from_low = shifted(high, "req", 1)
     from_high = shifted(low, "req", -1)
+    drafts_low = shifted(mix_inputs[HALF:], "req", 1)
+    drafts_high = shifted(mix_inputs[:HALF], "req", -1)
     queries, forget, values, conv, bias, gain, gate_t, up_t, down = prepare_call(
-        mix_inputs, conv_weight, forget_bias, norm_gain,
-        gate_weight.T, up_weight.T, down_weight,
+        drafts, in_hbm(conv_weight), in_hbm(forget_bias), in_hbm(norm_gain),
+        in_hbm(gate_weight.T), in_hbm(up_weight.T), in_hbm(down_weight),
     )
     mixed = mixer_call(
         owner_row, low, high, from_low, from_high, queries, forget, values, conv, bias, gain
     )
-    drafts_low = shifted(mix_inputs[HALF:], "req", 1)
-    drafts_high = shifted(mix_inputs[:HALF], "req", -1)
+    mixed, drafts_low, drafts_high = lax.optimization_barrier((mixed, drafts_low, drafts_high))
+    own_part, to_one, to_two, to_three = project(
+        mixed.reshape(slots, -1), out_weight, resid.reshape(slots, -1)
+    )
+    two = swapped(to_two, 2)
+    one = swapped(to_one, 1)
+    three = swapped(to_three, 3)
+    stream = (own_part + two.astype(F32) + one.astype(F32) + three.astype(F32)).astype(BF)
+    stream, drafts_low, drafts_high = lax.optimization_barrier((stream, drafts_low, drafts_high))
+    two = swapped(stream, 2)
+    one = swapped(stream, 1)
+    three = swapped(stream, 3)
     kept_states, kept_edges = keep_call(
-        owner_row, accepted, mix_inputs, drafts_low, drafts_high, held_edges, held_states,
-        conv, bias,
-    )
-    own_part, to_next, to_far, to_prev = project(
-        mixed.reshape(slots, -1), out_weight, resid.reshape(slots, -1)
-    )
-    far = shifted(to_far, "grp", 2)
-    following = shifted(to_next, "grp", 1)
-    preceding = shifted(to_prev, "grp", -1)
-    stream = (
-        own_part + far.astype(F32) + following.astype(F32) + preceding.astype(F32)
-    ).astype(BF)
-    far = shifted(stream, "grp", 2)
-    preceding = shifted(stream, "grp", 1)
-    following = shifted(stream, "grp", -1)
-    own_part, to_next, to_far, to_prev = ffn(
-        draft_lengths, stream, following, far, preceding, ffn_gain[None, :], gate_t, up_t, down
-    )
-    far = shifted(to_far, "grp", 2)
-    following = shifted(to_next, "grp", 1)
-    preceding = shifted(to_prev, "grp", -1)
-    layer_out = (
-        own_part + far.astype(F32) + following.astype(F32) + preceding.astype(F32)
-    ).astype(BF)
+        owner_row, accepted, drafts, drafts_low, drafts_high, held, states, conv, bias
+    )
+    one, two, three, kept_states, kept_edges = lax.optimization_barrier(
+        (one, two, three, kept_states, kept_edges)
+    )
+    own_part, to_one, to_two, to_three = ffn(
+        draft_lengths, stream, one, two, three, ffn_gain[None, :], gate_t, up_t, down
+    )
+    two = swapped(to_two, 2)
+    one = swapped(to_one, 1)
+    three = swapped(to_three, 3)
+    layer_out = (own_part + two.astype(F32) + one.astype(F32) + three.astype(F32)).astype(BF)
     return (layer_out.reshape(ROWS, DRAFT, -1), kept_states, kept_edges)
 
 

time: 70.1 us -> 57.7 us (0.82)
  the two profiles are of different devices: /device:TPU:4 before, /device:TPU:6 now
where the time goes in v4:
time: 57.7 us; the launch traced here: 57.4 us
  starting transfers between devices  25.5 us (44%)
  Pallas kernels  16.5 us (29%)
  waiting for transfers between devices  12.7 us (22%)
  local copies, waits for them, and re-layouts  1.11 us (2%)
  other arithmetic  0.81 us (1%)
  between operations  0.77 us (1%)
    pallas_call x4, Pallas kernels, call(): pl.pallas_call(kernel, name=kernel.__name__, out_shape=out_shape, in_spec...  13 us
    ppermute x4, starting transfers between devices, shifted(): lax.ppermute(block, axis, [(i, (i + step) % count) for i in range(count)])  13 us
    ppermute x9, starting transfers between devices, swapped(): return lax.ppermute(block, 'grp', [(i, i ^ step) for i in range(4)])  12.5 us
    ppermute x9, waiting for transfers between devices, swapped(): return lax.ppermute(block, 'grp', [(i, i ^ step) for i in range(4)])  11.4 us
    pallas_call x1, Pallas kernels, ffn(): pl.pallas_call(ffn_kernel, name='ffn', out_shape=(shape((slots, width), F...  3.16 us
    ppermute x4, waiting for transfers between devices, shifted(): lax.ppermute(block, axis, [(i, (i + step) % count) for i in range(count)])  1.3 us
  transfers between devices with their start and end apart: 13, of which 7 were waited for; matrix products, arithmetic and copies ran while one was open for 2% of the time, Pallas kernels for 20%

profile of v4, /device:TPU:6, one launch (start us, length us, event | category | flops | bytes accessed | tf_op | source)
XLA Modules:
  0.0 57.4 jit_solution(15137367059476897987)
XLA Ops:
  0.6 1.4 %pack.1 = (bf16[4,304,128]{2,1,0:T(8,128)(2,1)S(1)}, bf16[4,304,128]{2,1,0:T(8,128)(2,1)S(1)}) custom-call(f32[8,2,128,128]{3,2,1,0:T(8,128)} %state_ref.3, bf16[8,3,2,384]{3,2,1,0:T(2,128)(2,1)} %edge_ref.3), custom_call_target="tpu_custom_call" | custom-call | flops 1000000 | bytes 2000000 | tf_op jit(solution)/shard_map/pack/pallas_call | solution.py:34
  2.0 7.8 %collective-permute-start.1 = (bf16[4,304,128]{2,1,0:T(8,128)(2,1)S(1)}, bf16[4,304,128]{2,1,0:T(8,128)(2,1)S(1)}, u32[]{:S(2)}, u32[]{:S(2)}) collective-permute-start(bf16[4,304,128]{2,1,0:T(8,128)(2,1)S(1)} %get-tuple-element.35.low_ref), channel_id=1, source_target_pairs={{0,63},{1,0},{2,1},{3,2},{4,3},{5,4},{6,5},{7,6},{8,7},{9,8},{10,9... | collective-permute-start | bytes 933896 | tf_op jit(solution)/shard_map/ppermute | solution.py:452
  9.8 0.0 collective-permute-start
  9.9 1.1 %fusion = (bf16[4,16,2,384]{3,2,1,0:T(2,128)(2,1)S(1)}, bf16[4,16,2,384]{3,2,1,0:T(2,128)(2,1)S(1)}) fusion(bf16[8,16,2,384]{3,2,1,0:T(2,128)(2,1)} %draft_ref.3), kind=kLoop, calls=%fused_computation.2 | loop fusion | bytes 393216 | tf_op jit(solution)/shard_map/slice | solution.py:480
  10.9 5.1 %collective-permute-start.3 = (bf16[4,16,2,384]{3,2,1,0:T(2,128)(2,1)S(1)}, bf16[4,16,2,384]{3,2,1,0:T(2,128)(2,1)S(1)}, u32[]{:S(2)}, u32[]{:S(2)}) collective-permute-start(bf16[4,16,2,384]{3,2,1,0:T(2,128)(2,1)S(1)} %get-tuple-element.67), channel_id=1, source_target_pairs={{0,63},{1,0},{2,1},{3,2},{4,3},{5,4},{6,5},{7,6},{8,7},{9,8},{10,9... | collective-permute-start | bytes 294920 | tf_op jit(solution)/shard_map/ppermute | solution.py:452
  16.1 0.0 collective-permute-start.2
  16.1 0.0 copy-start.2
  16.1 0.0 copy-start
  16.1 0.0 copy-start.1
  16.1 3.9 %prepare.1 = (f32[8,2,16,128]{3,2,1,0:T(8,128)S(1)}, f32[8,2,16,128]{3,2,1,0:T(8,128)S(1)}, f32[8,2,16,128]{3,2,1,0:T(8,128)S(1)}, f32[4,2,384]{2,1,0:T(2,128)S(...) custom-call(bf16[8,16,2,384]{3,2,1,0:T(2,128)(2,1)} %draft_ref.3, ...), custom_call_target="tpu_custom_call" | custom-call | flops 5000000 | bytes 18000000 | tf_op jit(solution)/shard_map/prepare/pallas_call | solution.py:34
  20.0 0.0 copy-start.4
  20.0 0.0 copy-start.3
  20.0 0.0 copy-start.5
  20.0 0.0 collective-permute-done.1.from_high_ref
  20.0 0.0 collective-permute-done.from_low_ref
  20.0 0.0 copy-done.2
  20.0 2.1 %mixer.1 = bf16[8,16,256]{2,1,0:T(8,128)(2,1)S(1)} custom-call(s32[512]{0:T(512)S(1)} %copy-done.2, bf16[4,304,128]{2,1,0:T(8,128)(2,1)S(1)} %get-tuple-element.35.low_ref, bf16[4,304,128]{2,1,0:T(8,128)(2,1)S(1)} %get-tuple-element.36.high_ref, bf16[4,304,128]{2,1,0:T(8,128)(2,1)S(1)} %collective-permute-done.from_low_ref, ...), custom_call_target="tpu_custom_call" | custom-call | flops 20000000 | bytes 2000000 | tf_op jit(solution)/shard_map/mixer/pallas_call | solution.py:34
  22.1 0.0 collective-permute-done.3.high_ref
  22.1 1.3 %collective-permute-done.2.low_ref = bf16[4,16,2,384]{3,2,1,0:T(2,128)(2,1)S(1)} collective-permute-done((bf16[4,16,2,384]{3,2,1,0:T(2,128)(2,1)S(1)}, bf16[4,16,2,384]{3,2,1,0:T(2,128)(2,1)S(1)}, u32[]{:S(2)}, u32[]{:S(2)}) %collective-permute-start.2) | collective-permute-done | bytes 98336 | tf_op jit(solution)/shard_map/ppermute | solution.py:452
  23.4 0.0 copy-done
  23.4 0.0 copy-done.1
  23.4 0.3 project.1
  23.8 1.5 %collective-permute-start.4 = (bf16[128,512]{1,0:T(8,128)(2,1)S(1)}, bf16[128,512]{1,0:T(8,128)(2,1)S(1)}, u32[]{:S(2)}, u32[]{:S(2)}) collective-permute-start(bf16[128,512]{1,0:T(8,128)(2,1)S(1)} %get-tuple-element.45), channel_id=1, source_target_pairs={{0,128},{64,192},{128,0},{192,64},{1,129},{65,193},{129,1},{193,65... | collective-permute-start | bytes 393224 | tf_op jit(solution)/shard_map/ppermute | solution.py:447
  25.3 0.0 collective-permute-start.5
  25.3 2.7 %collective-permute-start.6 = (bf16[128,512]{1,0:T(8,128)(2,1)S(1)}, bf16[128,512]{1,0:T(8,128)(2,1)S(1)}, u32[]{:S(2)}, u32[]{:S(2)}) collective-permute-start(bf16[128,512]{1,0:T(8,128)(2,1)S(1)} %get-tuple-element.47), channel_id=1, source_target_pairs={{0,192},{64,128},{128,64},{192,0},{1,193},{65,129},{129,65},{193,1... | collective-permute-start | bytes 393224 | tf_op jit(solution)/shard_map/ppermute | solution.py:447
  27.9 2.5 %collective-permute-done.4 = bf16[128,512]{1,0:T(8,128)(2,1)S(1)} collective-permute-done((bf16[128,512]{1,0:T(8,128)(2,1)S(1)}, bf16[128,512]{1,0:T(8,128)(2,1)S(1)}, u32[]{:S(2)}, u32[]{:S(2)}) %collective-permute-start.4) | collective-permute-done | bytes 131104 | tf_op jit(solution)/shard_map/ppermute | solution.py:447
  30.4 0.8 %collective-permute-done.5 = bf16[128,512]{1,0:T(8,128)(2,1)S(1)} collective-permute-done((bf16[128,512]{1,0:T(8,128)(2,1)S(1)}, bf16[128,512]{1,0:T(8,128)(2,1)S(1)}, u32[]{:S(2)}, u32[]{:S(2)}) %collective-permute-start.5) | collective-permute-done | bytes 131104 | tf_op jit(solution)/shard_map/ppermute | solution.py:447
  31.2 3.2 %collective-permute-done.6 = bf16[128,512]{1,0:T(8,128)(2,1)S(1)} collective-permute-done((bf16[128,512]{1,0:T(8,128)(2,1)S(1)}, bf16[128,512]{1,0:T(8,128)(2,1)S(1)}, u32[]{:S(2)}, u32[]{:S(2)}) %collective-permute-start.6) | collective-permute-done | bytes 131104 | tf_op jit(solution)/shard_map/ppermute | solution.py:447
  34.4 0.1 add_convert_fusion.1.own_ref
  34.4 0.9 %collective-permute-start.9 = (bf16[128,512]{1,0:T(8,128)(2,1)S(1)}, bf16[128,512]{1,0:T(8,128)(2,1)S(1)}, u32[]{:S(2)}, u32[]{:S(2)}) collective-permute-start(bf16[128,512]{1,0:T(8,128)(2,1)S(1)} %add_convert_fusion.1.own_ref), channel_id=1, source_target_pairs={{0,192},{64,128},{128,64},{192,0},{1,193},{65,129},{129,65},{193,1... | collective-permute-start | bytes 393224 | tf_op jit(solution)/shard_map/ppermute | solution.py:447
  35.3 0.9 %collective-permute-start.8 = (bf16[128,512]{1,0:T(8,128)(2,1)S(1)}, bf16[128,512]{1,0:T(8,128)(2,1)S(1)}, u32[]{:S(2)}, u32[]{:S(2)}) collective-permute-start(bf16[128,512]{1,0:T(8,128)(2,1)S(1)} %add_convert_fusion.1.own_ref), channel_id=1, source_target_pairs={{0,128},{64,192},{128,0},{192,64},{1,129},{65,193},{129,1},{193,65... | collective-permute-start | bytes 393224 | tf_op jit(solution)/shard_map/ppermute | solution.py:447
  36.2 2.4 %collective-permute-start.7 = (bf16[128,512]{1,0:T(8,128)(2,1)S(1)}, bf16[128,512]{1,0:T(8,128)(2,1)S(1)}, u32[]{:S(2)}, u32[]{:S(2)}) collective-permute-start(bf16[128,512]{1,0:T(8,128)(2,1)S(1)} %add_convert_fusion.1.own_ref), channel_id=1, source_target_pairs={{0,64},{64,0},{128,192},{192,128},{1,65},{65,1},{129,193},{193,129... | collective-permute-start | bytes 393224 | tf_op jit(solution)/shard_map/ppermute | solution.py:447
  38.6 0.0 copy-done.4
  38.6 5.7 %keep.1 = (f32[8,2,128,128]{3,2,1,0:T(8,128)}, bf16[8,3,2,384]{3,2,1,0:T(2,128)(2,1)}) custom-call(s32[512]{0:T(512)S(1)} %copy-done.2, s32[512]{0:T(512)S(1)} %copy-done.4, bf16[8,16,2,384]{3,2,1,0:T(2,128)(2,1)} %draft_ref.3, bf16[4,16,2,384]{3,2,1,0:T(2,128)(2,1)S(1)} %collective-permute-done.2.low_ref, ...), custom_call_target="tpu_custom_call" | custom-call | flops 20000000 | bytes 3000000 | tf_op jit(solution)/shard_map/keep/pallas_call | solution.py:34
  44.3 0.0 collective-permute-done.9.prev_ref
  44.3 0.0 collective-permute-done.8.far_ref
  44.3 1.2 %collective-permute-done.7.next_ref = bf16[128,512]{1,0:T(8,128)(2,1)S(1)} collective-permute-done((bf16[128,512]{1,0:T(8,128)(2,1)S(1)}, bf16[128,512]{1,0:T(8,128)(2,1)S(1)}, u32[]{:S(2)}, u32[]{:S(2)}) %collective-permute-start.7) | collective-permute-done | bytes 131104 | tf_op jit(solution)/shard_map/ppermute | solution.py:447
  45.5 0.0 copy-done.3
  45.5 0.0 copy-done.5
  45.5 3.2 %ffn.1 = (f32[128,512]{1,0:T(8,128)S(1)}, bf16[128,512]{1,0:T(8,128)(2,1)S(1)}, bf16[128,512]{1,0:T(8,128)(2,1)S(1)}, bf16[128,512]{1,0:T(8,128)(2,1)S(1)}) custom-call(s32[512]{0:T(512)S(1)} %copy-done.5, bf16[128,512]{1,0:T(8,128)(2,1)S(1)} %add_convert_fusion.1.own_ref, bf16[128,512]{1,0:T(8,128)(2,1)S(1)} %collective-permute-done.7.next_ref, ...), custom_call_target="tpu_custom_call" | custom-call | flops 1100000000 | bytes 9000000 | tf_op jit(solution)/shard_map/ffn/pallas_call | solution.py:423
  48.7 0.2 collective-permute-start.10
  48.9 0.7 %collective-permute-start.11 = (bf16[128,512]{1,0:T(8,128)(2,1)S(1)}, bf16[128,512]{1,0:T(8,128)(2,1)S(1)}, u32[]{:S(2)}, u32[]{:S(2)}) collective-permute-start(bf16[128,512]{1,0:T(8,128)(2,1)S(1)} %get-tuple-element.63), channel_id=1, source_target_pairs={{0,64},{64,0},{128,192},{192,128},{1,65},{65,1},{129,193},{193,129... | collective-permute-start | bytes 393224 | tf_op jit(solution)/shard_map/ppermute | solution.py:447
  49.5 3.3 %collective-permute-start.12 = (bf16[128,512]{1,0:T(8,128)(2,1)S(1)}, bf16[128,512]{1,0:T(8,128)(2,1)S(1)}, u32[]{:S(2)}, u32[]{:S(2)}) collective-permute-start(bf16[128,512]{1,0:T(8,128)(2,1)S(1)} %get-tuple-element.64), channel_id=1, source_target_pairs={{0,192},{64,128},{128,64},{192,0},{1,193},{65,129},{129,65},{193,1... | collective-permute-start | bytes 393224 | tf_op jit(solution)/shard_map/ppermute | solution.py:447
  52.9 2.5 %collective-permute-done.10 = bf16[128,512]{1,0:T(8,128)(2,1)S(1)} collective-permute-done((bf16[128,512]{1,0:T(8,128)(2,1)S(1)}, bf16[128,512]{1,0:T(8,128)(2,1)S(1)}, u32[]{:S(2)}, u32[]{:S(2)}) %collective-permute-start.10) | collective-permute-done | bytes 131104 | tf_op jit(solution)/shard_map/ppermute | solution.py:447
  55.3 0.0 collective-permute-done.11
  55.3 1.3 %collective-permute-done.12 = bf16[128,512]{1,0:T(8,128)(2,1)S(1)} collective-permute-done((bf16[128,512]{1,0:T(8,128)(2,1)S(1)}, bf16[128,512]{1,0:T(8,128)(2,1)S(1)}, u32[]{:S(2)}, u32[]{:S(2)}) %collective-permute-start.12) | collective-permute-done | bytes 131104 | tf_op jit(solution)/shard_map/ppermute | solution.py:447
  56.6 0.7 %add_convert_fusion = bf16[128,512]{1,0:T(8,128)(2,1)} fusion(bf16[128,512]{1,0:T(8,128)(2,1)S(1)} %collective-permute-done.12, bf16[128,512]{1,0:T(8,128)(2,1)S(1)} %collective-permute-done.11, f32[128,512]{1,0:T(8,128)S(1)} %get-tuple-element.61, bf16[128,512]{1,0:T(8,128)(2,1)S(1)} %collective-permute-done.10), kind=kLoop, calls=%fused_computation | loop fusion | flops 458752 | bytes 786432 | tf_op jit(solution)/shard_map/convert_element_type | solution.py:512
Async XLA Ops:
  2.0 18.0 %collective-permute-start.1 = (bf16[4,304,128]{2,1,0:T(8,128)(2,1)S(1)}, bf16[4,304,128]{2,1,0:T(8,128)(2,1)S(1)}, u32[]{:S(2)}, u32[]{:S(2)}) collective-permute-start(bf16[4,304,128]{2,1,0:T(8,128)(2,1)S(1)} %get-tuple-element.35.low_ref), channel_id=1, source_target_pairs={{0,63},{1,0},{2,1},{3,2},{4,3},{5,4},{6,5},{7,6},{8,7},{9,8},{10,9... | collective-permute-start | bytes 933896 | tf_op jit(solution)/shard_map/ppermute | solution.py:452
  9.8 10.2 %collective-permute-start = (bf16[4,304,128]{2,1,0:T(8,128)(2,1)S(1)}, bf16[4,304,128]{2,1,0:T(8,128)(2,1)S(1)}, u32[]{:S(2)}, u32[]{:S(2)}) collective-permute-start(bf16[4,304,128]{2,1,0:T(8,128)(2,1)S(1)} %get-tuple-element.36.high_ref), channel_id=1, source_target_pairs={{0,1},{1,2},{2,3},{3,4},{4,5},{5,6},{6,7},{7,8},{8,9},{9,10},{10,1... | collective-permute-start | bytes 933896 | tf_op jit(solution)/shard_map/ppermute | solution.py:452
  10.9 11.2 %collective-permute-start.3 = (bf16[4,16,2,384]{3,2,1,0:T(2,128)(2,1)S(1)}, bf16[4,16,2,384]{3,2,1,0:T(2,128)(2,1)S(1)}, u32[]{:S(2)}, u32[]{:S(2)}) collective-permute-start(bf16[4,16,2,384]{3,2,1,0:T(2,128)(2,1)S(1)} %get-tuple-element.67), channel_id=1, source_target_pairs={{0,63},{1,0},{2,1},{3,2},{4,3},{5,4},{6,5},{7,6},{8,7},{9,8},{10,9... | collective-permute-start | bytes 294920 | tf_op jit(solution)/shard_map/ppermute | solution.py:452
  16.1 7.4 %collective-permute-start.2 = (bf16[4,16,2,384]{3,2,1,0:T(2,128)(2,1)S(1)}, bf16[4,16,2,384]{3,2,1,0:T(2,128)(2,1)S(1)}, u32[]{:S(2)}, u32[]{:S(2)}) collective-permute-start(bf16[4,16,2,384]{3,2,1,0:T(2,128)(2,1)S(1)} %get-tuple-element.68), channel_id=1, source_target_pairs={{0,1},{1,2},{2,3},{3,4},{4,5},{5,6},{6,7},{7,8},{8,9},{9,10},{10,1... | collective-permute-start | bytes 294920 | tf_op jit(solution)/shard_map/ppermute | solution.py:452
  16.1 3.9 %copy-start.2 = (s32[512]{0:T(512)S(1)}, s32[512]{0:T(512)}, u32[]{:S(2)}) copy-start(s32[512]{0:T(512)} %owner_ref.3) | copy-start | bytes 6148
  16.1 7.4 %copy-start = (bf16[256,2048]{1,0:T(8,128)(2,1)S(1)}, bf16[256,2048]{1,0:T(8,128)(2,1)}, u32[]{:S(2)}) copy-start(bf16[256,2048]{1,0:T(8,128)(2,1)} %weight_ref.1) | copy-start | bytes 3145732
  16.1 7.4 %copy-start.1 = (bf16[8,16,2048]{2,1,0:T(8,128)(2,1)S(1)}, bf16[8,16,2048]{2,1,0:T(8,128)(2,1)}, u32[]{:S(2)}) copy-start(bf16[8,16,2048]{2,1,0:T(8,128)(2,1)} %param.20) | copy-start | bytes 1572868
  20.0 18.7 %copy-start.4 = (s32[512]{0:T(512)S(1)}, s32[512]{0:T(512)}, u32[]{:S(2)}) copy-start(s32[512]{0:T(512)} %accept_ref.1) | copy-start | bytes 6148
  20.0 25.5 %copy-start.3 = (f32[2048]{0:T(1024)S(1)}, f32[2048]{0:T(1024)}, u32[]{:S(2)}) copy-start(f32[2048]{0:T(1024)} %param.21) | copy-start | bytes 24580
  20.0 25.5 %copy-start.5 = (s32[512]{0:T(512)S(1)}, s32[512]{0:T(512)}, u32[]{:S(2)}) copy-start(s32[512]{0:T(512)} %length_ref.1) | copy-start | bytes 6148
  23.8 6.7 %collective-permute-start.4 = (bf16[128,512]{1,0:T(8,128)(2,1)S(1)}, bf16[128,512]{1,0:T(8,128)(2,1)S(1)}, u32[]{:S(2)}, u32[]{:S(2)}) collective-permute-start(bf16[128,512]{1,0:T(8,128)(2,1)S(1)} %get-tuple-element.45), channel_id=1, source_target_pairs={{0,128},{64,192},{128,0},{192,64},{1,129},{65,193},{129,1},{193,65... | collective-permute-start | bytes 393224 | tf_op jit(solution)/shard_map/ppermute | solution.py:447
  25.3 5.9 %collective-permute-start.5 = (bf16[128,512]{1,0:T(8,128)(2,1)S(1)}, bf16[128,512]{1,0:T(8,128)(2,1)S(1)}, u32[]{:S(2)}, u32[]{:S(2)}) collective-permute-start(bf16[128,512]{1,0:T(8,128)(2,1)S(1)} %get-tuple-element.46), channel_id=1, source_target_pairs={{0,64},{64,0},{128,192},{192,128},{1,65},{65,1},{129,193},{193,129... | collective-permute-start | bytes 393224 | tf_op jit(solution)/shard_map/ppermute | solution.py:447
  25.3 9.1 %collective-permute-start.6 = (bf16[128,512]{1,0:T(8,128)(2,1)S(1)}, bf16[128,512]{1,0:T(8,128)(2,1)S(1)}, u32[]{:S(2)}, u32[]{:S(2)}) collective-permute-start(bf16[128,512]{1,0:T(8,128)(2,1)S(1)} %get-tuple-element.47), channel_id=1, source_target_pairs={{0,192},{64,128},{128,64},{192,0},{1,193},{65,129},{129,65},{193,1... | collective-permute-start | bytes 393224 | tf_op jit(solution)/shard_map/ppermute | solution.py:447
  34.4 9.9 %collective-permute-start.9 = (bf16[128,512]{1,0:T(8,128)(2,1)S(1)}, bf16[128,512]{1,0:T(8,128)(2,1)S(1)}, u32[]{:S(2)}, u32[]{:S(2)}) collective-permute-start(bf16[128,512]{1,0:T(8,128)(2,1)S(1)} %add_convert_fusion.1.own_ref), channel_id=1, source_target_pairs={{0,192},{64,128},{128,64},{192,0},{1,193},{65,129},{129,65},{193,1... | collective-permute-start | bytes 393224 | tf_op jit(solution)/shard_map/ppermute | solution.py:447
  35.3 9.0 %collective-permute-start.8 = (bf16[128,512]{1,0:T(8,128)(2,1)S(1)}, bf16[128,512]{1,0:T(8,128)(2,1)S(1)}, u32[]{:S(2)}, u32[]{:S(2)}) collective-permute-start(bf16[128,512]{1,0:T(8,128)(2,1)S(1)} %add_convert_fusion.1.own_ref), channel_id=1, source_target_pairs={{0,128},{64,192},{128,0},{192,64},{1,129},{65,193},{129,1},{193,65... | collective-permute-start | bytes 393224 | tf_op jit(solution)/shard_map/ppermute | solution.py:447
  36.2 9.3 %collective-permute-start.7 = (bf16[128,512]{1,0:T(8,128)(2,1)S(1)}, bf16[128,512]{1,0:T(8,128)(2,1)S(1)}, u32[]{:S(2)}, u32[]{:S(2)}) collective-permute-start(bf16[128,512]{1,0:T(8,128)(2,1)S(1)} %add_convert_fusion.1.own_ref), channel_id=1, source_target_pairs={{0,64},{64,0},{128,192},{192,128},{1,65},{65,1},{129,193},{193,129... | collective-permute-start | bytes 393224 | tf_op jit(solution)/shard_map/ppermute | solution.py:447
  48.7 6.6 %collective-permute-start.10 = (bf16[128,512]{1,0:T(8,128)(2,1)S(1)}, bf16[128,512]{1,0:T(8,128)(2,1)S(1)}, u32[]{:S(2)}, u32[]{:S(2)}) collective-permute-start(bf16[128,512]{1,0:T(8,128)(2,1)S(1)} %get-tuple-element.62), channel_id=1, source_target_pairs={{0,128},{64,192},{128,0},{192,64},{1,129},{65,193},{129,1},{193,65... | collective-permute-start | bytes 393224 | tf_op jit(solution)/shard_map/ppermute | solution.py:447
  48.9 6.4 %collective-permute-start.11 = (bf16[128,512]{1,0:T(8,128)(2,1)S(1)}, bf16[128,512]{1,0:T(8,128)(2,1)S(1)}, u32[]{:S(2)}, u32[]{:S(2)}) collective-permute-start(bf16[128,512]{1,0:T(8,128)(2,1)S(1)} %get-tuple-element.63), channel_id=1, source_target_pairs={{0,64},{64,0},{128,192},{192,128},{1,65},{65,1},{129,193},{193,129... | collective-permute-start | bytes 393224 | tf_op jit(solution)/shard_map/ppermute | solution.py:447
  49.5 7.1 %collective-permute-start.12 = (bf16[128,512]{1,0:T(8,128)(2,1)S(1)}, bf16[128,512]{1,0:T(8,128)(2,1)S(1)}, u32[]{:S(2)}, u32[]{:S(2)}) collective-permute-start(bf16[128,512]{1,0:T(8,128)(2,1)S(1)} %get-tuple-element.64), channel_id=1, source_target_pairs={{0,192},{64,128},{128,64},{192,0},{1,193},{65,129},{129,65},{193,1... | collective-permute-start | bytes 393224 | tf_op jit(solution)/shard_map/ppermute | solution.py:447

commit v5 on v4

v5 whole, which is shorter than its diff:
```python
import jax
import jax.numpy as jnp
from jax import lax
from jax.experimental import pallas as pl
from jax.experimental.pallas import tpu as pltpu
from jax.sharding import PartitionSpec as P

DK = 128
DRAFT = 16
CONV = 4
HALF = 4
ROWS = 2 * HALF
BF = jnp.bfloat16
PARAMS = pltpu.CompilerParams(vmem_limit_bytes=12 * 1024 * 1024)
F32 = jnp.float32
EDGES_AT = 2 * DK
DRAFTS_AT = EDGES_AT + 3 * DRAFT
PACKED = DRAFTS_AT + 3 * 2 * DRAFT
VM = pl.BlockSpec(memory_space=pltpu.VMEM)
SM = pl.BlockSpec(memory_space=pltpu.SMEM)
HB = pl.BlockSpec(memory_space=pltpu.HBM)


def row_of(half, place):
    parity = lax.axis_index("req") % 2
    base = (1 - parity if half == 0 else parity) * HALF
    return base + place


def source_of(owner_ref, row):
    me = lax.axis_index("req")
    partner = owner_ref[me * ROWS + row]
    return partner, partner // ROWS == me, partner % HALF


def block_of(block):
    return slice(block * DK, (block + 1) * DK)


def edges_of(block):
    return slice(EDGES_AT + block * DRAFT, EDGES_AT + (block + 1) * DRAFT)


def drafts_of(block):
    return slice(DRAFTS_AT + block * 2 * DRAFT, DRAFTS_AT + (block + 1) * 2 * DRAFT)


def call(kernel, out_shape, in_specs, scratch, flops, moved, *args):
    return pl.pallas_call(
        kernel,
        name=kernel.__name__,
        out_shape=out_shape,
        in_specs=in_specs,
        out_specs=jax.tree.map(lambda _: VM, out_shape),
        scratch_shapes=scratch,
        compiler_params=PARAMS,
        cost_estimate=pl.CostEstimate(flops=flops, bytes_accessed=moved, transcendentals=0),
    )(*args)


def pack(state_ref, edge_ref, draft_ref, far_ref, near_ref, states, edges, drafts, sems):
    copies = [
        pltpu.make_async_copy(state_ref.at[row], states.at[row], sems.at[row])
        for row in range(ROWS)
    ]
    edge_copy = pltpu.make_async_copy(edge_ref, edges, sems.at[ROWS])
    draft_copy = pltpu.make_async_copy(draft_ref, drafts, sems.at[ROWS + 1])
    draft_copy.start()
    edge_copy.start()
    for copy in copies:
        copy.start()
    edge_copy.wait()
    draft_copy.wait()
    for half, out_ref in ((1, far_ref), (0, near_ref)):
        for place in range(HALF):
            row = row_of(half, place)
            for block in range(3):
                columns = block_of(block)
                out_ref[place, edges_of(block), :] = jnp.zeros((DRAFT, DK), BF)
                start = EDGES_AT + block * DRAFT
                for step in range(CONV - 1):
                    out_ref[place, start + 2 * step : start + 2 * step + 2, :] = edges[
                        row, step, :, columns
                    ]
                start = DRAFTS_AT + block * 2 * DRAFT
                for step in range(DRAFT):
                    out_ref[place, start + 2 * step : start + 2 * step + 2, :] = drafts[
                        row, step, :, columns
                    ]
    for copy in copies:
        copy.wait()
    for half, out_ref in ((1, far_ref), (0, near_ref)):
        for place in range(HALF):
            for head in range(2):
                out_ref[place, block_of(head), :] = states[row_of(half, place), head].astype(BF)


def pack_call(states, edges, drafts):
    half = jax.ShapeDtypeStruct((HALF, PACKED, DK), BF)
    return call(
        pack, (half, half), [HB] * 3,
        [
            pltpu.VMEM(states.shape, F32),
            pltpu.VMEM(edges.shape, BF),
            pltpu.VMEM(drafts.shape, BF),
            pltpu.SemaphoreType.DMA((ROWS + 2,)),
        ],
        1_000_000, 2_000_000, states, edges, drafts,
    )


def convolve(window, conv_ref, slot, head, block):
    total = None
    for shift in range(CONV):
        taps = conv_ref[shift, head, block_of(block)]
        rows = window[slot, block, pl.ds(2 + 2 * shift + head, DRAFT, stride=2), :]
        term = taps[None, :] * rows
        total = term if total is None else total + term
    return total


def as_query(x):
    return x * jax.nn.sigmoid(x) * DK ** (-0.5)


def as_value(x):
    return x * jax.nn.sigmoid(x)


def prepare(
    near_ref, far_ref, conv_hbm, bias_hbm, gain_hbm,
    query_ref, forget_ref, value_ref, conv_ref, bias_ref, gain_ref, window, sems,
):
    pairs = ((conv_hbm, conv_ref), (bias_hbm, bias_ref), (gain_hbm, gain_ref))
    copies = [
        pltpu.make_async_copy(src, dst, sems.at[i]) for i, (src, dst) in enumerate(pairs)
    ]
    for copy in copies:
        copy.start()
    for slot in range(ROWS):
        own_ref = near_ref if slot < HALF else far_ref
        for block in range(3):
            window[slot, block, :8, :] = jnp.zeros((8, DK), F32)
            window[slot, block, 8:, :] = own_ref[slot % HALF, drafts_of(block), :].astype(F32)
    for copy in copies:
        copy.wait()
    half = DRAFT // 2
    for slot in range(ROWS):
        for head in range(2):
            queries, gates, values = [
                convolve(window, conv_ref, slot, head, block) for block in range(3)
            ]
            query_ref[slot, head, :half] = queries[:half]
            query_ref[slot, head, half:] = as_query(queries[half:])
            gates = gates + bias_ref[head, :][None, :]
            forget_ref[slot, head, :half] = gates[:half]
            forget_ref[slot, head, half:] = jax.nn.sigmoid(gates[half:])
            value_ref[slot, head, :half] = values[:half]
            value_ref[slot, head, half:] = as_value(values[half:])


def prepare_call(near, far, conv, bias, gain):
    rows = jax.ShapeDtypeStruct((ROWS, 2, DRAFT, DK), F32)
    copied = [jax.ShapeDtypeStruct(x.shape, x.dtype) for x in (conv, bias, gain)]
    return call(
        prepare, (rows, rows, rows, *copied), [VM, VM, HB, HB, HB],
        [pltpu.VMEM((ROWS, 3, 40, DK), F32), pltpu.SemaphoreType.DMA((3,))],
        5_000_000, 3_000_000, near, far, conv, bias, gain,
    )


def fetch(*refs):
    count = len(refs) // 2
    sems = refs[-1]
    copies = [
        pltpu.make_async_copy(refs[i], refs[count + i], sems.at[i]) for i in range(count)
    ]
    for copy in copies:
        copy.start()
    for copy in copies:
        copy.wait()


def fetch_call(*arrays):
    return call(
        fetch, tuple(jax.ShapeDtypeStruct(x.shape, x.dtype) for x in arrays), [HB] * len(arrays),
        [pltpu.SemaphoreType.DMA((len(arrays),))], 0, 17_000_000, *arrays,
    )


def mixer(
    owner_ref, near_ref, far_ref, from_near_ref, from_far_ref, query_ref, forget_ref, value_ref,
    conv_ref, bias_ref, gain_ref, mixed_ref, edges, states, query_scr, forget_scr, value_scr,
):
    half = DRAFT // 2
    for slot in range(ROWS):
        side = slot // HALF
        _, local, place = source_of(owner_ref, row_of(side, slot % HALF))
        mine_ref, other_ref = (near_ref, from_near_ref) if side == 0 else (far_ref, from_far_ref)
        for block in range(3):
            mine = mine_ref[slot % HALF, edges_of(block), :].astype(F32)
            other = other_ref[place, edges_of(block), :].astype(F32)
            edges[slot, block, :DRAFT, :] = jnp.where(local, mine, other)
            edges[slot, block, DRAFT:, :] = jnp.zeros((8, DK), F32)

        @pl.when(local)
        def _():
            states[slot] = mine_ref[slot % HALF, : 2 * DK, :]

        @pl.when(jnp.logical_not(local))
        def _():
            states[slot] = other_ref[place, : 2 * DK, :]

    sub_iota = lax.broadcasted_iota(jnp.int32, (1, DRAFT, DK), 1)

    def pair(step, _):
        base = step * 2
        for sub in range(2):
            slot = base + sub
            for head in range(2):
                lane = sub * 2 + head
                for block, (in_ref, out, act) in enumerate(
                    (
                        (query_ref, query_scr, as_query),
                        (forget_ref, forget_scr, jax.nn.sigmoid),
                        (value_ref, value_scr, as_value),
                    )
                ):
                    first = in_ref[slot, head, :half]
                    for shift in range(CONV - 1):
                        taps = conv_ref[shift, head, block_of(block)]
                        rows = edges[slot, block, pl.ds(2 * shift + head, half, stride=2), :]
                        first = first + taps[None, :] * rows
                    out[lane, :half] = act(first)
                    out[lane, half:] = in_ref[slot, head, half:]
        queries = query_scr[...]
        forget = forget_scr[...]
        values = value_scr[...]
        weights = jnp.zeros((4, DRAFT, DK), F32)
        decay = jnp.ones((4, 1, DK), F32)
        head_rows = []
        query_rows = []
        for t in range(DRAFT):
            forget_t = forget[:, t : t + 1, :]
            query_t = queries[:, t : t + 1, :]
            decay = decay * forget_t
            weights = jnp.where(sub_iota == t, 1.0 - forget_t, weights * forget_t)
            scores = jnp.sum(weights * query_t, axis=-1, keepdims=True)
            head_rows.append(jnp.sum(scores * values, axis=1, keepdims=True))
            query_rows.append(query_t * decay)
        local_out = jnp.concatenate(head_rows, axis=1)
        decayed = jnp.concatenate(query_rows, axis=1)
        for sub in range(2):
            slot = base + sub
            parity = lax.axis_index("req") % 2
            near_row = (1 - parity) * HALF + slot
            far_row = parity * HALF + slot - HALF
            row = jnp.where(slot < HALF, near_row, far_row)
            for head in range(2):
                lane = sub * 2 + head
                fine = decayed[lane]
                coarse = fine.astype(BF)
                stacked = jnp.concatenate([coarse, (fine - coarse.astype(F32)).astype(BF)], axis=0)
                both = jnp.dot(
                    stacked, states[slot, block_of(head), :], preferred_element_type=F32
                )
                out = local_out[lane] + (both[:DRAFT] + both[DRAFT:])
                scale = lax.rsqrt(jnp.mean(out * out, axis=-1, keepdims=True) + 1e-05)
                mixed_ref[row, :, block_of(head)] = (
                    out * scale * gain_ref[head, :][None, :]
                ).astype(BF)
        return 0

    lax.fori_loop(0, ROWS // 2, pair, 0)


def mixer_call(owner, near, far, from_near, from_far, queries, forget, values, conv, bias, gain):
    return call(
        mixer, jax.ShapeDtypeStruct((ROWS, DRAFT, 2 * DK), BF), [SM] + [VM] * 10,
        [
            pltpu.VMEM((ROWS, 3, 24, DK), F32),
            pltpu.VMEM((ROWS, 2 * DK, DK), BF),
            pltpu.VMEM((4, DRAFT, DK), F32),
            pltpu.VMEM((4, DRAFT, DK), F32),
            pltpu.VMEM((4, DRAFT, DK), F32),
        ],
        20_000_000, 2_000_000,
        owner, near, far, from_near, from_far, queries, forget, values, conv, bias, gain,
    )


def later(x, shift):
    return jnp.concatenate([x[shift:], jnp.ones((shift, DK), F32)], axis=0)


def split(x):
    coarse = x.astype(BF)
    return coarse, (x - coarse.astype(F32)).astype(BF)


def keep(
    owner_ref, accept_ref, near_ref, far_ref, from_near_ref, from_far_ref, state_ref, conv_ref,
    bias_ref, kept_ref, edges_out_ref, states, window, left, right, decays, sems,
):
    state_copies = [
        pltpu.make_async_copy(state_ref.at[row], states.at[row], sems.at[row])
        for row in range(ROWS)
    ]
    for copy in state_copies:
        copy.start()
    position = lax.broadcasted_iota(jnp.int32, (DRAFT, DK), 0)
    for slot in range(ROWS):
        side = slot // HALF
        row = row_of(side, slot % HALF)
        partner, local, place = source_of(owner_ref, row)
        length = accept_ref[partner]
        mine_ref, other_ref = (near_ref, from_near_ref) if side == 0 else (far_ref, from_far_ref)
        for block in range(3):
            mine = mine_ref[slot % HALF, drafts_of(block), :].astype(F32)
            other = other_ref[place, drafts_of(block), :].astype(F32)
            window[slot, block, 8:, :] = jnp.where(local, mine, other)
            window[slot, block, 2:8, :] = mine_ref[slot % HALF, edges_of(block), :].astype(F32)[:6]
        for head in range(2):
            gates = convolve(window, conv_ref, slot, head, 1) + bias_ref[head, :][None, :]
            values = as_value(convolve(window, conv_ref, slot, head, 2))
            forget = jax.nn.sigmoid(gates)
            inside = position < length
            weights = jnp.where(inside, 1.0 - forget, 0.0)
            factors = jnp.where(inside, forget, 1.0)
            after = later(factors, 1)
            for shift in (1, 2, 4, 8):
                after = after * later(after, shift)
            weight_high, weight_low = split(weights * after)
            value_high, value_low = split(values)
            left[slot, head] = jnp.concatenate([weight_high, weight_low, weight_high], axis=0)
            right[slot, head] = jnp.concatenate([value_high, value_high, value_low], axis=0)
            lane = 2 * slot + head
            decays[lane : lane + 1, :] = (factors * after)[:1, :]
        for block in range(3):
            turned = pltpu.roll(window[slot, block], 38 - 2 * length, 0)
            for step in range(CONV - 1):
                edges_out_ref[row, step, :, block_of(block)] = turned[
                    2 * step : 2 * step + 2
                ].astype(BF)
    columns = jnp.transpose(decays[...])
    for copy in state_copies:
        copy.wait()
    for slot in range(ROWS):
        row = row_of(slot // HALF, slot % HALF)
        for head in range(2):
            lane = 2 * slot + head
            update = lax.dot_general(
                left[slot, head], right[slot, head], (((0,), (0,)), ((), ())),
                preferred_element_type=F32,
            )
            kept_ref[row, head] = columns[:, lane : lane + 1] * states[row, head] + update


def keep_call(owner, accept, near, far, from_near, from_far, states, conv, bias):
    shape = jax.ShapeDtypeStruct
    return call(
        keep, (shape(states.shape, F32), shape((ROWS, CONV - 1, 2, 3 * DK), BF)),
        [SM, SM, VM, VM, VM, VM, HB, VM, VM],
        [
            pltpu.VMEM(states.shape, F32),
            pltpu.VMEM((ROWS, 3, 40, DK), F32),
            pltpu.VMEM((ROWS, 2, 3 * DRAFT, DK), BF),
            pltpu.VMEM((ROWS, 2, 3 * DRAFT, DK), BF),
            pltpu.VMEM((2 * ROWS, DK), F32),
            pltpu.SemaphoreType.DMA((ROWS,)),
        ],
        20_000_000, 3_000_000, owner, accept, near, far, from_near, from_far, states, conv, bias,
    )


def columns_of(step, width):
    place = lax.bitwise_xor(lax.axis_index("grp"), step)
    return pl.ds(pl.multiple_of(place * width, width), width)


def project_kernel(
    rows_ref, weight_ref, resid_ref, own_ref, next_ref, far_ref, prev_ref,
):
    width = own_ref.shape[1]
    rows = rows_ref[...]
    for step, out_ref in ((2, far_ref), (1, next_ref), (3, prev_ref)):
        part = jnp.dot(rows, weight_ref[:, columns_of(step, width)], preferred_element_type=F32)
        out_ref[...] = part.astype(BF)
    part = jnp.dot(rows, weight_ref[:, columns_of(0, width)], preferred_element_type=F32)
    own_ref[...] = part + resid_ref[:, columns_of(0, width)].astype(F32)


def project(rows, weight, resid):
    slots, model = resid.shape
    width = model // 4
    shape = jax.ShapeDtypeStruct
    return pl.pallas_call(
        project_kernel,
        name="project",
        out_shape=(
            shape((slots, width), F32),
            shape((slots, width), BF),
            shape((slots, width), BF),
            shape((slots, width), BF),
        ),
        in_specs=[VM] * 3,
        out_specs=tuple([VM] * 4),
        compiler_params=PARAMS,
        cost_estimate=pl.CostEstimate(
            flops=140_000_000, bytes_accessed=2_000_000, transcendentals=0
        ),
    )(rows, weight, resid)


def ffn_kernel(
    length_ref, own_ref, next_ref, far_ref, prev_ref, gain_ref, gate_ref, up_ref, down_ref,
    own_out_ref, next_out_ref, far_out_ref, prev_out_ref, normed_scr,
):
    width = own_ref.shape[1]
    parts = ((0, own_ref), (1, next_ref), (2, far_ref), (3, prev_ref))
    total = None
    for _, ref in parts:
        block = ref[...].astype(F32)
        square = jnp.sum(block * block, axis=-1, keepdims=True)
        total = square if total is None else total + square
    scale = lax.rsqrt(total / (4 * width) + 1e-05)
    for step, ref in parts:
        columns = columns_of(step, width)
        normed_scr[:, columns] = (ref[...].astype(F32) * scale * gain_ref[:, columns]).astype(BF)
    normed = normed_scr[...]
    dims = (((1,), (1,)), ((), ()))
    gate = lax.dot_general(normed, gate_ref[...], dims, preferred_element_type=F32)
    up = lax.dot_general(normed, up_ref[...], dims, preferred_element_type=F32)
    hidden = (gate * jax.nn.sigmoid(gate) * up).astype(BF)
    me = lax.axis_index("req")
    position = lax.broadcasted_iota(jnp.int32, (DRAFT, 1), 0)
    live = jnp.concatenate(
        [(position < length_ref[me * ROWS + row]).astype(F32) for row in range(ROWS)], axis=0
    )
    for step, out_ref in ((2, far_out_ref), (1, next_out_ref), (3, prev_out_ref)):
        part = jnp.dot(hidden, down_ref[:, columns_of(step, width)], preferred_element_type=F32)
        out_ref[...] = (part * live).astype(BF)
    part = jnp.dot(hidden, down_ref[:, columns_of(0, width)], preferred_element_type=F32)
    own_out_ref[...] = (part + own_ref[...].astype(F32)) * live


def ffn(lengths, own, following, far, preceding, gain, gate_t, up_t, down):
    slots, width = own.shape
    shape = jax.ShapeDtypeStruct
    return pl.pallas_call(
        ffn_kernel,
        name="ffn",
        out_shape=(
            shape((slots, width), F32),
            shape((slots, width), BF),
            shape((slots, width), BF),
            shape((slots, width), BF),
        ),
        in_specs=[SM] + [VM] * 8,
        out_specs=tuple([VM] * 4),
        scratch_shapes=[pltpu.VMEM((slots, 4 * width), BF)],
        compiler_params=PARAMS,
        cost_estimate=pl.CostEstimate(
            flops=1_100_000_000, bytes_accessed=9_000_000, transcendentals=100_000
        ),
    )(lengths, own, following, far, preceding, gain, gate_t, up_t, down)


def in_hbm(array):
    return pltpu.with_memory_space_constraint(array, pltpu.HBM)


def swapped(block, step):
    return lax.ppermute(block, "grp", [(i, i ^ step) for i in range(4)])


def shards(
    mix_inputs,
    conv_weight,
    forget_bias,
    norm_gain,
    out_weight,
    resid,
    ffn_gain,
    gate_weight,
    up_weight,
    down_weight,
    held_states,
    held_edges,
    draft_lengths,
    accepted,
    owner_row,
):
    slots = ROWS * DRAFT
    owner_row, accepted, draft_lengths = in_hbm(owner_row), in_hbm(accepted), in_hbm(draft_lengths)
    count = lax.axis_size("req")
    states = in_hbm(held_states)
    far, near = pack_call(states, in_hbm(held_edges), in_hbm(mix_inputs))
    across = [(i, (i + (1 if i % 2 else -1)) % count) for i in range(count)]
    from_far = lax.ppermute(far, "req", across)
    queries, forget, values, conv, bias, gain = prepare_call(
        near, far, in_hbm(conv_weight), in_hbm(forget_bias), in_hbm(norm_gain)
    )
    near, queries = lax.optimization_barrier((near, queries))
    from_near = lax.ppermute(near, "req", [(i, i ^ 1) for i in range(count)])
    mixed = mixer_call(
        owner_row, near, far, from_near, from_far, queries, forget, values, conv, bias, gain
    )
    own_part, to_one, to_two, to_three = project(
        mixed.reshape(slots, -1), out_weight, resid.reshape(slots, -1)
    )
    own_part, gate_weight, up_weight, down_weight = lax.optimization_barrier(
        (own_part, gate_weight, up_weight, down_weight)
    )
    gate_t, up_t, down = fetch_call(
        in_hbm(gate_weight.T), in_hbm(up_weight.T), in_hbm(down_weight)
    )
    two = swapped(to_two, 2)
    one = swapped(to_one, 1)
    three = swapped(to_three, 3)
    one, two, three, gate_t, up_t, down = lax.optimization_barrier(
        (one, two, three, gate_t, up_t, down)
    )
    stream = (own_part + two.astype(F32) + one.astype(F32) + three.astype(F32)).astype(BF)
    stream, from_near, from_far = lax.optimization_barrier((stream, from_near, from_far))
    two = swapped(stream, 2)
    one = swapped(stream, 1)
    three = swapped(stream, 3)
    kept_states, kept_edges = keep_call(
        owner_row, accepted, near, far, from_near, from_far, states, conv, bias
    )
    one, two, three, kept_states, kept_edges = lax.optimization_barrier(
        (one, two, three, kept_states, kept_edges)
    )
    own_part, to_one, to_two, to_three = ffn(
        draft_lengths, stream, one, two, three, ffn_gain[None, :], gate_t, up_t, down
    )
    two = swapped(to_two, 2)
    one = swapped(to_one, 1)
    three = swapped(to_three, 3)
    layer_out = (own_part + two.astype(F32) + one.astype(F32) + three.astype(F32)).astype(BF)
    return (layer_out.reshape(ROWS, DRAFT, -1), kept_states, kept_edges)


def solution(mesh):
    return jax.shard_map(
        shards,
        mesh=mesh,
        in_specs=(
            P("req", None, "grp", None),
            P(None, "grp", None),
            P("grp", None),
            P("grp", None),
            P("grp", None),
            P("req", None, None),
            P(),
            P(None, "grp"),
            P(None, "grp"),
            P("grp", None),
            P("req", "grp", None, None),
            P("req", None, "grp", None),
            P(),
            P(),
            P(),
        ),
        out_specs=(P("req", None, "grp"), P("req", "grp", None, None), P("req", None, "grp", None)),
        check_vma=False,
    )
```

time: 57.7 us -> 55.5 us (0.962)
  starting transfers between devices: 25.5 us -> 21.6 us
  waiting for transfers between devices: 12.7 us -> 16.4 us
  local copies, waits for them, and re-layouts: 1.11 us -> 0.01 us
  Pallas kernels: 16.5 us -> 15.6 us
    ppermute x4 -> x2, starting transfers between devices: 13 us -> 8.5 us  [the longest x1 8.41 us: shards(): from_far = lax.ppermute(far, 'req', across)]
    ppermute x4 -> x2, waiting for transfers between devices: 1.3 us -> 5.63 us  [the longest x1 5.63 us: shards(): from_far = lax.ppermute(far, 'req', across)]
    slice x1 -> x0, local copies, waits for them, and re-layouts: 1.08 us -> none  [shards(): drafts_high = shifted(mix_inputs[:HALF], 'req', -1)]
    pallas_call x4 -> x5, Pallas kernels: 13 us -> 12 us  [call(): pl.pallas_call(kernel, name=kernel.__name__, out_shape=out_shape, in_spec...]
    ppermute x9, waiting for transfers between devices: 11.4 us -> 10.8 us  [swapped(): return lax.ppermute(block, 'grp', [(i, i ^ step) for i in range(4)])]
    ppermute x9, starting transfers between devices: 12.5 us -> 13.1 us  [swapped(): return lax.ppermute(block, 'grp', [(i, i ^ step) for i in range(4)])]
  transfers between devices with their start and end apart: 13 -> 11, of which waited for: 7 -> 7; matrix products, arithmetic and copies ran while one was open for 2% -> 0% of each run, Pallas kernels for 20% -> 13%
where the time goes in v5:
time: 55.5 us; the launch traced here: 55.3 us
  starting transfers between devices  21.6 us (39%)
  waiting for transfers between devices  16.4 us (30%)
  Pallas kernels  15.6 us (28%)
  other arithmetic  0.8 us (1%)
  between operations  0.77 us (1%)
    ppermute x9, starting transfers between devices, swapped(): return lax.ppermute(block, 'grp', [(i, i ^ step) for i in range(4)])  13.1 us
    pallas_call x5, Pallas kernels, call(): pl.pallas_call(kernel, name=kernel.__name__, out_shape=out_shape, in_spec...  12 us
    ppermute x9, waiting for transfers between devices, swapped(): return lax.ppermute(block, 'grp', [(i, i ^ step) for i in range(4)])  10.8 us
    ppermute x1, starting transfers between devices, shards(): from_far = lax.ppermute(far, 'req', across)  8.41 us
    ppermute x1, waiting for transfers between devices, shards(): from_far = lax.ppermute(far, 'req', across)  5.63 us
    pallas_call x1, Pallas kernels, ffn(): pl.pallas_call(ffn_kernel, name='ffn', out_shape=(shape((slots, width), F...  3.27 us
  transfers between devices with their start and end apart: 11, of which 7 were waited for; matrix products, arithmetic and copies ran while one was open for 0% of the time, Pallas kernels for 13%

profile of v5, /device:TPU:6, one launch (start us, length us, event | category | flops | bytes accessed | tf_op | source)
XLA Modules:
  0.0 55.3 jit_solution(142622731540261715)
XLA Ops:
  0.6 0.0 copy-start.1
  0.6 0.0 copy-start
  0.7 1.6 %pack.1 = (bf16[4,400,128]{2,1,0:T(8,128)(2,1)S(1)}, bf16[4,400,128]{2,1,0:T(8,128)(2,1)S(1)}) custom-call(f32[8,2,128,128]{3,2,1,0:T(8,128)} %state_ref.3, bf16[8,3,2,384]{3,2,1,0:T(2,128)(2,1)} %edge_ref.1, bf16[8,16,2,384]{3,2,1,0:T(2,128)(2,1)} %draft_ref.1), custom_call_target="tpu_custom_call" | custom-call | flops 1000000 | bytes 2000000 | tf_op jit(solution)/shard_map/pack/pallas_call | solution.py:49
  2.3 0.9 %prepare.1 = (f32[8,2,16,128]{3,2,1,0:T(8,128)S(1)}, f32[8,2,16,128]{3,2,1,0:T(8,128)S(1)}, f32[8,2,16,128]{3,2,1,0:T(8,128)S(1)}, f32[4,2,384]{2,1,0:T(2,128)S(...) custom-call(bf16[4,400,128]{2,1,0:T(8,128)(2,1)S(1)} %get-tuple-element.47.near_ref, ...), custom_call_target="tpu_custom_call" | custom-call | flops 5000000 | bytes 3000000 | tf_op jit(solution)/shard_map/prepare/pallas_call | solution.py:49
  3.2 0.1 collective-permute-start
  3.3 8.4 %collective-permute-start.1 = (bf16[4,400,128]{2,1,0:T(8,128)(2,1)S(1)}, bf16[4,400,128]{2,1,0:T(8,128)(2,1)S(1)}, u32[]{:S(2)}, u32[]{:S(2)}) collective-permute-start(bf16[4,400,128]{2,1,0:T(8,128)(2,1)S(1)} %get-tuple-element.45.far_ref), channel_id=1, source_target_pairs={{0,63},{1,2},{2,1},{3,4},{4,3},{5,6},{6,5},{7,8},{8,7},{9,10},{10,... | collective-permute-start | bytes 1228808 | tf_op jit(solution)/shard_map/ppermute | solution.py:500
  11.7 0.0 collective-permute-done.from_near_ref
  11.7 5.6 %collective-permute-done.1.from_far_ref = bf16[4,400,128]{2,1,0:T(8,128)(2,1)S(1)} collective-permute-done((bf16[4,400,128]{2,1,0:T(8,128)(2,1)S(1)}, bf16[4,400,128]{2,1,0:T(8,128)(2,1)S(1)}, u32[]{:S(2)}, u32[]{:S(2)}) %collective-permute-start.1) | collective-permute-done | bytes 409632 | tf_op jit(solution)/shard_map/ppermute | solution.py:500
  17.3 2.2 %mixer.1 = bf16[8,16,256]{2,1,0:T(8,128)(2,1)S(1)} custom-call(s32[512]{0:T(512)} %owner_ref.3, bf16[4,400,128]{2,1,0:T(8,128)(2,1)S(1)} %get-tuple-element.47.near_ref, bf16[4,400,128]{2,1,0:T(8,128)(2,1)S(1)} %get-tuple-element.45.far_ref, bf16[4,400,128]{2,1,0:T(8,128)(2,1)S(1)} %collective-permute-done.from_near_ref, ...), custom_call_target="tpu_custom_call" | custom-call | flops 20000000 | bytes 2000000 | tf_op jit(solution)/shard_map/mixer/pallas_call | solution.py:49
  19.5 0.0 copy-done.1
  19.6 0.0 copy-done
  19.6 0.3 project.1
  19.9 0.9 %collective-permute-start.2 = (bf16[128,512]{1,0:T(8,128)(2,1)S(1)}, bf16[128,512]{1,0:T(8,128)(2,1)S(1)}, u32[]{:S(2)}, u32[]{:S(2)}) collective-permute-start(bf16[128,512]{1,0:T(8,128)(2,1)S(1)} %get-tuple-element.56), channel_id=1, source_target_pairs={{0,64},{64,0},{128,192},{192,128},{1,65},{65,1},{129,193},{193,129... | collective-permute-start | bytes 393224 | tf_op jit(solution)/shard_map/ppermute | solution.py:474
  20.8 1.1 %collective-permute-start.3 = (bf16[128,512]{1,0:T(8,128)(2,1)S(1)}, bf16[128,512]{1,0:T(8,128)(2,1)S(1)}, u32[]{:S(2)}, u32[]{:S(2)}) collective-permute-start(bf16[128,512]{1,0:T(8,128)(2,1)S(1)} %get-tuple-element.57), channel_id=1, source_target_pairs={{0,128},{64,192},{128,0},{192,64},{1,129},{65,193},{129,1},{193,65... | collective-permute-start | bytes 393224 | tf_op jit(solution)/shard_map/ppermute | solution.py:474
  21.9 2.8 %collective-permute-start.4 = (bf16[128,512]{1,0:T(8,128)(2,1)S(1)}, bf16[128,512]{1,0:T(8,128)(2,1)S(1)}, u32[]{:S(2)}, u32[]{:S(2)}) collective-permute-start(bf16[128,512]{1,0:T(8,128)(2,1)S(1)} %get-tuple-element.58), channel_id=1, source_target_pairs={{0,192},{64,128},{128,64},{192,0},{1,193},{65,129},{129,65},{193,1... | collective-permute-start | bytes 393224 | tf_op jit(solution)/shard_map/ppermute | solution.py:474
  24.7 3.6 %fetch.1 = (bf16[704,2048]{1,0:T(8,128)(2,1)S(1)}, bf16[704,2048]{1,0:T(8,128)(2,1)S(1)}, bf16[704,2048]{1,0:T(8,128)(2,1)S(1)}) custom-call(bf16[704,2048]{1,0:T(8,128)(2,1)} %bitcast.9, bf16[704,2048]{1,0:T(8,128)(2,1)} %bitcast.10, bf16[704,2048]{1,0:T(8,128)(2,1)} %refs_2_), custom_call_target="tpu_custom_call" | custom-call | bytes 17000000 | tf_op jit(solution)/shard_map/fetch/pallas_call | solution.py:49
  28.3 0.0 copy-start.2
  28.3 0.0 collective-permute-done.2
  28.3 0.0 collective-permute-done.3
  28.3 3.2 %collective-permute-done.4 = bf16[128,512]{1,0:T(8,128)(2,1)S(1)} collective-permute-done((bf16[128,512]{1,0:T(8,128)(2,1)S(1)}, bf16[128,512]{1,0:T(8,128)(2,1)S(1)}, u32[]{:S(2)}, u32[]{:S(2)}) %collective-permute-start.4) | collective-permute-done | bytes 131104 | tf_op jit(solution)/shard_map/ppermute | solution.py:474
  31.5 0.1 add_convert_fusion.1.own_ref
  31.6 1.8 %collective-permute-start.7 = (bf16[128,512]{1,0:T(8,128)(2,1)S(1)}, bf16[128,512]{1,0:T(8,128)(2,1)S(1)}, u32[]{:S(2)}, u32[]{:S(2)}) collective-permute-start(bf16[128,512]{1,0:T(8,128)(2,1)S(1)} %add_convert_fusion.1.own_ref), channel_id=1, source_target_pairs={{0,192},{64,128},{128,64},{192,0},{1,193},{65,129},{129,65},{193,1... | collective-permute-start | bytes 393224 | tf_op jit(solution)/shard_map/ppermute | solution.py:474
  33.4 0.0 collective-permute-start.6
  33.4 2.3 %collective-permute-start.5 = (bf16[128,512]{1,0:T(8,128)(2,1)S(1)}, bf16[128,512]{1,0:T(8,128)(2,1)S(1)}, u32[]{:S(2)}, u32[]{:S(2)}) collective-permute-start(bf16[128,512]{1,0:T(8,128)(2,1)S(1)} %add_convert_fusion.1.own_ref), channel_id=1, source_target_pairs={{0,64},{64,0},{128,192},{192,128},{1,65},{65,1},{129,193},{193,129... | collective-permute-start | bytes 393224 | tf_op jit(solution)/shard_map/ppermute | solution.py:474
  35.8 3.7 %keep.1 = (f32[8,2,128,128]{3,2,1,0:T(8,128)}, bf16[8,3,2,384]{3,2,1,0:T(2,128)(2,1)}) custom-call(s32[512]{0:T(512)} %owner_ref.3, s32[512]{0:T(512)} %accept_ref.1, bf16[4,400,128]{2,1,0:T(8,128)(2,1)S(1)} %get-tuple-element.47.near_ref, bf16[4,400,128]{2,1,0:T(8,128)(2,1)S(1)} %get-tuple-element.45.far_ref, ...), custom_call_target="tpu_custom_call" | custom-call | flops 20000000 | bytes 3000000 | tf_op jit(solution)/shard_map/keep/pallas_call | solution.py:49
  39.5 0.0 collective-permute-done.7.prev_ref
  39.5 1.3 %collective-permute-done.6.far_ref = bf16[128,512]{1,0:T(8,128)(2,1)S(1)} collective-permute-done((bf16[128,512]{1,0:T(8,128)(2,1)S(1)}, bf16[128,512]{1,0:T(8,128)(2,1)S(1)}, u32[]{:S(2)}, u32[]{:S(2)}) %collective-permute-start.6) | collective-permute-done | bytes 131104 | tf_op jit(solution)/shard_map/ppermute | solution.py:474
  40.8 1.8 %collective-permute-done.5.next_ref = bf16[128,512]{1,0:T(8,128)(2,1)S(1)} collective-permute-done((bf16[128,512]{1,0:T(8,128)(2,1)S(1)}, bf16[128,512]{1,0:T(8,128)(2,1)S(1)}, u32[]{:S(2)}, u32[]{:S(2)}) %collective-permute-start.5) | collective-permute-done | bytes 131104 | tf_op jit(solution)/shard_map/ppermute | solution.py:474
  42.6 0.0 copy-done.2
  42.6 3.3 %ffn.1 = (f32[128,512]{1,0:T(8,128)S(1)}, bf16[128,512]{1,0:T(8,128)(2,1)S(1)}, bf16[128,512]{1,0:T(8,128)(2,1)S(1)}, bf16[128,512]{1,0:T(8,128)(2,1)S(1)}) custom-call(s32[512]{0:T(512)} %length_ref.1, bf16[128,512]{1,0:T(8,128)(2,1)S(1)} %add_convert_fusion.1.own_ref, bf16[128,512]{1,0:T(8,128)(2,1)S(1)} %collective-permute-done.5.next_ref, ...), custom_call_target="tpu_custom_call" | custom-call | flops 1100000000 | bytes 9000000 | tf_op jit(solution)/shard_map/ffn/pallas_call | solution.py:450
  45.9 0.8 %collective-permute-start.8 = (bf16[128,512]{1,0:T(8,128)(2,1)S(1)}, bf16[128,512]{1,0:T(8,128)(2,1)S(1)}, u32[]{:S(2)}, u32[]{:S(2)}) collective-permute-start(bf16[128,512]{1,0:T(8,128)(2,1)S(1)} %get-tuple-element.80), channel_id=1, source_target_pairs={{0,128},{64,192},{128,0},{192,64},{1,129},{65,193},{129,1},{193,65... | collective-permute-start | bytes 393224 | tf_op jit(solution)/shard_map/ppermute | solution.py:474
  46.7 1.6 %collective-permute-start.9 = (bf16[128,512]{1,0:T(8,128)(2,1)S(1)}, bf16[128,512]{1,0:T(8,128)(2,1)S(1)}, u32[]{:S(2)}, u32[]{:S(2)}) collective-permute-start(bf16[128,512]{1,0:T(8,128)(2,1)S(1)} %get-tuple-element.81), channel_id=1, source_target_pairs={{0,64},{64,0},{128,192},{192,128},{1,65},{65,1},{129,193},{193,129... | collective-permute-start | bytes 393224 | tf_op jit(solution)/shard_map/ppermute | solution.py:474
  48.3 1.7 %collective-permute-start.10 = (bf16[128,512]{1,0:T(8,128)(2,1)S(1)}, bf16[128,512]{1,0:T(8,128)(2,1)S(1)}, u32[]{:S(2)}, u32[]{:S(2)}) collective-permute-start(bf16[128,512]{1,0:T(8,128)(2,1)S(1)} %get-tuple-element.82), channel_id=1, source_target_pairs={{0,192},{64,128},{128,64},{192,0},{1,193},{65,129},{129,65},{193,1... | collective-permute-start | bytes 393224 | tf_op jit(solution)/shard_map/ppermute | solution.py:474
  50.1 2.4 %collective-permute-done.8 = bf16[128,512]{1,0:T(8,128)(2,1)S(1)} collective-permute-done((bf16[128,512]{1,0:T(8,128)(2,1)S(1)}, bf16[128,512]{1,0:T(8,128)(2,1)S(1)}, u32[]{:S(2)}, u32[]{:S(2)}) %collective-permute-start.8) | collective-permute-done | bytes 131104 | tf_op jit(solution)/shard_map/ppermute | solution.py:474
  52.5 0.2 collective-permute-done.9
  52.7 1.8 %collective-permute-done.10 = bf16[128,512]{1,0:T(8,128)(2,1)S(1)} collective-permute-done((bf16[128,512]{1,0:T(8,128)(2,1)S(1)}, bf16[128,512]{1,0:T(8,128)(2,1)S(1)}, u32[]{:S(2)}, u32[]{:S(2)}) %collective-permute-start.10) | collective-permute-done | bytes 131104 | tf_op jit(solution)/shard_map/ppermute | solution.py:474
  54.5 0.7 %add_convert_fusion = bf16[128,512]{1,0:T(8,128)(2,1)} fusion(bf16[128,512]{1,0:T(8,128)(2,1)S(1)} %collective-permute-done.10, bf16[128,512]{1,0:T(8,128)(2,1)S(1)} %collective-permute-done.9, f32[128,512]{1,0:T(8,128)S(1)} %get-tuple-element.79, bf16[128,512]{1,0:T(8,128)(2,1)S(1)} %collective-permute-done.8), kind=kLoop, calls=%fused_computation | loop fusion | flops 458752 | bytes 786432 | tf_op jit(solution)/shard_map/convert_element_type | solution.py:541
Async XLA Ops:
  0.6 18.9 %copy-start.1 = (bf16[8,16,2048]{2,1,0:T(8,128)(2,1)S(1)}, bf16[8,16,2048]{2,1,0:T(8,128)(2,1)}, u32[]{:S(2)}) copy-start(bf16[8,16,2048]{2,1,0:T(8,128)(2,1)} %param.20) | copy-start | bytes 1572868
  0.6 18.9 %copy-start = (bf16[256,2048]{1,0:T(8,128)(2,1)S(1)}, bf16[256,2048]{1,0:T(8,128)(2,1)}, u32[]{:S(2)}) copy-start(bf16[256,2048]{1,0:T(8,128)(2,1)} %weight_ref.1) | copy-start | bytes 3145732
  3.2 8.5 %collective-permute-start = (bf16[4,400,128]{2,1,0:T(8,128)(2,1)S(1)}, bf16[4,400,128]{2,1,0:T(8,128)(2,1)S(1)}, u32[]{:S(2)}, u32[]{:S(2)}) collective-permute-start(bf16[4,400,128]{2,1,0:T(8,128)(2,1)S(1)} %get-tuple-element.47.near_ref), channel_id=1, source_target_pairs={{0,1},{1,0},{2,3},{3,2},{4,5},{5,4},{6,7},{7,6},{8,9},{9,8},{10,11... | collective-permute-start | bytes 1228808 | tf_op jit(solution)/shard_map/ppermute | solution.py:505
  3.3 14.0 %collective-permute-start.1 = (bf16[4,400,128]{2,1,0:T(8,128)(2,1)S(1)}, bf16[4,400,128]{2,1,0:T(8,128)(2,1)S(1)}, u32[]{:S(2)}, u32[]{:S(2)}) collective-permute-start(bf16[4,400,128]{2,1,0:T(8,128)(2,1)S(1)} %get-tuple-element.45.far_ref), channel_id=1, source_target_pairs={{0,63},{1,2},{2,1},{3,4},{4,3},{5,6},{6,5},{7,8},{8,7},{9,10},{10,... | collective-permute-start | bytes 1228808 | tf_op jit(solution)/shard_map/ppermute | solution.py:500
  19.9 8.4 %collective-permute-start.2 = (bf16[128,512]{1,0:T(8,128)(2,1)S(1)}, bf16[128,512]{1,0:T(8,128)(2,1)S(1)}, u32[]{:S(2)}, u32[]{:S(2)}) collective-permute-start(bf16[128,512]{1,0:T(8,128)(2,1)S(1)} %get-tuple-element.56), channel_id=1, source_target_pairs={{0,64},{64,0},{128,192},{192,128},{1,65},{65,1},{129,193},{193,129... | collective-permute-start | bytes 393224 | tf_op jit(solution)/shard_map/ppermute | solution.py:474
  20.8 7.5 %collective-permute-start.3 = (bf16[128,512]{1,0:T(8,128)(2,1)S(1)}, bf16[128,512]{1,0:T(8,128)(2,1)S(1)}, u32[]{:S(2)}, u32[]{:S(2)}) collective-permute-start(bf16[128,512]{1,0:T(8,128)(2,1)S(1)} %get-tuple-element.57), channel_id=1, source_target_pairs={{0,128},{64,192},{128,0},{192,64},{1,129},{65,193},{129,1},{193,65... | collective-permute-start | bytes 393224 | tf_op jit(solution)/shard_map/ppermute | solution.py:474
  21.9 9.6 %collective-permute-start.4 = (bf16[128,512]{1,0:T(8,128)(2,1)S(1)}, bf16[128,512]{1,0:T(8,128)(2,1)S(1)}, u32[]{:S(2)}, u32[]{:S(2)}) collective-permute-start(bf16[128,512]{1,0:T(8,128)(2,1)S(1)} %get-tuple-element.58), channel_id=1, source_target_pairs={{0,192},{64,128},{128,64},{192,0},{1,193},{65,129},{129,65},{193,1... | collective-permute-start | bytes 393224 | tf_op jit(solution)/shard_map/ppermute | solution.py:474
  28.3 14.4 %copy-start.2 = (f32[2048]{0:T(1024)S(1)}, f32[2048]{0:T(1024)}, u32[]{:S(2)}) copy-start(f32[2048]{0:T(1024)} %param.21) | copy-start | bytes 24580
  31.6 7.9 %collective-permute-start.7 = (bf16[128,512]{1,0:T(8,128)(2,1)S(1)}, bf16[128,512]{1,0:T(8,128)(2,1)S(1)}, u32[]{:S(2)}, u32[]{:S(2)}) collective-permute-start(bf16[128,512]{1,0:T(8,128)(2,1)S(1)} %add_convert_fusion.1.own_ref), channel_id=1, source_target_pairs={{0,192},{64,128},{128,64},{192,0},{1,193},{65,129},{129,65},{193,1... | collective-permute-start | bytes 393224 | tf_op jit(solution)/shard_map/ppermute | solution.py:474
  33.4 7.4 %collective-permute-start.6 = (bf16[128,512]{1,0:T(8,128)(2,1)S(1)}, bf16[128,512]{1,0:T(8,128)(2,1)S(1)}, u32[]{:S(2)}, u32[]{:S(2)}) collective-permute-start(bf16[128,512]{1,0:T(8,128)(2,1)S(1)} %add_convert_fusion.1.own_ref), channel_id=1, source_target_pairs={{0,128},{64,192},{128,0},{192,64},{1,129},{65,193},{129,1},{193,65... | collective-permute-start | bytes 393224 | tf_op jit(solution)/shard_map/ppermute | solution.py:474
  33.4 9.2 %collective-permute-start.5 = (bf16[128,512]{1,0:T(8,128)(2,1)S(1)}, bf16[128,512]{1,0:T(8,128)(2,1)S(1)}, u32[]{:S(2)}, u32[]{:S(2)}) collective-permute-start(bf16[128,512]{1,0:T(8,128)(2,1)S(1)} %add_convert_fusion.1.own_ref), channel_id=1, source_target_pairs={{0,64},{64,0},{128,192},{192,128},{1,65},{65,1},{129,193},{193,129... | collective-permute-start | bytes 393224 | tf_op jit(solution)/shard_map/ppermute | solution.py:474
  45.9 6.6 %collective-permute-start.8 = (bf16[128,512]{1,0:T(8,128)(2,1)S(1)}, bf16[128,512]{1,0:T(8,128)(2,1)S(1)}, u32[]{:S(2)}, u32[]{:S(2)}) collective-permute-start(bf16[128,512]{1,0:T(8,128)(2,1)S(1)} %get-tuple-element.80), channel_id=1, source_target_pairs={{0,128},{64,192},{128,0},{192,64},{1,129},{65,193},{129,1},{193,65... | collective-permute-start | bytes 393224 | tf_op jit(solution)/shard_map/ppermute | solution.py:474
  46.7 6.0 %collective-permute-start.9 = (bf16[128,512]{1,0:T(8,128)(2,1)S(1)}, bf16[128,512]{1,0:T(8,128)(2,1)S(1)}, u32[]{:S(2)}, u32[]{:S(2)}) collective-permute-start(bf16[128,512]{1,0:T(8,128)(2,1)S(1)} %get-tuple-element.81), channel_id=1, source_target_pairs={{0,64},{64,0},{128,192},{192,128},{1,65},{65,1},{129,193},{193,129... | collective-permute-start | bytes 393224 | tf_op jit(solution)/shard_map/ppermute | solution.py:474
  48.3 6.2 %collective-permute-start.10 = (bf16[128,512]{1,0:T(8,128)(2,1)S(1)}, bf16[128,512]{1,0:T(8,128)(2,1)S(1)}, u32[]{:S(2)}, u32[]{:S(2)}) collective-permute-start(bf16[128,512]{1,0:T(8,128)(2,1)S(1)} %get-tuple-element.82), channel_id=1, source_target_pairs={{0,192},{64,128},{128,64},{192,0},{1,193},{65,129},{129,65},{193,1... | collective-permute-start | bytes 393224 | tf_op jit(solution)/shard_map/ppermute | solution.py:474

commit v6 on v5

--- a/solution.py
+++ b/solution.py
@@ -58,7 +58,22 @@
     )(*args)
 
 
-def pack(state_ref, edge_ref, draft_ref, far_ref, near_ref, states, edges, drafts, sems):
+def columns_of(step, width):
+    place = lax.bitwise_xor(lax.axis_index("grp"), step)
+    return pl.ds(pl.multiple_of(place * width, width), width)
+
+
+def pack(
+    state_ref, edge_ref, draft_ref, weight_ref, far_ref, near_ref, one_ref, two_ref, three_ref,
+    states, edges, drafts, sems,
+):
+    width = one_ref.shape[1]
+    cuts = [
+        pltpu.make_async_copy(
+            weight_ref.at[:, columns_of(step, width)], out_ref, sems.at[ROWS + 1 + step]
+        )
+        for step, out_ref in ((1, one_ref), (2, two_ref), (3, three_ref))
+    ]
     copies = [
         pltpu.make_async_copy(state_ref.at[row], states.at[row], sems.at[row])
         for row in range(ROWS)
@@ -68,6 +83,8 @@
     draft_copy.start()
     edge_copy.start()
     for copy in copies:
+        copy.start()
+    for copy in cuts:
         copy.start()
     edge_copy.wait()
     draft_copy.wait()
@@ -93,19 +110,22 @@
         for place in range(HALF):
             for head in range(2):
                 out_ref[place, block_of(head), :] = states[row_of(half, place), head].astype(BF)
-
-
-def pack_call(states, edges, drafts):
+    for copy in cuts:
+        copy.wait()
+
+
+def pack_call(states, edges, drafts, weight):
     half = jax.ShapeDtypeStruct((HALF, PACKED, DK), BF)
+    cut = jax.ShapeDtypeStruct((weight.shape[0], weight.shape[1] // 4), BF)
     return call(
-        pack, (half, half), [HB] * 3,
+        pack, (half, half, cut, cut, cut), [HB] * 4,
         [
             pltpu.VMEM(states.shape, F32),
             pltpu.VMEM(edges.shape, BF),
             pltpu.VMEM(drafts.shape, BF),
-            pltpu.SemaphoreType.DMA((ROWS + 2,)),
+            pltpu.SemaphoreType.DMA((ROWS + 5,)),
         ],
-        1_000_000, 2_000_000, states, edges, drafts,
+        1_000_000, 3_000_000, states, edges, drafts, weight,
     )
 
 
@@ -127,9 +147,120 @@
     return x * jax.nn.sigmoid(x)
 
 
-def prepare(
-    near_ref, far_ref, conv_hbm, bias_hbm, gain_hbm,
-    query_ref, forget_ref, value_ref, conv_ref, bias_ref, gain_ref, window, sems,
+def prepare(slots, own_refs, window, conv_ref, bias_ref, query_ref, forget_ref, value_ref):
+    for slot in slots:
+        own_ref = own_refs[slot // HALF]
+        for block in range(3):
+            window[slot, block, :8, :] = jnp.zeros((8, DK), F32)
+            window[slot, block, 8:, :] = own_ref[slot % HALF, drafts_of(block), :].astype(F32)
+    half = DRAFT // 2
+    for slot in slots:
+        for head in range(2):
+            queries, gates, values = [
+                convolve(window, conv_ref, slot, head, block) for block in range(3)
+            ]
+            place = slot % HALF
+            query_ref[place, head, :half] = queries[:half]
+            query_ref[place, head, half:] = as_query(queries[half:])
+            gates = gates + bias_ref[head, :][None, :]
+            forget_ref[place, head, :half] = gates[:half]
+            forget_ref[place, head, half:] = jax.nn.sigmoid(gates[half:])
+            value_ref[place, head, :half] = values[:half]
+            value_ref[place, head, half:] = as_value(values[half:])
+
+
+def mix(
+    side, owner_ref, mine_ref, other_ref, query_ref, forget_ref, value_ref, conv_ref, gain_ref,
+    edges, states, query_scr, forget_scr, value_scr, store,
+):
+    half = DRAFT // 2
+    for slot in range(HALF):
+        _, local, place = source_of(owner_ref, row_of(side, slot))
+        for block in range(3):
+            mine = mine_ref[slot, edges_of(block), :].astype(F32)
+            other = other_ref[place, edges_of(block), :].astype(F32)
+            edges[slot, block, :DRAFT, :] = jnp.where(local, mine, other)
+            edges[slot, block, DRAFT:, :] = jnp.zeros((8, DK), F32)
+
+        @pl.when(local)
+        def _():
+            states[slot] = mine_ref[slot, : 2 * DK, :]
+
+        @pl.when(jnp.logical_not(local))
+        def _():
+            states[slot] = other_ref[place, : 2 * DK, :]
+
+    sub_iota = lax.broadcasted_iota(jnp.int32, (1, DRAFT, DK), 1)
+
+    def pair(step, _):
+        base = step * 2
+        for sub in range(2):
+            slot = base + sub
+            for head in range(2):
+                lane = sub * 2 + head
+                for block, (in_ref, out, act) in enumerate(
+                    (
+                        (query_ref, query_scr, as_query),
+                        (forget_ref, forget_scr, jax.nn.sigmoid),
+                        (value_ref, value_scr, as_value),
+                    )
+                ):
+                    first = in_ref[slot, head, :half]
+                    for shift in range(CONV - 1):
+                        taps = conv_ref[shift, head, block_of(block)]
+                        rows = edges[slot, block, pl.ds(2 * shift + head, half, stride=2), :]
+                        first = first + taps[None, :] * rows
+                    out[lane, :half] = act(first)
+                    out[lane, half:] = in_ref[slot, head, half:]
+        queries = query_scr[...]
+        forget = forget_scr[...]
+        values = value_scr[...]
+        weights = jnp.zeros((4, DRAFT, DK), F32)
+        decay = jnp.ones((4, 1, DK), F32)
+        head_rows = []
+        query_rows = []
+        for t in range(DRAFT):
+            forget_t = forget[:, t : t + 1, :]
+            query_t = queries[:, t : t + 1, :]
+            decay = decay * forget_t
+            weights = jnp.where(sub_iota == t, 1.0 - forget_t, weights * forget_t)
+            scores = jnp.sum(weights * query_t, axis=-1, keepdims=True)
+            head_rows.append(jnp.sum(scores * values, axis=1, keepdims=True))
+            query_rows.append(query_t * decay)
+        local_out = jnp.concatenate(head_rows, axis=1)
+        decayed = jnp.concatenate(query_rows, axis=1)
+        for sub in range(2):
+            slot = base + sub
+            for head in range(2):
+                lane = sub * 2 + head
+                fine = decayed[lane]
+                coarse = fine.astype(BF)
+                stacked = jnp.concatenate([coarse, (fine - coarse.astype(F32)).astype(BF)], axis=0)
+                both = jnp.dot(
+                    stacked, states[slot, block_of(head), :], preferred_element_type=F32
+                )
+                out = local_out[lane] + (both[:DRAFT] + both[DRAFT:])
+                scale = lax.rsqrt(jnp.mean(out * out, axis=-1, keepdims=True) + 1e-05)
+                store(slot, head, (out * scale * gain_ref[head, :][None, :]).astype(BF))
+        return 0
+
+    lax.fori_loop(0, HALF // 2, pair, 0)
+
+
+MIX_SCRATCH = [
+    pltpu.VMEM((HALF, 3, 24, DK), F32),
+    pltpu.VMEM((HALF, 2 * DK, DK), BF),
+    pltpu.VMEM((4, DRAFT, DK), F32),
+    pltpu.VMEM((4, DRAFT, DK), F32),
+    pltpu.VMEM((4, DRAFT, DK), F32),
+]
+
+
+def mix_near(
+    owner_ref, near_ref, far_ref, from_near_ref, conv_hbm, bias_hbm, gain_hbm,
+    mixed_ref, query_ref, forget_ref, value_ref, conv_ref, bias_ref, gain_ref,
+    window, near_query, near_forget, near_value, edges, states, query_scr, forget_scr, value_scr,
+    sems,
 ):
     pairs = ((conv_hbm, conv_ref), (bias_hbm, bias_ref), (gain_hbm, gain_ref))
     copies = [
@@ -137,35 +268,63 @@
     ]
     for copy in copies:
         copy.start()
-    for slot in range(ROWS):
-        own_ref = near_ref if slot < HALF else far_ref
-        for block in range(3):
-            window[slot, block, :8, :] = jnp.zeros((8, DK), F32)
-            window[slot, block, 8:, :] = own_ref[slot % HALF, drafts_of(block), :].astype(F32)
     for copy in copies:
         copy.wait()
-    half = DRAFT // 2
-    for slot in range(ROWS):
-        for head in range(2):
-            queries, gates, values = [
-                convolve(window, conv_ref, slot, head, block) for block in range(3)
-            ]
-            query_ref[slot, head, :half] = queries[:half]
-            query_ref[slot, head, half:] = as_query(queries[half:])
-            gates = gates + bias_ref[head, :][None, :]
-            forget_ref[slot, head, :half] = gates[:half]
-            forget_ref[slot, head, half:] = jax.nn.sigmoid(gates[half:])
-            value_ref[slot, head, :half] = values[:half]
-            value_ref[slot, head, half:] = as_value(values[half:])
-
-
-def prepare_call(near, far, conv, bias, gain):
-    rows = jax.ShapeDtypeStruct((ROWS, 2, DRAFT, DK), F32)
-    copied = [jax.ShapeDtypeStruct(x.shape, x.dtype) for x in (conv, bias, gain)]
+    own_refs = (near_ref, far_ref)
+    prepare(
+        range(HALF), own_refs, window, conv_ref, bias_ref, near_query, near_forget, near_value
+    )
+    prepare(
+        range(HALF, ROWS), own_refs, window, conv_ref, bias_ref, query_ref, forget_ref, value_ref
+    )
+
+    def store(slot, head, block):
+        mixed_ref[slot, :, block_of(head)] = block
+
+    mix(
+        0, owner_ref, near_ref, from_near_ref, near_query, near_forget, near_value, conv_ref,
+        gain_ref, edges, states, query_scr, forget_scr, value_scr, store,
+    )
+
+
+def mix_near_call(owner, near, far, from_near, conv, bias, gain):
+    shape = jax.ShapeDtypeStruct
+    rows = (HALF, 2, DRAFT, DK)
+    copied = [shape(x.shape, x.dtype) for x in (conv, bias, gain)]
     return call(
-        prepare, (rows, rows, rows, *copied), [VM, VM, HB, HB, HB],
-        [pltpu.VMEM((ROWS, 3, 40, DK), F32), pltpu.SemaphoreType.DMA((3,))],
-        5_000_000, 3_000_000, near, far, conv, bias, gain,
+        mix_near,
+        (shape((HALF, DRAFT, 2 * DK), BF), *[shape(rows, F32)] * 3, *copied),
+        [SM, VM, VM, VM, HB, HB, HB],
+        [pltpu.VMEM((ROWS, 3, 40, DK), F32)]
+        + [pltpu.VMEM(rows, F32)] * 3
+        + MIX_SCRATCH
+        + [pltpu.SemaphoreType.DMA((3,))],
+        15_000_000, 3_000_000, owner, near, far, from_near, conv, bias, gain,
+    )
+
+
+def mix_far(
+    owner_ref, near_mixed_ref, far_ref, from_far_ref, query_ref, forget_ref, value_ref,
+    conv_ref, gain_ref, mixed_ref, edges, states, query_scr, forget_scr, value_scr,
+):
+    parity = lax.axis_index("req") % 2
+    for slot in range(HALF):
+        mixed_ref[row_of(0, slot)] = near_mixed_ref[slot]
+
+    def store(slot, head, block):
+        mixed_ref[parity * HALF + slot, :, block_of(head)] = block
+
+    mix(
+        1, owner_ref, far_ref, from_far_ref, query_ref, forget_ref, value_ref, conv_ref,
+        gain_ref, edges, states, query_scr, forget_scr, value_scr, store,
+    )
+
+
+def mix_far_call(owner, near_mixed, far, from_far, queries, forget, values, conv, gain):
+    return call(
+        mix_far, jax.ShapeDtypeStruct((ROWS, DRAFT, 2 * DK), BF), [SM] + [VM] * 8, MIX_SCRATCH,
+        10_000_000, 2_000_000,
+        owner, near_mixed, far, from_far, queries, forget, values, conv, gain,
     )
 
 
@@ -373,43 +532,26 @@
     )
 
 
-def columns_of(step, width):
-    place = lax.bitwise_xor(lax.axis_index("grp"), step)
-    return pl.ds(pl.multiple_of(place * width, width), width)
-
-
-def project_kernel(
-    rows_ref, weight_ref, resid_ref, own_ref, next_ref, far_ref, prev_ref,
-):
-    width = own_ref.shape[1]
-    rows = rows_ref[...]
-    for step, out_ref in ((2, far_ref), (1, next_ref), (3, prev_ref)):
-        part = jnp.dot(rows, weight_ref[:, columns_of(step, width)], preferred_element_type=F32)
-        out_ref[...] = part.astype(BF)
-    part = jnp.dot(rows, weight_ref[:, columns_of(0, width)], preferred_element_type=F32)
-    own_ref[...] = part + resid_ref[:, columns_of(0, width)].astype(F32)
-
-
-def project(rows, weight, resid):
+def project(
+    own_ref, one_ref, two_ref, three_ref, weight_ref, from_one_ref, from_two_ref, from_three_ref,
+    resid_ref, stream_ref,
+):
+    width = stream_ref.shape[1]
+    columns = columns_of(0, width)
+    total = jnp.dot(own_ref[...], weight_ref[:, columns], preferred_element_type=F32)
+    for rows_ref, part_ref in (
+        (one_ref, from_one_ref), (two_ref, from_two_ref), (three_ref, from_three_ref)
+    ):
+        total = total + jnp.dot(rows_ref[...], part_ref[...], preferred_element_type=F32)
+    stream_ref[...] = (resid_ref[:, columns].astype(F32) + total).astype(BF)
+
+
+def project_call(mixed, others, weight, parts, resid):
     slots, model = resid.shape
-    width = model // 4
-    shape = jax.ShapeDtypeStruct
-    return pl.pallas_call(
-        project_kernel,
-        name="project",
-        out_shape=(
-            shape((slots, width), F32),
-            shape((slots, width), BF),
-            shape((slots, width), BF),
-            shape((slots, width), BF),
-        ),
-        in_specs=[VM] * 3,
-        out_specs=tuple([VM] * 4),
-        compiler_params=PARAMS,
-        cost_estimate=pl.CostEstimate(
-            flops=140_000_000, bytes_accessed=2_000_000, transcendentals=0
-        ),
-    )(rows, weight, resid)
+    return call(
+        project, jax.ShapeDtypeStruct((slots, model // 4), BF), [VM] * 9, [],
+        140_000_000, 3_000_000, mixed, *others, weight, *parts, resid,
+    )
 
 
 def ffn_kernel(
@@ -495,33 +637,29 @@
     owner_row, accepted, draft_lengths = in_hbm(owner_row), in_hbm(accepted), in_hbm(draft_lengths)
     count = lax.axis_size("req")
     states = in_hbm(held_states)
-    far, near = pack_call(states, in_hbm(held_edges), in_hbm(mix_inputs))
+    far, near, *cuts = pack_call(
+        states, in_hbm(held_edges), in_hbm(mix_inputs), in_hbm(out_weight)
+    )
     across = [(i, (i + (1 if i % 2 else -1)) % count) for i in range(count)]
     from_far = lax.ppermute(far, "req", across)
-    queries, forget, values, conv, bias, gain = prepare_call(
-        near, far, in_hbm(conv_weight), in_hbm(forget_bias), in_hbm(norm_gain)
-    )
-    near, queries = lax.optimization_barrier((near, queries))
     from_near = lax.ppermute(near, "req", [(i, i ^ 1) for i in range(count)])
-    mixed = mixer_call(
-        owner_row, near, far, from_near, from_far, queries, forget, values, conv, bias, gain
-    )
-    own_part, to_one, to_two, to_three = project(
-        mixed.reshape(slots, -1), out_weight, resid.reshape(slots, -1)
-    )
-    own_part, gate_weight, up_weight, down_weight = lax.optimization_barrier(
-        (own_part, gate_weight, up_weight, down_weight)
-    )
+    parts = [swapped(cut, step) for step, cut in ((1, cuts[0]), (2, cuts[1]), (3, cuts[2]))]
+    near_mixed, queries, forget, values, conv, bias, gain = mix_near_call(
+        owner_row, near, far, from_near,
+        in_hbm(conv_weight), in_hbm(forget_bias), in_hbm(norm_gain),
+    )
+    mixed = mix_far_call(
+        owner_row, near_mixed, far, from_far, queries, forget, values, conv, gain
+    ).reshape(slots, -1)
+    mixed, parts[0], gate_weight, up_weight, down_weight = lax.optimization_barrier(
+        (mixed, parts[0], gate_weight, up_weight, down_weight)
+    )
+    others = [swapped(mixed, step) for step in (1, 2, 3)]
     gate_t, up_t, down = fetch_call(
         in_hbm(gate_weight.T), in_hbm(up_weight.T), in_hbm(down_weight)
     )
-    two = swapped(to_two, 2)
-    one = swapped(to_one, 1)
-    three = swapped(to_three, 3)
-    one, two, three, gate_t, up_t, down = lax.optimization_barrier(
-        (one, two, three, gate_t, up_t, down)
-    )
-    stream = (own_part + two.astype(F32) + one.astype(F32) + three.astype(F32)).astype(BF)
+    *others, gate_t, up_t, down = lax.optimization_barrier((*others, gate_t, up_t, down))
+    stream = project_call(mixed, others, out_weight, parts, resid.reshape(slots, -1))
     stream, from_near, from_far = lax.optimization_barrier((stream, from_near, from_far))
     two = swapped(stream, 2)
     one = swapped(stream, 1)

time: 55.5 us -> 52.1 us (0.939)
  waiting for transfers between devices: 16.4 us -> 8.09 us
  starting transfers between devices: 21.6 us -> 25.7 us
  Pallas kernels: 15.6 us -> 16.5 us
    ppermute x1, waiting for transfers between devices: 5.63 us -> 0.01 us  [shards(): from_far = lax.ppermute(far, 'req', across)]
    ppermute x9 -> x12, starting transfers between devices: 13.1 us -> 17.2 us  [swapped(): return lax.ppermute(block, 'grp', [(i, i ^ step) for i in range(4)])]
    ppermute x9 -> x12, waiting for transfers between devices: 10.8 us -> 8.08 us  [swapped(): return lax.ppermute(block, 'grp', [(i, i ^ step) for i in range(4)])]
    pallas_call x5 -> x6, Pallas kernels: 12 us -> 13.3 us  [call(): pl.pallas_call(kernel, name=kernel.__name__, out_shape=out_shape, in_spec...]
  transfers between devices with their start and end apart: 11 -> 14, of which waited for: 7 -> 6; matrix products, arithmetic and copies ran while one was open for 0% -> 0% of each run, Pallas kernels for 13% -> 22%
where the time goes in v6:
time: 52.1 us; the launch traced here: 51.8 us
  starting transfers between devices  25.7 us (49%)
  Pallas kernels  16.5 us (32%)
  waiting for transfers between devices  8.09 us (16%)
  between operations  0.76 us (1%)
  other arithmetic  0.72 us (1%)
    ppermute x12, starting transfers between devices, swapped(): return lax.ppermute(block, 'grp', [(i, i ^ step) for i in range(4)])  17.2 us
    pallas_call x6, Pallas kernels, call(): pl.pallas_call(kernel, name=kernel.__name__, out_shape=out_shape, in_spec...  13.3 us
    ppermute x1, starting transfers between devices, shards(): from_far = lax.ppermute(far, 'req', across)  8.41 us
    ppermute x12, waiting for transfers between devices, swapped(): return lax.ppermute(block, 'grp', [(i, i ^ step) for i in range(4)])  8.08 us
    pallas_call x1, Pallas kernels, ffn(): pl.pallas_call(ffn_kernel, name='ffn', out_shape=(shape((slots, width), F...  3.27 us
  transfers between devices with their start and end apart: 14, of which 6 were waited for; matrix products, arithmetic and copies ran while one was open for 0% of the time, Pallas kernels for 22%

profile of v6, /device:TPU:6, one launch (start us, length us, event | category | flops | bytes accessed | tf_op | source)
XLA Modules:
  0.0 51.8 jit_solution(14950547156002652034)
XLA Ops:
  0.6 1.7 %pack.1 = (bf16[4,400,128]{2,1,0:T(8,128)(2,1)S(1)}, bf16[4,400,128]{2,1,0:T(8,128)(2,1)S(1)}, bf16[256,512]{1,0:T(8,128)(2,1)S(1)}, bf16[256,512]{1,0:T(8,128)(2,1)S(1)}, bf16[256,512]{1,0:T(8,128)(2,1)S(1)}) custom-call(f32[8,2,128,128]{3,2,1,0:T(8,128)} %state_ref.3, bf16[8,3,2,384]{3,2,1,0:T(2,128)(2,1)} %edge_ref.1, bf16[8,16,2,384]{3,2,1,0:T(2,128)(2,1)} %draft_ref.1, ...), custom_call_target="tpu_custom_call" | custom-call | flops 1000000 | bytes 3000000 | tf_op jit(solution)/shard_map/pack/pallas_call | solution.py:49
  2.4 0.1 collective-permute-start
  2.5 8.4 %collective-permute-start.1 = (bf16[4,400,128]{2,1,0:T(8,128)(2,1)S(1)}, bf16[4,400,128]{2,1,0:T(8,128)(2,1)S(1)}, u32[]{:S(2)}, u32[]{:S(2)}) collective-permute-start(bf16[4,400,128]{2,1,0:T(8,128)(2,1)S(1)} %get-tuple-element.44.far_ref), channel_id=1, source_target_pairs={{0,63},{1,2},{2,1},{3,4},{4,3},{5,6},{6,5},{7,8},{8,7},{9,10},{10,... | collective-permute-start | bytes 1228808 | tf_op jit(solution)/shard_map/ppermute | solution.py:644
  10.9 0.8 %collective-permute-start.2 = (bf16[256,512]{1,0:T(8,128)(2,1)S(1)}, bf16[256,512]{1,0:T(8,128)(2,1)S(1)}, u32[]{:S(2)}, u32[]{:S(2)}) collective-permute-start(bf16[256,512]{1,0:T(8,128)(2,1)S(1)} %get-tuple-element.51), channel_id=1, source_target_pairs={{0,64},{64,0},{128,192},{192,128},{1,65},{65,1},{129,193},{193,129... | collective-permute-start | bytes 786440 | tf_op jit(solution)/shard_map/ppermute | solution.py:616
  11.7 1.1 %collective-permute-start.6 = (bf16[256,512]{1,0:T(8,128)(2,1)S(1)}, bf16[256,512]{1,0:T(8,128)(2,1)S(1)}, u32[]{:S(2)}, u32[]{:S(2)}) collective-permute-start(bf16[256,512]{1,0:T(8,128)(2,1)S(1)} %get-tuple-element.63), channel_id=1, source_target_pairs={{0,128},{64,192},{128,0},{192,64},{1,129},{65,193},{129,1},{193,65... | collective-permute-start | bytes 786440 | tf_op jit(solution)/shard_map/ppermute | solution.py:616
  12.8 2.8 %collective-permute-start.7 = (bf16[256,512]{1,0:T(8,128)(2,1)S(1)}, bf16[256,512]{1,0:T(8,128)(2,1)S(1)}, u32[]{:S(2)}, u32[]{:S(2)}) collective-permute-start(bf16[256,512]{1,0:T(8,128)(2,1)S(1)} %get-tuple-element.64), channel_id=1, source_target_pairs={{0,192},{64,128},{128,64},{192,0},{1,193},{65,129},{129,65},{193,1... | collective-permute-start | bytes 786440 | tf_op jit(solution)/shard_map/ppermute | solution.py:616
  15.6 0.0 collective-permute-done.from_near_ref
  15.6 2.3 %mix_near.1 = (bf16[4,16,256]{2,1,0:T(8,128)(2,1)S(1)}, f32[4,2,16,128]{3,2,1,0:T(8,128)S(1)}, f32[4,2,16,128]{3,2,1,0:T(8,128)S(1)}, f32[4,2,16,128]{3,2,1,0:T(...) custom-call(s32[512]{0:T(512)} %owner_ref.5, ...), custom_call_target="tpu_custom_call" | custom-call | flops 15000000 | bytes 3000000 | tf_op jit(solution)/shard_map/mix_near/pallas_call | solution.py:49
  17.9 0.0 collective-permute-done.1.from_far_ref
  17.9 1.5 %mix_far.1 = bf16[8,16,256]{2,1,0:T(8,128)(2,1)S(1)} custom-call(s32[512]{0:T(512)} %owner_ref.5, bf16[4,16,256]{2,1,0:T(8,128)(2,1)S(1)} %get-tuple-element.45.near_mixed_ref, bf16[4,400,128]{2,1,0:T(8,128)(2,1)S(1)} %get-tuple-element.44.far_ref, bf16[4,400,128]{2,1,0:T(8,128)(2,1)S(1)} %collective-permute-done.1.from_far_ref, ...), custom_call_target="tpu_custom_call" | custom-call | flops 10000000 | bytes 2000000 | tf_op jit(solution)/shard_map/mix_far/pallas_call | solution.py:49
  19.4 0.0 collective-permute-done.2.from_one_ref
  19.4 0.6 %collective-permute-start.5 = (bf16[128,256]{1,0:T(8,128)(2,1)S(1)}, bf16[128,256]{1,0:T(8,128)(2,1)S(1)}, u32[]{:S(2)}, u32[]{:S(2)}) collective-permute-start(bf16[128,256]{1,0:T(8,128)(2,1)S(1)} %bitcast.7), channel_id=1, source_target_pairs={{0,192},{64,128},{128,64},{192,0},{1,193},{65,129},{129,65},{193,1... | collective-permute-start | bytes 196616 | tf_op jit(solution)/shard_map/ppermute | solution.py:616
  20.0 1.2 %collective-permute-start.4 = (bf16[128,256]{1,0:T(8,128)(2,1)S(1)}, bf16[128,256]{1,0:T(8,128)(2,1)S(1)}, u32[]{:S(2)}, u32[]{:S(2)}) collective-permute-start(bf16[128,256]{1,0:T(8,128)(2,1)S(1)} %bitcast.8), channel_id=1, source_target_pairs={{0,128},{64,192},{128,0},{192,64},{1,129},{65,193},{129,1},{193,65... | collective-permute-start | bytes 196616 | tf_op jit(solution)/shard_map/ppermute | solution.py:616
  21.2 2.4 %collective-permute-start.3 = (bf16[128,256]{1,0:T(8,128)(2,1)S(1)}, bf16[128,256]{1,0:T(8,128)(2,1)S(1)}, u32[]{:S(2)}, u32[]{:S(2)}) collective-permute-start(bf16[128,256]{1,0:T(8,128)(2,1)S(1)} %bitcast.9), channel_id=1, source_target_pairs={{0,64},{64,0},{128,192},{192,128},{1,65},{65,1},{129,193},{193,129... | collective-permute-start | bytes 196616 | tf_op jit(solution)/shard_map/ppermute | solution.py:616
  23.6 0.0 copy-start
  23.6 0.0 copy-start.1
  23.6 3.7 %fetch.1 = (bf16[704,2048]{1,0:T(8,128)(2,1)S(1)}, bf16[704,2048]{1,0:T(8,128)(2,1)S(1)}, bf16[704,2048]{1,0:T(8,128)(2,1)S(1)}) custom-call(bf16[704,2048]{1,0:T(8,128)(2,1)} %bitcast.12, bf16[704,2048]{1,0:T(8,128)(2,1)} %bitcast.13, bf16[704,2048]{1,0:T(8,128)(2,1)} %refs_2_), custom_call_target="tpu_custom_call" | custom-call | bytes 17000000 | tf_op jit(solution)/shard_map/fetch/pallas_call | solution.py:49
  27.3 0.0 copy-start.2
  27.3 0.0 collective-permute-done.5.three_ref
  27.3 0.0 collective-permute-done.4.two_ref
  27.3 0.6 %collective-permute-done.3.one_ref = bf16[128,256]{1,0:T(8,128)(2,1)S(1)} collective-permute-done((bf16[128,256]{1,0:T(8,128)(2,1)S(1)}, bf16[128,256]{1,0:T(8,128)(2,1)S(1)}, u32[]{:S(2)}, u32[]{:S(2)}) %collective-permute-start.3) | collective-permute-done | bytes 65568 | tf_op jit(solution)/shard_map/ppermute | solution.py:616
  27.9 0.0 collective-permute-done.6.from_two_ref
  27.9 0.0 collective-permute-done.7.from_three_ref
  27.9 0.0 copy-done
  27.9 0.0 copy-done.1
  27.9 0.3 project.1.own_ref
  28.3 2.1 %collective-permute-start.10 = (bf16[128,512]{1,0:T(8,128)(2,1)S(1)}, bf16[128,512]{1,0:T(8,128)(2,1)S(1)}, u32[]{:S(2)}, u32[]{:S(2)}) collective-permute-start(bf16[128,512]{1,0:T(8,128)(2,1)S(1)} %project.1.own_ref), channel_id=1, source_target_pairs={{0,192},{64,128},{128,64},{192,0},{1,193},{65,129},{129,65},{193,1... | collective-permute-start | bytes 393224 | tf_op jit(solution)/shard_map/ppermute | solution.py:616
  30.3 0.8 %collective-permute-start.9 = (bf16[128,512]{1,0:T(8,128)(2,1)S(1)}, bf16[128,512]{1,0:T(8,128)(2,1)S(1)}, u32[]{:S(2)}, u32[]{:S(2)}) collective-permute-start(bf16[128,512]{1,0:T(8,128)(2,1)S(1)} %project.1.own_ref), channel_id=1, source_target_pairs={{0,128},{64,192},{128,0},{192,64},{1,129},{65,193},{129,1},{193,65... | collective-permute-start | bytes 393224 | tf_op jit(solution)/shard_map/ppermute | solution.py:616
  31.1 1.3 %collective-permute-start.8 = (bf16[128,512]{1,0:T(8,128)(2,1)S(1)}, bf16[128,512]{1,0:T(8,128)(2,1)S(1)}, u32[]{:S(2)}, u32[]{:S(2)}) collective-permute-start(bf16[128,512]{1,0:T(8,128)(2,1)S(1)} %project.1.own_ref), channel_id=1, source_target_pairs={{0,64},{64,0},{128,192},{192,128},{1,65},{65,1},{129,193},{193,129... | collective-permute-start | bytes 393224 | tf_op jit(solution)/shard_map/ppermute | solution.py:616
  32.4 3.7 %keep.1 = (f32[8,2,128,128]{3,2,1,0:T(8,128)}, bf16[8,3,2,384]{3,2,1,0:T(2,128)(2,1)}) custom-call(s32[512]{0:T(512)} %owner_ref.5, s32[512]{0:T(512)} %accept_ref.1, bf16[4,400,128]{2,1,0:T(8,128)(2,1)S(1)} %get-tuple-element.43.near_ref, bf16[4,400,128]{2,1,0:T(8,128)(2,1)S(1)} %get-tuple-element.44.far_ref, ...), custom_call_target="tpu_custom_call" | custom-call | flops 20000000 | bytes 3000000 | tf_op jit(solution)/shard_map/keep/pallas_call | solution.py:49
  36.2 0.0 collective-permute-done.10.prev_ref
  36.2 1.2 %collective-permute-done.9.far_ref = bf16[128,512]{1,0:T(8,128)(2,1)S(1)} collective-permute-done((bf16[128,512]{1,0:T(8,128)(2,1)S(1)}, bf16[128,512]{1,0:T(8,128)(2,1)S(1)}, u32[]{:S(2)}, u32[]{:S(2)}) %collective-permute-start.9) | collective-permute-done | bytes 131104 | tf_op jit(solution)/shard_map/ppermute | solution.py:616
  37.4 1.1 %collective-permute-done.8.next_ref = bf16[128,512]{1,0:T(8,128)(2,1)S(1)} collective-permute-done((bf16[128,512]{1,0:T(8,128)(2,1)S(1)}, bf16[128,512]{1,0:T(8,128)(2,1)S(1)}, u32[]{:S(2)}, u32[]{:S(2)}) %collective-permute-start.8) | collective-permute-done | bytes 131104 | tf_op jit(solution)/shard_map/ppermute | solution.py:616
  38.5 0.0 copy-done.2
  38.5 3.3 %ffn.1 = (f32[128,512]{1,0:T(8,128)S(1)}, bf16[128,512]{1,0:T(8,128)(2,1)S(1)}, bf16[128,512]{1,0:T(8,128)(2,1)S(1)}, bf16[128,512]{1,0:T(8,128)(2,1)S(1)}) custom-call(s32[512]{0:T(512)} %length_ref.1, bf16[128,512]{1,0:T(8,128)(2,1)S(1)} %project.1.own_ref, bf16[128,512]{1,0:T(8,128)(2,1)S(1)} %collective-permute-done.8.next_ref, ...), custom_call_target="tpu_custom_call" | custom-call | flops 1100000000 | bytes 9000000 | tf_op jit(solution)/shard_map/ffn/pallas_call | solution.py:592
  41.7 1.8 %collective-permute-start.11 = (bf16[128,512]{1,0:T(8,128)(2,1)S(1)}, bf16[128,512]{1,0:T(8,128)(2,1)S(1)}, u32[]{:S(2)}, u32[]{:S(2)}) collective-permute-start(bf16[128,512]{1,0:T(8,128)(2,1)S(1)} %get-tuple-element.78), channel_id=1, source_target_pairs={{0,128},{64,192},{128,0},{192,64},{1,129},{65,193},{129,1},{193,65... | collective-permute-start | bytes 393224 | tf_op jit(solution)/shard_map/ppermute | solution.py:616
  43.5 1.4 %collective-permute-start.12 = (bf16[128,512]{1,0:T(8,128)(2,1)S(1)}, bf16[128,512]{1,0:T(8,128)(2,1)S(1)}, u32[]{:S(2)}, u32[]{:S(2)}) collective-permute-start(bf16[128,512]{1,0:T(8,128)(2,1)S(1)} %get-tuple-element.79), channel_id=1, source_target_pairs={{0,64},{64,0},{128,192},{192,128},{1,65},{65,1},{129,193},{193,129... | collective-permute-start | bytes 393224 | tf_op jit(solution)/shard_map/ppermute | solution.py:616
  45.0 1.0 %collective-permute-start.13 = (bf16[128,512]{1,0:T(8,128)(2,1)S(1)}, bf16[128,512]{1,0:T(8,128)(2,1)S(1)}, u32[]{:S(2)}, u32[]{:S(2)}) collective-permute-start(bf16[128,512]{1,0:T(8,128)(2,1)S(1)} %get-tuple-element.80), channel_id=1, source_target_pairs={{0,192},{64,128},{128,64},{192,0},{1,193},{65,129},{129,65},{193,1... | collective-permute-start | bytes 393224 | tf_op jit(solution)/shard_map/ppermute | solution.py:616
  45.9 2.4 %collective-permute-done.11 = bf16[128,512]{1,0:T(8,128)(2,1)S(1)} collective-permute-done((bf16[128,512]{1,0:T(8,128)(2,1)S(1)}, bf16[128,512]{1,0:T(8,128)(2,1)S(1)}, u32[]{:S(2)}, u32[]{:S(2)}) %collective-permute-start.11) | collective-permute-done | bytes 131104 | tf_op jit(solution)/shard_map/ppermute | solution.py:616
  48.3 1.0 %collective-permute-done.12 = bf16[128,512]{1,0:T(8,128)(2,1)S(1)} collective-permute-done((bf16[128,512]{1,0:T(8,128)(2,1)S(1)}, bf16[128,512]{1,0:T(8,128)(2,1)S(1)}, u32[]{:S(2)}, u32[]{:S(2)}) %collective-permute-start.12) | collective-permute-done | bytes 131104 | tf_op jit(solution)/shard_map/ppermute | solution.py:616
  49.3 1.8 %collective-permute-done.13 = bf16[128,512]{1,0:T(8,128)(2,1)S(1)} collective-permute-done((bf16[128,512]{1,0:T(8,128)(2,1)S(1)}, bf16[128,512]{1,0:T(8,128)(2,1)S(1)}, u32[]{:S(2)}, u32[]{:S(2)}) %collective-permute-start.13) | collective-permute-done | bytes 131104 | tf_op jit(solution)/shard_map/ppermute | solution.py:616
  51.1 0.7 %add_convert_fusion = bf16[128,512]{1,0:T(8,128)(2,1)} fusion(bf16[128,512]{1,0:T(8,128)(2,1)S(1)} %collective-permute-done.13, bf16[128,512]{1,0:T(8,128)(2,1)S(1)} %collective-permute-done.12, f32[128,512]{1,0:T(8,128)S(1)} %get-tuple-element.77, bf16[128,512]{1,0:T(8,128)(2,1)S(1)} %collective-permute-done.11), kind=kLoop, calls=%fused_computation | loop fusion | flops 458752 | bytes 786432 | tf_op jit(solution)/shard_map/convert_element_type | solution.py:679
Async XLA Ops:
  2.4 13.2 %collective-permute-start = (bf16[4,400,128]{2,1,0:T(8,128)(2,1)S(1)}, bf16[4,400,128]{2,1,0:T(8,128)(2,1)S(1)}, u32[]{:S(2)}, u32[]{:S(2)}) collective-permute-start(bf16[4,400,128]{2,1,0:T(8,128)(2,1)S(1)} %get-tuple-element.43.near_ref), channel_id=1, source_target_pairs={{0,1},{1,0},{2,3},{3,2},{4,5},{5,4},{6,7},{7,6},{8,9},{9,8},{10,11... | collective-permute-start | bytes 1228808 | tf_op jit(solution)/shard_map/ppermute | solution.py:645
  2.5 15.5 %collective-permute-start.1 = (bf16[4,400,128]{2,1,0:T(8,128)(2,1)S(1)}, bf16[4,400,128]{2,1,0:T(8,128)(2,1)S(1)}, u32[]{:S(2)}, u32[]{:S(2)}) collective-permute-start(bf16[4,400,128]{2,1,0:T(8,128)(2,1)S(1)} %get-tuple-element.44.far_ref), channel_id=1, source_target_pairs={{0,63},{1,2},{2,1},{3,4},{4,3},{5,6},{6,5},{7,8},{8,7},{9,10},{10,... | collective-permute-start | bytes 1228808 | tf_op jit(solution)/shard_map/ppermute | solution.py:644
  10.9 8.5 %collective-permute-start.2 = (bf16[256,512]{1,0:T(8,128)(2,1)S(1)}, bf16[256,512]{1,0:T(8,128)(2,1)S(1)}, u32[]{:S(2)}, u32[]{:S(2)}) collective-permute-start(bf16[256,512]{1,0:T(8,128)(2,1)S(1)} %get-tuple-element.51), channel_id=1, source_target_pairs={{0,64},{64,0},{128,192},{192,128},{1,65},{65,1},{129,193},{193,129... | collective-permute-start | bytes 786440 | tf_op jit(solution)/shard_map/ppermute | solution.py:616
  11.7 16.2 %collective-permute-start.6 = (bf16[256,512]{1,0:T(8,128)(2,1)S(1)}, bf16[256,512]{1,0:T(8,128)(2,1)S(1)}, u32[]{:S(2)}, u32[]{:S(2)}) collective-permute-start(bf16[256,512]{1,0:T(8,128)(2,1)S(1)} %get-tuple-element.63), channel_id=1, source_target_pairs={{0,128},{64,192},{128,0},{192,64},{1,129},{65,193},{129,1},{193,65... | collective-permute-start | bytes 786440 | tf_op jit(solution)/shard_map/ppermute | solution.py:616
  12.8 15.1 %collective-permute-start.7 = (bf16[256,512]{1,0:T(8,128)(2,1)S(1)}, bf16[256,512]{1,0:T(8,128)(2,1)S(1)}, u32[]{:S(2)}, u32[]{:S(2)}) collective-permute-start(bf16[256,512]{1,0:T(8,128)(2,1)S(1)} %get-tuple-element.64), channel_id=1, source_target_pairs={{0,192},{64,128},{128,64},{192,0},{1,193},{65,129},{129,65},{193,1... | collective-permute-start | bytes 786440 | tf_op jit(solution)/shard_map/ppermute | solution.py:616
  19.4 7.9 %collective-permute-start.5 = (bf16[128,256]{1,0:T(8,128)(2,1)S(1)}, bf16[128,256]{1,0:T(8,128)(2,1)S(1)}, u32[]{:S(2)}, u32[]{:S(2)}) collective-permute-start(bf16[128,256]{1,0:T(8,128)(2,1)S(1)} %bitcast.7), channel_id=1, source_target_pairs={{0,192},{64,128},{128,64},{192,0},{1,193},{65,129},{129,65},{193,1... | collective-permute-start | bytes 196616 | tf_op jit(solution)/shard_map/ppermute | solution.py:616
  20.0 7.3 %collective-permute-start.4 = (bf16[128,256]{1,0:T(8,128)(2,1)S(1)}, bf16[128,256]{1,0:T(8,128)(2,1)S(1)}, u32[]{:S(2)}, u32[]{:S(2)}) collective-permute-start(bf16[128,256]{1,0:T(8,128)(2,1)S(1)} %bitcast.8), channel_id=1, source_target_pairs={{0,128},{64,192},{128,0},{192,64},{1,129},{65,193},{129,1},{193,65... | collective-permute-start | bytes 196616 | tf_op jit(solution)/shard_map/ppermute | solution.py:616
  21.2 6.7 %collective-permute-start.3 = (bf16[128,256]{1,0:T(8,128)(2,1)S(1)}, bf16[128,256]{1,0:T(8,128)(2,1)S(1)}, u32[]{:S(2)}, u32[]{:S(2)}) collective-permute-start(bf16[128,256]{1,0:T(8,128)(2,1)S(1)} %bitcast.9), channel_id=1, source_target_pairs={{0,64},{64,0},{128,192},{192,128},{1,65},{65,1},{129,193},{193,129... | collective-permute-start | bytes 196616 | tf_op jit(solution)/shard_map/ppermute | solution.py:616
  23.6 4.3 %copy-start = (bf16[256,2048]{1,0:T(8,128)(2,1)S(1)}, bf16[256,2048]{1,0:T(8,128)(2,1)}, u32[]{:S(2)}) copy-start(bf16[256,2048]{1,0:T(8,128)(2,1)} %weight_ref.3) | copy-start | bytes 3145732
  23.6 4.3 %copy-start.1 = (bf16[8,16,2048]{2,1,0:T(8,128)(2,1)S(1)}, bf16[8,16,2048]{2,1,0:T(8,128)(2,1)}, u32[]{:S(2)}) copy-start(bf16[8,16,2048]{2,1,0:T(8,128)(2,1)} %param.20) | copy-start | bytes 1572868
  27.3 11.2 %copy-start.2 = (f32[2048]{0:T(1024)S(1)}, f32[2048]{0:T(1024)}, u32[]{:S(2)}) copy-start(f32[2048]{0:T(1024)} %param.21) | copy-start | bytes 24580
  28.3 7.9 %collective-permute-start.10 = (bf16[128,512]{1,0:T(8,128)(2,1)S(1)}, bf16[128,512]{1,0:T(8,128)(2,1)S(1)}, u32[]{:S(2)}, u32[]{:S(2)}) collective-permute-start(bf16[128,512]{1,0:T(8,128)(2,1)S(1)} %project.1.own_ref), channel_id=1, source_target_pairs={{0,192},{64,128},{128,64},{192,0},{1,193},{65,129},{129,65},{193,1... | collective-permute-start | bytes 393224 | tf_op jit(solution)/shard_map/ppermute | solution.py:616
  30.3 7.0 %collective-permute-start.9 = (bf16[128,512]{1,0:T(8,128)(2,1)S(1)}, bf16[128,512]{1,0:T(8,128)(2,1)S(1)}, u32[]{:S(2)}, u32[]{:S(2)}) collective-permute-start(bf16[128,512]{1,0:T(8,128)(2,1)S(1)} %project.1.own_ref), channel_id=1, source_target_pairs={{0,128},{64,192},{128,0},{192,64},{1,129},{65,193},{129,1},{193,65... | collective-permute-start | bytes 393224 | tf_op jit(solution)/shard_map/ppermute | solution.py:616
  31.1 7.3 %collective-permute-start.8 = (bf16[128,512]{1,0:T(8,128)(2,1)S(1)}, bf16[128,512]{1,0:T(8,128)(2,1)S(1)}, u32[]{:S(2)}, u32[]{:S(2)}) collective-permute-start(bf16[128,512]{1,0:T(8,128)(2,1)S(1)} %project.1.own_ref), channel_id=1, source_target_pairs={{0,64},{64,0},{128,192},{192,128},{1,65},{65,1},{129,193},{193,129... | collective-permute-start | bytes 393224 | tf_op jit(solution)/shard_map/ppermute | solution.py:616
  41.7 6.6 %collective-permute-start.11 = (bf16[128,512]{1,0:T(8,128)(2,1)S(1)}, bf16[128,512]{1,0:T(8,128)(2,1)S(1)}, u32[]{:S(2)}, u32[]{:S(2)}) collective-permute-start(bf16[128,512]{1,0:T(8,128)(2,1)S(1)} %get-tuple-element.78), channel_id=1, source_target_pairs={{0,128},{64,192},{128,0},{192,64},{1,129},{65,193},{129,1},{193,65... | collective-permute-start | bytes 393224 | tf_op jit(solution)/shard_map/ppermute | solution.py:616
  43.5 5.8 %collective-permute-start.12 = (bf16[128,512]{1,0:T(8,128)(2,1)S(1)}, bf16[128,512]{1,0:T(8,128)(2,1)S(1)}, u32[]{:S(2)}, u32[]{:S(2)}) collective-permute-start(bf16[128,512]{1,0:T(8,128)(2,1)S(1)} %get-tuple-element.79), channel_id=1, source_target_pairs={{0,64},{64,0},{128,192},{192,128},{1,65},{65,1},{129,193},{193,129... | collective-permute-start | bytes 393224 | tf_op jit(solution)/shard_map/ppermute | solution.py:616
  45.0 6.2 %collective-permute-start.13 = (bf16[128,512]{1,0:T(8,128)(2,1)S(1)}, bf16[128,512]{1,0:T(8,128)(2,1)S(1)}, u32[]{:S(2)}, u32[]{:S(2)}) collective-permute-start(bf16[128,512]{1,0:T(8,128)(2,1)S(1)} %get-tuple-element.80), channel_id=1, source_target_pairs={{0,192},{64,128},{128,64},{192,0},{1,193},{65,129},{129,65},{193,1... | collective-permute-start | bytes 393224 | tf_op jit(solution)/shard_map/ppermute | solution.py:616

commit v7 on v6

--- a/solution.py
+++ b/solution.py
@@ -58,21 +58,33 @@
     )(*args)
 
 
+def first_step():
+    return 1 + 2 * (lax.axis_index("req") % 2)
+
+
+def second_step():
+    return 3 - 2 * (lax.axis_index("req") % 2)
+
+
 def columns_of(step, width):
     place = lax.bitwise_xor(lax.axis_index("grp"), step)
     return pl.ds(pl.multiple_of(place * width, width), width)
 
 
 def pack(
-    state_ref, edge_ref, draft_ref, weight_ref, far_ref, near_ref, one_ref, two_ref, three_ref,
+    state_ref, edge_ref, draft_ref, weight_ref, far_ref, near_ref, first_ref, both_ref,
     states, edges, drafts, sems,
 ):
-    width = one_ref.shape[1]
+    width = first_ref.shape[1]
+    upper = both_ref.shape[0]
+    start = pl.multiple_of((lax.axis_index("req") % 2) * upper, upper)
     cuts = [
         pltpu.make_async_copy(
-            weight_ref.at[:, columns_of(step, width)], out_ref, sems.at[ROWS + 1 + step]
-        )
-        for step, out_ref in ((1, one_ref), (2, two_ref), (3, three_ref))
+            weight_ref.at[:, columns_of(first_step(), width)], first_ref, sems.at[ROWS + 2]
+        ),
+        pltpu.make_async_copy(
+            weight_ref.at[pl.ds(start, upper), columns_of(2, width)], both_ref, sems.at[ROWS + 3]
+        ),
     ]
     copies = [
         pltpu.make_async_copy(state_ref.at[row], states.at[row], sems.at[row])
@@ -116,14 +128,16 @@
 
 def pack_call(states, edges, drafts, weight):
     half = jax.ShapeDtypeStruct((HALF, PACKED, DK), BF)
-    cut = jax.ShapeDtypeStruct((weight.shape[0], weight.shape[1] // 4), BF)
+    width = weight.shape[1] // 4
+    first = jax.ShapeDtypeStruct((weight.shape[0], width), BF)
+    both = jax.ShapeDtypeStruct((weight.shape[0] // 2, width), BF)
     return call(
-        pack, (half, half, cut, cut, cut), [HB] * 4,
+        pack, (half, half, first, both), [HB] * 4,
         [
             pltpu.VMEM(states.shape, F32),
             pltpu.VMEM(edges.shape, BF),
             pltpu.VMEM(drafts.shape, BF),
-            pltpu.SemaphoreType.DMA((ROWS + 5,)),
+            pltpu.SemaphoreType.DMA((ROWS + 4,)),
         ],
         1_000_000, 3_000_000, states, edges, drafts, weight,
     )
@@ -533,42 +547,54 @@
 
 
 def project(
-    own_ref, one_ref, two_ref, three_ref, weight_ref, from_one_ref, from_two_ref, from_three_ref,
+    own_ref, first_ref, second_ref, weight_ref, from_first_ref, from_both_ref, chip_ref,
     resid_ref, stream_ref,
 ):
     width = stream_ref.shape[1]
+    depth = from_first_ref.shape[0]
     columns = columns_of(0, width)
-    total = jnp.dot(own_ref[...], weight_ref[:, columns], preferred_element_type=F32)
-    for rows_ref, part_ref in (
-        (one_ref, from_one_ref), (two_ref, from_two_ref), (three_ref, from_three_ref)
-    ):
-        total = total + jnp.dot(rows_ref[...], part_ref[...], preferred_element_type=F32)
+
+    def product(rows, part):
+        return jnp.dot(rows, part, preferred_element_type=F32)
+
+    total = product(own_ref[...], weight_ref[:, columns])
+    total = total + product(first_ref[...], from_first_ref[...])
+    total = total + product(second_ref[0], chip_ref[:depth])
+    parity = lax.axis_index("req") % 2
+    half = depth // 2
+    mine = pl.ds(pl.multiple_of(parity * half, half), half)
+    other = pl.ds(pl.multiple_of((1 - parity) * half, half), half)
+    total = total + product(second_ref[1, :, mine], from_both_ref[...])
+    total = total + product(second_ref[1, :, other], chip_ref[depth:])
     stream_ref[...] = (resid_ref[:, columns].astype(F32) + total).astype(BF)
 
 
-def project_call(mixed, others, weight, parts, resid):
+def project_call(mixed, first, second, weight, from_first, from_both, chip, resid):
     slots, model = resid.shape
     return call(
-        project, jax.ShapeDtypeStruct((slots, model // 4), BF), [VM] * 9, [],
-        140_000_000, 3_000_000, mixed, *others, weight, *parts, resid,
-    )
-
-
-def ffn_kernel(
-    length_ref, own_ref, next_ref, far_ref, prev_ref, gain_ref, gate_ref, up_ref, down_ref,
-    own_out_ref, next_out_ref, far_out_ref, prev_out_ref, normed_scr,
+        project, jax.ShapeDtypeStruct((slots, model // 4), BF), [VM] * 8, [],
+        140_000_000, 3_000_000, mixed, first, second, weight, from_first, from_both, chip, resid,
+    )
+
+
+def ffn(
+    length_ref, own_ref, first_ref, second_ref, gain_ref, gate_ref, up_ref, down_ref,
+    own_out_ref, second_out_ref, pair_out_ref, normed_scr,
 ):
     width = own_ref.shape[1]
-    parts = ((0, own_ref), (1, next_ref), (2, far_ref), (3, prev_ref))
+    parts = (
+        (0, own_ref[...]), (first_step(), first_ref[...]),
+        (second_step(), second_ref[0]), (2, second_ref[1]),
+    )
     total = None
-    for _, ref in parts:
-        block = ref[...].astype(F32)
+    for _, rows in parts:
+        block = rows.astype(F32)
         square = jnp.sum(block * block, axis=-1, keepdims=True)
         total = square if total is None else total + square
     scale = lax.rsqrt(total / (4 * width) + 1e-05)
-    for step, ref in parts:
+    for step, rows in parts:
         columns = columns_of(step, width)
-        normed_scr[:, columns] = (ref[...].astype(F32) * scale * gain_ref[:, columns]).astype(BF)
+        normed_scr[:, columns] = (rows.astype(F32) * scale * gain_ref[:, columns]).astype(BF)
     normed = normed_scr[...]
     dims = (((1,), (1,)), ((), ()))
     gate = lax.dot_general(normed, gate_ref[...], dims, preferred_element_type=F32)
@@ -579,41 +605,42 @@
     live = jnp.concatenate(
         [(position < length_ref[me * ROWS + row]).astype(F32) for row in range(ROWS)], axis=0
     )
-    for step, out_ref in ((2, far_out_ref), (1, next_out_ref), (3, prev_out_ref)):
+
+    def down(step):
         part = jnp.dot(hidden, down_ref[:, columns_of(step, width)], preferred_element_type=F32)
-        out_ref[...] = (part * live).astype(BF)
-    part = jnp.dot(hidden, down_ref[:, columns_of(0, width)], preferred_element_type=F32)
-    own_out_ref[...] = (part + own_ref[...].astype(F32)) * live
-
-
-def ffn(lengths, own, following, far, preceding, gain, gate_t, up_t, down):
+        return part * live
+
+    pair_out_ref[0] = down(first_step()).astype(BF)
+    pair_out_ref[1] = down(2).astype(BF)
+    second_out_ref[...] = down(second_step())
+    own_out_ref[...] = down(0) + own_ref[...].astype(F32) * live
+
+
+def ffn_call(lengths, own, first, second, gain, gate_t, up_t, down):
     slots, width = own.shape
     shape = jax.ShapeDtypeStruct
-    return pl.pallas_call(
-        ffn_kernel,
-        name="ffn",
-        out_shape=(
-            shape((slots, width), F32),
-            shape((slots, width), BF),
-            shape((slots, width), BF),
-            shape((slots, width), BF),
-        ),
-        in_specs=[SM] + [VM] * 8,
-        out_specs=tuple([VM] * 4),
-        scratch_shapes=[pltpu.VMEM((slots, 4 * width), BF)],
-        compiler_params=PARAMS,
-        cost_estimate=pl.CostEstimate(
-            flops=1_100_000_000, bytes_accessed=9_000_000, transcendentals=100_000
-        ),
-    )(lengths, own, following, far, preceding, gain, gate_t, up_t, down)
+    return call(
+        ffn,
+        (shape((slots, width), F32), shape((slots, width), F32), shape((2, slots, width), BF)),
+        [SM] + [VM] * 7,
+        [pltpu.VMEM((slots, 4 * width), BF)],
+        1_100_000_000, 9_000_000, lengths, own, first, second, gain, gate_t, up_t, down,
+    )
 
 
 def in_hbm(array):
     return pltpu.with_memory_space_constraint(array, pltpu.HBM)
 
 
-def swapped(block, step):
-    return lax.ppermute(block, "grp", [(i, i ^ step) for i in range(4)])
+def swapped(block, steps):
+    groups, count = lax.axis_size("grp"), lax.axis_size("req")
+    pairs = [
+        (g * count + d, (g ^ steps[d % 2]) * count + d) for g in range(groups) for d in range(count)
+    ]
+    return lax.ppermute(block, ("grp", "req"), pairs)
+
+
+FIRST, SECOND, BOTH = (1, 3), (3, 1), (2, 2)
 
 
 def shards(
@@ -643,7 +670,8 @@
     across = [(i, (i + (1 if i % 2 else -1)) % count) for i in range(count)]
     from_far = lax.ppermute(far, "req", across)
     from_near = lax.ppermute(near, "req", [(i, i ^ 1) for i in range(count)])
-    parts = [swapped(cut, step) for step, cut in ((1, cuts[0]), (2, cuts[1]), (3, cuts[2]))]
+    from_first = swapped(cuts[0], FIRST)
+    from_both = swapped(cuts[1], BOTH)
     near_mixed, queries, forget, values, conv, bias, gain = mix_near_call(
         owner_row, near, far, from_near,
         in_hbm(conv_weight), in_hbm(forget_bias), in_hbm(norm_gain),
@@ -651,32 +679,34 @@
     mixed = mix_far_call(
         owner_row, near_mixed, far, from_far, queries, forget, values, conv, gain
     ).reshape(slots, -1)
-    mixed, parts[0], gate_weight, up_weight, down_weight = lax.optimization_barrier(
-        (mixed, parts[0], gate_weight, up_weight, down_weight)
-    )
-    others = [swapped(mixed, step) for step in (1, 2, 3)]
-    gate_t, up_t, down = fetch_call(
-        in_hbm(gate_weight.T), in_hbm(up_weight.T), in_hbm(down_weight)
-    )
-    *others, gate_t, up_t, down = lax.optimization_barrier((*others, gate_t, up_t, down))
-    stream = project_call(mixed, others, out_weight, parts, resid.reshape(slots, -1))
-    stream, from_near, from_far = lax.optimization_barrier((stream, from_near, from_far))
-    two = swapped(stream, 2)
-    one = swapped(stream, 1)
-    three = swapped(stream, 3)
+    mixed, gate_weight, from_first, from_both = lax.optimization_barrier(
+        (mixed, gate_weight, from_first, from_both)
+    )
+    first = swapped(mixed, FIRST)
+    chip = lax.ppermute(
+        jnp.concatenate([from_first, from_both]), "req", [(i, i ^ 1) for i in range(count)]
+    )
+    (gate_t,) = fetch_call(in_hbm(gate_weight.T))
+    first, gate_t, up_weight = lax.optimization_barrier((first, gate_t, up_weight))
+    second = swapped(jnp.stack([mixed, first]), SECOND)
+    (up_t,) = fetch_call(in_hbm(up_weight.T))
+    second, up_t = lax.optimization_barrier((second, up_t))
+    stream = project_call(mixed, first, second, out_weight, from_first, from_both, chip, resid.reshape(slots, -1))
+    stream, down_weight = lax.optimization_barrier((stream, down_weight))
+    first = swapped(stream, FIRST)
+    (down,) = fetch_call(in_hbm(down_weight))
+    first, down, from_near, from_far = lax.optimization_barrier((first, down, from_near, from_far))
+    second = swapped(jnp.stack([stream, first]), SECOND)
     kept_states, kept_edges = keep_call(
         owner_row, accepted, near, far, from_near, from_far, states, conv, bias
     )
-    one, two, three, kept_states, kept_edges = lax.optimization_barrier(
-        (one, two, three, kept_states, kept_edges)
-    )
-    own_part, to_one, to_two, to_three = ffn(
-        draft_lengths, stream, one, two, three, ffn_gain[None, :], gate_t, up_t, down
-    )
-    two = swapped(to_two, 2)
-    one = swapped(to_one, 1)
-    three = swapped(to_three, 3)
-    layer_out = (own_part + two.astype(F32) + one.astype(F32) + three.astype(F32)).astype(BF)
+    second, kept_states, kept_edges = lax.optimization_barrier((second, kept_states, kept_edges))
+    own_part, for_second, pair = ffn_call(
+        draft_lengths, stream, first, second, ffn_gain[None, :], gate_t, up_t, down
+    )
+    pair = swapped(pair, FIRST)
+    second = swapped((for_second + pair[1].astype(F32)).astype(BF), SECOND)
+    layer_out = (own_part + pair[0].astype(F32) + second.astype(F32)).astype(BF)
     return (layer_out.reshape(ROWS, DRAFT, -1), kept_states, kept_edges)
 
 

time: 52.1 us -> 61.3 us (1.18); the launches traced: 51.8 us -> 60.4 us
  waiting for transfers between devices: 8.09 us -> 20.3 us
  starting transfers between devices: 25.7 us -> 20.2 us
  Pallas kernels: 16.5 us -> 18.3 us
    ppermute x12 -> x9, waiting for transfers between devices: 8.08 us -> 18.9 us  [the longest x8 18.9 us: swapped(): return lax.ppermute(block, ('grp', 'req'), pairs)]
    ppermute x12 -> x9, starting transfers between devices: 17.2 us -> 11.7 us  [the longest x8 11.7 us: swapped(): return lax.ppermute(block, ('grp', 'req'), pairs)]
    pallas_call x6 -> x9, Pallas kernels: 13.3 us -> 18.3 us  [call(): pl.pallas_call(kernel, name=kernel.__name__, out_shape=out_shape, in_spec...]
    pallas_call x1 -> x0, Pallas kernels: 3.27 us -> none  [ffn(): pl.pallas_call(ffn_kernel, name='ffn', out_shape=(shape((slots, width), F...]
    ppermute x1, waiting for transfers between devices: 0.01 us -> 1.35 us  [shards(): from_far = lax.ppermute(far, 'req', across)]
  transfers between devices with their start and end apart: 14 -> 11, of which waited for: 6 -> 8; matrix products, arithmetic and copies ran while one was open for 0% -> 0% of each run, Pallas kernels for 22% -> 22%
where the time goes in v7:
time: 61.3 us; the launch traced here: 60.4 us
  waiting for transfers between devices  20.3 us (33%)
  starting transfers between devices  20.2 us (33%)
  Pallas kernels  18.3 us (30%)
  other arithmetic  0.8 us (1%)
  between operations  0.77 us (1%)
    ppermute x8, waiting for transfers between devices, swapped(): return lax.ppermute(block, ('grp', 'req'), pairs)  18.9 us
    pallas_call x9, Pallas kernels, call(): pl.pallas_call(kernel, name=kernel.__name__, out_shape=out_shape, in_spec...  18.3 us
    ppermute x8, starting transfers between devices, swapped(): return lax.ppermute(block, ('grp', 'req'), pairs)  11.7 us
    ppermute x1, starting transfers between devices, shards(): from_far = lax.ppermute(far, 'req', across)  8.41 us
    ppermute x1, waiting for transfers between devices, shards(): from_far = lax.ppermute(far, 'req', across)  1.35 us
  transfers between devices with their start and end apart: 11, of which 8 were waited for; matrix products, arithmetic and copies ran while one was open for 0% of the time, Pallas kernels for 22%

profile of v7, /device:TPU:6, one launch (start us, length us, event | category | flops | bytes accessed | tf_op | source)
XLA Modules:
  0.0 60.4 jit_solution(3623098062683929942)
XLA Ops:
  0.6 1.6 %pack.1 = (bf16[4,400,128]{2,1,0:T(8,128)(2,1)S(1)}, bf16[4,400,128]{2,1,0:T(8,128)(2,1)S(1)}, bf16[256,512]{1,0:T(8,128)(2,1)S(1)}, bf16[128,512]{1,0:T(8,128)(2,1)S(1)}) custom-call(f32[8,2,128,128]{3,2,1,0:T(8,128)} %state_ref.3, bf16[8,3,2,384]{3,2,1,0:T(2,128)(2,1)} %edge_ref.1, bf16[8,16,2,384]{3,2,1,0:T(2,128)(2,1)} %draft_ref.1, ...), custom_call_target="tpu_custom_call" | custom-call | flops 1000000 | bytes 3000000 | tf_op jit(solution)/shard_map/pack/pallas_call | solution.py:49
  2.2 0.1 collective-permute-start
  2.3 8.4 %collective-permute-start.1 = (bf16[4,400,128]{2,1,0:T(8,128)(2,1)S(1)}, bf16[4,400,128]{2,1,0:T(8,128)(2,1)S(1)}, u32[]{:S(2)}, u32[]{:S(2)}) collective-permute-start(bf16[4,400,128]{2,1,0:T(8,128)(2,1)S(1)} %get-tuple-element.38.far_ref), channel_id=1, source_target_pairs={{0,63},{1,2},{2,1},{3,4},{4,3},{5,6},{6,5},{7,8},{8,7},{9,10},{10,... | collective-permute-start | bytes 1228808 | tf_op jit(solution)/shard_map/ppermute | solution.py:671
  10.8 0.8 %collective-permute-start.2 = (bf16[256,512]{1,0:T(8,128)(2,1)S(1)}, bf16[256,512]{1,0:T(8,128)(2,1)S(1)}, u32[]{:S(2)}, u32[]{:S(2)}) collective-permute-start(bf16[256,512]{1,0:T(8,128)(2,1)S(1)} %get-tuple-element.45), channel_id=1, source_target_pairs={{0,64},{1,193},{2,66},{3,195},{4,68},{5,197},{6,70},{7,199},{8,72}... | collective-permute-start | bytes 786440 | tf_op jit(solution)/shard_map/ppermute | solution.py:640
  11.6 1.1 %collective-permute-start.3 = (bf16[128,512]{1,0:T(8,128)(2,1)S(1)}, bf16[128,512]{1,0:T(8,128)(2,1)S(1)}, u32[]{:S(2)}, u32[]{:S(2)}) collective-permute-start(bf16[128,512]{1,0:T(8,128)(2,1)S(1)} %get-tuple-element.46), channel_id=1, source_target_pairs={{0,128},{1,129},{2,130},{3,131},{4,132},{5,133},{6,134},{7,135},{8... | collective-permute-start | bytes 393224 | tf_op jit(solution)/shard_map/ppermute | solution.py:640
  12.7 0.0 collective-permute-done.from_near_ref
  12.7 2.3 %mix_near.1 = (bf16[4,16,256]{2,1,0:T(8,128)(2,1)S(1)}, f32[4,2,16,128]{3,2,1,0:T(8,128)S(1)}, f32[4,2,16,128]{3,2,1,0:T(8,128)S(1)}, f32[4,2,16,128]{3,2,1,0:T(...) custom-call(s32[512]{0:T(512)} %owner_ref.5, ...), custom_call_target="tpu_custom_call" | custom-call | flops 15000000 | bytes 3000000 | tf_op jit(solution)/shard_map/mix_near/pallas_call | solution.py:49
  15.0 1.4 %collective-permute-done.1.from_far_ref = bf16[4,400,128]{2,1,0:T(8,128)(2,1)S(1)} collective-permute-done((bf16[4,400,128]{2,1,0:T(8,128)(2,1)S(1)}, bf16[4,400,128]{2,1,0:T(8,128)(2,1)S(1)}, u32[]{:S(2)}, u32[]{:S(2)}) %collective-permute-start.1) | collective-permute-done | bytes 409632 | tf_op jit(solution)/shard_map/ppermute | solution.py:671
  16.4 1.5 %mix_far.1 = bf16[8,16,256]{2,1,0:T(8,128)(2,1)S(1)} custom-call(s32[512]{0:T(512)} %owner_ref.5, bf16[4,16,256]{2,1,0:T(8,128)(2,1)S(1)} %get-tuple-element.39.near_mixed_ref, bf16[4,400,128]{2,1,0:T(8,128)(2,1)S(1)} %get-tuple-element.38.far_ref, bf16[4,400,128]{2,1,0:T(8,128)(2,1)S(1)} %collective-permute-done.1.from_far_ref, ...), custom_call_target="tpu_custom_call" | custom-call | flops 10000000 | bytes 2000000 | tf_op jit(solution)/shard_map/mix_far/pallas_call | solution.py:49
  17.9 0.6 collective-permute-done.3.from_both_ref
  18.4 0.0 collective-permute-done.2.from_first_ref
  18.5 0.1 collective-permute-start.6
  18.6 1.0 %collective-permute-start.4 = (bf16[128,256]{1,0:T(8,128)(2,1)S(1)}, bf16[128,256]{1,0:T(8,128)(2,1)S(1)}, u32[]{:S(2)}, u32[]{:S(2)}) collective-permute-start(bf16[128,256]{1,0:T(8,128)(2,1)S(1)} %bitcast.21), channel_id=1, source_target_pairs={{0,64},{1,193},{2,66},{3,195},{4,68},{5,197},{6,70},{7,199},{8,72}... | collective-permute-start | bytes 196616 | tf_op jit(solution)/shard_map/ppermute | solution.py:640
  19.6 1.8 %fetch.3.gate_ref = bf16[704,2048]{1,0:T(8,128)(2,1)S(1)} custom-call(bf16[704,2048]{1,0:T(8,128)(2,1)} %bitcast.28), custom_call_target="tpu_custom_call" | custom-call | bytes 17000000 | tf_op jit(solution)/shard_map/fetch/pallas_call | solution.py:49
  21.4 1.5 %collective-permute-done.4.first_ref = bf16[128,256]{1,0:T(8,128)(2,1)S(1)} collective-permute-done((bf16[128,256]{1,0:T(8,128)(2,1)S(1)}, bf16[128,256]{1,0:T(8,128)(2,1)S(1)}, u32[]{:S(2)}, u32[]{:S(2)}) %collective-permute-start.4) | collective-permute-done | bytes 65568 | tf_op jit(solution)/shard_map/ppermute | solution.py:640
  22.9 2.8 %collective-permute-start.5 = (bf16[2,128,256]{2,1,0:T(8,128)(2,1)S(1)}, bf16[2,128,256]{2,1,0:T(8,128)(2,1)S(1)}, u32[]{:S(2)}, u32[]{:S(2)}) collective-permute-start(bf16[2,128,256]{2,1,0:T(8,128)(2,1)S(1)} %pad_maximum_fusion.2), channel_id=1, source_target_pairs={{0,192},{1,65},{2,194},{3,67},{4,196},{5,69},{6,198},{7,71},{8,200... | collective-permute-start | bytes 393224 | tf_op jit(solution)/shard_map/ppermute | solution.py:640
  25.8 0.0 copy-start
  25.8 0.0 copy-start.1
  25.8 1.9 %fetch.4.up_ref = bf16[704,2048]{1,0:T(8,128)(2,1)S(1)} custom-call(bf16[704,2048]{1,0:T(8,128)(2,1)} %bitcast.29), custom_call_target="tpu_custom_call" | custom-call | bytes 17000000 | tf_op jit(solution)/shard_map/fetch/pallas_call | solution.py:49
  27.7 1.5 %collective-permute-done.5.second_ref = bf16[2,128,256]{2,1,0:T(8,128)(2,1)S(1)} collective-permute-done((bf16[2,128,256]{2,1,0:T(8,128)(2,1)S(1)}, bf16[2,128,256]{2,1,0:T(8,128)(2,1)S(1)}, u32[]{:S(2)}, u32[]{:S(2)}) %collective-permute-start.5) | collective-permute-done | bytes 131104 | tf_op jit(solution)/shard_map/ppermute | solution.py:640
  29.2 0.0 collective-permute-done.6.chip_ref
  29.2 0.0 copy-done
  29.2 0.0 copy-done.1
  29.2 0.3 project.1.own_ref
  29.6 0.1 collective-permute-start.7
  29.7 1.8 %fetch.5.down_ref = bf16[704,2048]{1,0:T(8,128)(2,1)S(1)} custom-call(bf16[704,2048]{1,0:T(8,128)(2,1)} %refs_0_), custom_call_target="tpu_custom_call" | custom-call | bytes 17000000 | tf_op jit(solution)/shard_map/fetch/pallas_call | solution.py:49
  31.5 0.0 copy-start.2
  31.5 3.1 %collective-permute-done.7.first_ref = bf16[128,512]{1,0:T(8,128)(2,1)S(1)} collective-permute-done((bf16[128,512]{1,0:T(8,128)(2,1)S(1)}, bf16[128,512]{1,0:T(8,128)(2,1)S(1)}, u32[]{:S(2)}, u32[]{:S(2)}) %collective-permute-start.7) | collective-permute-done | bytes 131104 | tf_op jit(solution)/shard_map/ppermute | solution.py:640
  34.7 2.8 %collective-permute-start.8 = (bf16[2,128,512]{2,1,0:T(8,128)(2,1)S(1)}, bf16[2,128,512]{2,1,0:T(8,128)(2,1)S(1)}, u32[]{:S(2)}, u32[]{:S(2)}) collective-permute-start(bf16[2,128,512]{2,1,0:T(8,128)(2,1)S(1)} %pad_maximum_fusion.1), channel_id=1, source_target_pairs={{0,192},{1,65},{2,194},{3,67},{4,196},{5,69},{6,198},{7,71},{8,200... | collective-permute-start | bytes 786440 | tf_op jit(solution)/shard_map/ppermute | solution.py:640
  37.5 3.7 %keep.1 = (f32[8,2,128,128]{3,2,1,0:T(8,128)}, bf16[8,3,2,384]{3,2,1,0:T(2,128)(2,1)}) custom-call(s32[512]{0:T(512)} %owner_ref.5, s32[512]{0:T(512)} %accept_ref.1, bf16[4,400,128]{2,1,0:T(8,128)(2,1)S(1)} %get-tuple-element.37.near_ref, bf16[4,400,128]{2,1,0:T(8,128)(2,1)S(1)} %get-tuple-element.38.far_ref, ...), custom_call_target="tpu_custom_call" | custom-call | flops 20000000 | bytes 3000000 | tf_op jit(solution)/shard_map/keep/pallas_call | solution.py:49
  41.3 1.1 %collective-permute-done.8.second_ref = bf16[2,128,512]{2,1,0:T(8,128)(2,1)S(1)} collective-permute-done((bf16[2,128,512]{2,1,0:T(8,128)(2,1)S(1)}, bf16[2,128,512]{2,1,0:T(8,128)(2,1)S(1)}, u32[]{:S(2)}, u32[]{:S(2)}) %collective-permute-start.8) | collective-permute-done | bytes 262176 | tf_op jit(solution)/shard_map/ppermute | solution.py:640
  42.3 0.0 copy-done.2
  42.3 3.2 %ffn.1 = (f32[128,512]{1,0:T(8,128)S(1)}, f32[128,512]{1,0:T(8,128)S(1)}, bf16[2,128,512]{2,1,0:T(8,128)(2,1)S(1)}) custom-call(s32[512]{0:T(512)} %length_ref.1, bf16[128,512]{1,0:T(8,128)(2,1)S(1)} %project.1.own_ref, bf16[128,512]{1,0:T(8,128)(2,1)S(1)} %collective-permute-done.7.first_ref, bf16[2,128,512]{2,1,0:T(8,128)(2,1)S(1)} %collective-permute-done.8.second_ref, ...), custom_call_target="tpu_custom_call" | custom-call | flops 1100000000 | bytes 9000000 | tf_op jit(solution)/shard_map/ffn/pallas_call | solution.py:49
  45.6 0.1 collective-permute-start.9
  45.7 7.7 %collective-permute-done.9 = bf16[2,128,512]{2,1,0:T(8,128)(2,1)S(1)} collective-permute-done((bf16[2,128,512]{2,1,0:T(8,128)(2,1)S(1)}, bf16[2,128,512]{2,1,0:T(8,128)(2,1)S(1)}, u32[]{:S(2)}, u32[]{:S(2)}) %collective-permute-start.9) | collective-permute-done | bytes 262176 | tf_op jit(solution)/shard_map/ppermute | solution.py:640
  53.4 2.9 %collective-permute-start.10 = (bf16[128,512]{1,0:T(8,128)(2,1)S(1)}, bf16[128,512]{1,0:T(8,128)(2,1)S(1)}, u32[]{:S(2)}, u32[]{:S(2)}) collective-permute-start(bf16[128,512]{1,0:T(8,128)(2,1)S(1)} %fusion), channel_id=1, source_target_pairs={{0,192},{1,65},{2,194},{3,67},{4,196},{5,69},{6,198},{7,71},{8,200... | collective-permute-start | bytes 393224 | tf_op jit(solution)/shard_map/ppermute | solution.py:640
  56.3 3.4 %collective-permute-done.10 = bf16[128,512]{1,0:T(8,128)(2,1)S(1)} collective-permute-done((bf16[128,512]{1,0:T(8,128)(2,1)S(1)}, bf16[128,512]{1,0:T(8,128)(2,1)S(1)}, u32[]{:S(2)}, u32[]{:S(2)}) %collective-permute-start.10) | collective-permute-done | bytes 131104 | tf_op jit(solution)/shard_map/ppermute | solution.py:640
  59.7 0.7 %fusion.2 = bf16[128,512]{1,0:T(8,128)(2,1)} fusion(f32[128,512]{1,0:T(8,128)S(1)} %get-tuple-element.66, bf16[128,512]{1,0:T(8,128)(2,1)S(1)} %collective-permute-done.10, bf16[2,128,512]{2,1,0:T(8,128)(2,1)S(1)} %collective-permute-done.9), kind=kLoop, calls=%fused_computation.6 | loop fusion | flops 327680 | bytes 655360 | tf_op jit(solution)/shard_map/convert_element_type | solution.py:709
  (4 shorter events, 0.1 us)
Async XLA Ops:
  2.2 10.5 %collective-permute-start = (bf16[4,400,128]{2,1,0:T(8,128)(2,1)S(1)}, bf16[4,400,128]{2,1,0:T(8,128)(2,1)S(1)}, u32[]{:S(2)}, u32[]{:S(2)}) collective-permute-start(bf16[4,400,128]{2,1,0:T(8,128)(2,1)S(1)} %get-tuple-element.37.near_ref), channel_id=1, source_target_pairs={{0,1},{1,0},{2,3},{3,2},{4,5},{5,4},{6,7},{7,6},{8,9},{9,8},{10,11... | collective-permute-start | bytes 1228808 | tf_op jit(solution)/shard_map/ppermute | solution.py:672
  2.3 14.0 %collective-permute-start.1 = (bf16[4,400,128]{2,1,0:T(8,128)(2,1)S(1)}, bf16[4,400,128]{2,1,0:T(8,128)(2,1)S(1)}, u32[]{:S(2)}, u32[]{:S(2)}) collective-permute-start(bf16[4,400,128]{2,1,0:T(8,128)(2,1)S(1)} %get-tuple-element.38.far_ref), channel_id=1, source_target_pairs={{0,63},{1,2},{2,1},{3,4},{4,3},{5,6},{6,5},{7,8},{8,7},{9,10},{10,... | collective-permute-start | bytes 1228808 | tf_op jit(solution)/shard_map/ppermute | solution.py:671
  10.8 7.7 %collective-permute-start.2 = (bf16[256,512]{1,0:T(8,128)(2,1)S(1)}, bf16[256,512]{1,0:T(8,128)(2,1)S(1)}, u32[]{:S(2)}, u32[]{:S(2)}) collective-permute-start(bf16[256,512]{1,0:T(8,128)(2,1)S(1)} %get-tuple-element.45), channel_id=1, source_target_pairs={{0,64},{1,193},{2,66},{3,195},{4,68},{5,197},{6,70},{7,199},{8,72}... | collective-permute-start | bytes 786440 | tf_op jit(solution)/shard_map/ppermute | solution.py:640
  11.6 6.9 %collective-permute-start.3 = (bf16[128,512]{1,0:T(8,128)(2,1)S(1)}, bf16[128,512]{1,0:T(8,128)(2,1)S(1)}, u32[]{:S(2)}, u32[]{:S(2)}) collective-permute-start(bf16[128,512]{1,0:T(8,128)(2,1)S(1)} %get-tuple-element.46), channel_id=1, source_target_pairs={{0,128},{1,129},{2,130},{3,131},{4,132},{5,133},{6,134},{7,135},{8... | collective-permute-start | bytes 393224 | tf_op jit(solution)/shard_map/ppermute | solution.py:640
  18.5 10.7 %collective-permute-start.6 = (bf16[384,512]{1,0:T(8,128)(2,1)S(1)}, bf16[384,512]{1,0:T(8,128)(2,1)S(1)}, u32[]{:S(2)}, u32[]{:S(2)}) collective-permute-start(bf16[384,512]{1,0:T(8,128)(2,1)S(1)} %pad_maximum_fusion), channel_id=1, source_target_pairs={{0,1},{1,0},{2,3},{3,2},{4,5},{5,4},{6,7},{7,6},{8,9},{9,8},{10,11... | collective-permute-start | bytes 1179656 | tf_op jit(solution)/shard_map/ppermute | solution.py:686
  18.6 4.4 %collective-permute-start.4 = (bf16[128,256]{1,0:T(8,128)(2,1)S(1)}, bf16[128,256]{1,0:T(8,128)(2,1)S(1)}, u32[]{:S(2)}, u32[]{:S(2)}) collective-permute-start(bf16[128,256]{1,0:T(8,128)(2,1)S(1)} %bitcast.21), channel_id=1, source_target_pairs={{0,64},{1,193},{2,66},{3,195},{4,68},{5,197},{6,70},{7,199},{8,72}... | collective-permute-start | bytes 196616 | tf_op jit(solution)/shard_map/ppermute | solution.py:640
  22.9 6.3 %collective-permute-start.5 = (bf16[2,128,256]{2,1,0:T(8,128)(2,1)S(1)}, bf16[2,128,256]{2,1,0:T(8,128)(2,1)S(1)}, u32[]{:S(2)}, u32[]{:S(2)}) collective-permute-start(bf16[2,128,256]{2,1,0:T(8,128)(2,1)S(1)} %pad_maximum_fusion.2), channel_id=1, source_target_pairs={{0,192},{1,65},{2,194},{3,67},{4,196},{5,69},{6,198},{7,71},{8,200... | collective-permute-start | bytes 393224 | tf_op jit(solution)/shard_map/ppermute | solution.py:640
  25.8 3.4 %copy-start = (bf16[256,2048]{1,0:T(8,128)(2,1)S(1)}, bf16[256,2048]{1,0:T(8,128)(2,1)}, u32[]{:S(2)}) copy-start(bf16[256,2048]{1,0:T(8,128)(2,1)} %weight_ref.3) | copy-start | bytes 3145732
  25.8 3.4 %copy-start.1 = (bf16[8,16,2048]{2,1,0:T(8,128)(2,1)S(1)}, bf16[8,16,2048]{2,1,0:T(8,128)(2,1)}, u32[]{:S(2)}) copy-start(bf16[8,16,2048]{2,1,0:T(8,128)(2,1)} %param.20) | copy-start | bytes 1572868
  29.6 5.1 %collective-permute-start.7 = (bf16[128,512]{1,0:T(8,128)(2,1)S(1)}, bf16[128,512]{1,0:T(8,128)(2,1)S(1)}, u32[]{:S(2)}, u32[]{:S(2)}) collective-permute-start(bf16[128,512]{1,0:T(8,128)(2,1)S(1)} %project.1.own_ref), channel_id=1, source_target_pairs={{0,64},{1,193},{2,66},{3,195},{4,68},{5,197},{6,70},{7,199},{8,72}... | collective-permute-start | bytes 393224 | tf_op jit(solution)/shard_map/ppermute | solution.py:640
  31.5 10.8 %copy-start.2 = (f32[2048]{0:T(1024)S(1)}, f32[2048]{0:T(1024)}, u32[]{:S(2)}) copy-start(f32[2048]{0:T(1024)} %param.21) | copy-start | bytes 24580
  34.7 7.7 %collective-permute-start.8 = (bf16[2,128,512]{2,1,0:T(8,128)(2,1)S(1)}, bf16[2,128,512]{2,1,0:T(8,128)(2,1)S(1)}, u32[]{:S(2)}, u32[]{:S(2)}) collective-permute-start(bf16[2,128,512]{2,1,0:T(8,128)(2,1)S(1)} %pad_maximum_fusion.1), channel_id=1, source_target_pairs={{0,192},{1,65},{2,194},{3,67},{4,196},{5,69},{6,198},{7,71},{8,200... | collective-permute-start | bytes 786440 | tf_op jit(solution)/shard_map/ppermute | solution.py:640
  45.6 7.8 %collective-permute-start.9 = (bf16[2,128,512]{2,1,0:T(8,128)(2,1)S(1)}, bf16[2,128,512]{2,1,0:T(8,128)(2,1)S(1)}, u32[]{:S(2)}, u32[]{:S(2)}) collective-permute-start(bf16[2,128,512]{2,1,0:T(8,128)(2,1)S(1)} %get-tuple-element.67), channel_id=1, source_target_pairs={{0,64},{1,193},{2,66},{3,195},{4,68},{5,197},{6,70},{7,199},{8,72}... | collective-permute-start | bytes 786440 | tf_op jit(solution)/shard_map/ppermute | solution.py:640
  53.4 6.3 %collective-permute-start.10 = (bf16[128,512]{1,0:T(8,128)(2,1)S(1)}, bf16[128,512]{1,0:T(8,128)(2,1)S(1)}, u32[]{:S(2)}, u32[]{:S(2)}) collective-permute-start(bf16[128,512]{1,0:T(8,128)(2,1)S(1)} %fusion), channel_id=1, source_target_pairs={{0,192},{1,65},{2,194},{3,67},{4,196},{5,69},{6,198},{7,71},{8,200... | collective-permute-start | bytes 393224 | tf_op jit(solution)/shard_map/ppermute | solution.py:640

commit v8 on v6

--- a/solution.py
+++ b/solution.py
@@ -64,15 +64,15 @@
 
 
 def pack(
-    state_ref, edge_ref, draft_ref, weight_ref, far_ref, near_ref, one_ref, two_ref, three_ref,
+    state_ref, edge_ref, draft_ref, weight_ref, far_ref, near_ref, one_ref, three_ref,
     states, edges, drafts, sems,
 ):
     width = one_ref.shape[1]
     cuts = [
         pltpu.make_async_copy(
-            weight_ref.at[:, columns_of(step, width)], out_ref, sems.at[ROWS + 1 + step]
+            weight_ref.at[:, columns_of(step, width)], out_ref, sems.at[ROWS + 2 + i]
         )
-        for step, out_ref in ((1, one_ref), (2, two_ref), (3, three_ref))
+        for i, (step, out_ref) in enumerate(((1, one_ref), (3, three_ref)))
     ]
     copies = [
         pltpu.make_async_copy(state_ref.at[row], states.at[row], sems.at[row])
@@ -118,12 +118,12 @@
     half = jax.ShapeDtypeStruct((HALF, PACKED, DK), BF)
     cut = jax.ShapeDtypeStruct((weight.shape[0], weight.shape[1] // 4), BF)
     return call(
-        pack, (half, half, cut, cut, cut), [HB] * 4,
+        pack, (half, half, cut, cut), [HB] * 4,
         [
             pltpu.VMEM(states.shape, F32),
             pltpu.VMEM(edges.shape, BF),
             pltpu.VMEM(drafts.shape, BF),
-            pltpu.SemaphoreType.DMA((ROWS + 5,)),
+            pltpu.SemaphoreType.DMA((ROWS + 4,)),
         ],
         1_000_000, 3_000_000, states, edges, drafts, weight,
     )
@@ -305,7 +305,8 @@
 
 def mix_far(
     owner_ref, near_mixed_ref, far_ref, from_far_ref, query_ref, forget_ref, value_ref,
-    conv_ref, gain_ref, mixed_ref, edges, states, query_scr, forget_scr, value_scr,
+    conv_ref, gain_ref, weight_ref, mixed_ref, part_ref,
+    edges, states, query_scr, forget_scr, value_scr,
 ):
     parity = lax.axis_index("req") % 2
     for slot in range(HALF):
@@ -318,13 +319,22 @@
         1, owner_ref, far_ref, from_far_ref, query_ref, forget_ref, value_ref, conv_ref,
         gain_ref, edges, states, query_scr, forget_scr, value_scr, store,
     )
-
-
-def mix_far_call(owner, near_mixed, far, from_far, queries, forget, values, conv, gain):
+    rows = mixed_ref[...].reshape(ROWS * DRAFT, 2 * DK)
+    block = weight_ref[:, columns_of(2, part_ref.shape[1])]
+    part_ref[...] = jnp.dot(rows, block, preferred_element_type=F32).astype(BF)
+
+
+def mix_far_call(owner, near_mixed, far, from_far, queries, forget, values, conv, gain, weight):
+    shape = jax.ShapeDtypeStruct
     return call(
-        mix_far, jax.ShapeDtypeStruct((ROWS, DRAFT, 2 * DK), BF), [SM] + [VM] * 8, MIX_SCRATCH,
-        10_000_000, 2_000_000,
-        owner, near_mixed, far, from_far, queries, forget, values, conv, gain,
+        mix_far,
+        (
+            shape((ROWS, DRAFT, 2 * DK), BF),
+            shape((ROWS * DRAFT, weight.shape[1] // 4), BF),
+        ),
+        [SM] + [VM] * 9, MIX_SCRATCH,
+        50_000_000, 2_000_000,
+        owner, near_mixed, far, from_far, queries, forget, values, conv, gain, weight,
     )
 
 
@@ -533,24 +543,23 @@
 
 
 def project(
-    own_ref, one_ref, two_ref, three_ref, weight_ref, from_one_ref, from_two_ref, from_three_ref,
+    own_ref, one_ref, three_ref, weight_ref, from_one_ref, from_three_ref, part_ref,
     resid_ref, stream_ref,
 ):
     width = stream_ref.shape[1]
     columns = columns_of(0, width)
     total = jnp.dot(own_ref[...], weight_ref[:, columns], preferred_element_type=F32)
-    for rows_ref, part_ref in (
-        (one_ref, from_one_ref), (two_ref, from_two_ref), (three_ref, from_three_ref)
-    ):
-        total = total + jnp.dot(rows_ref[...], part_ref[...], preferred_element_type=F32)
+    total = total + jnp.dot(one_ref[...], from_one_ref[...], preferred_element_type=F32)
+    total = total + jnp.dot(three_ref[...], from_three_ref[...], preferred_element_type=F32)
+    total = total + part_ref[...].astype(F32)
     stream_ref[...] = (resid_ref[:, columns].astype(F32) + total).astype(BF)
 
 
-def project_call(mixed, others, weight, parts, resid):
+def project_call(mixed, one, three, weight, parts, part, resid):
     slots, model = resid.shape
     return call(
-        project, jax.ShapeDtypeStruct((slots, model // 4), BF), [VM] * 9, [],
-        140_000_000, 3_000_000, mixed, *others, weight, *parts, resid,
+        project, jax.ShapeDtypeStruct((slots, model // 4), BF), [VM] * 8, [],
+        100_000_000, 3_000_000, mixed, one, three, weight, *parts, part, resid,
     )
 
 
@@ -643,23 +652,28 @@
     across = [(i, (i + (1 if i % 2 else -1)) % count) for i in range(count)]
     from_far = lax.ppermute(far, "req", across)
     from_near = lax.ppermute(near, "req", [(i, i ^ 1) for i in range(count)])
-    parts = [swapped(cut, step) for step, cut in ((1, cuts[0]), (2, cuts[1]), (3, cuts[2]))]
+    parts = [swapped(cut, step) for step, cut in ((1, cuts[0]), (3, cuts[1]))]
     near_mixed, queries, forget, values, conv, bias, gain = mix_near_call(
         owner_row, near, far, from_near,
         in_hbm(conv_weight), in_hbm(forget_bias), in_hbm(norm_gain),
     )
-    mixed = mix_far_call(
-        owner_row, near_mixed, far, from_far, queries, forget, values, conv, gain
-    ).reshape(slots, -1)
-    mixed, parts[0], gate_weight, up_weight, down_weight = lax.optimization_barrier(
-        (mixed, parts[0], gate_weight, up_weight, down_weight)
-    )
-    others = [swapped(mixed, step) for step in (1, 2, 3)]
+    mixed, part = mix_far_call(
+        owner_row, near_mixed, far, from_far, queries, forget, values, conv, gain, out_weight
+    )
+    mixed = mixed.reshape(slots, -1)
+    mixed, part, gate_weight, up_weight, down_weight = lax.optimization_barrier(
+        (mixed, part, gate_weight, up_weight, down_weight)
+    )
+    part = swapped(part, 2)
+    one = swapped(mixed, 1)
+    three = swapped(mixed, 3)
     gate_t, up_t, down = fetch_call(
         in_hbm(gate_weight.T), in_hbm(up_weight.T), in_hbm(down_weight)
     )
-    *others, gate_t, up_t, down = lax.optimization_barrier((*others, gate_t, up_t, down))
-    stream = project_call(mixed, others, out_weight, parts, resid.reshape(slots, -1))
+    part, one, three, gate_t, up_t, down = lax.optimization_barrier(
+        (part, one, three, gate_t, up_t, down)
+    )
+    stream = project_call(mixed, one, three, out_weight, parts, part, resid.reshape(slots, -1))
     stream, from_near, from_far = lax.optimization_barrier((stream, from_near, from_far))
     two = swapped(stream, 2)
     one = swapped(stream, 1)

time: 52.1 us -> 51.5 us (0.988)
  starting transfers between devices: 25.7 us -> 22.5 us
  waiting for transfers between devices: 8.09 us -> 10.6 us
    ppermute x12 -> x11, starting transfers between devices: 17.2 us -> 14 us  [swapped(): return lax.ppermute(block, 'grp', [(i, i ^ step) for i in range(4)])]
    ppermute x1, waiting for transfers between devices: 0.01 us -> 1.33 us  [shards(): from_far = lax.ppermute(far, 'req', across)]
    ppermute x12 -> x11, waiting for transfers between devices: 8.08 us -> 9.29 us  [swapped(): return lax.ppermute(block, 'grp', [(i, i ^ step) for i in range(4)])]
  transfers between devices with their start and end apart: 14 -> 13, of which waited for: 6 -> 7; matrix products, arithmetic and copies ran while one was open for 0% -> 0% of each run, Pallas kernels for 22% -> 22%
where the time goes in v8:
time: 51.5 us; the launch traced here: 51.2 us
  starting transfers between devices  22.5 us (44%)
  Pallas kernels  16.6 us (32%)
  waiting for transfers between devices  10.6 us (21%)
  between operations  0.74 us (1%)
  other arithmetic  0.73 us (1%)
    ppermute x11, starting transfers between devices, swapped(): return lax.ppermute(block, 'grp', [(i, i ^ step) for i in range(4)])  14 us
    pallas_call x6, Pallas kernels, call(): pl.pallas_call(kernel, name=kernel.__name__, out_shape=out_shape, in_spec...  13.3 us
    ppermute x11, waiting for transfers between devices, swapped(): return lax.ppermute(block, 'grp', [(i, i ^ step) for i in range(4)])  9.29 us
    ppermute x1, starting transfers between devices, shards(): from_far = lax.ppermute(far, 'req', across)  8.41 us
    pallas_call x1, Pallas kernels, ffn(): pl.pallas_call(ffn_kernel, name='ffn', out_shape=(shape((slots, width), F...  3.27 us
    ppermute x1, waiting for transfers between devices, shards(): from_far = lax.ppermute(far, 'req', across)  1.33 us
  transfers between devices with their start and end apart: 13, of which 7 were waited for; matrix products, arithmetic and copies ran while one was open for 0% of the time, Pallas kernels for 22%

profile of v8, /device:TPU:6, one launch (start us, length us, event | category | flops | bytes accessed | tf_op | source)
XLA Modules:
  0.0 51.2 jit_solution(18430340947434208208)
XLA Ops:
  0.6 0.0 copy-start
  0.6 1.7 %pack.1 = (bf16[4,400,128]{2,1,0:T(8,128)(2,1)S(1)}, bf16[4,400,128]{2,1,0:T(8,128)(2,1)S(1)}, bf16[256,512]{1,0:T(8,128)(2,1)S(1)}, bf16[256,512]{1,0:T(8,128)(2,1)S(1)}) custom-call(f32[8,2,128,128]{3,2,1,0:T(8,128)} %state_ref.3, bf16[8,3,2,384]{3,2,1,0:T(2,128)(2,1)} %edge_ref.1, bf16[8,16,2,384]{3,2,1,0:T(2,128)(2,1)} %draft_ref.1, ...), custom_call_target="tpu_custom_call" | custom-call | flops 1000000 | bytes 3000000 | tf_op jit(solution)/shard_map/pack/pallas_call | solution.py:49
  2.4 0.1 collective-permute-start
  2.5 8.4 %collective-permute-start.1 = (bf16[4,400,128]{2,1,0:T(8,128)(2,1)S(1)}, bf16[4,400,128]{2,1,0:T(8,128)(2,1)S(1)}, u32[]{:S(2)}, u32[]{:S(2)}) collective-permute-start(bf16[4,400,128]{2,1,0:T(8,128)(2,1)S(1)} %get-tuple-element.45.far_ref), channel_id=1, source_target_pairs={{0,63},{1,2},{2,1},{3,4},{4,3},{5,6},{6,5},{7,8},{8,7},{9,10},{10,... | collective-permute-start | bytes 1228808 | tf_op jit(solution)/shard_map/ppermute | solution.py:653
  10.9 0.8 %collective-permute-start.5 = (bf16[256,512]{1,0:T(8,128)(2,1)S(1)}, bf16[256,512]{1,0:T(8,128)(2,1)S(1)}, u32[]{:S(2)}, u32[]{:S(2)}) collective-permute-start(bf16[256,512]{1,0:T(8,128)(2,1)S(1)} %get-tuple-element.64), channel_id=1, source_target_pairs={{0,64},{64,0},{128,192},{192,128},{1,65},{65,1},{129,193},{193,129... | collective-permute-start | bytes 786440 | tf_op jit(solution)/shard_map/ppermute | solution.py:625
  11.7 1.1 %collective-permute-start.6 = (bf16[256,512]{1,0:T(8,128)(2,1)S(1)}, bf16[256,512]{1,0:T(8,128)(2,1)S(1)}, u32[]{:S(2)}, u32[]{:S(2)}) collective-permute-start(bf16[256,512]{1,0:T(8,128)(2,1)S(1)} %get-tuple-element.65), channel_id=1, source_target_pairs={{0,192},{64,128},{128,64},{192,0},{1,193},{65,129},{129,65},{193,1... | collective-permute-start | bytes 786440 | tf_op jit(solution)/shard_map/ppermute | solution.py:625
  12.8 0.0 collective-permute-done.from_near_ref
  12.8 2.3 %mix_near.1 = (bf16[4,16,256]{2,1,0:T(8,128)(2,1)S(1)}, f32[4,2,16,128]{3,2,1,0:T(8,128)S(1)}, f32[4,2,16,128]{3,2,1,0:T(8,128)S(1)}, f32[4,2,16,128]{3,2,1,0:T(...) custom-call(s32[512]{0:T(512)} %owner_ref.5, ...), custom_call_target="tpu_custom_call" | custom-call | flops 15000000 | bytes 3000000 | tf_op jit(solution)/shard_map/mix_near/pallas_call | solution.py:49
  15.2 1.3 %collective-permute-done.1.from_far_ref = bf16[4,400,128]{2,1,0:T(8,128)(2,1)S(1)} collective-permute-done((bf16[4,400,128]{2,1,0:T(8,128)(2,1)S(1)}, bf16[4,400,128]{2,1,0:T(8,128)(2,1)S(1)}, u32[]{:S(2)}, u32[]{:S(2)}) %collective-permute-start.1) | collective-permute-done | bytes 409632 | tf_op jit(solution)/shard_map/ppermute | solution.py:653
  16.5 0.0 copy-done
  16.5 1.7 %mix_far.1 = (bf16[8,16,256]{2,1,0:T(8,128)(2,1)S(1)}, bf16[128,512]{1,0:T(8,128)(2,1)S(1)}) custom-call(s32[512]{0:T(512)} %owner_ref.5, bf16[4,16,256]{2,1,0:T(8,128)(2,1)S(1)} %get-tuple-element.46.near_mixed_ref, bf16[4,400,128]{2,1,0:T(8,128)(2,1)S(1)} %get-tuple-element.45.far_ref, bf16[4,400,128]{2,1,0:T(8,128)(2,1)S(1)} %collective-permute-done.1.from_far_ref, ...), custom_call_target="tpu_custom_call" | custom-call | flops 50000000 | bytes 2000000 | tf_op jit(solution)/shard_map/mix_far/pallas_call | solution.py:49
  18.2 1.5 %collective-permute-start.2 = (bf16[128,512]{1,0:T(8,128)(2,1)S(1)}, bf16[128,512]{1,0:T(8,128)(2,1)S(1)}, u32[]{:S(2)}, u32[]{:S(2)}) collective-permute-start(bf16[128,512]{1,0:T(8,128)(2,1)S(1)} %get-tuple-element.55), channel_id=1, source_target_pairs={{0,128},{64,192},{128,0},{192,64},{1,129},{65,193},{129,1},{193,65... | collective-permute-start | bytes 393224 | tf_op jit(solution)/shard_map/ppermute | solution.py:625
  19.7 2.1 %collective-permute-start.4 = (bf16[128,256]{1,0:T(8,128)(2,1)S(1)}, bf16[128,256]{1,0:T(8,128)(2,1)S(1)}, u32[]{:S(2)}, u32[]{:S(2)}) collective-permute-start(bf16[128,256]{1,0:T(8,128)(2,1)S(1)} %bitcast.7), channel_id=1, source_target_pairs={{0,192},{64,128},{128,64},{192,0},{1,193},{65,129},{129,65},{193,1... | collective-permute-start | bytes 196616 | tf_op jit(solution)/shard_map/ppermute | solution.py:625
  21.8 0.0 collective-permute-start.3
  21.8 0.0 copy-start.1
  21.8 3.6 %fetch.1 = (bf16[704,2048]{1,0:T(8,128)(2,1)S(1)}, bf16[704,2048]{1,0:T(8,128)(2,1)S(1)}, bf16[704,2048]{1,0:T(8,128)(2,1)S(1)}) custom-call(bf16[704,2048]{1,0:T(8,128)(2,1)} %bitcast.11, bf16[704,2048]{1,0:T(8,128)(2,1)} %bitcast.12, bf16[704,2048]{1,0:T(8,128)(2,1)} %refs_2_), custom_call_target="tpu_custom_call" | custom-call | bytes 17000000 | tf_op jit(solution)/shard_map/fetch/pallas_call | solution.py:49
  25.4 0.0 copy-start.2
  25.4 0.9 %collective-permute-done.4.three_ref = bf16[128,256]{1,0:T(8,128)(2,1)S(1)} collective-permute-done((bf16[128,256]{1,0:T(8,128)(2,1)S(1)}, bf16[128,256]{1,0:T(8,128)(2,1)S(1)}, u32[]{:S(2)}, u32[]{:S(2)}) %collective-permute-start.4) | collective-permute-done | bytes 65568 | tf_op jit(solution)/shard_map/ppermute | solution.py:625
  26.3 0.5 collective-permute-done.3.one_ref
  26.7 0.0 collective-permute-done.2.part_ref
  26.8 0.0 collective-permute-done.5.from_one_ref
  26.8 0.0 collective-permute-done.6.from_three_ref
  26.8 0.0 copy-done.1
  26.8 0.3 project.1.own_ref
  27.1 2.6 %collective-permute-start.9 = (bf16[128,512]{1,0:T(8,128)(2,1)S(1)}, bf16[128,512]{1,0:T(8,128)(2,1)S(1)}, u32[]{:S(2)}, u32[]{:S(2)}) collective-permute-start(bf16[128,512]{1,0:T(8,128)(2,1)S(1)} %project.1.own_ref), channel_id=1, source_target_pairs={{0,192},{64,128},{128,64},{192,0},{1,193},{65,129},{129,65},{193,1... | collective-permute-start | bytes 393224 | tf_op jit(solution)/shard_map/ppermute | solution.py:625
  29.7 0.3 collective-permute-start.8
  29.9 1.3 %collective-permute-start.7 = (bf16[128,512]{1,0:T(8,128)(2,1)S(1)}, bf16[128,512]{1,0:T(8,128)(2,1)S(1)}, u32[]{:S(2)}, u32[]{:S(2)}) collective-permute-start(bf16[128,512]{1,0:T(8,128)(2,1)S(1)} %project.1.own_ref), channel_id=1, source_target_pairs={{0,64},{64,0},{128,192},{192,128},{1,65},{65,1},{129,193},{193,129... | collective-permute-start | bytes 393224 | tf_op jit(solution)/shard_map/ppermute | solution.py:625
  31.2 3.7 %keep.1 = (f32[8,2,128,128]{3,2,1,0:T(8,128)}, bf16[8,3,2,384]{3,2,1,0:T(2,128)(2,1)}) custom-call(s32[512]{0:T(512)} %owner_ref.5, s32[512]{0:T(512)} %accept_ref.1, bf16[4,400,128]{2,1,0:T(8,128)(2,1)S(1)} %get-tuple-element.44.near_ref, bf16[4,400,128]{2,1,0:T(8,128)(2,1)S(1)} %get-tuple-element.45.far_ref, ...), custom_call_target="tpu_custom_call" | custom-call | flops 20000000 | bytes 3000000 | tf_op jit(solution)/shard_map/keep/pallas_call | solution.py:49
  35.0 0.0 collective-permute-done.9.prev_ref
  35.0 1.8 %collective-permute-done.8.far_ref = bf16[128,512]{1,0:T(8,128)(2,1)S(1)} collective-permute-done((bf16[128,512]{1,0:T(8,128)(2,1)S(1)}, bf16[128,512]{1,0:T(8,128)(2,1)S(1)}, u32[]{:S(2)}, u32[]{:S(2)}) %collective-permute-start.8) | collective-permute-done | bytes 131104 | tf_op jit(solution)/shard_map/ppermute | solution.py:625
  36.8 0.0 collective-permute-done.7.next_ref
  36.8 0.0 copy-done.2
  36.8 3.3 %ffn.1 = (f32[128,512]{1,0:T(8,128)S(1)}, bf16[128,512]{1,0:T(8,128)(2,1)S(1)}, bf16[128,512]{1,0:T(8,128)(2,1)S(1)}, bf16[128,512]{1,0:T(8,128)(2,1)S(1)}) custom-call(s32[512]{0:T(512)} %length_ref.1, bf16[128,512]{1,0:T(8,128)(2,1)S(1)} %project.1.own_ref, bf16[128,512]{1,0:T(8,128)(2,1)S(1)} %collective-permute-done.7.next_ref, ...), custom_call_target="tpu_custom_call" | custom-call | flops 1100000000 | bytes 9000000 | tf_op jit(solution)/shard_map/ffn/pallas_call | solution.py:601
  40.0 2.9 %collective-permute-start.10 = (bf16[128,512]{1,0:T(8,128)(2,1)S(1)}, bf16[128,512]{1,0:T(8,128)(2,1)S(1)}, u32[]{:S(2)}, u32[]{:S(2)}) collective-permute-start(bf16[128,512]{1,0:T(8,128)(2,1)S(1)} %get-tuple-element.80), channel_id=1, source_target_pairs={{0,128},{64,192},{128,0},{192,64},{1,129},{65,193},{129,1},{193,65... | collective-permute-start | bytes 393224 | tf_op jit(solution)/shard_map/ppermute | solution.py:625
  42.9 1.4 %collective-permute-start.11 = (bf16[128,512]{1,0:T(8,128)(2,1)S(1)}, bf16[128,512]{1,0:T(8,128)(2,1)S(1)}, u32[]{:S(2)}, u32[]{:S(2)}) collective-permute-start(bf16[128,512]{1,0:T(8,128)(2,1)S(1)} %get-tuple-element.81), channel_id=1, source_target_pairs={{0,64},{64,0},{128,192},{192,128},{1,65},{65,1},{129,193},{193,129... | collective-permute-start | bytes 393224 | tf_op jit(solution)/shard_map/ppermute | solution.py:625
  44.3 0.0 collective-permute-start.12
  44.3 2.2 %collective-permute-done.10 = bf16[128,512]{1,0:T(8,128)(2,1)S(1)} collective-permute-done((bf16[128,512]{1,0:T(8,128)(2,1)S(1)}, bf16[128,512]{1,0:T(8,128)(2,1)S(1)}, u32[]{:S(2)}, u32[]{:S(2)}) %collective-permute-start.10) | collective-permute-done | bytes 131104 | tf_op jit(solution)/shard_map/ppermute | solution.py:625
  46.6 2.1 %collective-permute-done.11 = bf16[128,512]{1,0:T(8,128)(2,1)S(1)} collective-permute-done((bf16[128,512]{1,0:T(8,128)(2,1)S(1)}, bf16[128,512]{1,0:T(8,128)(2,1)S(1)}, u32[]{:S(2)}, u32[]{:S(2)}) %collective-permute-start.11) | collective-permute-done | bytes 131104 | tf_op jit(solution)/shard_map/ppermute | solution.py:625
  48.7 1.8 %collective-permute-done.12 = bf16[128,512]{1,0:T(8,128)(2,1)S(1)} collective-permute-done((bf16[128,512]{1,0:T(8,128)(2,1)S(1)}, bf16[128,512]{1,0:T(8,128)(2,1)S(1)}, u32[]{:S(2)}, u32[]{:S(2)}) %collective-permute-start.12) | collective-permute-done | bytes 131104 | tf_op jit(solution)/shard_map/ppermute | solution.py:625
  50.5 0.7 %add_convert_fusion = bf16[128,512]{1,0:T(8,128)(2,1)} fusion(bf16[128,512]{1,0:T(8,128)(2,1)S(1)} %collective-permute-done.12, bf16[128,512]{1,0:T(8,128)(2,1)S(1)} %collective-permute-done.11, f32[128,512]{1,0:T(8,128)S(1)} %get-tuple-element.79, bf16[128,512]{1,0:T(8,128)(2,1)S(1)} %collective-permute-done.10), kind=kLoop, calls=%fused_computation | loop fusion | flops 458752 | bytes 786432 | tf_op jit(solution)/shard_map/convert_element_type | solution.py:693
Async XLA Ops:
  0.6 15.9 %copy-start = (bf16[256,2048]{1,0:T(8,128)(2,1)S(1)}, bf16[256,2048]{1,0:T(8,128)(2,1)}, u32[]{:S(2)}) copy-start(bf16[256,2048]{1,0:T(8,128)(2,1)} %weight_ref.5) | copy-start | bytes 3145732
  2.4 10.5 %collective-permute-start = (bf16[4,400,128]{2,1,0:T(8,128)(2,1)S(1)}, bf16[4,400,128]{2,1,0:T(8,128)(2,1)S(1)}, u32[]{:S(2)}, u32[]{:S(2)}) collective-permute-start(bf16[4,400,128]{2,1,0:T(8,128)(2,1)S(1)} %get-tuple-element.44.near_ref), channel_id=1, source_target_pairs={{0,1},{1,0},{2,3},{3,2},{4,5},{5,4},{6,7},{7,6},{8,9},{9,8},{10,11... | collective-permute-start | bytes 1228808 | tf_op jit(solution)/shard_map/ppermute | solution.py:654
  2.5 14.0 %collective-permute-start.1 = (bf16[4,400,128]{2,1,0:T(8,128)(2,1)S(1)}, bf16[4,400,128]{2,1,0:T(8,128)(2,1)S(1)}, u32[]{:S(2)}, u32[]{:S(2)}) collective-permute-start(bf16[4,400,128]{2,1,0:T(8,128)(2,1)S(1)} %get-tuple-element.45.far_ref), channel_id=1, source_target_pairs={{0,63},{1,2},{2,1},{3,4},{4,3},{5,6},{6,5},{7,8},{8,7},{9,10},{10,... | collective-permute-start | bytes 1228808 | tf_op jit(solution)/shard_map/ppermute | solution.py:653
  10.9 15.9 %collective-permute-start.5 = (bf16[256,512]{1,0:T(8,128)(2,1)S(1)}, bf16[256,512]{1,0:T(8,128)(2,1)S(1)}, u32[]{:S(2)}, u32[]{:S(2)}) collective-permute-start(bf16[256,512]{1,0:T(8,128)(2,1)S(1)} %get-tuple-element.64), channel_id=1, source_target_pairs={{0,64},{64,0},{128,192},{192,128},{1,65},{65,1},{129,193},{193,129... | collective-permute-start | bytes 786440 | tf_op jit(solution)/shard_map/ppermute | solution.py:625
  11.7 15.1 %collective-permute-start.6 = (bf16[256,512]{1,0:T(8,128)(2,1)S(1)}, bf16[256,512]{1,0:T(8,128)(2,1)S(1)}, u32[]{:S(2)}, u32[]{:S(2)}) collective-permute-start(bf16[256,512]{1,0:T(8,128)(2,1)S(1)} %get-tuple-element.65), channel_id=1, source_target_pairs={{0,192},{64,128},{128,64},{192,0},{1,193},{65,129},{129,65},{193,1... | collective-permute-start | bytes 786440 | tf_op jit(solution)/shard_map/ppermute | solution.py:625
  18.2 8.6 %collective-permute-start.2 = (bf16[128,512]{1,0:T(8,128)(2,1)S(1)}, bf16[128,512]{1,0:T(8,128)(2,1)S(1)}, u32[]{:S(2)}, u32[]{:S(2)}) collective-permute-start(bf16[128,512]{1,0:T(8,128)(2,1)S(1)} %get-tuple-element.55), channel_id=1, source_target_pairs={{0,128},{64,192},{128,0},{192,64},{1,129},{65,193},{129,1},{193,65... | collective-permute-start | bytes 393224 | tf_op jit(solution)/shard_map/ppermute | solution.py:625
  19.7 6.6 %collective-permute-start.4 = (bf16[128,256]{1,0:T(8,128)(2,1)S(1)}, bf16[128,256]{1,0:T(8,128)(2,1)S(1)}, u32[]{:S(2)}, u32[]{:S(2)}) collective-permute-start(bf16[128,256]{1,0:T(8,128)(2,1)S(1)} %bitcast.7), channel_id=1, source_target_pairs={{0,192},{64,128},{128,64},{192,0},{1,193},{65,129},{129,65},{193,1... | collective-permute-start | bytes 196616 | tf_op jit(solution)/shard_map/ppermute | solution.py:625
  21.8 5.0 %collective-permute-start.3 = (bf16[128,256]{1,0:T(8,128)(2,1)S(1)}, bf16[128,256]{1,0:T(8,128)(2,1)S(1)}, u32[]{:S(2)}, u32[]{:S(2)}) collective-permute-start(bf16[128,256]{1,0:T(8,128)(2,1)S(1)} %bitcast.8), channel_id=1, source_target_pairs={{0,64},{64,0},{128,192},{192,128},{1,65},{65,1},{129,193},{193,129... | collective-permute-start | bytes 196616 | tf_op jit(solution)/shard_map/ppermute | solution.py:625
  21.8 5.0 %copy-start.1 = (bf16[8,16,2048]{2,1,0:T(8,128)(2,1)S(1)}, bf16[8,16,2048]{2,1,0:T(8,128)(2,1)}, u32[]{:S(2)}) copy-start(bf16[8,16,2048]{2,1,0:T(8,128)(2,1)} %param.20) | copy-start | bytes 1572868
  25.4 11.4 %copy-start.2 = (f32[2048]{0:T(1024)S(1)}, f32[2048]{0:T(1024)}, u32[]{:S(2)}) copy-start(f32[2048]{0:T(1024)} %param.21) | copy-start | bytes 24580
  27.1 7.9 %collective-permute-start.9 = (bf16[128,512]{1,0:T(8,128)(2,1)S(1)}, bf16[128,512]{1,0:T(8,128)(2,1)S(1)}, u32[]{:S(2)}, u32[]{:S(2)}) collective-permute-start(bf16[128,512]{1,0:T(8,128)(2,1)S(1)} %project.1.own_ref), channel_id=1, source_target_pairs={{0,192},{64,128},{128,64},{192,0},{1,193},{65,129},{129,65},{193,1... | collective-permute-start | bytes 393224 | tf_op jit(solution)/shard_map/ppermute | solution.py:625
  29.7 7.1 %collective-permute-start.8 = (bf16[128,512]{1,0:T(8,128)(2,1)S(1)}, bf16[128,512]{1,0:T(8,128)(2,1)S(1)}, u32[]{:S(2)}, u32[]{:S(2)}) collective-permute-start(bf16[128,512]{1,0:T(8,128)(2,1)S(1)} %project.1.own_ref), channel_id=1, source_target_pairs={{0,128},{64,192},{128,0},{192,64},{1,129},{65,193},{129,1},{193,65... | collective-permute-start | bytes 393224 | tf_op jit(solution)/shard_map/ppermute | solution.py:625
  29.9 6.8 %collective-permute-start.7 = (bf16[128,512]{1,0:T(8,128)(2,1)S(1)}, bf16[128,512]{1,0:T(8,128)(2,1)S(1)}, u32[]{:S(2)}, u32[]{:S(2)}) collective-permute-start(bf16[128,512]{1,0:T(8,128)(2,1)S(1)} %project.1.own_ref), channel_id=1, source_target_pairs={{0,64},{64,0},{128,192},{192,128},{1,65},{65,1},{129,193},{193,129... | collective-permute-start | bytes 393224 | tf_op jit(solution)/shard_map/ppermute | solution.py:625
  40.0 6.6 %collective-permute-start.10 = (bf16[128,512]{1,0:T(8,128)(2,1)S(1)}, bf16[128,512]{1,0:T(8,128)(2,1)S(1)}, u32[]{:S(2)}, u32[]{:S(2)}) collective-permute-start(bf16[128,512]{1,0:T(8,128)(2,1)S(1)} %get-tuple-element.80), channel_id=1, source_target_pairs={{0,128},{64,192},{128,0},{192,64},{1,129},{65,193},{129,1},{193,65... | collective-permute-start | bytes 393224 | tf_op jit(solution)/shard_map/ppermute | solution.py:625
  42.9 5.8 %collective-permute-start.11 = (bf16[128,512]{1,0:T(8,128)(2,1)S(1)}, bf16[128,512]{1,0:T(8,128)(2,1)S(1)}, u32[]{:S(2)}, u32[]{:S(2)}) collective-permute-start(bf16[128,512]{1,0:T(8,128)(2,1)S(1)} %get-tuple-element.81), channel_id=1, source_target_pairs={{0,64},{64,0},{128,192},{192,128},{1,65},{65,1},{129,193},{193,129... | collective-permute-start | bytes 393224 | tf_op jit(solution)/shard_map/ppermute | solution.py:625
  44.3 6.2 %collective-permute-start.12 = (bf16[128,512]{1,0:T(8,128)(2,1)S(1)}, bf16[128,512]{1,0:T(8,128)(2,1)S(1)}, u32[]{:S(2)}, u32[]{:S(2)}) collective-permute-start(bf16[128,512]{1,0:T(8,128)(2,1)S(1)} %get-tuple-element.82), channel_id=1, source_target_pairs={{0,192},{64,128},{128,64},{192,0},{1,193},{65,129},{129,65},{193,1... | collective-permute-start | bytes 393224 | tf_op jit(solution)/shard_map/ppermute | solution.py:625

commit v9 on v8

--- a/solution.py
+++ b/solution.py
@@ -563,58 +563,72 @@
     )
 
 
-def ffn_kernel(
-    length_ref, own_ref, next_ref, far_ref, prev_ref, gain_ref, gate_ref, up_ref, down_ref,
-    own_out_ref, next_out_ref, far_out_ref, prev_out_ref, normed_scr,
+NT = (((1,), (1,)), ((), ()))
+
+
+def gated(rows, step, gain_ref, gate_ref, up_ref):
+    block = rows.astype(F32)
+    square = jnp.sum(block * block, axis=-1, keepdims=True)
+    columns = columns_of(step, rows.shape[1])
+    scaled = (block * gain_ref[:, columns]).astype(BF)
+    gate = lax.dot_general(scaled, gate_ref[:, columns], NT, preferred_element_type=F32)
+    up = lax.dot_general(scaled, up_ref[:, columns], NT, preferred_element_type=F32)
+    return square, gate, up
+
+
+def ffn_first(
+    own_ref, two_ref, three_ref, gain_ref, gate_ref, up_ref, square_ref, gate_out_ref, up_out_ref,
+):
+    total = None
+    for step, ref in ((0, own_ref), (2, two_ref), (3, three_ref)):
+        parts = gated(ref[...], step, gain_ref, gate_ref, up_ref)
+        total = parts if total is None else [x + y for x, y in zip(total, parts)]
+    square_ref[...] = jnp.broadcast_to(total[0], square_ref.shape)
+    gate_out_ref[...] = total[1]
+    up_out_ref[...] = total[2]
+
+
+def ffn_first_call(own, two, three, gain, gate_t, up_t):
+    slots, hidden = own.shape[0], gate_t.shape[0]
+    shape = jax.ShapeDtypeStruct
+    return call(
+        ffn_first,
+        (shape((slots, DK), F32), shape((slots, hidden), F32), shape((slots, hidden), F32)),
+        [VM] * 6, [], 550_000_000, 5_000_000, own, two, three, gain, gate_t, up_t,
+    )
+
+
+def ffn_last(
+    length_ref, own_ref, one_ref, gain_ref, gate_ref, up_ref, down_ref,
+    square_ref, gate_in_ref, up_in_ref, own_out_ref, one_out_ref, two_out_ref, three_out_ref,
 ):
     width = own_ref.shape[1]
-    parts = ((0, own_ref), (1, next_ref), (2, far_ref), (3, prev_ref))
-    total = None
-    for _, ref in parts:
-        block = ref[...].astype(F32)
-        square = jnp.sum(block * block, axis=-1, keepdims=True)
-        total = square if total is None else total + square
+    square, gate, up = gated(one_ref[...], 1, gain_ref, gate_ref, up_ref)
+    total = square + square_ref[:, :1]
     scale = lax.rsqrt(total / (4 * width) + 1e-05)
-    for step, ref in parts:
-        columns = columns_of(step, width)
-        normed_scr[:, columns] = (ref[...].astype(F32) * scale * gain_ref[:, columns]).astype(BF)
-    normed = normed_scr[...]
-    dims = (((1,), (1,)), ((), ()))
-    gate = lax.dot_general(normed, gate_ref[...], dims, preferred_element_type=F32)
-    up = lax.dot_general(normed, up_ref[...], dims, preferred_element_type=F32)
+    gate = (gate + gate_in_ref[...]) * scale
+    up = (up + up_in_ref[...]) * scale
     hidden = (gate * jax.nn.sigmoid(gate) * up).astype(BF)
     me = lax.axis_index("req")
     position = lax.broadcasted_iota(jnp.int32, (DRAFT, 1), 0)
     live = jnp.concatenate(
         [(position < length_ref[me * ROWS + row]).astype(F32) for row in range(ROWS)], axis=0
     )
-    for step, out_ref in ((2, far_out_ref), (1, next_out_ref), (3, prev_out_ref)):
+    for step, out_ref in ((2, two_out_ref), (1, one_out_ref), (3, three_out_ref)):
         part = jnp.dot(hidden, down_ref[:, columns_of(step, width)], preferred_element_type=F32)
         out_ref[...] = (part * live).astype(BF)
     part = jnp.dot(hidden, down_ref[:, columns_of(0, width)], preferred_element_type=F32)
     own_out_ref[...] = (part + own_ref[...].astype(F32)) * live
 
 
-def ffn(lengths, own, following, far, preceding, gain, gate_t, up_t, down):
+def ffn_last_call(lengths, own, one, gain, gate_t, up_t, down, *partial):
     slots, width = own.shape
     shape = jax.ShapeDtypeStruct
-    return pl.pallas_call(
-        ffn_kernel,
-        name="ffn",
-        out_shape=(
-            shape((slots, width), F32),
-            shape((slots, width), BF),
-            shape((slots, width), BF),
-            shape((slots, width), BF),
-        ),
-        in_specs=[SM] + [VM] * 8,
-        out_specs=tuple([VM] * 4),
-        scratch_shapes=[pltpu.VMEM((slots, 4 * width), BF)],
-        compiler_params=PARAMS,
-        cost_estimate=pl.CostEstimate(
-            flops=1_100_000_000, bytes_accessed=9_000_000, transcendentals=100_000
-        ),
-    )(lengths, own, following, far, preceding, gain, gate_t, up_t, down)
+    part = shape((slots, width), BF)
+    return call(
+        ffn_last, (shape((slots, width), F32), part, part, part), [SM] + [VM] * 9, [],
+        550_000_000, 5_000_000, lengths, own, one, gain, gate_t, up_t, down, *partial,
+    )
 
 
 def in_hbm(array):
@@ -674,22 +688,21 @@
         (part, one, three, gate_t, up_t, down)
     )
     stream = project_call(mixed, one, three, out_weight, parts, part, resid.reshape(slots, -1))
-    stream, from_near, from_far = lax.optimization_barrier((stream, from_near, from_far))
     two = swapped(stream, 2)
+    three = swapped(stream, 3)
     one = swapped(stream, 1)
-    three = swapped(stream, 3)
-    kept_states, kept_edges = keep_call(
-        owner_row, accepted, near, far, from_near, from_far, states, conv, bias
-    )
-    one, two, three, kept_states, kept_edges = lax.optimization_barrier(
-        (one, two, three, kept_states, kept_edges)
-    )
-    own_part, to_one, to_two, to_three = ffn(
-        draft_lengths, stream, one, two, three, ffn_gain[None, :], gate_t, up_t, down
+    gain_row = ffn_gain[None, :]
+    partial = ffn_first_call(stream, two, three, gain_row, gate_t, up_t)
+    own_part, to_one, to_two, to_three = ffn_last_call(
+        draft_lengths, stream, one, gain_row, gate_t, up_t, down, *partial
     )
     two = swapped(to_two, 2)
     one = swapped(to_one, 1)
     three = swapped(to_three, 3)
+    own_part, from_near, from_far = lax.optimization_barrier((own_part, from_near, from_far))
+    kept_states, kept_edges = keep_call(
+        owner_row, accepted, near, far, from_near, from_far, states, conv, bias
+    )
     layer_out = (own_part + two.astype(F32) + one.astype(F32) + three.astype(F32)).astype(BF)
     return (layer_out.reshape(ROWS, DRAFT, -1), kept_states, kept_edges)
 

time: 51.5 us -> 50.1 us (0.973)
  waiting for transfers between devices: 10.6 us -> 9.32 us
    pallas_call x1 -> x0, Pallas kernels: 3.27 us -> none  [ffn(): pl.pallas_call(ffn_kernel, name='ffn', out_shape=(shape((slots, width), F...]
    pallas_call x6 -> x8, Pallas kernels: 13.3 us -> 16.6 us  [call(): pl.pallas_call(kernel, name=kernel.__name__, out_shape=out_shape, in_spec...]
    ppermute x11, waiting for transfers between devices: 9.29 us -> 7.99 us  [swapped(): return lax.ppermute(block, 'grp', [(i, i ^ step) for i in range(4)])]
  transfers between devices with their start and end apart: 13 -> 13, of which waited for: 7 -> 6; matrix products, arithmetic and copies ran while one was open for 0% -> 0% of each run, Pallas kernels for 22% -> 26%
where the time goes in v9:
time: 50.1 us; the launch traced here: 49.8 us
  starting transfers between devices  22.4 us (45%)
  Pallas kernels  16.6 us (33%)
  waiting for transfers between devices  9.32 us (19%)
  between operations  0.75 us (1%)
  other arithmetic  0.73 us (1%)
    pallas_call x8, Pallas kernels, call(): pl.pallas_call(kernel, name=kernel.__name__, out_shape=out_shape, in_spec...  16.6 us
    ppermute x11, starting transfers between devices, swapped(): return lax.ppermute(block, 'grp', [(i, i ^ step) for i in range(4)])  13.9 us
    ppermute x1, starting transfers between devices, shards(): from_far = lax.ppermute(far, 'req', across)  8.41 us
    ppermute x11, waiting for transfers between devices, swapped(): return lax.ppermute(block, 'grp', [(i, i ^ step) for i in range(4)])  7.99 us
    ppermute x1, waiting for transfers between devices, shards(): from_far = lax.ppermute(far, 'req', across)  1.33 us
  transfers between devices with their start and end apart: 13, of which 6 were waited for; matrix products, arithmetic and copies ran while one was open for 0% of the time, Pallas kernels for 26%

profile of v9, /device:TPU:6, one launch (start us, length us, event | category | flops | bytes accessed | tf_op | source)
XLA Modules:
  0.0 49.8 jit_solution(11513368669234650759)
XLA Ops:
  0.6 0.0 copy-start
  0.6 1.7 %pack.1 = (bf16[4,400,128]{2,1,0:T(8,128)(2,1)S(1)}, bf16[4,400,128]{2,1,0:T(8,128)(2,1)S(1)}, bf16[256,512]{1,0:T(8,128)(2,1)S(1)}, bf16[256,512]{1,0:T(8,128)(2,1)S(1)}) custom-call(f32[8,2,128,128]{3,2,1,0:T(8,128)} %state_ref.3, bf16[8,3,2,384]{3,2,1,0:T(2,128)(2,1)} %edge_ref.1, bf16[8,16,2,384]{3,2,1,0:T(2,128)(2,1)} %draft_ref.1, ...), custom_call_target="tpu_custom_call" | custom-call | flops 1000000 | bytes 3000000 | tf_op jit(solution)/shard_map/pack/pallas_call | solution.py:49
  2.4 0.1 collective-permute-start
  2.5 8.4 %collective-permute-start.1 = (bf16[4,400,128]{2,1,0:T(8,128)(2,1)S(1)}, bf16[4,400,128]{2,1,0:T(8,128)(2,1)S(1)}, u32[]{:S(2)}, u32[]{:S(2)}) collective-permute-start(bf16[4,400,128]{2,1,0:T(8,128)(2,1)S(1)} %get-tuple-element.43.far_ref), channel_id=1, source_target_pairs={{0,63},{1,2},{2,1},{3,4},{4,3},{5,6},{6,5},{7,8},{8,7},{9,10},{10,... | collective-permute-start | bytes 1228808 | tf_op jit(solution)/shard_map/ppermute | solution.py:667
  10.9 0.8 %collective-permute-start.5 = (bf16[256,512]{1,0:T(8,128)(2,1)S(1)}, bf16[256,512]{1,0:T(8,128)(2,1)S(1)}, u32[]{:S(2)}, u32[]{:S(2)}) collective-permute-start(bf16[256,512]{1,0:T(8,128)(2,1)S(1)} %get-tuple-element.62), channel_id=1, source_target_pairs={{0,64},{64,0},{128,192},{192,128},{1,65},{65,1},{129,193},{193,129... | collective-permute-start | bytes 786440 | tf_op jit(solution)/shard_map/ppermute | solution.py:639
  11.7 1.1 %collective-permute-start.6 = (bf16[256,512]{1,0:T(8,128)(2,1)S(1)}, bf16[256,512]{1,0:T(8,128)(2,1)S(1)}, u32[]{:S(2)}, u32[]{:S(2)}) collective-permute-start(bf16[256,512]{1,0:T(8,128)(2,1)S(1)} %get-tuple-element.63), channel_id=1, source_target_pairs={{0,192},{64,128},{128,64},{192,0},{1,193},{65,129},{129,65},{193,1... | collective-permute-start | bytes 786440 | tf_op jit(solution)/shard_map/ppermute | solution.py:639
  12.8 0.0 collective-permute-done.from_near_ref
  12.8 2.3 %mix_near.1 = (bf16[4,16,256]{2,1,0:T(8,128)(2,1)S(1)}, f32[4,2,16,128]{3,2,1,0:T(8,128)S(1)}, f32[4,2,16,128]{3,2,1,0:T(8,128)S(1)}, f32[4,2,16,128]{3,2,1,0:T(...) custom-call(s32[512]{0:T(512)} %owner_ref.5, ...), custom_call_target="tpu_custom_call" | custom-call | flops 15000000 | bytes 3000000 | tf_op jit(solution)/shard_map/mix_near/pallas_call | solution.py:49
  15.2 1.3 %collective-permute-done.1.from_far_ref = bf16[4,400,128]{2,1,0:T(8,128)(2,1)S(1)} collective-permute-done((bf16[4,400,128]{2,1,0:T(8,128)(2,1)S(1)}, bf16[4,400,128]{2,1,0:T(8,128)(2,1)S(1)}, u32[]{:S(2)}, u32[]{:S(2)}) %collective-permute-start.1) | collective-permute-done | bytes 409632 | tf_op jit(solution)/shard_map/ppermute | solution.py:667
  16.5 0.0 copy-done
  16.5 1.7 %mix_far.1 = (bf16[8,16,256]{2,1,0:T(8,128)(2,1)S(1)}, bf16[128,512]{1,0:T(8,128)(2,1)S(1)}) custom-call(s32[512]{0:T(512)} %owner_ref.5, bf16[4,16,256]{2,1,0:T(8,128)(2,1)S(1)} %get-tuple-element.44.near_mixed_ref, bf16[4,400,128]{2,1,0:T(8,128)(2,1)S(1)} %get-tuple-element.43.far_ref, bf16[4,400,128]{2,1,0:T(8,128)(2,1)S(1)} %collective-permute-done.1.from_far_ref, ...), custom_call_target="tpu_custom_call" | custom-call | flops 50000000 | bytes 2000000 | tf_op jit(solution)/shard_map/mix_far/pallas_call | solution.py:49
  18.2 1.5 %collective-permute-start.2 = (bf16[128,512]{1,0:T(8,128)(2,1)S(1)}, bf16[128,512]{1,0:T(8,128)(2,1)S(1)}, u32[]{:S(2)}, u32[]{:S(2)}) collective-permute-start(bf16[128,512]{1,0:T(8,128)(2,1)S(1)} %get-tuple-element.53), channel_id=1, source_target_pairs={{0,128},{64,192},{128,0},{192,64},{1,129},{65,193},{129,1},{193,65... | collective-permute-start | bytes 393224 | tf_op jit(solution)/shard_map/ppermute | solution.py:639
  19.7 2.1 %collective-permute-start.4 = (bf16[128,256]{1,0:T(8,128)(2,1)S(1)}, bf16[128,256]{1,0:T(8,128)(2,1)S(1)}, u32[]{:S(2)}, u32[]{:S(2)}) collective-permute-start(bf16[128,256]{1,0:T(8,128)(2,1)S(1)} %bitcast.7), channel_id=1, source_target_pairs={{0,192},{64,128},{128,64},{192,0},{1,193},{65,129},{129,65},{193,1... | collective-permute-start | bytes 196616 | tf_op jit(solution)/shard_map/ppermute | solution.py:639
  21.8 0.0 collective-permute-start.3
  21.8 0.0 copy-start.1
  21.8 0.0 copy-start.2
  21.8 3.6 %fetch.1 = (bf16[704,2048]{1,0:T(8,128)(2,1)S(1)}, bf16[704,2048]{1,0:T(8,128)(2,1)S(1)}, bf16[704,2048]{1,0:T(8,128)(2,1)S(1)}) custom-call(bf16[704,2048]{1,0:T(8,128)(2,1)} %bitcast.12, bf16[704,2048]{1,0:T(8,128)(2,1)} %bitcast.13, bf16[704,2048]{1,0:T(8,128)(2,1)} %refs_2_), custom_call_target="tpu_custom_call" | custom-call | bytes 17000000 | tf_op jit(solution)/shard_map/fetch/pallas_call | solution.py:49
  25.4 0.9 %collective-permute-done.4.three_ref = bf16[128,256]{1,0:T(8,128)(2,1)S(1)} collective-permute-done((bf16[128,256]{1,0:T(8,128)(2,1)S(1)}, bf16[128,256]{1,0:T(8,128)(2,1)S(1)}, u32[]{:S(2)}, u32[]{:S(2)}) %collective-permute-start.4) | collective-permute-done | bytes 65568 | tf_op jit(solution)/shard_map/ppermute | solution.py:639
  26.3 0.5 collective-permute-done.3.one_ref
  26.7 0.0 collective-permute-done.2.part_ref
  26.7 0.0 collective-permute-done.5.from_one_ref
  26.8 0.0 collective-permute-done.6.from_three_ref
  26.8 0.0 copy-done.1
  26.8 0.3 project.1.own_ref
  27.1 2.6 %collective-permute-start.9 = (bf16[128,512]{1,0:T(8,128)(2,1)S(1)}, bf16[128,512]{1,0:T(8,128)(2,1)S(1)}, u32[]{:S(2)}, u32[]{:S(2)}) collective-permute-start(bf16[128,512]{1,0:T(8,128)(2,1)S(1)} %project.1.own_ref), channel_id=1, source_target_pairs={{0,192},{64,128},{128,64},{192,0},{1,193},{65,129},{129,65},{193,1... | collective-permute-start | bytes 393224 | tf_op jit(solution)/shard_map/ppermute | solution.py:639
  29.7 0.3 collective-permute-start.8
  29.9 1.3 %collective-permute-start.7 = (bf16[128,512]{1,0:T(8,128)(2,1)S(1)}, bf16[128,512]{1,0:T(8,128)(2,1)S(1)}, u32[]{:S(2)}, u32[]{:S(2)}) collective-permute-start(bf16[128,512]{1,0:T(8,128)(2,1)S(1)} %project.1.own_ref), channel_id=1, source_target_pairs={{0,64},{64,0},{128,192},{192,128},{1,65},{65,1},{129,193},{193,129... | collective-permute-start | bytes 393224 | tf_op jit(solution)/shard_map/ppermute | solution.py:639
  31.2 2.4 %collective-permute-done.9.three_ref = bf16[128,512]{1,0:T(8,128)(2,1)S(1)} collective-permute-done((bf16[128,512]{1,0:T(8,128)(2,1)S(1)}, bf16[128,512]{1,0:T(8,128)(2,1)S(1)}, u32[]{:S(2)}, u32[]{:S(2)}) %collective-permute-start.9) | collective-permute-done | bytes 131104 | tf_op jit(solution)/shard_map/ppermute | solution.py:639
  33.7 3.1 %collective-permute-done.8.two_ref = bf16[128,512]{1,0:T(8,128)(2,1)S(1)} collective-permute-done((bf16[128,512]{1,0:T(8,128)(2,1)S(1)}, bf16[128,512]{1,0:T(8,128)(2,1)S(1)}, u32[]{:S(2)}, u32[]{:S(2)}) %collective-permute-start.8) | collective-permute-done | bytes 131104 | tf_op jit(solution)/shard_map/ppermute | solution.py:639
  36.8 0.0 copy-done.2
  36.8 1.4 %ffn_first.1 = (f32[128,128]{1,0:T(8,128)S(1)}, f32[128,704]{1,0:T(8,128)S(1)}, f32[128,704]{1,0:T(8,128)S(1)}) custom-call(bf16[128,512]{1,0:T(8,128)(2,1)S(1)} %project.1.own_ref, bf16[128,512]{1,0:T(8,128)(2,1)S(1)} %collective-permute-done.8.two_ref, bf16[128,512]{1,0:T(8,128)(2,1)S(1)} %collective-permute-done.9.three_ref, f32[1,2048]{1,0:T(1,128)S(1)} %bitcast.10, ...), custom_call_target="tpu_custom_call" | custom-call | flops 550000000 | bytes 5000000 | tf_op jit(solution)/shard_map/ffn_first/pallas_call | solution.py:49
  38.2 0.0 collective-permute-done.7.one_ref
  38.2 1.8 %ffn_last.1 = (f32[128,512]{1,0:T(8,128)S(1)}, bf16[128,512]{1,0:T(8,128)(2,1)S(1)}, bf16[128,512]{1,0:T(8,128)(2,1)S(1)}, bf16[128,512]{1,0:T(8,128)(2,1)S(1)}) custom-call(s32[512]{0:T(512)} %length_ref.1, bf16[128,512]{1,0:T(8,128)(2,1)S(1)} %project.1.own_ref, bf16[128,512]{1,0:T(8,128)(2,1)S(1)} %collective-permute-done.7.one_ref, ...), custom_call_target="tpu_custom_call" | custom-call | flops 550000000 | bytes 5000000 | tf_op jit(solution)/shard_map/ffn_last/pallas_call | solution.py:49
  40.0 1.4 %collective-permute-start.10 = (bf16[128,512]{1,0:T(8,128)(2,1)S(1)}, bf16[128,512]{1,0:T(8,128)(2,1)S(1)}, u32[]{:S(2)}, u32[]{:S(2)}) collective-permute-start(bf16[128,512]{1,0:T(8,128)(2,1)S(1)} %get-tuple-element.73), channel_id=1, source_target_pairs={{0,128},{64,192},{128,0},{192,64},{1,129},{65,193},{129,1},{193,65... | collective-permute-start | bytes 393224 | tf_op jit(solution)/shard_map/ppermute | solution.py:639
  41.4 1.5 %collective-permute-start.11 = (bf16[128,512]{1,0:T(8,128)(2,1)S(1)}, bf16[128,512]{1,0:T(8,128)(2,1)S(1)}, u32[]{:S(2)}, u32[]{:S(2)}) collective-permute-start(bf16[128,512]{1,0:T(8,128)(2,1)S(1)} %get-tuple-element.74), channel_id=1, source_target_pairs={{0,64},{64,0},{128,192},{192,128},{1,65},{65,1},{129,193},{193,129... | collective-permute-start | bytes 393224 | tf_op jit(solution)/shard_map/ppermute | solution.py:639
  42.9 1.3 %collective-permute-start.12 = (bf16[128,512]{1,0:T(8,128)(2,1)S(1)}, bf16[128,512]{1,0:T(8,128)(2,1)S(1)}, u32[]{:S(2)}, u32[]{:S(2)}) collective-permute-start(bf16[128,512]{1,0:T(8,128)(2,1)S(1)} %get-tuple-element.75), channel_id=1, source_target_pairs={{0,192},{64,128},{128,64},{192,0},{1,193},{65,129},{129,65},{193,1... | collective-permute-start | bytes 393224 | tf_op jit(solution)/shard_map/ppermute | solution.py:639
  44.2 3.7 %keep.1 = (f32[8,2,128,128]{3,2,1,0:T(8,128)}, bf16[8,3,2,384]{3,2,1,0:T(2,128)(2,1)}) custom-call(s32[512]{0:T(512)} %owner_ref.5, s32[512]{0:T(512)} %accept_ref.1, bf16[4,400,128]{2,1,0:T(8,128)(2,1)S(1)} %get-tuple-element.42.near_ref, bf16[4,400,128]{2,1,0:T(8,128)(2,1)S(1)} %get-tuple-element.43.far_ref, ...), custom_call_target="tpu_custom_call" | custom-call | flops 20000000 | bytes 3000000 | tf_op jit(solution)/shard_map/keep/pallas_call | solution.py:49
  48.0 0.0 collective-permute-done.10
  48.0 0.0 collective-permute-done.11
  48.0 1.1 %collective-permute-done.12 = bf16[128,512]{1,0:T(8,128)(2,1)S(1)} collective-permute-done((bf16[128,512]{1,0:T(8,128)(2,1)S(1)}, bf16[128,512]{1,0:T(8,128)(2,1)S(1)}, u32[]{:S(2)}, u32[]{:S(2)}) %collective-permute-start.12) | collective-permute-done | bytes 131104 | tf_op jit(solution)/shard_map/ppermute | solution.py:639
  49.1 0.7 %add_convert_fusion = bf16[128,512]{1,0:T(8,128)(2,1)} fusion(bf16[128,512]{1,0:T(8,128)(2,1)S(1)} %collective-permute-done.12, bf16[128,512]{1,0:T(8,128)(2,1)S(1)} %collective-permute-done.11, f32[128,512]{1,0:T(8,128)S(1)} %get-tuple-element.72, bf16[128,512]{1,0:T(8,128)(2,1)S(1)} %collective-permute-done.10), kind=kLoop, calls=%fused_computation | loop fusion | flops 458752 | bytes 786432 | tf_op jit(solution)/shard_map/convert_element_type | solution.py:706
Async XLA Ops:
  0.6 15.9 %copy-start = (bf16[256,2048]{1,0:T(8,128)(2,1)S(1)}, bf16[256,2048]{1,0:T(8,128)(2,1)}, u32[]{:S(2)}) copy-start(bf16[256,2048]{1,0:T(8,128)(2,1)} %weight_ref.5) | copy-start | bytes 3145732
  2.4 10.5 %collective-permute-start = (bf16[4,400,128]{2,1,0:T(8,128)(2,1)S(1)}, bf16[4,400,128]{2,1,0:T(8,128)(2,1)S(1)}, u32[]{:S(2)}, u32[]{:S(2)}) collective-permute-start(bf16[4,400,128]{2,1,0:T(8,128)(2,1)S(1)} %get-tuple-element.42.near_ref), channel_id=1, source_target_pairs={{0,1},{1,0},{2,3},{3,2},{4,5},{5,4},{6,7},{7,6},{8,9},{9,8},{10,11... | collective-permute-start | bytes 1228808 | tf_op jit(solution)/shard_map/ppermute | solution.py:668
  2.5 14.0 %collective-permute-start.1 = (bf16[4,400,128]{2,1,0:T(8,128)(2,1)S(1)}, bf16[4,400,128]{2,1,0:T(8,128)(2,1)S(1)}, u32[]{:S(2)}, u32[]{:S(2)}) collective-permute-start(bf16[4,400,128]{2,1,0:T(8,128)(2,1)S(1)} %get-tuple-element.43.far_ref), channel_id=1, source_target_pairs={{0,63},{1,2},{2,1},{3,4},{4,3},{5,6},{6,5},{7,8},{8,7},{9,10},{10,... | collective-permute-start | bytes 1228808 | tf_op jit(solution)/shard_map/ppermute | solution.py:667
  10.9 15.9 %collective-permute-start.5 = (bf16[256,512]{1,0:T(8,128)(2,1)S(1)}, bf16[256,512]{1,0:T(8,128)(2,1)S(1)}, u32[]{:S(2)}, u32[]{:S(2)}) collective-permute-start(bf16[256,512]{1,0:T(8,128)(2,1)S(1)} %get-tuple-element.62), channel_id=1, source_target_pairs={{0,64},{64,0},{128,192},{192,128},{1,65},{65,1},{129,193},{193,129... | collective-permute-start | bytes 786440 | tf_op jit(solution)/shard_map/ppermute | solution.py:639
  11.7 15.0 %collective-permute-start.6 = (bf16[256,512]{1,0:T(8,128)(2,1)S(1)}, bf16[256,512]{1,0:T(8,128)(2,1)S(1)}, u32[]{:S(2)}, u32[]{:S(2)}) collective-permute-start(bf16[256,512]{1,0:T(8,128)(2,1)S(1)} %get-tuple-element.63), channel_id=1, source_target_pairs={{0,192},{64,128},{128,64},{192,0},{1,193},{65,129},{129,65},{193,1... | collective-permute-start | bytes 786440 | tf_op jit(solution)/shard_map/ppermute | solution.py:639
  18.2 8.6 %collective-permute-start.2 = (bf16[128,512]{1,0:T(8,128)(2,1)S(1)}, bf16[128,512]{1,0:T(8,128)(2,1)S(1)}, u32[]{:S(2)}, u32[]{:S(2)}) collective-permute-start(bf16[128,512]{1,0:T(8,128)(2,1)S(1)} %get-tuple-element.53), channel_id=1, source_target_pairs={{0,128},{64,192},{128,0},{192,64},{1,129},{65,193},{129,1},{193,65... | collective-permute-start | bytes 393224 | tf_op jit(solution)/shard_map/ppermute | solution.py:639
  19.7 6.6 %collective-permute-start.4 = (bf16[128,256]{1,0:T(8,128)(2,1)S(1)}, bf16[128,256]{1,0:T(8,128)(2,1)S(1)}, u32[]{:S(2)}, u32[]{:S(2)}) collective-permute-start(bf16[128,256]{1,0:T(8,128)(2,1)S(1)} %bitcast.7), channel_id=1, source_target_pairs={{0,192},{64,128},{128,64},{192,0},{1,193},{65,129},{129,65},{193,1... | collective-permute-start | bytes 196616 | tf_op jit(solution)/shard_map/ppermute | solution.py:639
  21.8 5.0 %collective-permute-start.3 = (bf16[128,256]{1,0:T(8,128)(2,1)S(1)}, bf16[128,256]{1,0:T(8,128)(2,1)S(1)}, u32[]{:S(2)}, u32[]{:S(2)}) collective-permute-start(bf16[128,256]{1,0:T(8,128)(2,1)S(1)} %bitcast.8), channel_id=1, source_target_pairs={{0,64},{64,0},{128,192},{192,128},{1,65},{65,1},{129,193},{193,129... | collective-permute-start | bytes 196616 | tf_op jit(solution)/shard_map/ppermute | solution.py:639
  21.8 5.0 %copy-start.1 = (bf16[8,16,2048]{2,1,0:T(8,128)(2,1)S(1)}, bf16[8,16,2048]{2,1,0:T(8,128)(2,1)}, u32[]{:S(2)}) copy-start(bf16[8,16,2048]{2,1,0:T(8,128)(2,1)} %param.20) | copy-start | bytes 1572868
  21.8 15.0 %copy-start.2 = (f32[2048]{0:T(1024)S(1)}, f32[2048]{0:T(1024)}, u32[]{:S(2)}) copy-start(f32[2048]{0:T(1024)} %param.21) | copy-start | bytes 24580
  27.1 6.6 %collective-permute-start.9 = (bf16[128,512]{1,0:T(8,128)(2,1)S(1)}, bf16[128,512]{1,0:T(8,128)(2,1)S(1)}, u32[]{:S(2)}, u32[]{:S(2)}) collective-permute-start(bf16[128,512]{1,0:T(8,128)(2,1)S(1)} %project.1.own_ref), channel_id=1, source_target_pairs={{0,192},{64,128},{128,64},{192,0},{1,193},{65,129},{129,65},{193,1... | collective-permute-start | bytes 393224 | tf_op jit(solution)/shard_map/ppermute | solution.py:639
  29.7 7.1 %collective-permute-start.8 = (bf16[128,512]{1,0:T(8,128)(2,1)S(1)}, bf16[128,512]{1,0:T(8,128)(2,1)S(1)}, u32[]{:S(2)}, u32[]{:S(2)}) collective-permute-start(bf16[128,512]{1,0:T(8,128)(2,1)S(1)} %project.1.own_ref), channel_id=1, source_target_pairs={{0,128},{64,192},{128,0},{192,64},{1,129},{65,193},{129,1},{193,65... | collective-permute-start | bytes 393224 | tf_op jit(solution)/shard_map/ppermute | solution.py:639
  29.9 8.3 %collective-permute-start.7 = (bf16[128,512]{1,0:T(8,128)(2,1)S(1)}, bf16[128,512]{1,0:T(8,128)(2,1)S(1)}, u32[]{:S(2)}, u32[]{:S(2)}) collective-permute-start(bf16[128,512]{1,0:T(8,128)(2,1)S(1)} %project.1.own_ref), channel_id=1, source_target_pairs={{0,64},{64,0},{128,192},{192,128},{1,65},{65,1},{129,193},{193,129... | collective-permute-start | bytes 393224 | tf_op jit(solution)/shard_map/ppermute | solution.py:639
  40.0 7.9 %collective-permute-start.10 = (bf16[128,512]{1,0:T(8,128)(2,1)S(1)}, bf16[128,512]{1,0:T(8,128)(2,1)S(1)}, u32[]{:S(2)}, u32[]{:S(2)}) collective-permute-start(bf16[128,512]{1,0:T(8,128)(2,1)S(1)} %get-tuple-element.73), channel_id=1, source_target_pairs={{0,128},{64,192},{128,0},{192,64},{1,129},{65,193},{129,1},{193,65... | collective-permute-start | bytes 393224 | tf_op jit(solution)/shard_map/ppermute | solution.py:639
  41.4 6.6 %collective-permute-start.11 = (bf16[128,512]{1,0:T(8,128)(2,1)S(1)}, bf16[128,512]{1,0:T(8,128)(2,1)S(1)}, u32[]{:S(2)}, u32[]{:S(2)}) collective-permute-start(bf16[128,512]{1,0:T(8,128)(2,1)S(1)} %get-tuple-element.74), channel_id=1, source_target_pairs={{0,64},{64,0},{128,192},{192,128},{1,65},{65,1},{129,193},{193,129... | collective-permute-start | bytes 393224 | tf_op jit(solution)/shard_map/ppermute | solution.py:639
  42.9 6.2 %collective-permute-start.12 = (bf16[128,512]{1,0:T(8,128)(2,1)S(1)}, bf16[128,512]{1,0:T(8,128)(2,1)S(1)}, u32[]{:S(2)}, u32[]{:S(2)}) collective-permute-start(bf16[128,512]{1,0:T(8,128)(2,1)S(1)} %get-tuple-element.75), channel_id=1, source_target_pairs={{0,192},{64,128},{128,64},{192,0},{1,193},{65,129},{129,65},{193,1... | collective-permute-start | bytes 393224 | tf_op jit(solution)/shard_map/ppermute | solution.py:639

commit v10 on v9

--- a/solution.py
+++ b/solution.py
@@ -335,126 +335,6 @@
         [SM] + [VM] * 9, MIX_SCRATCH,
         50_000_000, 2_000_000,
         owner, near_mixed, far, from_far, queries, forget, values, conv, gain, weight,
-    )
-
-
-def fetch(*refs):
-    count = len(refs) // 2
-    sems = refs[-1]
-    copies = [
-        pltpu.make_async_copy(refs[i], refs[count + i], sems.at[i]) for i in range(count)
-    ]
-    for copy in copies:
-        copy.start()
-    for copy in copies:
-        copy.wait()
-
-
-def fetch_call(*arrays):
-    return call(
-        fetch, tuple(jax.ShapeDtypeStruct(x.shape, x.dtype) for x in arrays), [HB] * len(arrays),
-        [pltpu.SemaphoreType.DMA((len(arrays),))], 0, 17_000_000, *arrays,
-    )
-
-
-def mixer(
-    owner_ref, near_ref, far_ref, from_near_ref, from_far_ref, query_ref, forget_ref, value_ref,
-    conv_ref, bias_ref, gain_ref, mixed_ref, edges, states, query_scr, forget_scr, value_scr,
-):
-    half = DRAFT // 2
-    for slot in range(ROWS):
-        side = slot // HALF
-        _, local, place = source_of(owner_ref, row_of(side, slot % HALF))
-        mine_ref, other_ref = (near_ref, from_near_ref) if side == 0 else (far_ref, from_far_ref)
-        for block in range(3):
-            mine = mine_ref[slot % HALF, edges_of(block), :].astype(F32)
-            other = other_ref[place, edges_of(block), :].astype(F32)
-            edges[slot, block, :DRAFT, :] = jnp.where(local, mine, other)
-            edges[slot, block, DRAFT:, :] = jnp.zeros((8, DK), F32)
-
-        @pl.when(local)
-        def _():
-            states[slot] = mine_ref[slot % HALF, : 2 * DK, :]
-
-        @pl.when(jnp.logical_not(local))
-        def _():
-            states[slot] = other_ref[place, : 2 * DK, :]
-
-    sub_iota = lax.broadcasted_iota(jnp.int32, (1, DRAFT, DK), 1)
-
-    def pair(step, _):
-        base = step * 2
-        for sub in range(2):
-            slot = base + sub
-            for head in range(2):
-                lane = sub * 2 + head
-                for block, (in_ref, out, act) in enumerate(
-                    (
-                        (query_ref, query_scr, as_query),
-                        (forget_ref, forget_scr, jax.nn.sigmoid),
-                        (value_ref, value_scr, as_value),
-                    )
-                ):
-                    first = in_ref[slot, head, :half]
-                    for shift in range(CONV - 1):
-                        taps = conv_ref[shift, head, block_of(block)]
-                        rows = edges[slot, block, pl.ds(2 * shift + head, half, stride=2), :]
-                        first = first + taps[None, :] * rows
-                    out[lane, :half] = act(first)
-                    out[lane, half:] = in_ref[slot, head, half:]
-        queries = query_scr[...]
-        forget = forget_scr[...]
-        values = value_scr[...]
-        weights = jnp.zeros((4, DRAFT, DK), F32)
-        decay = jnp.ones((4, 1, DK), F32)
-        head_rows = []
-        query_rows = []
-        for t in range(DRAFT):
-            forget_t = forget[:, t : t + 1, :]
-            query_t = queries[:, t : t + 1, :]
-            decay = decay * forget_t
-            weights = jnp.where(sub_iota == t, 1.0 - forget_t, weights * forget_t)
-            scores = jnp.sum(weights * query_t, axis=-1, keepdims=True)
-            head_rows.append(jnp.sum(scores * values, axis=1, keepdims=True))
-            query_rows.append(query_t * decay)
-        local_out = jnp.concatenate(head_rows, axis=1)
-        decayed = jnp.concatenate(query_rows, axis=1)
-        for sub in range(2):
-            slot = base + sub
-            parity = lax.axis_index("req") % 2
-            near_row = (1 - parity) * HALF + slot
-            far_row = parity * HALF + slot - HALF
-            row = jnp.where(slot < HALF, near_row, far_row)
-            for head in range(2):
-                lane = sub * 2 + head
-                fine = decayed[lane]
-                coarse = fine.astype(BF)
-                stacked = jnp.concatenate([coarse, (fine - coarse.astype(F32)).astype(BF)], axis=0)
-                both = jnp.dot(
-                    stacked, states[slot, block_of(head), :], preferred_element_type=F32
-                )
-                out = local_out[lane] + (both[:DRAFT] + both[DRAFT:])
-                scale = lax.rsqrt(jnp.mean(out * out, axis=-1, keepdims=True) + 1e-05)
-                mixed_ref[row, :, block_of(head)] = (
-                    out * scale * gain_ref[head, :][None, :]
-                ).astype(BF)
-        return 0
-
-    lax.fori_loop(0, ROWS // 2, pair, 0)
-
-
-def mixer_call(owner, near, far, from_near, from_far, queries, forget, values, conv, bias, gain):
-    return call(
-        mixer, jax.ShapeDtypeStruct((ROWS, DRAFT, 2 * DK), BF), [SM] + [VM] * 10,
-        [
-            pltpu.VMEM((ROWS, 3, 24, DK), F32),
-            pltpu.VMEM((ROWS, 2 * DK, DK), BF),
-            pltpu.VMEM((4, DRAFT, DK), F32),
-            pltpu.VMEM((4, DRAFT, DK), F32),
-            pltpu.VMEM((4, DRAFT, DK), F32),
-        ],
-        20_000_000, 2_000_000,
-        owner, near, far, from_near, from_far, queries, forget, values, conv, bias, gain,
     )
 
 
@@ -675,18 +555,10 @@
         owner_row, near_mixed, far, from_far, queries, forget, values, conv, gain, out_weight
     )
     mixed = mixed.reshape(slots, -1)
-    mixed, part, gate_weight, up_weight, down_weight = lax.optimization_barrier(
-        (mixed, part, gate_weight, up_weight, down_weight)
-    )
     part = swapped(part, 2)
     one = swapped(mixed, 1)
     three = swapped(mixed, 3)
-    gate_t, up_t, down = fetch_call(
-        in_hbm(gate_weight.T), in_hbm(up_weight.T), in_hbm(down_weight)
-    )
-    part, one, three, gate_t, up_t, down = lax.optimization_barrier(
-        (part, one, three, gate_t, up_t, down)
-    )
+    gate_t, up_t, down = gate_weight.T, up_weight.T, down_weight
     stream = project_call(mixed, one, three, out_weight, parts, part, resid.reshape(slots, -1))
     two = swapped(stream, 2)
     three = swapped(stream, 3)

time: 50.1 us -> 49.7 us (level)
  Pallas kernels: 16.6 us -> 13.1 us
  waiting for transfers between devices: 9.32 us -> 11.9 us
    pallas_call x8 -> x7, Pallas kernels: 16.6 us -> 13.1 us  [call(): pl.pallas_call(kernel, name=kernel.__name__, out_shape=out_shape, in_spec...]
    ppermute x11, waiting for transfers between devices: 7.99 us -> 10.8 us  [swapped(): return lax.ppermute(block, 'grp', [(i, i ^ step) for i in range(4)])]
  transfers between devices with their start and end apart: 13 -> 13, of which waited for: 6 -> 6; matrix products, arithmetic and copies ran while one was open for 0% -> 0% of each run, Pallas kernels for 26% -> 19%
where the time goes in v10:
time: 49.7 us; the launch traced here: 49.4 us
  starting transfers between devices  22.4 us (45%)
  Pallas kernels  13.1 us (26%)
  waiting for transfers between devices  11.9 us (24%)
  between operations  0.76 us (2%)
  other arithmetic  0.73 us (1%)
    ppermute x11, starting transfers between devices, swapped(): return lax.ppermute(block, 'grp', [(i, i ^ step) for i in range(4)])  13.9 us
    pallas_call x7, Pallas kernels, call(): pl.pallas_call(kernel, name=kernel.__name__, out_shape=out_shape, in_spec...  13.1 us
    ppermute x11, waiting for transfers between devices, swapped(): return lax.ppermute(block, 'grp', [(i, i ^ step) for i in range(4)])  10.8 us
    ppermute x1, starting transfers between devices, shards(): from_far = lax.ppermute(far, 'req', across)  8.41 us
    ppermute x1, waiting for transfers between devices, shards(): from_far = lax.ppermute(far, 'req', across)  1.19 us
  transfers between devices with their start and end apart: 13, of which 6 were waited for; matrix products, arithmetic and copies ran while one was open for 0% of the time, Pallas kernels for 19%

profile of v10, /device:TPU:6, one launch (start us, length us, event | category | flops | bytes accessed | tf_op | source)
XLA Modules:
  0.0 49.4 jit_solution(11978168831955100406)
XLA Ops:
  0.6 0.0 copy-start.2
  0.6 0.0 copy-start.4
  0.7 1.7 %pack.1 = (bf16[4,400,128]{2,1,0:T(8,128)(2,1)S(1)}, bf16[4,400,128]{2,1,0:T(8,128)(2,1)S(1)}, bf16[256,512]{1,0:T(8,128)(2,1)S(1)}, bf16[256,512]{1,0:T(8,128)(2,1)S(1)}) custom-call(f32[8,2,128,128]{3,2,1,0:T(8,128)} %state_ref.3, bf16[8,3,2,384]{3,2,1,0:T(2,128)(2,1)} %edge_ref.1, bf16[8,16,2,384]{3,2,1,0:T(2,128)(2,1)} %draft_ref.1, ...), custom_call_target="tpu_custom_call" | custom-call | flops 1000000 | bytes 3000000 | tf_op jit(solution)/shard_map/pack/pallas_call | solution.py:49
  2.4 0.1 collective-permute-start
  2.5 8.4 %collective-permute-start.1 = (bf16[4,400,128]{2,1,0:T(8,128)(2,1)S(1)}, bf16[4,400,128]{2,1,0:T(8,128)(2,1)S(1)}, u32[]{:S(2)}, u32[]{:S(2)}) collective-permute-start(bf16[4,400,128]{2,1,0:T(8,128)(2,1)S(1)} %get-tuple-element.29.far_ref), channel_id=1, source_target_pairs={{0,63},{1,2},{2,1},{3,4},{4,3},{5,6},{6,5},{7,8},{8,7},{9,10},{10,... | collective-permute-start | bytes 1228808 | tf_op jit(solution)/shard_map/ppermute | solution.py:547
  10.9 0.8 %collective-permute-start.4 = (bf16[256,512]{1,0:T(8,128)(2,1)S(1)}, bf16[256,512]{1,0:T(8,128)(2,1)S(1)}, u32[]{:S(2)}, u32[]{:S(2)}) collective-permute-start(bf16[256,512]{1,0:T(8,128)(2,1)S(1)} %get-tuple-element.37), channel_id=1, source_target_pairs={{0,64},{64,0},{128,192},{192,128},{1,65},{65,1},{129,193},{193,129... | collective-permute-start | bytes 786440 | tf_op jit(solution)/shard_map/ppermute | solution.py:519
  11.7 0.0 copy-start
  11.7 0.0 copy-start.1
  11.7 0.0 copy-start.5
  11.8 1.1 %collective-permute-start.5 = (bf16[256,512]{1,0:T(8,128)(2,1)S(1)}, bf16[256,512]{1,0:T(8,128)(2,1)S(1)}, u32[]{:S(2)}, u32[]{:S(2)}) collective-permute-start(bf16[256,512]{1,0:T(8,128)(2,1)S(1)} %get-tuple-element.38), channel_id=1, source_target_pairs={{0,192},{64,128},{128,64},{192,0},{1,193},{65,129},{129,65},{193,1... | collective-permute-start | bytes 786440 | tf_op jit(solution)/shard_map/ppermute | solution.py:519
  12.9 0.0 collective-permute-done.from_near_ref
  12.9 2.5 %mix_near.1 = (bf16[4,16,256]{2,1,0:T(8,128)(2,1)S(1)}, f32[4,2,16,128]{3,2,1,0:T(8,128)S(1)}, f32[4,2,16,128]{3,2,1,0:T(8,128)S(1)}, f32[4,2,16,128]{3,2,1,0:T(...) custom-call(s32[512]{0:T(512)} %owner_ref.5, ...), custom_call_target="tpu_custom_call" | custom-call | flops 15000000 | bytes 3000000 | tf_op jit(solution)/shard_map/mix_near/pallas_call | solution.py:49
  15.4 1.2 %collective-permute-done.1.from_far_ref = bf16[4,400,128]{2,1,0:T(8,128)(2,1)S(1)} collective-permute-done((bf16[4,400,128]{2,1,0:T(8,128)(2,1)S(1)}, bf16[4,400,128]{2,1,0:T(8,128)(2,1)S(1)}, u32[]{:S(2)}, u32[]{:S(2)}) %collective-permute-start.1) | collective-permute-done | bytes 409632 | tf_op jit(solution)/shard_map/ppermute | solution.py:547
  16.6 0.0 copy-done.2
  16.6 1.7 %mix_far.1 = (bf16[8,16,256]{2,1,0:T(8,128)(2,1)S(1)}, bf16[128,512]{1,0:T(8,128)(2,1)S(1)}) custom-call(s32[512]{0:T(512)} %owner_ref.5, bf16[4,16,256]{2,1,0:T(8,128)(2,1)S(1)} %get-tuple-element.30.near_mixed_ref, bf16[4,400,128]{2,1,0:T(8,128)(2,1)S(1)} %get-tuple-element.29.far_ref, bf16[4,400,128]{2,1,0:T(8,128)(2,1)S(1)} %collective-permute-done.1.from_far_ref, ...), custom_call_target="tpu_custom_call" | custom-call | flops 50000000 | bytes 2000000 | tf_op jit(solution)/shard_map/mix_far/pallas_call | solution.py:49
  18.2 1.5 %collective-permute-start.6 = (bf16[128,512]{1,0:T(8,128)(2,1)S(1)}, bf16[128,512]{1,0:T(8,128)(2,1)S(1)}, u32[]{:S(2)}, u32[]{:S(2)}) collective-permute-start(bf16[128,512]{1,0:T(8,128)(2,1)S(1)} %get-tuple-element.39), channel_id=1, source_target_pairs={{0,128},{64,192},{128,0},{192,64},{1,129},{65,193},{129,1},{193,65... | collective-permute-start | bytes 393224 | tf_op jit(solution)/shard_map/ppermute | solution.py:519
  19.7 2.1 %collective-permute-start.3 = (bf16[128,256]{1,0:T(8,128)(2,1)S(1)}, bf16[128,256]{1,0:T(8,128)(2,1)S(1)}, u32[]{:S(2)}, u32[]{:S(2)}) collective-permute-start(bf16[128,256]{1,0:T(8,128)(2,1)S(1)} %bitcast.11), channel_id=1, source_target_pairs={{0,192},{64,128},{128,64},{192,0},{1,193},{65,129},{129,65},{193,1... | collective-permute-start | bytes 196616 | tf_op jit(solution)/shard_map/ppermute | solution.py:519
  21.8 0.0 collective-permute-start.2
  21.8 0.0 collective-permute-done.4.from_one_ref
  21.8 0.0 collective-permute-done.5.from_three_ref
  21.8 4.5 %collective-permute-done.3.three_ref = bf16[128,256]{1,0:T(8,128)(2,1)S(1)} collective-permute-done((bf16[128,256]{1,0:T(8,128)(2,1)S(1)}, bf16[128,256]{1,0:T(8,128)(2,1)S(1)}, u32[]{:S(2)}, u32[]{:S(2)}) %collective-permute-start.3) | collective-permute-done | bytes 65568 | tf_op jit(solution)/shard_map/ppermute | solution.py:519
  26.3 0.5 collective-permute-done.2.one_ref
  26.8 0.0 collective-permute-done.6.part_ref
  26.8 0.0 copy-done.4
  26.8 0.3 project.1.own_ref
  27.1 2.6 %collective-permute-start.9 = (bf16[128,512]{1,0:T(8,128)(2,1)S(1)}, bf16[128,512]{1,0:T(8,128)(2,1)S(1)}, u32[]{:S(2)}, u32[]{:S(2)}) collective-permute-start(bf16[128,512]{1,0:T(8,128)(2,1)S(1)} %project.1.own_ref), channel_id=1, source_target_pairs={{0,192},{64,128},{128,64},{192,0},{1,193},{65,129},{129,65},{193,1... | collective-permute-start | bytes 393224 | tf_op jit(solution)/shard_map/ppermute | solution.py:519
  29.7 0.3 collective-permute-start.8
  30.0 1.2 %collective-permute-start.7 = (bf16[128,512]{1,0:T(8,128)(2,1)S(1)}, bf16[128,512]{1,0:T(8,128)(2,1)S(1)}, u32[]{:S(2)}, u32[]{:S(2)}) collective-permute-start(bf16[128,512]{1,0:T(8,128)(2,1)S(1)} %project.1.own_ref), channel_id=1, source_target_pairs={{0,64},{64,0},{128,192},{192,128},{1,65},{65,1},{129,193},{193,129... | collective-permute-start | bytes 393224 | tf_op jit(solution)/shard_map/ppermute | solution.py:519
  31.2 2.4 %collective-permute-done.9.three_ref = bf16[128,512]{1,0:T(8,128)(2,1)S(1)} collective-permute-done((bf16[128,512]{1,0:T(8,128)(2,1)S(1)}, bf16[128,512]{1,0:T(8,128)(2,1)S(1)}, u32[]{:S(2)}, u32[]{:S(2)}) %collective-permute-start.9) | collective-permute-done | bytes 131104 | tf_op jit(solution)/shard_map/ppermute | solution.py:519
  33.6 2.7 %collective-permute-done.8.two_ref = bf16[128,512]{1,0:T(8,128)(2,1)S(1)} collective-permute-done((bf16[128,512]{1,0:T(8,128)(2,1)S(1)}, bf16[128,512]{1,0:T(8,128)(2,1)S(1)}, u32[]{:S(2)}, u32[]{:S(2)}) %collective-permute-start.8) | collective-permute-done | bytes 131104 | tf_op jit(solution)/shard_map/ppermute | solution.py:519
  36.3 0.0 copy-done
  36.3 0.0 copy-done.1
  36.3 0.0 copy-done.5
  36.3 0.0 copy-start.3
  36.4 1.4 %ffn_first.1 = (f32[128,128]{1,0:T(8,128)S(1)}, f32[128,704]{1,0:T(8,128)S(1)}, f32[128,704]{1,0:T(8,128)S(1)}) custom-call(bf16[128,512]{1,0:T(8,128)(2,1)S(1)} %project.1.own_ref, bf16[128,512]{1,0:T(8,128)(2,1)S(1)} %collective-permute-done.8.two_ref, bf16[128,512]{1,0:T(8,128)(2,1)S(1)} %collective-permute-done.9.three_ref, f32[1,2048]{1,0:T(1,128)S(1)} %bitcast.14, ...), custom_call_target="tpu_custom_call" | custom-call | flops 550000000 | bytes 5000000 | tf_op jit(solution)/shard_map/ffn_first/pallas_call | solution.py:49
  37.8 0.0 collective-permute-done.7.one_ref
  37.8 0.3 copy-done.3
  38.2 1.8 %ffn_last.1 = (f32[128,512]{1,0:T(8,128)S(1)}, bf16[128,512]{1,0:T(8,128)(2,1)S(1)}, bf16[128,512]{1,0:T(8,128)(2,1)S(1)}, bf16[128,512]{1,0:T(8,128)(2,1)S(1)}) custom-call(s32[512]{0:T(512)} %length_ref.1, bf16[128,512]{1,0:T(8,128)(2,1)S(1)} %project.1.own_ref, bf16[128,512]{1,0:T(8,128)(2,1)S(1)} %collective-permute-done.7.one_ref, ...), custom_call_target="tpu_custom_call" | custom-call | flops 550000000 | bytes 5000000 | tf_op jit(solution)/shard_map/ffn_last/pallas_call | solution.py:49
  40.0 1.5 %collective-permute-start.10 = (bf16[128,512]{1,0:T(8,128)(2,1)S(1)}, bf16[128,512]{1,0:T(8,128)(2,1)S(1)}, u32[]{:S(2)}, u32[]{:S(2)}) collective-permute-start(bf16[128,512]{1,0:T(8,128)(2,1)S(1)} %get-tuple-element.45), channel_id=1, source_target_pairs={{0,128},{64,192},{128,0},{192,64},{1,129},{65,193},{129,1},{193,65... | collective-permute-start | bytes 393224 | tf_op jit(solution)/shard_map/ppermute | solution.py:519
  41.5 1.0 %collective-permute-start.11 = (bf16[128,512]{1,0:T(8,128)(2,1)S(1)}, bf16[128,512]{1,0:T(8,128)(2,1)S(1)}, u32[]{:S(2)}, u32[]{:S(2)}) collective-permute-start(bf16[128,512]{1,0:T(8,128)(2,1)S(1)} %get-tuple-element.46), channel_id=1, source_target_pairs={{0,64},{64,0},{128,192},{192,128},{1,65},{65,1},{129,193},{193,129... | collective-permute-start | bytes 393224 | tf_op jit(solution)/shard_map/ppermute | solution.py:519
  42.5 1.7 %collective-permute-start.12 = (bf16[128,512]{1,0:T(8,128)(2,1)S(1)}, bf16[128,512]{1,0:T(8,128)(2,1)S(1)}, u32[]{:S(2)}, u32[]{:S(2)}) collective-permute-start(bf16[128,512]{1,0:T(8,128)(2,1)S(1)} %get-tuple-element.47), channel_id=1, source_target_pairs={{0,192},{64,128},{128,64},{192,0},{1,193},{65,129},{129,65},{193,1... | collective-permute-start | bytes 393224 | tf_op jit(solution)/shard_map/ppermute | solution.py:519
  44.2 3.7 %keep.1 = (f32[8,2,128,128]{3,2,1,0:T(8,128)}, bf16[8,3,2,384]{3,2,1,0:T(2,128)(2,1)}) custom-call(s32[512]{0:T(512)} %owner_ref.5, s32[512]{0:T(512)} %accept_ref.1, bf16[4,400,128]{2,1,0:T(8,128)(2,1)S(1)} %get-tuple-element.28.near_ref, bf16[4,400,128]{2,1,0:T(8,128)(2,1)S(1)} %get-tuple-element.29.far_ref, ...), custom_call_target="tpu_custom_call" | custom-call | flops 20000000 | bytes 3000000 | tf_op jit(solution)/shard_map/keep/pallas_call | solution.py:49
  47.9 0.0 collective-permute-done.10
  47.9 0.0 collective-permute-done.11
  47.9 0.7 %collective-permute-done.12 = bf16[128,512]{1,0:T(8,128)(2,1)S(1)} collective-permute-done((bf16[128,512]{1,0:T(8,128)(2,1)S(1)}, bf16[128,512]{1,0:T(8,128)(2,1)S(1)}, u32[]{:S(2)}, u32[]{:S(2)}) %collective-permute-start.12) | collective-permute-done | bytes 131104 | tf_op jit(solution)/shard_map/ppermute | solution.py:519
  48.6 0.7 %add_convert_fusion = bf16[128,512]{1,0:T(8,128)(2,1)} fusion(bf16[128,512]{1,0:T(8,128)(2,1)S(1)} %collective-permute-done.12, bf16[128,512]{1,0:T(8,128)(2,1)S(1)} %collective-permute-done.11, f32[128,512]{1,0:T(8,128)S(1)} %get-tuple-element.44, bf16[128,512]{1,0:T(8,128)(2,1)S(1)} %collective-permute-done.10), kind=kLoop, calls=%fused_computation | loop fusion | flops 458752 | bytes 786432 | tf_op jit(solution)/shard_map/convert_element_type | solution.py:578
Async XLA Ops:
  0.6 15.9 %copy-start.2 = (bf16[256,2048]{1,0:T(8,128)(2,1)S(1)}, bf16[256,2048]{1,0:T(8,128)(2,1)}, u32[]{:S(2)}) copy-start(bf16[256,2048]{1,0:T(8,128)(2,1)} %weight_ref.5) | copy-start | bytes 3145732
  0.6 26.1 %copy-start.4 = (bf16[8,16,2048]{2,1,0:T(8,128)(2,1)S(1)}, bf16[8,16,2048]{2,1,0:T(8,128)(2,1)}, u32[]{:S(2)}) copy-start(bf16[8,16,2048]{2,1,0:T(8,128)(2,1)} %param.20) | copy-start | bytes 1572868
  2.4 10.5 %collective-permute-start = (bf16[4,400,128]{2,1,0:T(8,128)(2,1)S(1)}, bf16[4,400,128]{2,1,0:T(8,128)(2,1)S(1)}, u32[]{:S(2)}, u32[]{:S(2)}) collective-permute-start(bf16[4,400,128]{2,1,0:T(8,128)(2,1)S(1)} %get-tuple-element.28.near_ref), channel_id=1, source_target_pairs={{0,1},{1,0},{2,3},{3,2},{4,5},{5,4},{6,7},{7,6},{8,9},{9,8},{10,11... | collective-permute-start | bytes 1228808 | tf_op jit(solution)/shard_map/ppermute | solution.py:548
  2.5 14.0 %collective-permute-start.1 = (bf16[4,400,128]{2,1,0:T(8,128)(2,1)S(1)}, bf16[4,400,128]{2,1,0:T(8,128)(2,1)S(1)}, u32[]{:S(2)}, u32[]{:S(2)}) collective-permute-start(bf16[4,400,128]{2,1,0:T(8,128)(2,1)S(1)} %get-tuple-element.29.far_ref), channel_id=1, source_target_pairs={{0,63},{1,2},{2,1},{3,4},{4,3},{5,6},{6,5},{7,8},{8,7},{9,10},{10,... | collective-permute-start | bytes 1228808 | tf_op jit(solution)/shard_map/ppermute | solution.py:547
  10.9 10.9 %collective-permute-start.4 = (bf16[256,512]{1,0:T(8,128)(2,1)S(1)}, bf16[256,512]{1,0:T(8,128)(2,1)S(1)}, u32[]{:S(2)}, u32[]{:S(2)}) collective-permute-start(bf16[256,512]{1,0:T(8,128)(2,1)S(1)} %get-tuple-element.37), channel_id=1, source_target_pairs={{0,64},{64,0},{128,192},{192,128},{1,65},{65,1},{129,193},{193,129... | collective-permute-start | bytes 786440 | tf_op jit(solution)/shard_map/ppermute | solution.py:519
  11.7 24.6 %copy-start = (bf16[2048,704]{0,1:T(8,128)(2,1)S(1)}, bf16[2048,704]{0,1:T(8,128)(2,1)}, u32[]{:S(2)}) copy-start(bf16[2048,704]{0,1:T(8,128)(2,1)} %param.22) | copy-start | bytes 8650756
  11.7 24.6 %copy-start.1 = (bf16[2048,704]{0,1:T(8,128)(2,1)S(1)}, bf16[2048,704]{0,1:T(8,128)(2,1)}, u32[]{:S(2)}) copy-start(bf16[2048,704]{0,1:T(8,128)(2,1)} %param.23) | copy-start | bytes 8650756
  11.7 24.6 %copy-start.5 = (f32[2048]{0:T(1024)S(1)}, f32[2048]{0:T(1024)}, u32[]{:S(2)}) copy-start(f32[2048]{0:T(1024)} %param.21) | copy-start | bytes 24580
  11.8 10.1 %collective-permute-start.5 = (bf16[256,512]{1,0:T(8,128)(2,1)S(1)}, bf16[256,512]{1,0:T(8,128)(2,1)S(1)}, u32[]{:S(2)}, u32[]{:S(2)}) collective-permute-start(bf16[256,512]{1,0:T(8,128)(2,1)S(1)} %get-tuple-element.38), channel_id=1, source_target_pairs={{0,192},{64,128},{128,64},{192,0},{1,193},{65,129},{129,65},{193,1... | collective-permute-start | bytes 786440 | tf_op jit(solution)/shard_map/ppermute | solution.py:519
  18.2 8.6 %collective-permute-start.6 = (bf16[128,512]{1,0:T(8,128)(2,1)S(1)}, bf16[128,512]{1,0:T(8,128)(2,1)S(1)}, u32[]{:S(2)}, u32[]{:S(2)}) collective-permute-start(bf16[128,512]{1,0:T(8,128)(2,1)S(1)} %get-tuple-element.39), channel_id=1, source_target_pairs={{0,128},{64,192},{128,0},{192,64},{1,129},{65,193},{129,1},{193,65... | collective-permute-start | bytes 393224 | tf_op jit(solution)/shard_map/ppermute | solution.py:519
  19.7 6.6 %collective-permute-start.3 = (bf16[128,256]{1,0:T(8,128)(2,1)S(1)}, bf16[128,256]{1,0:T(8,128)(2,1)S(1)}, u32[]{:S(2)}, u32[]{:S(2)}) collective-permute-start(bf16[128,256]{1,0:T(8,128)(2,1)S(1)} %bitcast.11), channel_id=1, source_target_pairs={{0,192},{64,128},{128,64},{192,0},{1,193},{65,129},{129,65},{193,1... | collective-permute-start | bytes 196616 | tf_op jit(solution)/shard_map/ppermute | solution.py:519
  21.8 5.0 %collective-permute-start.2 = (bf16[128,256]{1,0:T(8,128)(2,1)S(1)}, bf16[128,256]{1,0:T(8,128)(2,1)S(1)}, u32[]{:S(2)}, u32[]{:S(2)}) collective-permute-start(bf16[128,256]{1,0:T(8,128)(2,1)S(1)} %bitcast.12), channel_id=1, source_target_pairs={{0,64},{64,0},{128,192},{192,128},{1,65},{65,1},{129,193},{193,129... | collective-permute-start | bytes 196616 | tf_op jit(solution)/shard_map/ppermute | solution.py:519
  27.1 6.5 %collective-permute-start.9 = (bf16[128,512]{1,0:T(8,128)(2,1)S(1)}, bf16[128,512]{1,0:T(8,128)(2,1)S(1)}, u32[]{:S(2)}, u32[]{:S(2)}) collective-permute-start(bf16[128,512]{1,0:T(8,128)(2,1)S(1)} %project.1.own_ref), channel_id=1, source_target_pairs={{0,192},{64,128},{128,64},{192,0},{1,193},{65,129},{129,65},{193,1... | collective-permute-start | bytes 393224 | tf_op jit(solution)/shard_map/ppermute | solution.py:519
  29.7 6.6 %collective-permute-start.8 = (bf16[128,512]{1,0:T(8,128)(2,1)S(1)}, bf16[128,512]{1,0:T(8,128)(2,1)S(1)}, u32[]{:S(2)}, u32[]{:S(2)}) collective-permute-start(bf16[128,512]{1,0:T(8,128)(2,1)S(1)} %project.1.own_ref), channel_id=1, source_target_pairs={{0,128},{64,192},{128,0},{192,64},{1,129},{65,193},{129,1},{193,65... | collective-permute-start | bytes 393224 | tf_op jit(solution)/shard_map/ppermute | solution.py:519
  30.0 7.8 %collective-permute-start.7 = (bf16[128,512]{1,0:T(8,128)(2,1)S(1)}, bf16[128,512]{1,0:T(8,128)(2,1)S(1)}, u32[]{:S(2)}, u32[]{:S(2)}) collective-permute-start(bf16[128,512]{1,0:T(8,128)(2,1)S(1)} %project.1.own_ref), channel_id=1, source_target_pairs={{0,64},{64,0},{128,192},{192,128},{1,65},{65,1},{129,193},{193,129... | collective-permute-start | bytes 393224 | tf_op jit(solution)/shard_map/ppermute | solution.py:519
  36.3 1.8 %copy-start.3 = (bf16[704,2048]{1,0:T(8,128)(2,1)S(1)}, bf16[704,2048]{1,0:T(8,128)(2,1)}, u32[]{:S(2)}) copy-start(bf16[704,2048]{1,0:T(8,128)(2,1)} %down_ref.1) | copy-start | bytes 8650756
  40.0 7.9 %collective-permute-start.10 = (bf16[128,512]{1,0:T(8,128)(2,1)S(1)}, bf16[128,512]{1,0:T(8,128)(2,1)S(1)}, u32[]{:S(2)}, u32[]{:S(2)}) collective-permute-start(bf16[128,512]{1,0:T(8,128)(2,1)S(1)} %get-tuple-element.45), channel_id=1, source_target_pairs={{0,128},{64,192},{128,0},{192,64},{1,129},{65,193},{129,1},{193,65... | collective-permute-start | bytes 393224 | tf_op jit(solution)/shard_map/ppermute | solution.py:519
  41.5 6.4 %collective-permute-start.11 = (bf16[128,512]{1,0:T(8,128)(2,1)S(1)}, bf16[128,512]{1,0:T(8,128)(2,1)S(1)}, u32[]{:S(2)}, u32[]{:S(2)}) collective-permute-start(bf16[128,512]{1,0:T(8,128)(2,1)S(1)} %get-tuple-element.46), channel_id=1, source_target_pairs={{0,64},{64,0},{128,192},{192,128},{1,65},{65,1},{129,193},{193,129... | collective-permute-start | bytes 393224 | tf_op jit(solution)/shard_map/ppermute | solution.py:519
  42.5 6.2 %collective-permute-start.12 = (bf16[128,512]{1,0:T(8,128)(2,1)S(1)}, bf16[128,512]{1,0:T(8,128)(2,1)S(1)}, u32[]{:S(2)}, u32[]{:S(2)}) collective-permute-start(bf16[128,512]{1,0:T(8,128)(2,1)S(1)} %get-tuple-element.47), channel_id=1, source_target_pairs={{0,192},{64,128},{128,64},{192,0},{1,193},{65,129},{129,65},{193,1... | collective-permute-start | bytes 393224 | tf_op jit(solution)/shard_map/ppermute | solution.py:519

commit v11 on v10

--- a/solution.py
+++ b/solution.py
@@ -63,69 +63,78 @@
     return pl.ds(pl.multiple_of(place * width, width), width)
 
 
-def pack(
-    state_ref, edge_ref, draft_ref, weight_ref, far_ref, near_ref, one_ref, three_ref,
+def fill_pack(half, out_ref, state_ref, edge_ref, draft_ref, states, edges, drafts, sems):
+    rows = pl.ds(row_of(half, 0), HALF)
+    state_copy = pltpu.make_async_copy(state_ref.at[rows], states, sems.at[0])
+    edge_copy = pltpu.make_async_copy(edge_ref.at[rows], edges, sems.at[1])
+    draft_copy = pltpu.make_async_copy(draft_ref.at[rows], drafts, sems.at[2])
+    draft_copy.start()
+    edge_copy.start()
+    state_copy.start()
+    edge_copy.wait()
+    draft_copy.wait()
+    for place in range(HALF):
+        for block in range(3):
+            columns = block_of(block)
+            out_ref[place, edges_of(block), :] = jnp.zeros((DRAFT, DK), BF)
+            start = EDGES_AT + block * DRAFT
+            for step in range(CONV - 1):
+                out_ref[place, start + 2 * step : start + 2 * step + 2, :] = edges[
+                    place, step, :, columns
+                ]
+            start = DRAFTS_AT + block * 2 * DRAFT
+            for step in range(DRAFT):
+                out_ref[place, start + 2 * step : start + 2 * step + 2, :] = drafts[
+                    place, step, :, columns
+                ]
+    state_copy.wait()
+    for place in range(HALF):
+        for head in range(2):
+            out_ref[place, block_of(head), :] = states[place, head].astype(BF)
+
+
+def pack_far(state_ref, edge_ref, draft_ref, far_ref, states, edges, drafts, sems):
+    fill_pack(1, far_ref, state_ref, edge_ref, draft_ref, states, edges, drafts, sems)
+
+
+def pack_near(
+    state_ref, edge_ref, draft_ref, weight_ref, near_ref, one_ref, three_ref,
     states, edges, drafts, sems,
 ):
     width = one_ref.shape[1]
     cuts = [
         pltpu.make_async_copy(
-            weight_ref.at[:, columns_of(step, width)], out_ref, sems.at[ROWS + 2 + i]
+            weight_ref.at[:, columns_of(step, width)], out_ref, sems.at[3 + i]
         )
         for i, (step, out_ref) in enumerate(((1, one_ref), (3, three_ref)))
     ]
-    copies = [
-        pltpu.make_async_copy(state_ref.at[row], states.at[row], sems.at[row])
-        for row in range(ROWS)
-    ]
-    edge_copy = pltpu.make_async_copy(edge_ref, edges, sems.at[ROWS])
-    draft_copy = pltpu.make_async_copy(draft_ref, drafts, sems.at[ROWS + 1])
-    draft_copy.start()
-    edge_copy.start()
-    for copy in copies:
-        copy.start()
     for copy in cuts:
         copy.start()
-    edge_copy.wait()
-    draft_copy.wait()
-    for half, out_ref in ((1, far_ref), (0, near_ref)):
-        for place in range(HALF):
-            row = row_of(half, place)
-            for block in range(3):
-                columns = block_of(block)
-                out_ref[place, edges_of(block), :] = jnp.zeros((DRAFT, DK), BF)
-                start = EDGES_AT + block * DRAFT
-                for step in range(CONV - 1):
-                    out_ref[place, start + 2 * step : start + 2 * step + 2, :] = edges[
-                        row, step, :, columns
-                    ]
-                start = DRAFTS_AT + block * 2 * DRAFT
-                for step in range(DRAFT):
-                    out_ref[place, start + 2 * step : start + 2 * step + 2, :] = drafts[
-                        row, step, :, columns
-                    ]
-    for copy in copies:
-        copy.wait()
-    for half, out_ref in ((1, far_ref), (0, near_ref)):
-        for place in range(HALF):
-            for head in range(2):
-                out_ref[place, block_of(head), :] = states[row_of(half, place), head].astype(BF)
+    fill_pack(0, near_ref, state_ref, edge_ref, draft_ref, states, edges, drafts, sems)
     for copy in cuts:
         copy.wait()
 
 
-def pack_call(states, edges, drafts, weight):
+def pack_scratch(states, edges, drafts):
+    return [
+        pltpu.VMEM((HALF, *states.shape[1:]), F32),
+        pltpu.VMEM((HALF, *edges.shape[1:]), BF),
+        pltpu.VMEM((HALF, *drafts.shape[1:]), BF),
+        pltpu.SemaphoreType.DMA((5,)),
+    ]
+
+
+def pack_far_call(*args):
+    half = jax.ShapeDtypeStruct((HALF, PACKED + DRAFT, DK), BF)
+    return call(pack_far, half, [HB] * 3, pack_scratch(*args), 500_000, 1_000_000, *args)
+
+
+def pack_near_call(states, edges, drafts, weight):
     half = jax.ShapeDtypeStruct((HALF, PACKED, DK), BF)
     cut = jax.ShapeDtypeStruct((weight.shape[0], weight.shape[1] // 4), BF)
     return call(
-        pack, (half, half, cut, cut), [HB] * 4,
-        [
-            pltpu.VMEM(states.shape, F32),
-            pltpu.VMEM(edges.shape, BF),
-            pltpu.VMEM(drafts.shape, BF),
-            pltpu.SemaphoreType.DMA((ROWS + 4,)),
-        ],
-        1_000_000, 3_000_000, states, edges, drafts, weight,
+        pack_near, (half, cut, cut), [HB] * 4, pack_scratch(states, edges, drafts),
+        500_000, 2_000_000, states, edges, drafts, weight,
     )
 
 
@@ -540,11 +549,11 @@
     owner_row, accepted, draft_lengths = in_hbm(owner_row), in_hbm(accepted), in_hbm(draft_lengths)
     count = lax.axis_size("req")
     states = in_hbm(held_states)
-    far, near, *cuts = pack_call(
-        states, in_hbm(held_edges), in_hbm(mix_inputs), in_hbm(out_weight)
-    )
     across = [(i, (i + (1 if i % 2 else -1)) % count) for i in range(count)]
+    held, drafts = in_hbm(held_edges), in_hbm(mix_inputs)
+    far = pack_far_call(states, held, drafts)
     from_far = lax.ppermute(far, "req", across)
+    near, *cuts = pack_near_call(states, held, drafts, in_hbm(out_weight))
     from_near = lax.ppermute(near, "req", [(i, i ^ 1) for i in range(count)])
     parts = [swapped(cut, step) for step, cut in ((1, cuts[0]), (3, cuts[1]))]
     near_mixed, queries, forget, values, conv, bias, gain = mix_near_call(

time: 49.7 us -> 49.5 us (level)
  Pallas kernels: 13.1 us -> 14 us
  waiting for transfers between devices: 11.9 us -> 11 us
    ppermute x1, waiting for transfers between devices: 1.19 us -> 0.01 us  [shards(): from_far = lax.ppermute(far, 'req', across)]
    pallas_call x7 -> x8, Pallas kernels: 13.1 us -> 14 us  [call(): pl.pallas_call(kernel, name=kernel.__name__, out_shape=out_shape, in_spec...]
    ppermute x1, starting transfers between devices: 8.41 us -> 7.83 us  [shards(): from_far = lax.ppermute(far, 'req', across)]
  transfers between devices with their start and end apart: 13 -> 13, of which waited for: 6 -> 5; matrix products, arithmetic and copies ran while one was open for 0% -> 0% of each run, Pallas kernels for 19% -> 22%
where the time goes in v11:
time: 49.5 us; the launch traced here: 49 us
  starting transfers between devices  22.1 us (45%)
  Pallas kernels  14 us (28%)
  waiting for transfers between devices  11 us (22%)
  between operations  0.78 us (2%)
  other arithmetic  0.73 us (1%)
    ppermute x11, starting transfers between devices, swapped(): return lax.ppermute(block, 'grp', [(i, i ^ step) for i in range(4)])  14.1 us
    pallas_call x8, Pallas kernels, call(): pl.pallas_call(kernel, name=kernel.__name__, out_shape=out_shape, in_spec...  14 us
    ppermute x11, waiting for transfers between devices, swapped(): return lax.ppermute(block, 'grp', [(i, i ^ step) for i in range(4)])  11 us
    ppermute x1, starting transfers between devices, shards(): from_far = lax.ppermute(far, 'req', across)  7.83 us
  transfers between devices with their start and end apart: 13, of which 5 were waited for; matrix products, arithmetic and copies ran while one was open for 0% of the time, Pallas kernels for 22%

profile of v11, /device:TPU:6, one launch (start us, length us, event | category | flops | bytes accessed | tf_op | source)
XLA Modules:
  0.0 49.0 jit_solution(3877301678794076573)
XLA Ops:
  0.6 0.0 copy-start.2
  0.6 1.3 %pack_far.1.far_ref = bf16[4,416,128]{2,1,0:T(8,128)(2,1)S(1)} custom-call(f32[8,2,128,128]{3,2,1,0:T(8,128)} %state_ref.5, bf16[8,3,2,384]{3,2,1,0:T(2,128)(2,1)} %edge_ref.3, bf16[8,16,2,384]{3,2,1,0:T(2,128)(2,1)} %draft_ref.3), custom_call_target="tpu_custom_call" | custom-call | flops 500000 | bytes 1000000 | tf_op jit(solution)/shard_map/pack_far/pallas_call | solution.py:49
  1.9 0.0 copy-start.4
  1.9 7.8 %collective-permute-start.1 = (bf16[4,416,128]{2,1,0:T(8,128)(2,1)S(1)}, bf16[4,416,128]{2,1,0:T(8,128)(2,1)S(1)}, u32[]{:S(2)}, u32[]{:S(2)}) collective-permute-start(bf16[4,416,128]{2,1,0:T(8,128)(2,1)S(1)} %pack_far.1.far_ref), channel_id=1, source_target_pairs={{0,63},{1,2},{2,1},{3,4},{4,3},{5,6},{6,5},{7,8},{8,7},{9,10},{10,... | collective-permute-start | bytes 1277960 | tf_op jit(solution)/shard_map/ppermute | solution.py:555
  9.8 1.3 %pack_near.1 = (bf16[4,400,128]{2,1,0:T(8,128)(2,1)S(1)}, bf16[256,512]{1,0:T(8,128)(2,1)S(1)}, bf16[256,512]{1,0:T(8,128)(2,1)S(1)}) custom-call(f32[8,2,128,128]{3,2,1,0:T(8,128)} %state_ref.5, bf16[8,3,2,384]{3,2,1,0:T(2,128)(2,1)} %edge_ref.3, bf16[8,16,2,384]{3,2,1,0:T(2,128)(2,1)} %draft_ref.3, bf16[256,2048]{1,0:T(8,128)(2,1)} %weight_ref.5), custom_call_target="tpu_custom_call" | custom-call | flops 500000 | bytes 2000000 | tf_op jit(solution)/shard_map/pack_near/pallas_call | solution.py:49
  11.1 0.1 collective-permute-start
  11.2 0.9 %collective-permute-start.4 = (bf16[256,512]{1,0:T(8,128)(2,1)S(1)}, bf16[256,512]{1,0:T(8,128)(2,1)S(1)}, u32[]{:S(2)}, u32[]{:S(2)}) collective-permute-start(bf16[256,512]{1,0:T(8,128)(2,1)S(1)} %get-tuple-element.35), channel_id=1, source_target_pairs={{0,64},{64,0},{128,192},{192,128},{1,65},{65,1},{129,193},{193,129... | collective-permute-start | bytes 786440 | tf_op jit(solution)/shard_map/ppermute | solution.py:528
  12.1 0.0 copy-start
  12.1 0.0 copy-start.1
  12.1 0.0 copy-start.5
  12.1 1.1 %collective-permute-start.5 = (bf16[256,512]{1,0:T(8,128)(2,1)S(1)}, bf16[256,512]{1,0:T(8,128)(2,1)S(1)}, u32[]{:S(2)}, u32[]{:S(2)}) collective-permute-start(bf16[256,512]{1,0:T(8,128)(2,1)S(1)} %get-tuple-element.36), channel_id=1, source_target_pairs={{0,192},{64,128},{128,64},{192,0},{1,193},{65,129},{129,65},{193,1... | collective-permute-start | bytes 786440 | tf_op jit(solution)/shard_map/ppermute | solution.py:528
  13.3 0.0 collective-permute-done.from_near_ref
  13.3 2.5 %mix_near.1 = (bf16[4,16,256]{2,1,0:T(8,128)(2,1)S(1)}, f32[4,2,16,128]{3,2,1,0:T(8,128)S(1)}, f32[4,2,16,128]{3,2,1,0:T(8,128)S(1)}, f32[4,2,16,128]{3,2,1,0:T(...) custom-call(s32[512]{0:T(512)} %owner_ref.5, ...), custom_call_target="tpu_custom_call" | custom-call | flops 15000000 | bytes 3000000 | tf_op jit(solution)/shard_map/mix_near/pallas_call | solution.py:49
  15.7 0.0 collective-permute-done.1.from_far_ref
  15.7 0.0 copy-done.2
  15.8 1.7 %mix_far.1 = (bf16[8,16,256]{2,1,0:T(8,128)(2,1)S(1)}, bf16[128,512]{1,0:T(8,128)(2,1)S(1)}) custom-call(s32[512]{0:T(512)} %owner_ref.5, bf16[4,16,256]{2,1,0:T(8,128)(2,1)S(1)} %get-tuple-element.28.near_mixed_ref, bf16[4,416,128]{2,1,0:T(8,128)(2,1)S(1)} %pack_far.1.far_ref, bf16[4,416,128]{2,1,0:T(8,128)(2,1)S(1)} %collective-permute-done.1.from_far_ref, ...), custom_call_target="tpu_custom_call" | custom-call | flops 50000000 | bytes 2000000 | tf_op jit(solution)/shard_map/mix_far/pallas_call | solution.py:49
  17.4 2.1 %collective-permute-start.6 = (bf16[128,512]{1,0:T(8,128)(2,1)S(1)}, bf16[128,512]{1,0:T(8,128)(2,1)S(1)}, u32[]{:S(2)}, u32[]{:S(2)}) collective-permute-start(bf16[128,512]{1,0:T(8,128)(2,1)S(1)} %get-tuple-element.37), channel_id=1, source_target_pairs={{0,128},{64,192},{128,0},{192,64},{1,129},{65,193},{129,1},{193,65... | collective-permute-start | bytes 393224 | tf_op jit(solution)/shard_map/ppermute | solution.py:528
  19.5 1.6 %collective-permute-start.3 = (bf16[128,256]{1,0:T(8,128)(2,1)S(1)}, bf16[128,256]{1,0:T(8,128)(2,1)S(1)}, u32[]{:S(2)}, u32[]{:S(2)}) collective-permute-start(bf16[128,256]{1,0:T(8,128)(2,1)S(1)} %bitcast.11), channel_id=1, source_target_pairs={{0,192},{64,128},{128,64},{192,0},{1,193},{65,129},{129,65},{193,1... | collective-permute-start | bytes 196616 | tf_op jit(solution)/shard_map/ppermute | solution.py:528
  21.1 0.0 collective-permute-start.2
  21.1 0.0 collective-permute-done.4.from_one_ref
  21.1 3.3 %collective-permute-done.5.from_three_ref = bf16[256,512]{1,0:T(8,128)(2,1)S(1)} collective-permute-done((bf16[256,512]{1,0:T(8,128)(2,1)S(1)}, bf16[256,512]{1,0:T(8,128)(2,1)S(1)}, u32[]{:S(2)}, u32[]{:S(2)}) %collective-permute-start.5) | collective-permute-done | bytes 262176 | tf_op jit(solution)/shard_map/ppermute | solution.py:528
  24.5 1.5 %collective-permute-done.3.three_ref = bf16[128,256]{1,0:T(8,128)(2,1)S(1)} collective-permute-done((bf16[128,256]{1,0:T(8,128)(2,1)S(1)}, bf16[128,256]{1,0:T(8,128)(2,1)S(1)}, u32[]{:S(2)}, u32[]{:S(2)}) %collective-permute-start.3) | collective-permute-done | bytes 65568 | tf_op jit(solution)/shard_map/ppermute | solution.py:528
  25.9 0.0 collective-permute-done.2.one_ref
  25.9 0.0 collective-permute-done.6.part_ref
  25.9 0.0 copy-done.4
  25.9 0.3 project.1.own_ref
  26.2 1.8 %collective-permute-start.9 = (bf16[128,512]{1,0:T(8,128)(2,1)S(1)}, bf16[128,512]{1,0:T(8,128)(2,1)S(1)}, u32[]{:S(2)}, u32[]{:S(2)}) collective-permute-start(bf16[128,512]{1,0:T(8,128)(2,1)S(1)} %project.1.own_ref), channel_id=1, source_target_pairs={{0,192},{64,128},{128,64},{192,0},{1,193},{65,129},{129,65},{193,1... | collective-permute-start | bytes 393224 | tf_op jit(solution)/shard_map/ppermute | solution.py:528
  28.0 1.1 %collective-permute-start.8 = (bf16[128,512]{1,0:T(8,128)(2,1)S(1)}, bf16[128,512]{1,0:T(8,128)(2,1)S(1)}, u32[]{:S(2)}, u32[]{:S(2)}) collective-permute-start(bf16[128,512]{1,0:T(8,128)(2,1)S(1)} %project.1.own_ref), channel_id=1, source_target_pairs={{0,128},{64,192},{128,0},{192,64},{1,129},{65,193},{129,1},{193,65... | collective-permute-start | bytes 393224 | tf_op jit(solution)/shard_map/ppermute | solution.py:528
  29.2 1.2 %collective-permute-start.7 = (bf16[128,512]{1,0:T(8,128)(2,1)S(1)}, bf16[128,512]{1,0:T(8,128)(2,1)S(1)}, u32[]{:S(2)}, u32[]{:S(2)}) collective-permute-start(bf16[128,512]{1,0:T(8,128)(2,1)S(1)} %project.1.own_ref), channel_id=1, source_target_pairs={{0,64},{64,0},{128,192},{192,128},{1,65},{65,1},{129,193},{193,129... | collective-permute-start | bytes 393224 | tf_op jit(solution)/shard_map/ppermute | solution.py:528
  30.4 5.3 %collective-permute-done.9.three_ref = bf16[128,512]{1,0:T(8,128)(2,1)S(1)} collective-permute-done((bf16[128,512]{1,0:T(8,128)(2,1)S(1)}, bf16[128,512]{1,0:T(8,128)(2,1)S(1)}, u32[]{:S(2)}, u32[]{:S(2)}) %collective-permute-start.9) | collective-permute-done | bytes 131104 | tf_op jit(solution)/shard_map/ppermute | solution.py:528
  35.7 0.3 collective-permute-done.8.two_ref
  35.9 0.0 copy-done
  35.9 0.0 copy-done.1
  36.0 0.0 copy-done.5
  36.0 0.0 copy-start.3
  36.0 1.5 %ffn_first.1 = (f32[128,128]{1,0:T(8,128)S(1)}, f32[128,704]{1,0:T(8,128)S(1)}, f32[128,704]{1,0:T(8,128)S(1)}) custom-call(bf16[128,512]{1,0:T(8,128)(2,1)S(1)} %project.1.own_ref, bf16[128,512]{1,0:T(8,128)(2,1)S(1)} %collective-permute-done.8.two_ref, bf16[128,512]{1,0:T(8,128)(2,1)S(1)} %collective-permute-done.9.three_ref, f32[1,2048]{1,0:T(1,128)S(1)} %bitcast.14, ...), custom_call_target="tpu_custom_call" | custom-call | flops 550000000 | bytes 5000000 | tf_op jit(solution)/shard_map/ffn_first/pallas_call | solution.py:49
  37.4 0.0 collective-permute-done.7.one_ref
  37.4 0.3 copy-done.3
  37.8 1.8 %ffn_last.1 = (f32[128,512]{1,0:T(8,128)S(1)}, bf16[128,512]{1,0:T(8,128)(2,1)S(1)}, bf16[128,512]{1,0:T(8,128)(2,1)S(1)}, bf16[128,512]{1,0:T(8,128)(2,1)S(1)}) custom-call(s32[512]{0:T(512)} %length_ref.1, bf16[128,512]{1,0:T(8,128)(2,1)S(1)} %project.1.own_ref, bf16[128,512]{1,0:T(8,128)(2,1)S(1)} %collective-permute-done.7.one_ref, ...), custom_call_target="tpu_custom_call" | custom-call | flops 550000000 | bytes 5000000 | tf_op jit(solution)/shard_map/ffn_last/pallas_call | solution.py:49
  39.6 1.2 %collective-permute-start.10 = (bf16[128,512]{1,0:T(8,128)(2,1)S(1)}, bf16[128,512]{1,0:T(8,128)(2,1)S(1)}, u32[]{:S(2)}, u32[]{:S(2)}) collective-permute-start(bf16[128,512]{1,0:T(8,128)(2,1)S(1)} %get-tuple-element.43), channel_id=1, source_target_pairs={{0,128},{64,192},{128,0},{192,64},{1,129},{65,193},{129,1},{193,65... | collective-permute-start | bytes 393224 | tf_op jit(solution)/shard_map/ppermute | solution.py:528
  40.8 1.3 %collective-permute-start.11 = (bf16[128,512]{1,0:T(8,128)(2,1)S(1)}, bf16[128,512]{1,0:T(8,128)(2,1)S(1)}, u32[]{:S(2)}, u32[]{:S(2)}) collective-permute-start(bf16[128,512]{1,0:T(8,128)(2,1)S(1)} %get-tuple-element.44), channel_id=1, source_target_pairs={{0,64},{64,0},{128,192},{192,128},{1,65},{65,1},{129,193},{193,129... | collective-permute-start | bytes 393224 | tf_op jit(solution)/shard_map/ppermute | solution.py:528
  42.1 1.7 %collective-permute-start.12 = (bf16[128,512]{1,0:T(8,128)(2,1)S(1)}, bf16[128,512]{1,0:T(8,128)(2,1)S(1)}, u32[]{:S(2)}, u32[]{:S(2)}) collective-permute-start(bf16[128,512]{1,0:T(8,128)(2,1)S(1)} %get-tuple-element.45), channel_id=1, source_target_pairs={{0,192},{64,128},{128,64},{192,0},{1,193},{65,129},{129,65},{193,1... | collective-permute-start | bytes 393224 | tf_op jit(solution)/shard_map/ppermute | solution.py:528
  43.8 3.7 %keep.1 = (f32[8,2,128,128]{3,2,1,0:T(8,128)}, bf16[8,3,2,384]{3,2,1,0:T(2,128)(2,1)}) custom-call(s32[512]{0:T(512)} %owner_ref.5, s32[512]{0:T(512)} %accept_ref.1, bf16[4,400,128]{2,1,0:T(8,128)(2,1)S(1)} %get-tuple-element.27.near_ref, bf16[4,416,128]{2,1,0:T(8,128)(2,1)S(1)} %pack_far.1.far_ref, ...), custom_call_target="tpu_custom_call" | custom-call | flops 20000000 | bytes 3000000 | tf_op jit(solution)/shard_map/keep/pallas_call | solution.py:49
  47.5 0.0 collective-permute-done.10
  47.5 0.0 collective-permute-done.11
  47.6 0.7 %collective-permute-done.12 = bf16[128,512]{1,0:T(8,128)(2,1)S(1)} collective-permute-done((bf16[128,512]{1,0:T(8,128)(2,1)S(1)}, bf16[128,512]{1,0:T(8,128)(2,1)S(1)}, u32[]{:S(2)}, u32[]{:S(2)}) %collective-permute-start.12) | collective-permute-done | bytes 131104 | tf_op jit(solution)/shard_map/ppermute | solution.py:528
  48.3 0.7 %add_convert_fusion = bf16[128,512]{1,0:T(8,128)(2,1)} fusion(bf16[128,512]{1,0:T(8,128)(2,1)S(1)} %collective-permute-done.12, bf16[128,512]{1,0:T(8,128)(2,1)S(1)} %collective-permute-done.11, f32[128,512]{1,0:T(8,128)S(1)} %get-tuple-element.42, bf16[128,512]{1,0:T(8,128)(2,1)S(1)} %collective-permute-done.10), kind=kLoop, calls=%fused_computation | loop fusion | flops 458752 | bytes 786432 | tf_op jit(solution)/shard_map/convert_element_type | solution.py:587
Async XLA Ops:
  0.6 15.1 %copy-start.2 = (bf16[256,2048]{1,0:T(8,128)(2,1)S(1)}, bf16[256,2048]{1,0:T(8,128)(2,1)}, u32[]{:S(2)}) copy-start(bf16[256,2048]{1,0:T(8,128)(2,1)} %weight_ref.5) | copy-start | bytes 3145732
  1.9 24.0 %copy-start.4 = (bf16[8,16,2048]{2,1,0:T(8,128)(2,1)S(1)}, bf16[8,16,2048]{2,1,0:T(8,128)(2,1)}, u32[]{:S(2)}) copy-start(bf16[8,16,2048]{2,1,0:T(8,128)(2,1)} %param.20) | copy-start | bytes 1572868
  1.9 13.8 %collective-permute-start.1 = (bf16[4,416,128]{2,1,0:T(8,128)(2,1)S(1)}, bf16[4,416,128]{2,1,0:T(8,128)(2,1)S(1)}, u32[]{:S(2)}, u32[]{:S(2)}) collective-permute-start(bf16[4,416,128]{2,1,0:T(8,128)(2,1)S(1)} %pack_far.1.far_ref), channel_id=1, source_target_pairs={{0,63},{1,2},{2,1},{3,4},{4,3},{5,6},{6,5},{7,8},{8,7},{9,10},{10,... | collective-permute-start | bytes 1277960 | tf_op jit(solution)/shard_map/ppermute | solution.py:555
  11.1 2.2 %collective-permute-start = (bf16[4,400,128]{2,1,0:T(8,128)(2,1)S(1)}, bf16[4,400,128]{2,1,0:T(8,128)(2,1)S(1)}, u32[]{:S(2)}, u32[]{:S(2)}) collective-permute-start(bf16[4,400,128]{2,1,0:T(8,128)(2,1)S(1)} %get-tuple-element.27.near_ref), channel_id=1, source_target_pairs={{0,1},{1,0},{2,3},{3,2},{4,5},{5,4},{6,7},{7,6},{8,9},{9,8},{10,11... | collective-permute-start | bytes 1228808 | tf_op jit(solution)/shard_map/ppermute | solution.py:557
  11.2 9.9 %collective-permute-start.4 = (bf16[256,512]{1,0:T(8,128)(2,1)S(1)}, bf16[256,512]{1,0:T(8,128)(2,1)S(1)}, u32[]{:S(2)}, u32[]{:S(2)}) collective-permute-start(bf16[256,512]{1,0:T(8,128)(2,1)S(1)} %get-tuple-element.35), channel_id=1, source_target_pairs={{0,64},{64,0},{128,192},{192,128},{1,65},{65,1},{129,193},{193,129... | collective-permute-start | bytes 786440 | tf_op jit(solution)/shard_map/ppermute | solution.py:528
  12.1 23.8 %copy-start = (bf16[2048,704]{0,1:T(8,128)(2,1)S(1)}, bf16[2048,704]{0,1:T(8,128)(2,1)}, u32[]{:S(2)}) copy-start(bf16[2048,704]{0,1:T(8,128)(2,1)} %param.22) | copy-start | bytes 8650756
  12.1 23.8 %copy-start.1 = (bf16[2048,704]{0,1:T(8,128)(2,1)S(1)}, bf16[2048,704]{0,1:T(8,128)(2,1)}, u32[]{:S(2)}) copy-start(bf16[2048,704]{0,1:T(8,128)(2,1)} %param.23) | copy-start | bytes 8650756
  12.1 23.8 %copy-start.5 = (f32[2048]{0:T(1024)S(1)}, f32[2048]{0:T(1024)}, u32[]{:S(2)}) copy-start(f32[2048]{0:T(1024)} %param.21) | copy-start | bytes 24580
  12.1 12.3 %collective-permute-start.5 = (bf16[256,512]{1,0:T(8,128)(2,1)S(1)}, bf16[256,512]{1,0:T(8,128)(2,1)S(1)}, u32[]{:S(2)}, u32[]{:S(2)}) collective-permute-start(bf16[256,512]{1,0:T(8,128)(2,1)S(1)} %get-tuple-element.36), channel_id=1, source_target_pairs={{0,192},{64,128},{128,64},{192,0},{1,193},{65,129},{129,65},{193,1... | collective-permute-start | bytes 786440 | tf_op jit(solution)/shard_map/ppermute | solution.py:528
  17.4 8.5 %collective-permute-start.6 = (bf16[128,512]{1,0:T(8,128)(2,1)S(1)}, bf16[128,512]{1,0:T(8,128)(2,1)S(1)}, u32[]{:S(2)}, u32[]{:S(2)}) collective-permute-start(bf16[128,512]{1,0:T(8,128)(2,1)S(1)} %get-tuple-element.37), channel_id=1, source_target_pairs={{0,128},{64,192},{128,0},{192,64},{1,129},{65,193},{129,1},{193,65... | collective-permute-start | bytes 393224 | tf_op jit(solution)/shard_map/ppermute | solution.py:528
  19.5 6.4 %collective-permute-start.3 = (bf16[128,256]{1,0:T(8,128)(2,1)S(1)}, bf16[128,256]{1,0:T(8,128)(2,1)S(1)}, u32[]{:S(2)}, u32[]{:S(2)}) collective-permute-start(bf16[128,256]{1,0:T(8,128)(2,1)S(1)} %bitcast.11), channel_id=1, source_target_pairs={{0,192},{64,128},{128,64},{192,0},{1,193},{65,129},{129,65},{193,1... | collective-permute-start | bytes 196616 | tf_op jit(solution)/shard_map/ppermute | solution.py:528
  21.1 4.8 %collective-permute-start.2 = (bf16[128,256]{1,0:T(8,128)(2,1)S(1)}, bf16[128,256]{1,0:T(8,128)(2,1)S(1)}, u32[]{:S(2)}, u32[]{:S(2)}) collective-permute-start(bf16[128,256]{1,0:T(8,128)(2,1)S(1)} %bitcast.12), channel_id=1, source_target_pairs={{0,64},{64,0},{128,192},{192,128},{1,65},{65,1},{129,193},{193,129... | collective-permute-start | bytes 196616 | tf_op jit(solution)/shard_map/ppermute | solution.py:528
  26.2 9.5 %collective-permute-start.9 = (bf16[128,512]{1,0:T(8,128)(2,1)S(1)}, bf16[128,512]{1,0:T(8,128)(2,1)S(1)}, u32[]{:S(2)}, u32[]{:S(2)}) collective-permute-start(bf16[128,512]{1,0:T(8,128)(2,1)S(1)} %project.1.own_ref), channel_id=1, source_target_pairs={{0,192},{64,128},{128,64},{192,0},{1,193},{65,129},{129,65},{193,1... | collective-permute-start | bytes 393224 | tf_op jit(solution)/shard_map/ppermute | solution.py:528
  28.0 7.9 %collective-permute-start.8 = (bf16[128,512]{1,0:T(8,128)(2,1)S(1)}, bf16[128,512]{1,0:T(8,128)(2,1)S(1)}, u32[]{:S(2)}, u32[]{:S(2)}) collective-permute-start(bf16[128,512]{1,0:T(8,128)(2,1)S(1)} %project.1.own_ref), channel_id=1, source_target_pairs={{0,128},{64,192},{128,0},{192,64},{1,129},{65,193},{129,1},{193,65... | collective-permute-start | bytes 393224 | tf_op jit(solution)/shard_map/ppermute | solution.py:528
  29.2 8.2 %collective-permute-start.7 = (bf16[128,512]{1,0:T(8,128)(2,1)S(1)}, bf16[128,512]{1,0:T(8,128)(2,1)S(1)}, u32[]{:S(2)}, u32[]{:S(2)}) collective-permute-start(bf16[128,512]{1,0:T(8,128)(2,1)S(1)} %project.1.own_ref), channel_id=1, source_target_pairs={{0,64},{64,0},{128,192},{192,128},{1,65},{65,1},{129,193},{193,129... | collective-permute-start | bytes 393224 | tf_op jit(solution)/shard_map/ppermute | solution.py:528
  36.0 1.8 %copy-start.3 = (bf16[704,2048]{1,0:T(8,128)(2,1)S(1)}, bf16[704,2048]{1,0:T(8,128)(2,1)}, u32[]{:S(2)}) copy-start(bf16[704,2048]{1,0:T(8,128)(2,1)} %down_ref.1) | copy-start | bytes 8650756
  39.6 7.9 %collective-permute-start.10 = (bf16[128,512]{1,0:T(8,128)(2,1)S(1)}, bf16[128,512]{1,0:T(8,128)(2,1)S(1)}, u32[]{:S(2)}, u32[]{:S(2)}) collective-permute-start(bf16[128,512]{1,0:T(8,128)(2,1)S(1)} %get-tuple-element.43), channel_id=1, source_target_pairs={{0,128},{64,192},{128,0},{192,64},{1,129},{65,193},{129,1},{193,65... | collective-permute-start | bytes 393224 | tf_op jit(solution)/shard_map/ppermute | solution.py:528
  40.8 6.7 %collective-permute-start.11 = (bf16[128,512]{1,0:T(8,128)(2,1)S(1)}, bf16[128,512]{1,0:T(8,128)(2,1)S(1)}, u32[]{:S(2)}, u32[]{:S(2)}) collective-permute-start(bf16[128,512]{1,0:T(8,128)(2,1)S(1)} %get-tuple-element.44), channel_id=1, source_target_pairs={{0,64},{64,0},{128,192},{192,128},{1,65},{65,1},{129,193},{193,129... | collective-permute-start | bytes 393224 | tf_op jit(solution)/shard_map/ppermute | solution.py:528
  42.1 6.2 %collective-permute-start.12 = (bf16[128,512]{1,0:T(8,128)(2,1)S(1)}, bf16[128,512]{1,0:T(8,128)(2,1)S(1)}, u32[]{:S(2)}, u32[]{:S(2)}) collective-permute-start(bf16[128,512]{1,0:T(8,128)(2,1)S(1)} %get-tuple-element.45), channel_id=1, source_target_pairs={{0,192},{64,128},{128,64},{192,0},{1,193},{65,129},{129,65},{193,1... | collective-permute-start | bytes 393224 | tf_op jit(solution)/shard_map/ppermute | solution.py:528

commit v12 on v11

--- a/solution.py
+++ b/solution.py
@@ -219,11 +219,12 @@
                         taps = conv_ref[shift, head, block_of(block)]
                         rows = edges[slot, block, pl.ds(2 * shift + head, half, stride=2), :]
                         first = first + taps[None, :] * rows
-                    out[lane, :half] = act(first)
-                    out[lane, half:] = in_ref[slot, head, half:]
-        queries = query_scr[...]
-        forget = forget_scr[...]
-        values = value_scr[...]
+                    out[4 * step + lane, :half] = act(first)
+                    out[4 * step + lane, half:] = in_ref[slot, head, half:]
+        lanes = slice(4 * step, 4 * step + 4)
+        queries = query_scr[lanes]
+        forget = forget_scr[lanes]
+        values = value_scr[lanes]
         weights = jnp.zeros((4, DRAFT, DK), F32)
         decay = jnp.ones((4, 1, DK), F32)
         head_rows = []
@@ -253,15 +254,16 @@
                 store(slot, head, (out * scale * gain_ref[head, :][None, :]).astype(BF))
         return 0
 
-    lax.fori_loop(0, HALF // 2, pair, 0)
+    for step in range(HALF // 2):
+        pair(step, 0)
 
 
 MIX_SCRATCH = [
     pltpu.VMEM((HALF, 3, 24, DK), F32),
     pltpu.VMEM((HALF, 2 * DK, DK), BF),
-    pltpu.VMEM((4, DRAFT, DK), F32),
-    pltpu.VMEM((4, DRAFT, DK), F32),
-    pltpu.VMEM((4, DRAFT, DK), F32),
+    pltpu.VMEM((8, DRAFT, DK), F32),
+    pltpu.VMEM((8, DRAFT, DK), F32),
+    pltpu.VMEM((8, DRAFT, DK), F32),
 ]
 
 

time: 49.5 us -> 49.3 us (level)
  transfers between devices with their start and end apart: 13 -> 13, of which waited for: 5 -> 5; matrix products, arithmetic and copies ran while one was open for 0% -> 0% of each run, Pallas kernels for 22% -> 21%
where the time goes in v12:
time: 49.3 us; the launch traced here: 48.9 us
  starting transfers between devices  22.1 us (45%)
  Pallas kernels  13.7 us (28%)
  waiting for transfers between devices  11.3 us (23%)
  between operations  0.78 us (2%)
  other arithmetic  0.73 us (1%)
    ppermute x11, starting transfers between devices, swapped(): return lax.ppermute(block, 'grp', [(i, i ^ step) for i in range(4)])  14.1 us
    pallas_call x8, Pallas kernels, call(): pl.pallas_call(kernel, name=kernel.__name__, out_shape=out_shape, in_spec...  13.7 us
    ppermute x11, waiting for transfers between devices, swapped(): return lax.ppermute(block, 'grp', [(i, i ^ step) for i in range(4)])  11.3 us
    ppermute x1, starting transfers between devices, shards(): from_far = lax.ppermute(far, 'req', across)  7.83 us
  transfers between devices with their start and end apart: 13, of which 5 were waited for; matrix products, arithmetic and copies ran while one was open for 0% of the time, Pallas kernels for 21%

profile of v12, /device:TPU:6, one launch (start us, length us, event | category | flops | bytes accessed | tf_op | source)
XLA Modules:
  0.0 48.9 jit_solution(16109312678282543897)
XLA Ops:
  0.6 0.0 copy-start.2
  0.6 1.3 %pack_far.1.far_ref = bf16[4,416,128]{2,1,0:T(8,128)(2,1)S(1)} custom-call(f32[8,2,128,128]{3,2,1,0:T(8,128)} %state_ref.5, bf16[8,3,2,384]{3,2,1,0:T(2,128)(2,1)} %edge_ref.3, bf16[8,16,2,384]{3,2,1,0:T(2,128)(2,1)} %draft_ref.3), custom_call_target="tpu_custom_call" | custom-call | flops 500000 | bytes 1000000 | tf_op jit(solution)/shard_map/pack_far/pallas_call | solution.py:49
  1.9 0.0 copy-start.4
  1.9 7.8 %collective-permute-start.1 = (bf16[4,416,128]{2,1,0:T(8,128)(2,1)S(1)}, bf16[4,416,128]{2,1,0:T(8,128)(2,1)S(1)}, u32[]{:S(2)}, u32[]{:S(2)}) collective-permute-start(bf16[4,416,128]{2,1,0:T(8,128)(2,1)S(1)} %pack_far.1.far_ref), channel_id=1, source_target_pairs={{0,63},{1,2},{2,1},{3,4},{4,3},{5,6},{6,5},{7,8},{8,7},{9,10},{10,... | collective-permute-start | bytes 1277960 | tf_op jit(solution)/shard_map/ppermute | solution.py:557
  9.8 1.3 %pack_near.1 = (bf16[4,400,128]{2,1,0:T(8,128)(2,1)S(1)}, bf16[256,512]{1,0:T(8,128)(2,1)S(1)}, bf16[256,512]{1,0:T(8,128)(2,1)S(1)}) custom-call(f32[8,2,128,128]{3,2,1,0:T(8,128)} %state_ref.5, bf16[8,3,2,384]{3,2,1,0:T(2,128)(2,1)} %edge_ref.3, bf16[8,16,2,384]{3,2,1,0:T(2,128)(2,1)} %draft_ref.3, bf16[256,2048]{1,0:T(8,128)(2,1)} %weight_ref.5), custom_call_target="tpu_custom_call" | custom-call | flops 500000 | bytes 2000000 | tf_op jit(solution)/shard_map/pack_near/pallas_call | solution.py:49
  11.1 0.1 collective-permute-start
  11.2 0.9 %collective-permute-start.4 = (bf16[256,512]{1,0:T(8,128)(2,1)S(1)}, bf16[256,512]{1,0:T(8,128)(2,1)S(1)}, u32[]{:S(2)}, u32[]{:S(2)}) collective-permute-start(bf16[256,512]{1,0:T(8,128)(2,1)S(1)} %get-tuple-element.35), channel_id=1, source_target_pairs={{0,64},{64,0},{128,192},{192,128},{1,65},{65,1},{129,193},{193,129... | collective-permute-start | bytes 786440 | tf_op jit(solution)/shard_map/ppermute | solution.py:530
  12.1 0.0 copy-start
  12.1 0.0 copy-start.1
  12.1 0.0 copy-start.5
  12.1 1.1 %collective-permute-start.5 = (bf16[256,512]{1,0:T(8,128)(2,1)S(1)}, bf16[256,512]{1,0:T(8,128)(2,1)S(1)}, u32[]{:S(2)}, u32[]{:S(2)}) collective-permute-start(bf16[256,512]{1,0:T(8,128)(2,1)S(1)} %get-tuple-element.36), channel_id=1, source_target_pairs={{0,192},{64,128},{128,64},{192,0},{1,193},{65,129},{129,65},{193,1... | collective-permute-start | bytes 786440 | tf_op jit(solution)/shard_map/ppermute | solution.py:530
  13.3 0.0 collective-permute-done.from_near_ref
  13.3 2.3 %mix_near.1 = (bf16[4,16,256]{2,1,0:T(8,128)(2,1)S(1)}, f32[4,2,16,128]{3,2,1,0:T(8,128)S(1)}, f32[4,2,16,128]{3,2,1,0:T(8,128)S(1)}, f32[4,2,16,128]{3,2,1,0:T(...) custom-call(s32[512]{0:T(512)} %owner_ref.5, ...), custom_call_target="tpu_custom_call" | custom-call | flops 15000000 | bytes 3000000 | tf_op jit(solution)/shard_map/mix_near/pallas_call | solution.py:49
  15.6 0.0 collective-permute-done.1.from_far_ref
  15.6 0.0 copy-done.2
  15.6 1.5 %mix_far.1 = (bf16[8,16,256]{2,1,0:T(8,128)(2,1)S(1)}, bf16[128,512]{1,0:T(8,128)(2,1)S(1)}) custom-call(s32[512]{0:T(512)} %owner_ref.5, bf16[4,16,256]{2,1,0:T(8,128)(2,1)S(1)} %get-tuple-element.28.near_mixed_ref, bf16[4,416,128]{2,1,0:T(8,128)(2,1)S(1)} %pack_far.1.far_ref, bf16[4,416,128]{2,1,0:T(8,128)(2,1)S(1)} %collective-permute-done.1.from_far_ref, ...), custom_call_target="tpu_custom_call" | custom-call | flops 50000000 | bytes 2000000 | tf_op jit(solution)/shard_map/mix_far/pallas_call | solution.py:49
  17.1 2.1 %collective-permute-start.6 = (bf16[128,512]{1,0:T(8,128)(2,1)S(1)}, bf16[128,512]{1,0:T(8,128)(2,1)S(1)}, u32[]{:S(2)}, u32[]{:S(2)}) collective-permute-start(bf16[128,512]{1,0:T(8,128)(2,1)S(1)} %get-tuple-element.37), channel_id=1, source_target_pairs={{0,128},{64,192},{128,0},{192,64},{1,129},{65,193},{129,1},{193,65... | collective-permute-start | bytes 393224 | tf_op jit(solution)/shard_map/ppermute | solution.py:530
  19.2 1.6 %collective-permute-start.3 = (bf16[128,256]{1,0:T(8,128)(2,1)S(1)}, bf16[128,256]{1,0:T(8,128)(2,1)S(1)}, u32[]{:S(2)}, u32[]{:S(2)}) collective-permute-start(bf16[128,256]{1,0:T(8,128)(2,1)S(1)} %bitcast.11), channel_id=1, source_target_pairs={{0,192},{64,128},{128,64},{192,0},{1,193},{65,129},{129,65},{193,1... | collective-permute-start | bytes 196616 | tf_op jit(solution)/shard_map/ppermute | solution.py:530
  20.9 0.0 collective-permute-start.2
  20.9 0.0 collective-permute-done.4.from_one_ref
  20.9 3.9 %collective-permute-done.5.from_three_ref = bf16[256,512]{1,0:T(8,128)(2,1)S(1)} collective-permute-done((bf16[256,512]{1,0:T(8,128)(2,1)S(1)}, bf16[256,512]{1,0:T(8,128)(2,1)S(1)}, u32[]{:S(2)}, u32[]{:S(2)}) %collective-permute-start.5) | collective-permute-done | bytes 262176 | tf_op jit(solution)/shard_map/ppermute | solution.py:530
  24.8 1.1 %collective-permute-done.3.three_ref = bf16[128,256]{1,0:T(8,128)(2,1)S(1)} collective-permute-done((bf16[128,256]{1,0:T(8,128)(2,1)S(1)}, bf16[128,256]{1,0:T(8,128)(2,1)S(1)}, u32[]{:S(2)}, u32[]{:S(2)}) %collective-permute-start.3) | collective-permute-done | bytes 65568 | tf_op jit(solution)/shard_map/ppermute | solution.py:530
  25.9 0.0 collective-permute-done.2.one_ref
  25.9 0.0 collective-permute-done.6.part_ref
  25.9 0.0 copy-done.4
  25.9 0.3 project.1.own_ref
  26.2 1.6 %collective-permute-start.9 = (bf16[128,512]{1,0:T(8,128)(2,1)S(1)}, bf16[128,512]{1,0:T(8,128)(2,1)S(1)}, u32[]{:S(2)}, u32[]{:S(2)}) collective-permute-start(bf16[128,512]{1,0:T(8,128)(2,1)S(1)} %project.1.own_ref), channel_id=1, source_target_pairs={{0,192},{64,128},{128,64},{192,0},{1,193},{65,129},{129,65},{193,1... | collective-permute-start | bytes 393224 | tf_op jit(solution)/shard_map/ppermute | solution.py:530
  27.8 1.1 %collective-permute-start.8 = (bf16[128,512]{1,0:T(8,128)(2,1)S(1)}, bf16[128,512]{1,0:T(8,128)(2,1)S(1)}, u32[]{:S(2)}, u32[]{:S(2)}) collective-permute-start(bf16[128,512]{1,0:T(8,128)(2,1)S(1)} %project.1.own_ref), channel_id=1, source_target_pairs={{0,128},{64,192},{128,0},{192,64},{1,129},{65,193},{129,1},{193,65... | collective-permute-start | bytes 393224 | tf_op jit(solution)/shard_map/ppermute | solution.py:530
  28.9 1.5 %collective-permute-start.7 = (bf16[128,512]{1,0:T(8,128)(2,1)S(1)}, bf16[128,512]{1,0:T(8,128)(2,1)S(1)}, u32[]{:S(2)}, u32[]{:S(2)}) collective-permute-start(bf16[128,512]{1,0:T(8,128)(2,1)S(1)} %project.1.own_ref), channel_id=1, source_target_pairs={{0,64},{64,0},{128,192},{192,128},{1,65},{65,1},{129,193},{193,129... | collective-permute-start | bytes 393224 | tf_op jit(solution)/shard_map/ppermute | solution.py:530
  30.4 5.0 %collective-permute-done.9.three_ref = bf16[128,512]{1,0:T(8,128)(2,1)S(1)} collective-permute-done((bf16[128,512]{1,0:T(8,128)(2,1)S(1)}, bf16[128,512]{1,0:T(8,128)(2,1)S(1)}, u32[]{:S(2)}, u32[]{:S(2)}) %collective-permute-start.9) | collective-permute-done | bytes 131104 | tf_op jit(solution)/shard_map/ppermute | solution.py:530
  35.4 0.3 collective-permute-done.8.two_ref
  35.7 0.0 copy-done
  35.7 0.0 copy-done.1
  35.7 0.0 copy-done.5
  35.7 0.0 copy-start.3
  35.7 1.4 %ffn_first.1 = (f32[128,128]{1,0:T(8,128)S(1)}, f32[128,704]{1,0:T(8,128)S(1)}, f32[128,704]{1,0:T(8,128)S(1)}) custom-call(bf16[128,512]{1,0:T(8,128)(2,1)S(1)} %project.1.own_ref, bf16[128,512]{1,0:T(8,128)(2,1)S(1)} %collective-permute-done.8.two_ref, bf16[128,512]{1,0:T(8,128)(2,1)S(1)} %collective-permute-done.9.three_ref, f32[1,2048]{1,0:T(1,128)S(1)} %bitcast.14, ...), custom_call_target="tpu_custom_call" | custom-call | flops 550000000 | bytes 5000000 | tf_op jit(solution)/shard_map/ffn_first/pallas_call | solution.py:49
  37.1 0.0 collective-permute-done.7.one_ref
  37.1 0.3 copy-done.3
  37.5 1.8 %ffn_last.1 = (f32[128,512]{1,0:T(8,128)S(1)}, bf16[128,512]{1,0:T(8,128)(2,1)S(1)}, bf16[128,512]{1,0:T(8,128)(2,1)S(1)}, bf16[128,512]{1,0:T(8,128)(2,1)S(1)}) custom-call(s32[512]{0:T(512)} %length_ref.1, bf16[128,512]{1,0:T(8,128)(2,1)S(1)} %project.1.own_ref, bf16[128,512]{1,0:T(8,128)(2,1)S(1)} %collective-permute-done.7.one_ref, ...), custom_call_target="tpu_custom_call" | custom-call | flops 550000000 | bytes 5000000 | tf_op jit(solution)/shard_map/ffn_last/pallas_call | solution.py:49
  39.3 1.2 %collective-permute-start.10 = (bf16[128,512]{1,0:T(8,128)(2,1)S(1)}, bf16[128,512]{1,0:T(8,128)(2,1)S(1)}, u32[]{:S(2)}, u32[]{:S(2)}) collective-permute-start(bf16[128,512]{1,0:T(8,128)(2,1)S(1)} %get-tuple-element.43), channel_id=1, source_target_pairs={{0,128},{64,192},{128,0},{192,64},{1,129},{65,193},{129,1},{193,65... | collective-permute-start | bytes 393224 | tf_op jit(solution)/shard_map/ppermute | solution.py:530
  40.5 1.5 %collective-permute-start.11 = (bf16[128,512]{1,0:T(8,128)(2,1)S(1)}, bf16[128,512]{1,0:T(8,128)(2,1)S(1)}, u32[]{:S(2)}, u32[]{:S(2)}) collective-permute-start(bf16[128,512]{1,0:T(8,128)(2,1)S(1)} %get-tuple-element.44), channel_id=1, source_target_pairs={{0,64},{64,0},{128,192},{192,128},{1,65},{65,1},{129,193},{193,129... | collective-permute-start | bytes 393224 | tf_op jit(solution)/shard_map/ppermute | solution.py:530
  42.0 1.5 %collective-permute-start.12 = (bf16[128,512]{1,0:T(8,128)(2,1)S(1)}, bf16[128,512]{1,0:T(8,128)(2,1)S(1)}, u32[]{:S(2)}, u32[]{:S(2)}) collective-permute-start(bf16[128,512]{1,0:T(8,128)(2,1)S(1)} %get-tuple-element.45), channel_id=1, source_target_pairs={{0,192},{64,128},{128,64},{192,0},{1,193},{65,129},{129,65},{193,1... | collective-permute-start | bytes 393224 | tf_op jit(solution)/shard_map/ppermute | solution.py:530
  43.5 3.7 %keep.1 = (f32[8,2,128,128]{3,2,1,0:T(8,128)}, bf16[8,3,2,384]{3,2,1,0:T(2,128)(2,1)}) custom-call(s32[512]{0:T(512)} %owner_ref.5, s32[512]{0:T(512)} %accept_ref.1, bf16[4,400,128]{2,1,0:T(8,128)(2,1)S(1)} %get-tuple-element.27.near_ref, bf16[4,416,128]{2,1,0:T(8,128)(2,1)S(1)} %pack_far.1.far_ref, ...), custom_call_target="tpu_custom_call" | custom-call | flops 20000000 | bytes 3000000 | tf_op jit(solution)/shard_map/keep/pallas_call | solution.py:49
  47.3 0.0 collective-permute-done.10
  47.3 0.0 collective-permute-done.11
  47.3 0.9 %collective-permute-done.12 = bf16[128,512]{1,0:T(8,128)(2,1)S(1)} collective-permute-done((bf16[128,512]{1,0:T(8,128)(2,1)S(1)}, bf16[128,512]{1,0:T(8,128)(2,1)S(1)}, u32[]{:S(2)}, u32[]{:S(2)}) %collective-permute-start.12) | collective-permute-done | bytes 131104 | tf_op jit(solution)/shard_map/ppermute | solution.py:530
  48.2 0.7 %add_convert_fusion = bf16[128,512]{1,0:T(8,128)(2,1)} fusion(bf16[128,512]{1,0:T(8,128)(2,1)S(1)} %collective-permute-done.12, bf16[128,512]{1,0:T(8,128)(2,1)S(1)} %collective-permute-done.11, f32[128,512]{1,0:T(8,128)S(1)} %get-tuple-element.42, bf16[128,512]{1,0:T(8,128)(2,1)S(1)} %collective-permute-done.10), kind=kLoop, calls=%fused_computation | loop fusion | flops 458752 | bytes 786432 | tf_op jit(solution)/shard_map/convert_element_type | solution.py:589
Async XLA Ops:
  0.6 15.0 %copy-start.2 = (bf16[256,2048]{1,0:T(8,128)(2,1)S(1)}, bf16[256,2048]{1,0:T(8,128)(2,1)}, u32[]{:S(2)}) copy-start(bf16[256,2048]{1,0:T(8,128)(2,1)} %weight_ref.5) | copy-start | bytes 3145732
  1.9 24.0 %copy-start.4 = (bf16[8,16,2048]{2,1,0:T(8,128)(2,1)S(1)}, bf16[8,16,2048]{2,1,0:T(8,128)(2,1)}, u32[]{:S(2)}) copy-start(bf16[8,16,2048]{2,1,0:T(8,128)(2,1)} %param.20) | copy-start | bytes 1572868
  1.9 13.7 %collective-permute-start.1 = (bf16[4,416,128]{2,1,0:T(8,128)(2,1)S(1)}, bf16[4,416,128]{2,1,0:T(8,128)(2,1)S(1)}, u32[]{:S(2)}, u32[]{:S(2)}) collective-permute-start(bf16[4,416,128]{2,1,0:T(8,128)(2,1)S(1)} %pack_far.1.far_ref), channel_id=1, source_target_pairs={{0,63},{1,2},{2,1},{3,4},{4,3},{5,6},{6,5},{7,8},{8,7},{9,10},{10,... | collective-permute-start | bytes 1277960 | tf_op jit(solution)/shard_map/ppermute | solution.py:557
  11.1 2.2 %collective-permute-start = (bf16[4,400,128]{2,1,0:T(8,128)(2,1)S(1)}, bf16[4,400,128]{2,1,0:T(8,128)(2,1)S(1)}, u32[]{:S(2)}, u32[]{:S(2)}) collective-permute-start(bf16[4,400,128]{2,1,0:T(8,128)(2,1)S(1)} %get-tuple-element.27.near_ref), channel_id=1, source_target_pairs={{0,1},{1,0},{2,3},{3,2},{4,5},{5,4},{6,7},{7,6},{8,9},{9,8},{10,11... | collective-permute-start | bytes 1228808 | tf_op jit(solution)/shard_map/ppermute | solution.py:559
  11.2 9.7 %collective-permute-start.4 = (bf16[256,512]{1,0:T(8,128)(2,1)S(1)}, bf16[256,512]{1,0:T(8,128)(2,1)S(1)}, u32[]{:S(2)}, u32[]{:S(2)}) collective-permute-start(bf16[256,512]{1,0:T(8,128)(2,1)S(1)} %get-tuple-element.35), channel_id=1, source_target_pairs={{0,64},{64,0},{128,192},{192,128},{1,65},{65,1},{129,193},{193,129... | collective-permute-start | bytes 786440 | tf_op jit(solution)/shard_map/ppermute | solution.py:530
  12.1 23.6 %copy-start = (bf16[2048,704]{0,1:T(8,128)(2,1)S(1)}, bf16[2048,704]{0,1:T(8,128)(2,1)}, u32[]{:S(2)}) copy-start(bf16[2048,704]{0,1:T(8,128)(2,1)} %param.22) | copy-start | bytes 8650756
  12.1 23.6 %copy-start.1 = (bf16[2048,704]{0,1:T(8,128)(2,1)S(1)}, bf16[2048,704]{0,1:T(8,128)(2,1)}, u32[]{:S(2)}) copy-start(bf16[2048,704]{0,1:T(8,128)(2,1)} %param.23) | copy-start | bytes 8650756
  12.1 23.6 %copy-start.5 = (f32[2048]{0:T(1024)S(1)}, f32[2048]{0:T(1024)}, u32[]{:S(2)}) copy-start(f32[2048]{0:T(1024)} %param.21) | copy-start | bytes 24580
  12.1 12.7 %collective-permute-start.5 = (bf16[256,512]{1,0:T(8,128)(2,1)S(1)}, bf16[256,512]{1,0:T(8,128)(2,1)S(1)}, u32[]{:S(2)}, u32[]{:S(2)}) collective-permute-start(bf16[256,512]{1,0:T(8,128)(2,1)S(1)} %get-tuple-element.36), channel_id=1, source_target_pairs={{0,192},{64,128},{128,64},{192,0},{1,193},{65,129},{129,65},{193,1... | collective-permute-start | bytes 786440 | tf_op jit(solution)/shard_map/ppermute | solution.py:530
  17.1 8.8 %collective-permute-start.6 = (bf16[128,512]{1,0:T(8,128)(2,1)S(1)}, bf16[128,512]{1,0:T(8,128)(2,1)S(1)}, u32[]{:S(2)}, u32[]{:S(2)}) collective-permute-start(bf16[128,512]{1,0:T(8,128)(2,1)S(1)} %get-tuple-element.37), channel_id=1, source_target_pairs={{0,128},{64,192},{128,0},{192,64},{1,129},{65,193},{129,1},{193,65... | collective-permute-start | bytes 393224 | tf_op jit(solution)/shard_map/ppermute | solution.py:530
  19.2 6.7 %collective-permute-start.3 = (bf16[128,256]{1,0:T(8,128)(2,1)S(1)}, bf16[128,256]{1,0:T(8,128)(2,1)S(1)}, u32[]{:S(2)}, u32[]{:S(2)}) collective-permute-start(bf16[128,256]{1,0:T(8,128)(2,1)S(1)} %bitcast.11), channel_id=1, source_target_pairs={{0,192},{64,128},{128,64},{192,0},{1,193},{65,129},{129,65},{193,1... | collective-permute-start | bytes 196616 | tf_op jit(solution)/shard_map/ppermute | solution.py:530
  20.9 5.1 %collective-permute-start.2 = (bf16[128,256]{1,0:T(8,128)(2,1)S(1)}, bf16[128,256]{1,0:T(8,128)(2,1)S(1)}, u32[]{:S(2)}, u32[]{:S(2)}) collective-permute-start(bf16[128,256]{1,0:T(8,128)(2,1)S(1)} %bitcast.12), channel_id=1, source_target_pairs={{0,64},{64,0},{128,192},{192,128},{1,65},{65,1},{129,193},{193,129... | collective-permute-start | bytes 196616 | tf_op jit(solution)/shard_map/ppermute | solution.py:530
  26.2 9.2 %collective-permute-start.9 = (bf16[128,512]{1,0:T(8,128)(2,1)S(1)}, bf16[128,512]{1,0:T(8,128)(2,1)S(1)}, u32[]{:S(2)}, u32[]{:S(2)}) collective-permute-start(bf16[128,512]{1,0:T(8,128)(2,1)S(1)} %project.1.own_ref), channel_id=1, source_target_pairs={{0,192},{64,128},{128,64},{192,0},{1,193},{65,129},{129,65},{193,1... | collective-permute-start | bytes 393224 | tf_op jit(solution)/shard_map/ppermute | solution.py:530
  27.8 7.9 %collective-permute-start.8 = (bf16[128,512]{1,0:T(8,128)(2,1)S(1)}, bf16[128,512]{1,0:T(8,128)(2,1)S(1)}, u32[]{:S(2)}, u32[]{:S(2)}) collective-permute-start(bf16[128,512]{1,0:T(8,128)(2,1)S(1)} %project.1.own_ref), channel_id=1, source_target_pairs={{0,128},{64,192},{128,0},{192,64},{1,129},{65,193},{129,1},{193,65... | collective-permute-start | bytes 393224 | tf_op jit(solution)/shard_map/ppermute | solution.py:530
  28.9 8.2 %collective-permute-start.7 = (bf16[128,512]{1,0:T(8,128)(2,1)S(1)}, bf16[128,512]{1,0:T(8,128)(2,1)S(1)}, u32[]{:S(2)}, u32[]{:S(2)}) collective-permute-start(bf16[128,512]{1,0:T(8,128)(2,1)S(1)} %project.1.own_ref), channel_id=1, source_target_pairs={{0,64},{64,0},{128,192},{192,128},{1,65},{65,1},{129,193},{193,129... | collective-permute-start | bytes 393224 | tf_op jit(solution)/shard_map/ppermute | solution.py:530
  35.7 1.8 %copy-start.3 = (bf16[704,2048]{1,0:T(8,128)(2,1)S(1)}, bf16[704,2048]{1,0:T(8,128)(2,1)}, u32[]{:S(2)}) copy-start(bf16[704,2048]{1,0:T(8,128)(2,1)} %down_ref.1) | copy-start | bytes 8650756
  39.3 7.9 %collective-permute-start.10 = (bf16[128,512]{1,0:T(8,128)(2,1)S(1)}, bf16[128,512]{1,0:T(8,128)(2,1)S(1)}, u32[]{:S(2)}, u32[]{:S(2)}) collective-permute-start(bf16[128,512]{1,0:T(8,128)(2,1)S(1)} %get-tuple-element.43), channel_id=1, source_target_pairs={{0,128},{64,192},{128,0},{192,64},{1,129},{65,193},{129,1},{193,65... | collective-permute-start | bytes 393224 | tf_op jit(solution)/shard_map/ppermute | solution.py:530
  40.5 6.7 %collective-permute-start.11 = (bf16[128,512]{1,0:T(8,128)(2,1)S(1)}, bf16[128,512]{1,0:T(8,128)(2,1)S(1)}, u32[]{:S(2)}, u32[]{:S(2)}) collective-permute-start(bf16[128,512]{1,0:T(8,128)(2,1)S(1)} %get-tuple-element.44), channel_id=1, source_target_pairs={{0,64},{64,0},{128,192},{192,128},{1,65},{65,1},{129,193},{193,129... | collective-permute-start | bytes 393224 | tf_op jit(solution)/shard_map/ppermute | solution.py:530
  42.0 6.2 %collective-permute-start.12 = (bf16[128,512]{1,0:T(8,128)(2,1)S(1)}, bf16[128,512]{1,0:T(8,128)(2,1)S(1)}, u32[]{:S(2)}, u32[]{:S(2)}) collective-permute-start(bf16[128,512]{1,0:T(8,128)(2,1)S(1)} %get-tuple-element.45), channel_id=1, source_target_pairs={{0,192},{64,128},{128,64},{192,0},{1,193},{65,129},{129,65},{193,1... | collective-permute-start | bytes 393224 | tf_op jit(solution)/shard_map/ppermute | solution.py:530

commit v13 on v12

--- a/solution.py
+++ b/solution.py
@@ -579,14 +579,14 @@
     own_part, to_one, to_two, to_three = ffn_last_call(
         draft_lengths, stream, one, gain_row, gate_t, up_t, down, *partial
     )
+    three = swapped(to_three, 3)
     two = swapped(to_two, 2)
     one = swapped(to_one, 1)
-    three = swapped(to_three, 3)
     own_part, from_near, from_far = lax.optimization_barrier((own_part, from_near, from_far))
     kept_states, kept_edges = keep_call(
         owner_row, accepted, near, far, from_near, from_far, states, conv, bias
     )
-    layer_out = (own_part + two.astype(F32) + one.astype(F32) + three.astype(F32)).astype(BF)
+    layer_out = (own_part + three.astype(F32) + two.astype(F32) + one.astype(F32)).astype(BF)
     return (layer_out.reshape(ROWS, DRAFT, -1), kept_states, kept_edges)
 
 

time: 49.3 us -> 49.3 us (level)
  transfers between devices with their start and end apart: 13 -> 13, of which waited for: 5 -> 6; matrix products, arithmetic and copies ran while one was open for 0% -> 0% of each run, Pallas kernels for 21% -> 21%
where the time goes in v13:
time: 49.3 us; the launch traced here: 48.6 us
  starting transfers between devices  22.1 us (45%)
  Pallas kernels  13.7 us (28%)
  waiting for transfers between devices  10.9 us (22%)
  between operations  0.77 us (2%)
  other arithmetic  0.73 us (1%)
    ppermute x11, starting transfers between devices, swapped(): return lax.ppermute(block, 'grp', [(i, i ^ step) for i in range(4)])  14.1 us
    pallas_call x8, Pallas kernels, call(): pl.pallas_call(kernel, name=kernel.__name__, out_shape=out_shape, in_spec...  13.7 us
    ppermute x11, waiting for transfers between devices, swapped(): return lax.ppermute(block, 'grp', [(i, i ^ step) for i in range(4)])  10.9 us
    ppermute x1, starting transfers between devices, shards(): from_far = lax.ppermute(far, 'req', across)  7.83 us
  transfers between devices with their start and end apart: 13, of which 6 were waited for; matrix products, arithmetic and copies ran while one was open for 0% of the time, Pallas kernels for 21%

profile of v13, /device:TPU:6, one launch (start us, length us, event | category | flops | bytes accessed | tf_op | source)
XLA Modules:
  0.0 48.6 jit_solution(1504308565594442138)
XLA Ops:
  0.6 0.0 copy-start.2
  0.6 1.3 %pack_far.1.far_ref = bf16[4,416,128]{2,1,0:T(8,128)(2,1)S(1)} custom-call(f32[8,2,128,128]{3,2,1,0:T(8,128)} %state_ref.5, bf16[8,3,2,384]{3,2,1,0:T(2,128)(2,1)} %edge_ref.3, bf16[8,16,2,384]{3,2,1,0:T(2,128)(2,1)} %draft_ref.3), custom_call_target="tpu_custom_call" | custom-call | flops 500000 | bytes 1000000 | tf_op jit(solution)/shard_map/pack_far/pallas_call | solution.py:49
  1.9 0.0 copy-start.4
  1.9 7.8 %collective-permute-start.1 = (bf16[4,416,128]{2,1,0:T(8,128)(2,1)S(1)}, bf16[4,416,128]{2,1,0:T(8,128)(2,1)S(1)}, u32[]{:S(2)}, u32[]{:S(2)}) collective-permute-start(bf16[4,416,128]{2,1,0:T(8,128)(2,1)S(1)} %pack_far.1.far_ref), channel_id=1, source_target_pairs={{0,63},{1,2},{2,1},{3,4},{4,3},{5,6},{6,5},{7,8},{8,7},{9,10},{10,... | collective-permute-start | bytes 1277960 | tf_op jit(solution)/shard_map/ppermute | solution.py:557
  9.8 1.3 %pack_near.1 = (bf16[4,400,128]{2,1,0:T(8,128)(2,1)S(1)}, bf16[256,512]{1,0:T(8,128)(2,1)S(1)}, bf16[256,512]{1,0:T(8,128)(2,1)S(1)}) custom-call(f32[8,2,128,128]{3,2,1,0:T(8,128)} %state_ref.5, bf16[8,3,2,384]{3,2,1,0:T(2,128)(2,1)} %edge_ref.3, bf16[8,16,2,384]{3,2,1,0:T(2,128)(2,1)} %draft_ref.3, bf16[256,2048]{1,0:T(8,128)(2,1)} %weight_ref.5), custom_call_target="tpu_custom_call" | custom-call | flops 500000 | bytes 2000000 | tf_op jit(solution)/shard_map/pack_near/pallas_call | solution.py:49
  11.1 0.1 collective-permute-start
  11.2 0.9 %collective-permute-start.4 = (bf16[256,512]{1,0:T(8,128)(2,1)S(1)}, bf16[256,512]{1,0:T(8,128)(2,1)S(1)}, u32[]{:S(2)}, u32[]{:S(2)}) collective-permute-start(bf16[256,512]{1,0:T(8,128)(2,1)S(1)} %get-tuple-element.35), channel_id=1, source_target_pairs={{0,64},{64,0},{128,192},{192,128},{1,65},{65,1},{129,193},{193,129... | collective-permute-start | bytes 786440 | tf_op jit(solution)/shard_map/ppermute | solution.py:530
  12.1 0.0 copy-start
  12.1 0.0 copy-start.1
  12.1 0.0 copy-start.5
  12.1 1.1 %collective-permute-start.5 = (bf16[256,512]{1,0:T(8,128)(2,1)S(1)}, bf16[256,512]{1,0:T(8,128)(2,1)S(1)}, u32[]{:S(2)}, u32[]{:S(2)}) collective-permute-start(bf16[256,512]{1,0:T(8,128)(2,1)S(1)} %get-tuple-element.36), channel_id=1, source_target_pairs={{0,192},{64,128},{128,64},{192,0},{1,193},{65,129},{129,65},{193,1... | collective-permute-start | bytes 786440 | tf_op jit(solution)/shard_map/ppermute | solution.py:530
  13.3 0.0 collective-permute-done.from_near_ref
  13.3 2.3 %mix_near.1 = (bf16[4,16,256]{2,1,0:T(8,128)(2,1)S(1)}, f32[4,2,16,128]{3,2,1,0:T(8,128)S(1)}, f32[4,2,16,128]{3,2,1,0:T(8,128)S(1)}, f32[4,2,16,128]{3,2,1,0:T(...) custom-call(s32[512]{0:T(512)} %owner_ref.5, ...), custom_call_target="tpu_custom_call" | custom-call | flops 15000000 | bytes 3000000 | tf_op jit(solution)/shard_map/mix_near/pallas_call | solution.py:49
  15.6 0.0 collective-permute-done.1.from_far_ref
  15.6 0.0 copy-done.2
  15.6 1.5 %mix_far.1 = (bf16[8,16,256]{2,1,0:T(8,128)(2,1)S(1)}, bf16[128,512]{1,0:T(8,128)(2,1)S(1)}) custom-call(s32[512]{0:T(512)} %owner_ref.5, bf16[4,16,256]{2,1,0:T(8,128)(2,1)S(1)} %get-tuple-element.28.near_mixed_ref, bf16[4,416,128]{2,1,0:T(8,128)(2,1)S(1)} %pack_far.1.far_ref, bf16[4,416,128]{2,1,0:T(8,128)(2,1)S(1)} %collective-permute-done.1.from_far_ref, ...), custom_call_target="tpu_custom_call" | custom-call | flops 50000000 | bytes 2000000 | tf_op jit(solution)/shard_map/mix_far/pallas_call | solution.py:49
  17.1 2.1 %collective-permute-start.6 = (bf16[128,512]{1,0:T(8,128)(2,1)S(1)}, bf16[128,512]{1,0:T(8,128)(2,1)S(1)}, u32[]{:S(2)}, u32[]{:S(2)}) collective-permute-start(bf16[128,512]{1,0:T(8,128)(2,1)S(1)} %get-tuple-element.37), channel_id=1, source_target_pairs={{0,128},{64,192},{128,0},{192,64},{1,129},{65,193},{129,1},{193,65... | collective-permute-start | bytes 393224 | tf_op jit(solution)/shard_map/ppermute | solution.py:530
  19.2 1.6 %collective-permute-start.3 = (bf16[128,256]{1,0:T(8,128)(2,1)S(1)}, bf16[128,256]{1,0:T(8,128)(2,1)S(1)}, u32[]{:S(2)}, u32[]{:S(2)}) collective-permute-start(bf16[128,256]{1,0:T(8,128)(2,1)S(1)} %bitcast.11), channel_id=1, source_target_pairs={{0,192},{64,128},{128,64},{192,0},{1,193},{65,129},{129,65},{193,1... | collective-permute-start | bytes 196616 | tf_op jit(solution)/shard_map/ppermute | solution.py:530
  20.9 0.0 collective-permute-start.2
  20.9 0.0 collective-permute-done.4.from_one_ref
  20.9 3.9 %collective-permute-done.5.from_three_ref = bf16[256,512]{1,0:T(8,128)(2,1)S(1)} collective-permute-done((bf16[256,512]{1,0:T(8,128)(2,1)S(1)}, bf16[256,512]{1,0:T(8,128)(2,1)S(1)}, u32[]{:S(2)}, u32[]{:S(2)}) %collective-permute-start.5) | collective-permute-done | bytes 262176 | tf_op jit(solution)/shard_map/ppermute | solution.py:530
  24.8 1.1 %collective-permute-done.3.three_ref = bf16[128,256]{1,0:T(8,128)(2,1)S(1)} collective-permute-done((bf16[128,256]{1,0:T(8,128)(2,1)S(1)}, bf16[128,256]{1,0:T(8,128)(2,1)S(1)}, u32[]{:S(2)}, u32[]{:S(2)}) %collective-permute-start.3) | collective-permute-done | bytes 65568 | tf_op jit(solution)/shard_map/ppermute | solution.py:530
  25.9 0.0 collective-permute-done.2.one_ref
  25.9 0.0 collective-permute-done.6.part_ref
  25.9 0.0 copy-done.4
  25.9 0.3 project.1.own_ref
  26.2 1.6 %collective-permute-start.9 = (bf16[128,512]{1,0:T(8,128)(2,1)S(1)}, bf16[128,512]{1,0:T(8,128)(2,1)S(1)}, u32[]{:S(2)}, u32[]{:S(2)}) collective-permute-start(bf16[128,512]{1,0:T(8,128)(2,1)S(1)} %project.1.own_ref), channel_id=1, source_target_pairs={{0,192},{64,128},{128,64},{192,0},{1,193},{65,129},{129,65},{193,1... | collective-permute-start | bytes 393224 | tf_op jit(solution)/shard_map/ppermute | solution.py:530
  27.8 1.1 %collective-permute-start.8 = (bf16[128,512]{1,0:T(8,128)(2,1)S(1)}, bf16[128,512]{1,0:T(8,128)(2,1)S(1)}, u32[]{:S(2)}, u32[]{:S(2)}) collective-permute-start(bf16[128,512]{1,0:T(8,128)(2,1)S(1)} %project.1.own_ref), channel_id=1, source_target_pairs={{0,128},{64,192},{128,0},{192,64},{1,129},{65,193},{129,1},{193,65... | collective-permute-start | bytes 393224 | tf_op jit(solution)/shard_map/ppermute | solution.py:530
  28.9 1.5 %collective-permute-start.7 = (bf16[128,512]{1,0:T(8,128)(2,1)S(1)}, bf16[128,512]{1,0:T(8,128)(2,1)S(1)}, u32[]{:S(2)}, u32[]{:S(2)}) collective-permute-start(bf16[128,512]{1,0:T(8,128)(2,1)S(1)} %project.1.own_ref), channel_id=1, source_target_pairs={{0,64},{64,0},{128,192},{192,128},{1,65},{65,1},{129,193},{193,129... | collective-permute-start | bytes 393224 | tf_op jit(solution)/shard_map/ppermute | solution.py:530
  30.4 5.0 %collective-permute-done.9.three_ref = bf16[128,512]{1,0:T(8,128)(2,1)S(1)} collective-permute-done((bf16[128,512]{1,0:T(8,128)(2,1)S(1)}, bf16[128,512]{1,0:T(8,128)(2,1)S(1)}, u32[]{:S(2)}, u32[]{:S(2)}) %collective-permute-start.9) | collective-permute-done | bytes 131104 | tf_op jit(solution)/shard_map/ppermute | solution.py:530
  35.4 0.3 collective-permute-done.8.two_ref
  35.7 0.0 copy-done
  35.7 0.0 copy-done.1
  35.7 0.0 copy-done.5
  35.7 0.0 copy-start.3
  35.7 1.4 %ffn_first.1 = (f32[128,128]{1,0:T(8,128)S(1)}, f32[128,704]{1,0:T(8,128)S(1)}, f32[128,704]{1,0:T(8,128)S(1)}) custom-call(bf16[128,512]{1,0:T(8,128)(2,1)S(1)} %project.1.own_ref, bf16[128,512]{1,0:T(8,128)(2,1)S(1)} %collective-permute-done.8.two_ref, bf16[128,512]{1,0:T(8,128)(2,1)S(1)} %collective-permute-done.9.three_ref, f32[1,2048]{1,0:T(1,128)S(1)} %bitcast.14, ...), custom_call_target="tpu_custom_call" | custom-call | flops 550000000 | bytes 5000000 | tf_op jit(solution)/shard_map/ffn_first/pallas_call | solution.py:49
  37.1 0.0 collective-permute-done.7.one_ref
  37.2 0.3 copy-done.3
  37.5 1.8 %ffn_last.1 = (f32[128,512]{1,0:T(8,128)S(1)}, bf16[128,512]{1,0:T(8,128)(2,1)S(1)}, bf16[128,512]{1,0:T(8,128)(2,1)S(1)}, bf16[128,512]{1,0:T(8,128)(2,1)S(1)}) custom-call(s32[512]{0:T(512)} %length_ref.1, bf16[128,512]{1,0:T(8,128)(2,1)S(1)} %project.1.own_ref, bf16[128,512]{1,0:T(8,128)(2,1)S(1)} %collective-permute-done.7.one_ref, ...), custom_call_target="tpu_custom_call" | custom-call | flops 550000000 | bytes 5000000 | tf_op jit(solution)/shard_map/ffn_last/pallas_call | solution.py:49
  39.3 1.8 %collective-permute-start.10 = (bf16[128,512]{1,0:T(8,128)(2,1)S(1)}, bf16[128,512]{1,0:T(8,128)(2,1)S(1)}, u32[]{:S(2)}, u32[]{:S(2)}) collective-permute-start(bf16[128,512]{1,0:T(8,128)(2,1)S(1)} %get-tuple-element.43), channel_id=1, source_target_pairs={{0,192},{64,128},{128,64},{192,0},{1,193},{65,129},{129,65},{193,1... | collective-permute-start | bytes 393224 | tf_op jit(solution)/shard_map/ppermute | solution.py:530
  41.2 0.1 collective-permute-start.11
  41.3 2.2 %collective-permute-start.12 = (bf16[128,512]{1,0:T(8,128)(2,1)S(1)}, bf16[128,512]{1,0:T(8,128)(2,1)S(1)}, u32[]{:S(2)}, u32[]{:S(2)}) collective-permute-start(bf16[128,512]{1,0:T(8,128)(2,1)S(1)} %get-tuple-element.45), channel_id=1, source_target_pairs={{0,64},{64,0},{128,192},{192,128},{1,65},{65,1},{129,193},{193,129... | collective-permute-start | bytes 393224 | tf_op jit(solution)/shard_map/ppermute | solution.py:530
  43.5 3.7 %keep.1 = (f32[8,2,128,128]{3,2,1,0:T(8,128)}, bf16[8,3,2,384]{3,2,1,0:T(2,128)(2,1)}) custom-call(s32[512]{0:T(512)} %owner_ref.5, s32[512]{0:T(512)} %accept_ref.1, bf16[4,400,128]{2,1,0:T(8,128)(2,1)S(1)} %get-tuple-element.27.near_ref, bf16[4,416,128]{2,1,0:T(8,128)(2,1)S(1)} %pack_far.1.far_ref, ...), custom_call_target="tpu_custom_call" | custom-call | flops 20000000 | bytes 3000000 | tf_op jit(solution)/shard_map/keep/pallas_call | solution.py:49
  47.3 0.0 collective-permute-done.10
  47.3 0.4 collective-permute-done.11
  47.6 0.2 collective-permute-done.12
  47.8 0.7 %add_convert_fusion = bf16[128,512]{1,0:T(8,128)(2,1)} fusion(bf16[128,512]{1,0:T(8,128)(2,1)S(1)} %collective-permute-done.12, bf16[128,512]{1,0:T(8,128)(2,1)S(1)} %collective-permute-done.11, f32[128,512]{1,0:T(8,128)S(1)} %get-tuple-element.42, bf16[128,512]{1,0:T(8,128)(2,1)S(1)} %collective-permute-done.10), kind=kLoop, calls=%fused_computation | loop fusion | flops 458752 | bytes 786432 | tf_op jit(solution)/shard_map/convert_element_type | solution.py:589
Async XLA Ops:
  0.6 15.0 %copy-start.2 = (bf16[256,2048]{1,0:T(8,128)(2,1)S(1)}, bf16[256,2048]{1,0:T(8,128)(2,1)}, u32[]{:S(2)}) copy-start(bf16[256,2048]{1,0:T(8,128)(2,1)} %weight_ref.5) | copy-start | bytes 3145732
  1.9 24.0 %copy-start.4 = (bf16[8,16,2048]{2,1,0:T(8,128)(2,1)S(1)}, bf16[8,16,2048]{2,1,0:T(8,128)(2,1)}, u32[]{:S(2)}) copy-start(bf16[8,16,2048]{2,1,0:T(8,128)(2,1)} %param.20) | copy-start | bytes 1572868
  1.9 13.7 %collective-permute-start.1 = (bf16[4,416,128]{2,1,0:T(8,128)(2,1)S(1)}, bf16[4,416,128]{2,1,0:T(8,128)(2,1)S(1)}, u32[]{:S(2)}, u32[]{:S(2)}) collective-permute-start(bf16[4,416,128]{2,1,0:T(8,128)(2,1)S(1)} %pack_far.1.far_ref), channel_id=1, source_target_pairs={{0,63},{1,2},{2,1},{3,4},{4,3},{5,6},{6,5},{7,8},{8,7},{9,10},{10,... | collective-permute-start | bytes 1277960 | tf_op jit(solution)/shard_map/ppermute | solution.py:557
  11.1 2.2 %collective-permute-start = (bf16[4,400,128]{2,1,0:T(8,128)(2,1)S(1)}, bf16[4,400,128]{2,1,0:T(8,128)(2,1)S(1)}, u32[]{:S(2)}, u32[]{:S(2)}) collective-permute-start(bf16[4,400,128]{2,1,0:T(8,128)(2,1)S(1)} %get-tuple-element.27.near_ref), channel_id=1, source_target_pairs={{0,1},{1,0},{2,3},{3,2},{4,5},{5,4},{6,7},{7,6},{8,9},{9,8},{10,11... | collective-permute-start | bytes 1228808 | tf_op jit(solution)/shard_map/ppermute | solution.py:559
  11.2 9.7 %collective-permute-start.4 = (bf16[256,512]{1,0:T(8,128)(2,1)S(1)}, bf16[256,512]{1,0:T(8,128)(2,1)S(1)}, u32[]{:S(2)}, u32[]{:S(2)}) collective-permute-start(bf16[256,512]{1,0:T(8,128)(2,1)S(1)} %get-tuple-element.35), channel_id=1, source_target_pairs={{0,64},{64,0},{128,192},{192,128},{1,65},{65,1},{129,193},{193,129... | collective-permute-start | bytes 786440 | tf_op jit(solution)/shard_map/ppermute | solution.py:530
  12.1 23.6 %copy-start = (bf16[2048,704]{0,1:T(8,128)(2,1)S(1)}, bf16[2048,704]{0,1:T(8,128)(2,1)}, u32[]{:S(2)}) copy-start(bf16[2048,704]{0,1:T(8,128)(2,1)} %param.22) | copy-start | bytes 8650756
  12.1 23.6 %copy-start.1 = (bf16[2048,704]{0,1:T(8,128)(2,1)S(1)}, bf16[2048,704]{0,1:T(8,128)(2,1)}, u32[]{:S(2)}) copy-start(bf16[2048,704]{0,1:T(8,128)(2,1)} %param.23) | copy-start | bytes 8650756
  12.1 23.6 %copy-start.5 = (f32[2048]{0:T(1024)S(1)}, f32[2048]{0:T(1024)}, u32[]{:S(2)}) copy-start(f32[2048]{0:T(1024)} %param.21) | copy-start | bytes 24580
  12.1 12.7 %collective-permute-start.5 = (bf16[256,512]{1,0:T(8,128)(2,1)S(1)}, bf16[256,512]{1,0:T(8,128)(2,1)S(1)}, u32[]{:S(2)}, u32[]{:S(2)}) collective-permute-start(bf16[256,512]{1,0:T(8,128)(2,1)S(1)} %get-tuple-element.36), channel_id=1, source_target_pairs={{0,192},{64,128},{128,64},{192,0},{1,193},{65,129},{129,65},{193,1... | collective-permute-start | bytes 786440 | tf_op jit(solution)/shard_map/ppermute | solution.py:530
  17.1 8.8 %collective-permute-start.6 = (bf16[128,512]{1,0:T(8,128)(2,1)S(1)}, bf16[128,512]{1,0:T(8,128)(2,1)S(1)}, u32[]{:S(2)}, u32[]{:S(2)}) collective-permute-start(bf16[128,512]{1,0:T(8,128)(2,1)S(1)} %get-tuple-element.37), channel_id=1, source_target_pairs={{0,128},{64,192},{128,0},{192,64},{1,129},{65,193},{129,1},{193,65... | collective-permute-start | bytes 393224 | tf_op jit(solution)/shard_map/ppermute | solution.py:530
  19.2 6.7 %collective-permute-start.3 = (bf16[128,256]{1,0:T(8,128)(2,1)S(1)}, bf16[128,256]{1,0:T(8,128)(2,1)S(1)}, u32[]{:S(2)}, u32[]{:S(2)}) collective-permute-start(bf16[128,256]{1,0:T(8,128)(2,1)S(1)} %bitcast.11), channel_id=1, source_target_pairs={{0,192},{64,128},{128,64},{192,0},{1,193},{65,129},{129,65},{193,1... | collective-permute-start | bytes 196616 | tf_op jit(solution)/shard_map/ppermute | solution.py:530
  20.9 5.0 %collective-permute-start.2 = (bf16[128,256]{1,0:T(8,128)(2,1)S(1)}, bf16[128,256]{1,0:T(8,128)(2,1)S(1)}, u32[]{:S(2)}, u32[]{:S(2)}) collective-permute-start(bf16[128,256]{1,0:T(8,128)(2,1)S(1)} %bitcast.12), channel_id=1, source_target_pairs={{0,64},{64,0},{128,192},{192,128},{1,65},{65,1},{129,193},{193,129... | collective-permute-start | bytes 196616 | tf_op jit(solution)/shard_map/ppermute | solution.py:530
  26.2 9.2 %collective-permute-start.9 = (bf16[128,512]{1,0:T(8,128)(2,1)S(1)}, bf16[128,512]{1,0:T(8,128)(2,1)S(1)}, u32[]{:S(2)}, u32[]{:S(2)}) collective-permute-start(bf16[128,512]{1,0:T(8,128)(2,1)S(1)} %project.1.own_ref), channel_id=1, source_target_pairs={{0,192},{64,128},{128,64},{192,0},{1,193},{65,129},{129,65},{193,1... | collective-permute-start | bytes 393224 | tf_op jit(solution)/shard_map/ppermute | solution.py:530
  27.8 7.9 %collective-permute-start.8 = (bf16[128,512]{1,0:T(8,128)(2,1)S(1)}, bf16[128,512]{1,0:T(8,128)(2,1)S(1)}, u32[]{:S(2)}, u32[]{:S(2)}) collective-permute-start(bf16[128,512]{1,0:T(8,128)(2,1)S(1)} %project.1.own_ref), channel_id=1, source_target_pairs={{0,128},{64,192},{128,0},{192,64},{1,129},{65,193},{129,1},{193,65... | collective-permute-start | bytes 393224 | tf_op jit(solution)/shard_map/ppermute | solution.py:530
  28.9 8.2 %collective-permute-start.7 = (bf16[128,512]{1,0:T(8,128)(2,1)S(1)}, bf16[128,512]{1,0:T(8,128)(2,1)S(1)}, u32[]{:S(2)}, u32[]{:S(2)}) collective-permute-start(bf16[128,512]{1,0:T(8,128)(2,1)S(1)} %project.1.own_ref), channel_id=1, source_target_pairs={{0,64},{64,0},{128,192},{192,128},{1,65},{65,1},{129,193},{193,129... | collective-permute-start | bytes 393224 | tf_op jit(solution)/shard_map/ppermute | solution.py:530
  35.7 1.8 %copy-start.3 = (bf16[704,2048]{1,0:T(8,128)(2,1)S(1)}, bf16[704,2048]{1,0:T(8,128)(2,1)}, u32[]{:S(2)}) copy-start(bf16[704,2048]{1,0:T(8,128)(2,1)} %down_ref.1) | copy-start | bytes 8650756
  39.3 7.9 %collective-permute-start.10 = (bf16[128,512]{1,0:T(8,128)(2,1)S(1)}, bf16[128,512]{1,0:T(8,128)(2,1)S(1)}, u32[]{:S(2)}, u32[]{:S(2)}) collective-permute-start(bf16[128,512]{1,0:T(8,128)(2,1)S(1)} %get-tuple-element.43), channel_id=1, source_target_pairs={{0,192},{64,128},{128,64},{192,0},{1,193},{65,129},{129,65},{193,1... | collective-permute-start | bytes 393224 | tf_op jit(solution)/shard_map/ppermute | solution.py:530
  41.2 6.5 %collective-permute-start.11 = (bf16[128,512]{1,0:T(8,128)(2,1)S(1)}, bf16[128,512]{1,0:T(8,128)(2,1)S(1)}, u32[]{:S(2)}, u32[]{:S(2)}) collective-permute-start(bf16[128,512]{1,0:T(8,128)(2,1)S(1)} %get-tuple-element.44), channel_id=1, source_target_pairs={{0,128},{64,192},{128,0},{192,64},{1,129},{65,193},{129,1},{193,65... | collective-permute-start | bytes 393224 | tf_op jit(solution)/shard_map/ppermute | solution.py:530
  41.3 6.6 %collective-permute-start.12 = (bf16[128,512]{1,0:T(8,128)(2,1)S(1)}, bf16[128,512]{1,0:T(8,128)(2,1)S(1)}, u32[]{:S(2)}, u32[]{:S(2)}) collective-permute-start(bf16[128,512]{1,0:T(8,128)(2,1)S(1)} %get-tuple-element.45), channel_id=1, source_target_pairs={{0,64},{64,0},{128,192},{192,128},{1,65},{65,1},{129,193},{193,129... | collective-permute-start | bytes 393224 | tf_op jit(solution)/shard_map/ppermute | solution.py:530
